TPU v7x, 32 devices: a whole 2x2x4 slice. The times are simulated.
32 devices in a mesh: tm: 8 (over z, x), head: 4 (over y, core).
Axes of the slice: x: 2, y: 2, z: 4, core: 2. Of those that a mesh axis runs over, the one named last changes fastest.
Arguments:
- query_vectors: bfloat16 [4096, 5120], P('tm', 'head'), may hold values from -10 to 10
- key_vectors: bfloat16 [4096, 5120], P('tm', 'head'), may hold values from -4 to 4
- value_vectors: bfloat16 [4096, 5120], P('tm', 'head'), may hold values from -8 to 8
- band_table: int32 [8, 8], replicated, may hold values from 0 to 4, as said below
- out_weight: bfloat16 [5120, 5120], P('head'), may hold values from -0.078125 to 0.078125
Outputs:
- block_output: bfloat16 [4096, 5120], P('tm', 'head')
Inputs may be any that keep to these rules, and one draw needn't show every extreme that they name: band_table[t][t] is 0; for t != s it is b or b + 1, where b is the number of binary digits of |t - s|.
All inputs are finite; a program needn't handle non-finite values.
Results may differ from a plain program's by a relative error of at most 0.012.
Values may be sent and summed in bfloat16 or wider, within the bound.
No kernel may reach another device: no remote copies, remote signals or barrier semaphores. Data moves between devices by JAX's collectives and lax.ppermute only.
A program may use at most 256 MiB of HBM per device.

v0:
```python
import math

import jax
import jax.numpy as jnp
import numpy as np
from jax import lax
from jax.experimental import pallas as pl
from jax.experimental.pallas import tpu as pltpu
from jax.sharding import PartitionSpec as P

HEAD_DIM = 128
MASKED = -1e30
AXES = ("tm", "head")
F32 = jnp.float32
BF16 = jnp.bfloat16


def prefix_order(row_count):
    rows = np.arange(0, row_count, 2)
    zeros = [(r & -r).bit_length() if r else 64 for r in rows.tolist()]
    return rows[np.argsort([-z for z in zeros], kind="stable")]


def pack_kernel(order_ref, key_ref, value_ref, *out_refs, cuts):
    picks = order_ref.shape[0]
    row_count = key_ref.shape[0]
    column = lax.broadcasted_iota(jnp.int32, (picks, row_count), 1)
    choose = jnp.where(order_ref[...] == column, 1.0, 0.0).astype(BF16)
    for plane, source in enumerate((key_ref, value_ref)):
        picked = jnp.dot(choose, source[...], preferred_element_type=F32).astype(BF16)
        for out_ref, (low, high) in zip(out_refs, cuts):
            out_ref[plane] = picked[low:high]


def pack(key_vectors, value_vectors, order, cuts):
    row_count, width = key_vectors.shape
    tile = 256
    picks = len(order)
    rows = jnp.asarray(order.astype(np.int32)[:, None])
    return pl.pallas_call(
        lambda *refs: pack_kernel(*refs, cuts=cuts),
        grid=(width // tile,),
        in_specs=[
            pl.BlockSpec((picks, 1), lambda j: (0, 0)),
            pl.BlockSpec((row_count, tile), lambda j: (0, j)),
            pl.BlockSpec((row_count, tile), lambda j: (0, j)),
        ],
        out_specs=[
            pl.BlockSpec((2, high - low, tile), lambda j: (0, 0, j)) for low, high in cuts
        ],
        out_shape=[jax.ShapeDtypeStruct((2, high - low, width), BF16) for low, high in cuts],
        name="pack",
        cost_estimate=pl.CostEstimate(
            flops=4 * picks * row_count * width, bytes_accessed=8 * row_count * width, transcendentals=0
        ),
    )(rows, key_vectors, value_vectors)


def attend_kernel(*refs, buffers, own, first, last, row_tile):
    refs = list(refs)
    query_ref = refs.pop(0)
    if own:
        keys = [refs.pop(0)[...]]
        values = [refs.pop(0)[...]]
    else:
        keys, values = ([], [])
    for _ in range(buffers):
        packed = refs.pop(0)
        keys.append(packed[0])
        values.append(packed[1])
    bias = None if own else refs.pop(0)[...]
    if not first:
        state_in, accum_in = (refs.pop(0), refs.pop(0))
    out_refs = refs
    key = keys[0] if len(keys) == 1 else jnp.concatenate(keys, axis=0)
    value = values[0] if len(values) == 1 else jnp.concatenate(values, axis=0)
    factor = math.log2(math.e) / math.sqrt(HEAD_DIM)
    for low in range(0, query_ref.shape[0], row_tile):
        rows = pl.ds(low, row_tile)
        scores = lax.dot_general(
            query_ref[rows, :], key, (((1,), (1,)), ((), ())), preferred_element_type=F32
        )
        scores = scores * factor
        if bias is not None:
            scores = scores + bias
        top = jnp.max(scores, axis=1, keepdims=True)
        if not first:
            top_in = state_in[rows, :][:, :1]
            top = jnp.maximum(top, top_in)
            shrink = jnp.exp2(top_in - top)
        weights = jnp.exp2(scores - top)
        total = jnp.sum(weights, axis=1, keepdims=True)
        accum = jnp.dot(weights.astype(BF16), value, preferred_element_type=F32)
        if not first:
            total = total + shrink * state_in[rows, :][:, 64:65]
            accum = accum + shrink * accum_in[rows, :]
        if last:
            out_refs[0][rows, :] = (accum / total).astype(BF16)
        else:
            lane = lax.broadcasted_iota(jnp.int32, (row_tile, HEAD_DIM), 1)
            out_refs[0][rows, :] = jnp.where(lane < 64, top, total)
            out_refs[1][rows, :] = accum


def attend(query_vectors, own_pair, buffers, bias, carry, last, name):
    row_count, width = query_vectors.shape
    head_count = width // HEAD_DIM
    whole = pl.BlockSpec((row_count, HEAD_DIM), lambda h: (0, h))
    operands, specs = ([query_vectors], [whole])
    own = own_pair is not None
    count = 0
    if own:
        operands += list(own_pair)
        specs += [whole, whole]
        count += row_count
    for buffer in buffers:
        operands.append(buffer)
        specs.append(pl.BlockSpec((2, buffer.shape[1], HEAD_DIM), lambda h: (0, 0, h)))
        count += buffer.shape[1]
    if not own:
        operands.append(bias)
        specs.append(pl.BlockSpec((1, count), lambda h: (0, 0)))
    first = carry is None
    if not first:
        operands += list(carry)
        specs += [whole, whole]
    if last:
        shapes = [jax.ShapeDtypeStruct((row_count, width), BF16)]
    else:
        shapes = [jax.ShapeDtypeStruct((row_count, width), F32)] * 2
    return pl.pallas_call(
        lambda *refs: attend_kernel(
            *refs, buffers=len(buffers), own=own, first=first, last=last, row_tile=256
        ),
        grid=(head_count,),
        in_specs=specs,
        out_specs=[whole] * len(shapes),
        out_shape=shapes,
        name=name,
        cost_estimate=pl.CostEstimate(
            flops=4 * row_count * count * width,
            bytes_accessed=4 * row_count * width,
            transcendentals=row_count * count * head_count,
        ),
    )(*operands)


def project_kernel(place_ref, mine_ref, other_ref, weight_ref, moved_ref, out_ref):
    total = jnp.dot(mine_ref[...], weight_ref[...], preferred_element_type=F32)
    total = total + jnp.dot(other_ref[...], moved_ref[...], preferred_element_type=F32)
    out_ref[...] = total.astype(out_ref.dtype)


def project(place, mine, other, weight, moved, half, out_type, name):
    rows, depth = mine.shape
    width = moved.shape[1]
    tile = 256
    steps = width // tile
    return pl.pallas_call(
        project_kernel,
        grid_spec=pltpu.PrefetchScalarGridSpec(
            num_scalar_prefetch=1,
            grid=(steps,),
            in_specs=[
                pl.BlockSpec((rows, depth), lambda j, place: (0, 0)),
                pl.BlockSpec((rows, depth), lambda j, place: (0, 0)),
                pl.BlockSpec((depth, tile), lambda j, place: (0, place[0] * steps + j)),
                pl.BlockSpec((depth, tile), lambda j, place: (half, j)),
            ],
            out_specs=pl.BlockSpec((rows, tile), lambda j, place: (0, j)),
        ),
        out_shape=jax.ShapeDtypeStruct((rows, width), out_type),
        name=name,
        cost_estimate=pl.CostEstimate(
            flops=4 * rows * depth * width, bytes_accessed=4 * depth * width, transcendentals=0
        ),
    )(place, mine, other, weight, moved)


def per_device(query_vectors, key_vectors, value_vectors, band_table, out_weight):
    row_count, width = query_vectors.shape
    block_count = lax.axis_size("tm")
    group_count = lax.axis_size("head")
    my_block = lax.axis_index("tm")
    my_group = lax.axis_index("head")
    table_row = lax.dynamic_index_in_dim(band_table, my_block, 0, keepdims=False)

    def move(array, block_to, group_to=lambda h: h):
        route = []
        for t in range(block_count):
            for h in range(group_count):
                to = block_to(t)
                if to is not None and 0 <= to < block_count:
                    route.append((t * group_count + h, to * group_count + group_to(h)))
        return lax.ppermute(array, AXES, route)

    def bias_of(pieces):
        blocks = jnp.stack([jnp.asarray(block, jnp.int32) for block, _, _ in pieces])
        number = np.concatenate([np.full(n, i) for i, (_, _, n) in enumerate(pieces)])
        rank = np.concatenate([np.arange(a, a + n) for _, a, n in pieces]).astype(np.int32)
        member = jnp.asarray(number[None, :] == np.arange(len(pieces))[:, None])
        here = jnp.arange(block_count, dtype=jnp.int32)[None, :] == blocks[:, None]
        band = jnp.sum(jnp.where(here, table_row[None, :], 0), axis=1)
        kept = jnp.where(jnp.any(here, axis=1), jnp.right_shift(jnp.int32(row_count), band), 0)
        limit = jnp.sum(jnp.where(member, kept[:, None], 0), axis=0)
        return jnp.where(jnp.asarray(rank) < limit, 0.0, MASKED).astype(F32)[None, :]

    order = prefix_order(row_count)
    near = row_count // 2
    if block_count == 8:
        a, ab = (row_count // 8, row_count // 4)
        even = my_block % 2 == 0
        side = jnp.where(even, 1, -1)
        z = my_block // 2
        sent_bc, sent_a, sent_ab = pack(
            key_vectors, value_vectors, order, [(a, near), (0, a), (0, ab)]
        )
        twin = lambda t: t ^ 1
        far_way = lambda t: t + 2 if t % 2 == 0 else t - 2
        near_way = lambda t: t - 2 if t % 2 == 0 else t + 2
        x_bc = move(sent_bc, twin)
        x_a = move(sent_a, twin)
        z_far = move(sent_ab, far_way)
        z_near = move(sent_ab, near_way)
        z_two = move(sent_ab, lambda t: t ^ 4)
        near_bc = move(x_bc, far_way)
        cross_far = move(z_far, lambda t: t ^ 1 if 0 <= (t - 2 if t % 2 == 0 else t + 2) < 8 else None)
        cross_near = move(
            z_near[:, :a], lambda t: t ^ 1 if 0 <= (t + 2 if t % 2 == 0 else t - 2) < 8 else None
        )
        z_three = move(z_two[:, :a], lambda t: {4: 6, 5: 7, 2: 0, 3: 1}.get(t))
        cross_two = move(z_two, twin)
        cross_three = move(z_three, lambda t: t ^ 1 if t in (0, 1, 6, 7) else None)
        partner = my_block ^ 1
        far_block = my_block - 2 * side
        near_block = my_block + 2 * side
        two = my_block ^ 4
        three = jnp.where((z == 0) | (z == 3), 6 - 2 * z + my_block % 2, -1)
        adjacent = my_block - side
        far_cross = my_block + 3 * side
        two_cross = two ^ 1
        three_cross = jnp.where(three >= 0, three ^ 1, -1)
        stages = [
            [(x_bc, partner, a), (x_a, partner, 0), (z_far, far_block, 0), (z_near, near_block, 0)],
            [
                (z_two, two, 0),
                (near_bc, adjacent, a),
                (cross_near, adjacent, 0),
                (cross_far, far_cross, 0),
            ],
            [(cross_two, two_cross, 0), (z_three, three, 0), (cross_three, three_cross, 0)],
        ]
    else:
        (packed,) = pack(key_vectors, value_vectors, order, [(0, near)])
        received, blocks = ([], [])
        for distance in range(1, block_count):
            rows = row_count >> distance.bit_length()
            for sign in (1, -1):
                received.append(move(packed[:, :rows], lambda t: t + sign * distance))
                blocks.append((my_block - sign * distance, 0, rows))
        joined = jnp.concatenate(received, axis=1)
        stages = [[(joined, blocks)]]

    core = lambda h: h ^ 1
    mine = my_group % 2
    level = my_group // 2
    out_width = out_weight.shape[1] // group_count
    columns = lambda number: lax.dynamic_slice_in_dim(out_weight, number * out_width, out_width, 1)
    theirs = jnp.concatenate(
        [columns(2 * (1 - level) + 1 - mine), columns(2 * level + 1 - mine)], axis=0
    )
    moved = move(theirs, lambda t: t, core)

    carry = attend(query_vectors, (key_vectors, value_vectors), [], None, None, False, "own")
    for number, stage in enumerate(stages):
        last = number == len(stages) - 1
        if block_count == 8:
            pieces = [(block, low, buffer.shape[1]) for buffer, block, low in stage]
            buffers = [buffer for buffer, _, _ in stage]
        else:
            buffers = [stage[0][0]]
            pieces = stage[0][1]
        carry = attend(
            query_vectors, None, buffers, bias_of(pieces), carry, last, f"stage{number}"
        )
    attention = carry[0]
    other = move(attention, lambda t: t, core)
    away = jnp.reshape(2 * (1 - level) + mine, (1,))
    home = jnp.reshape(2 * level + mine, (1,))
    sent = project(away, attention, other, out_weight, moved, 0, BF16, "away")
    arrived = move(sent, lambda t: t, lambda h: h ^ 2)
    kept = project(home, attention, other, out_weight, moved, 1, F32, "home")
    return (kept + arrived.astype(F32)).astype(BF16)


def solution(mesh):
    in_specs = (P("tm", "head"), P("tm", "head"), P("tm", "head"), P(), P("head", None))
    out_specs = P("tm", "head")
    return jax.shard_map(
        per_device, mesh=mesh, in_specs=in_specs, out_specs=out_specs, check_vma=False
    )
```

profile of v0, /device:TPU:0, one launch (start us, length us, event | category | flops | bytes accessed | tf_op | source)
XLA Modules:
  0.0 191.3 jit_solution(7310970954001800927)
XLA Ops:
  0.0 3.4 %constant_dynamic-slice_fusion.1 = (bf16[1280,1280]{1,0:T(8,128)(2,1)S(1)}, bf16[1280,1280]{1,0:T(8,128)(2,1)S(1)}) fusion(bf16[1280,5120]{1,0:T(8,128)(2,1)} %weight_ref.3, s32[]{:T(128)S(6)} %select_n.117, s32[]{:T(128)S(6)} %select_n.118), kind=kLoop, calls=%fused_computation.18 | loop fusion | bytes 13107208 | tf_op jit(solution)/shard_map/dynamic_slice | solution.py:268
  3.4 3.1 %pad_maximum_fusion = bf16[2560,1280]{1,0:T(8,128)(2,1)} fusion(bf16[1280,1280]{1,0:T(8,128)(2,1)S(1)} %get-tuple-element.26, bf16[1280,1280]{1,0:T(8,128)(2,1)S(1)} %get-tuple-element.25), kind=kLoop, calls=%fused_computation | loop fusion | flops 13107200 | bytes 13107200 | tf_op jit(solution)/shard_map/concatenate | solution.py:269
  7.1 5.1 %pack.1 = (bf16[2,192,1280]{2,1,0:T(8,128)(2,1)}, bf16[2,64,1280]{2,1,0:T(8,128)(2,1)}, bf16[2,128,1280]{2,1,0:T(8,128)(2,1)}) custom-call(s32[256,1]{1,0:T(8,128)} %constant.87.clone.refs_0_, bf16[512,1280]{1,0:T(8,128)(2,1)} %refs_1_.3, bf16[512,1280]{1,0:T(8,128)(2,1)} %refs_2_.3), custom_call_target="tpu_custom_call" | custom-call | flops 671088640 | bytes 5242880 | tf_op jit(solution)/shard_map/pack/pallas_call | solution.py:40
  13.5 6.0 %collective-permute-start.8 = (bf16[2,128,1280]{2,1,0:T(8,128)(2,1)}, bf16[2,128,1280]{2,1,0:T(8,128)(2,1)}, u32[]{:S(2)}, u32[]{:S(2)}) collective-permute-start(bf16[2,128,1280]{2,1,0:T(8,128)(2,1)} %get-tuple-element.14), channel_id=1, source_target_pairs={{0,8},{1,9},{2,10},{3,11},{8,16},{9,17},{10,18},{11,19},{12,4},{13... | collective-permute-start | bytes 1966088 | tf_op jit(solution)/shard_map/ppermute | solution.py:195
  19.4 2.3 %collective-permute-start = (bf16[2,128,1280]{2,1,0:T(8,128)(2,1)}, bf16[2,128,1280]{2,1,0:T(8,128)(2,1)S(1)}, u32[]{:S(2)}, u32[]{:S(2)}) collective-permute-start(bf16[2,128,1280]{2,1,0:T(8,128)(2,1)} %get-tuple-element.14), channel_id=1, source_target_pairs={{0,16},{1,17},{2,18},{3,19},{4,20},{5,21},{6,22},{7,23},{8,24},{9,... | collective-permute-start | bytes 1966088 | tf_op jit(solution)/shard_map/ppermute | solution.py:195
  21.7 1.5 collective-permute-start.4
  24.9 20.3 %collective-permute-done.4.refs_1_ = bf16[2,192,1280]{2,1,0:T(8,128)(2,1)S(1)} collective-permute-done((bf16[2,192,1280]{2,1,0:T(8,128)(2,1)}, bf16[2,192,1280]{2,1,0:T(8,128)(2,1)S(1)}, u32[]{:S(2)}, u32[]{:S(2)}) %collective-permute-start.4) | collective-permute-done | bytes 983072 | tf_op jit(solution)/shard_map/ppermute | solution.py:195
  45.2 4.0 %collective-permute-start.5 = (bf16[2,192,1280]{2,1,0:T(8,128)(2,1)S(1)}, bf16[2,192,1280]{2,1,0:T(8,128)(2,1)S(1)}, u32[]{:S(2)}, u32[]{:S(2)}) collective-permute-start(bf16[2,192,1280]{2,1,0:T(8,128)(2,1)S(1)} %collective-permute-done.4.refs_1_), channel_id=1, source_target_pairs={{0,8},{1,9},{2,10},{3,11},{8,16},{9,17},{10,18},{11,19},{12,4},{13... | collective-permute-start | bytes 2949128 | tf_op jit(solution)/shard_map/ppermute | solution.py:195
  49.9 4.7 %collective-permute-start.7 = (bf16[2,64,1280]{2,1,0:T(8,128)(2,1)S(1)}, bf16[2,64,1280]{2,1,0:T(8,128)(2,1)}, u32[]{:S(2)}, u32[]{:S(2)}) collective-permute-start(bf16[2,64,1280]{2,1,0:T(8,128)(2,1)S(1)} %slice.9), channel_id=1, source_target_pairs={{0,4},{1,5},{2,6},{3,7},{8,12},{9,13},{10,14},{11,15},{12,8},{13,9... | collective-permute-start | bytes 983048 | tf_op jit(solution)/shard_map/ppermute | solution.py:195
  54.7 6.8 %collective-permute-done.refs_1_ = bf16[2,128,1280]{2,1,0:T(8,128)(2,1)S(1)} collective-permute-done((bf16[2,128,1280]{2,1,0:T(8,128)(2,1)}, bf16[2,128,1280]{2,1,0:T(8,128)(2,1)S(1)}, u32[]{:S(2)}, u32[]{:S(2)}) %collective-permute-start) | collective-permute-done | bytes 655392 | tf_op jit(solution)/shard_map/ppermute | solution.py:195
  62.9 1.3 collective-permute-start.2
  64.2 6.5 %collective-permute-start.1 = (bf16[2,128,1280]{2,1,0:T(8,128)(2,1)S(1)}, bf16[2,128,1280]{2,1,0:T(8,128)(2,1)}, u32[]{:S(2)}, u32[]{:S(2)}) collective-permute-start(bf16[2,128,1280]{2,1,0:T(8,128)(2,1)S(1)} %collective-permute-done.refs_1_), channel_id=1, source_target_pairs={{0,4},{1,5},{2,6},{3,7},{4,0},{5,1},{6,2},{7,3},{8,12},{9,13},{10,... | collective-permute-start | bytes 1966088 | tf_op jit(solution)/shard_map/ppermute | solution.py:195
  71.3 2.9 %collective-permute-done.2.refs_2_ = bf16[2,64,1280]{2,1,0:T(8,128)(2,1)} collective-permute-done((bf16[2,64,1280]{2,1,0:T(8,128)(2,1)S(1)}, bf16[2,64,1280]{2,1,0:T(8,128)(2,1)}, u32[]{:S(2)}, u32[]{:S(2)}) %collective-permute-start.2) | collective-permute-done | bytes 327712 | tf_op jit(solution)/shard_map/ppermute | solution.py:195
  74.2 19.4 %collective-permute-start.3 = (bf16[2,64,1280]{2,1,0:T(8,128)(2,1)}, bf16[2,64,1280]{2,1,0:T(8,128)(2,1)}, u32[]{:S(2)}, u32[]{:S(2)}) collective-permute-start(bf16[2,64,1280]{2,1,0:T(8,128)(2,1)} %collective-permute-done.2.refs_2_), channel_id=1, source_target_pairs={{0,4},{1,5},{2,6},{3,7},{4,0},{5,1},{6,2},{7,3},{24,28},{25,29},{2... | collective-permute-start | bytes 983048 | tf_op jit(solution)/shard_map/ppermute | solution.py:195
  93.5 11.3 %own.1 = (f32[512,1280]{1,0:T(8,128)}, f32[512,1280]{1,0:T(8,128)}) custom-call(bf16[512,1280]{1,0:T(8,128)(2,1)} %refs_0_.8, bf16[512,1280]{1,0:T(8,128)(2,1)} %refs_1_.3, bf16[512,1280]{1,0:T(8,128)(2,1)} %refs_2_.3), custom_call_target="tpu_custom_call" | custom-call | flops 1342177280 | bytes 2621440 | tf_op jit(solution)/shard_map/own/pallas_call | solution.py:131
  104.9 13.3 %stage0.1 = (f32[512,1280]{1,0:T(8,128)}, f32[512,1280]{1,0:T(8,128)}) custom-call(bf16[512,1280]{1,0:T(8,128)(2,1)} %refs_0_.8, bf16[2,192,1280]{2,1,0:T(8,128)(2,1)} %copy-done.5, bf16[2,64,1280]{2,1,0:T(8,128)(2,1)} %copy-done.7, bf16[2,128,1280]{2,1,0:T(8,128)(2,1)} %collective-permute-done.8.refs_3_, bf16[2,128,1280]{2,1,0:T(8,128)(2,1)} %copy-done.4, ...), custom_call_target="tpu_custom_call" | custom-call | flops 1342177280 | bytes 2621440 | tf_op jit(solution)/shard_map/stage0/pallas_call | solution.py:131
  119.1 13.3 %stage1.1 = (f32[512,1280]{1,0:T(8,128)}, f32[512,1280]{1,0:T(8,128)}) custom-call(bf16[512,1280]{1,0:T(8,128)(2,1)} %refs_0_.8, bf16[2,128,1280]{2,1,0:T(8,128)(2,1)} %copy-done.3, bf16[2,192,1280]{2,1,0:T(8,128)(2,1)} %copy-done.6, bf16[2,64,1280]{2,1,0:T(8,128)(2,1)} %collective-permute-done.7.refs_3_, ...), custom_call_target="tpu_custom_call" | custom-call | flops 1342177280 | bytes 2621440 | tf_op jit(solution)/shard_map/stage1/pallas_call | solution.py:131
  132.4 12.1 %stage2.1.mine_ref = bf16[512,1280]{1,0:T(8,128)(2,1)} custom-call(bf16[512,1280]{1,0:T(8,128)(2,1)} %refs_0_.8, bf16[2,128,1280]{2,1,0:T(8,128)(2,1)} %collective-permute-done.1.refs_1_, bf16[2,64,1280]{2,1,0:T(8,128)(2,1)} %collective-permute-done.2.refs_2_, bf16[2,64,1280]{2,1,0:T(8,128)(2,1)} %collective-permute-done.3.refs_3_, f32[1,256]{1,0:T(1,128)} %bitcast.18, ...), custom_call_target="tpu_custom_call" | custom-call | flops 671088640 | bytes 2621440 | tf_op jit(solution)/shard_map/stage2/pallas_call | solution.py:131
  144.5 3.2 %collective-permute-done.11.other_ref = bf16[512,1280]{1,0:T(8,128)(2,1)S(1)} collective-permute-done((bf16[512,1280]{1,0:T(8,128)(2,1)}, bf16[512,1280]{1,0:T(8,128)(2,1)S(1)}, u32[]{:S(2)}, u32[]{:S(2)}) %collective-permute-start.11) | collective-permute-done | bytes 1310752 | tf_op jit(solution)/shard_map/ppermute | solution.py:195
  148.8 8.2 %away.1 = bf16[512,1280]{1,0:T(8,128)(2,1)} custom-call(s32[1]{0:T(128)} %bitcast.14.place_ref, bf16[512,1280]{1,0:T(8,128)(2,1)} %stage2.1.mine_ref, bf16[512,1280]{1,0:T(8,128)(2,1)} %copy-done.2, bf16[1280,5120]{1,0:T(8,128)(2,1)} %weight_ref.3, bf16[2560,1280]{1,0:T(8,128)(2,1)} %collective-permute-done.12.moved_ref), custom_call_target="tpu_custom_call" | custom-call | flops 3355443200 | bytes 6553600 | tf_op jit(solution)/shard_map/away/pallas_call | solution.py:159
  157.1 1.5 collective-permute-start.13
  158.6 8.6 %home.1 = f32[512,1280]{1,0:T(8,128)} custom-call(s32[1]{0:T(128)} %bitcast.place_ref, bf16[512,1280]{1,0:T(8,128)(2,1)} %stage2.1.mine_ref, bf16[512,1280]{1,0:T(8,128)(2,1)} %copy-done.2, bf16[1280,5120]{1,0:T(8,128)(2,1)} %weight_ref.3, bf16[2560,1280]{1,0:T(8,128)(2,1)} %collective-permute-done.12.moved_ref), custom_call_target="tpu_custom_call" | custom-call | flops 3355443200 | bytes 6553600 | tf_op jit(solution)/shard_map/home/pallas_call | solution.py:159
  167.2 20.9 %collective-permute-done.13 = bf16[512,1280]{1,0:T(8,128)(2,1)S(1)} collective-permute-done((bf16[512,1280]{1,0:T(8,128)(2,1)}, bf16[512,1280]{1,0:T(8,128)(2,1)S(1)}, u32[]{:S(2)}, u32[]{:S(2)}) %collective-permute-start.13) | collective-permute-done | bytes 1310752 | tf_op jit(solution)/shard_map/ppermute | solution.py:195
  188.1 3.1 %add_convert_fusion = bf16[512,1280]{1,0:T(8,128)(2,1)} fusion(f32[512,1280]{1,0:T(8,128)} %home.1, bf16[512,1280]{1,0:T(8,128)(2,1)S(1)} %collective-permute-done.13), kind=kLoop, calls=%fused_computation.1 | loop fusion | flops 1966080 | bytes 5242880 | tf_op jit(solution)/shard_map/convert_element_type | solution.py:293
  (61 shorter events, 8.3 us)
Async XLA Ops:
  0.0 23.2 %copy-start = (s32[8,8]{1,0:T(8,128)S(1)}, s32[8,8]{1,0:T(8,128)}, u32[]{:S(2)}) copy-start(s32[8,8]{1,0:T(8,128)} %param.15) | copy-start | bytes 772
  6.5 17.7 %copy-start.13 = (pred[3,256]{1,0:T(4,128)(4,1)S(1)}, pred[3,256]{1,0:T(4,128)(4,1)}, u32[]{:S(2)}) copy-start(pred[3,256]{1,0:T(4,128)(4,1)} %constant.92.clone) | copy-start | bytes 2308
  6.5 17.8 %copy-start.9 = (s32[512]{0:T(512)S(1)}, s32[512]{0:T(512)}, u32[]{:S(2)}) copy-start(s32[512]{0:T(512)} %constant.89.clone) | copy-start | bytes 6148
  6.5 42.7 %copy-start.12 = (s32[256]{0:T(256)S(1)}, s32[256]{0:T(256)}, u32[]{:S(2)}) copy-start(s32[256]{0:T(256)} %constant.93.clone) | copy-start | bytes 3076
  6.5 64.1 %copy-start.10 = (pred[4,512]{1,0:T(4,128)(4,1)S(1)}, pred[4,512]{1,0:T(4,128)(4,1)}, u32[]{:S(2)}) copy-start(pred[4,512]{1,0:T(4,128)(4,1)} %constant.90.clone) | copy-start | bytes 6148
  6.5 64.2 %copy-start.8 = (s32[512]{0:T(512)S(1)}, s32[512]{0:T(512)}, u32[]{:S(2)}) copy-start(s32[512]{0:T(512)} %constant.91.clone) | copy-start | bytes 6148
  6.6 141.2 %collective-permute-start.12 = (bf16[2560,1280]{1,0:T(8,128)(2,1)}, bf16[2560,1280]{1,0:T(8,128)(2,1)}, u32[]{:S(2)}, u32[]{:S(2)}) collective-permute-start(bf16[2560,1280]{1,0:T(8,128)(2,1)} %pad_maximum_fusion), channel_id=1, source_target_pairs={{0,1},{1,0},{2,3},{3,2},{4,5},{5,4},{6,7},{7,6},{8,9},{9,8},{10,11... | collective-permute-start | bytes 19660808 | tf_op jit(solution)/shard_map/ppermute | solution.py:195
  12.2 37.7 %collective-permute-start.6 = (bf16[2,128,1280]{2,1,0:T(8,128)(2,1)}, bf16[2,128,1280]{2,1,0:T(8,128)(2,1)S(1)}, u32[]{:S(2)}, u32[]{:S(2)}) collective-permute-start(bf16[2,128,1280]{2,1,0:T(8,128)(2,1)} %get-tuple-element.14), channel_id=1, source_target_pairs={{4,12},{5,13},{6,14},{7,15},{8,0},{9,1},{10,2},{11,3},{12,20},{13,... | collective-permute-start | bytes 1966088 | tf_op jit(solution)/shard_map/ppermute | solution.py:195
  13.5 36.4 %collective-permute-start.8 = (bf16[2,128,1280]{2,1,0:T(8,128)(2,1)}, bf16[2,128,1280]{2,1,0:T(8,128)(2,1)}, u32[]{:S(2)}, u32[]{:S(2)}) collective-permute-start(bf16[2,128,1280]{2,1,0:T(8,128)(2,1)} %get-tuple-element.14), channel_id=1, source_target_pairs={{0,8},{1,9},{2,10},{3,11},{8,16},{9,17},{10,18},{11,19},{12,4},{13... | collective-permute-start | bytes 1966088 | tf_op jit(solution)/shard_map/ppermute | solution.py:195
  19.4 42.1 %collective-permute-start = (bf16[2,128,1280]{2,1,0:T(8,128)(2,1)}, bf16[2,128,1280]{2,1,0:T(8,128)(2,1)S(1)}, u32[]{:S(2)}, u32[]{:S(2)}) collective-permute-start(bf16[2,128,1280]{2,1,0:T(8,128)(2,1)} %get-tuple-element.14), channel_id=1, source_target_pairs={{0,16},{1,17},{2,18},{3,19},{4,20},{5,21},{6,22},{7,23},{8,24},{9,... | collective-permute-start | bytes 1966088 | tf_op jit(solution)/shard_map/ppermute | solution.py:195
  21.7 23.5 %collective-permute-start.4 = (bf16[2,192,1280]{2,1,0:T(8,128)(2,1)}, bf16[2,192,1280]{2,1,0:T(8,128)(2,1)S(1)}, u32[]{:S(2)}, u32[]{:S(2)}) collective-permute-start(bf16[2,192,1280]{2,1,0:T(8,128)(2,1)} %get-tuple-element.15), channel_id=1, source_target_pairs={{0,4},{1,5},{2,6},{3,7},{4,0},{5,1},{6,2},{7,3},{8,12},{9,13},{10,... | collective-permute-start | bytes 2949128 | tf_op jit(solution)/shard_map/ppermute | solution.py:195
  45.2 59.6 %copy-start.5 = (bf16[2,192,1280]{2,1,0:T(8,128)(2,1)}, bf16[2,192,1280]{2,1,0:T(8,128)(2,1)S(1)}, u32[]{:S(2)}) copy-start(bf16[2,192,1280]{2,1,0:T(8,128)(2,1)S(1)} %collective-permute-done.4.refs_1_) | copy-start | bytes 2949124
  45.2 72.9 %collective-permute-start.5 = (bf16[2,192,1280]{2,1,0:T(8,128)(2,1)S(1)}, bf16[2,192,1280]{2,1,0:T(8,128)(2,1)S(1)}, u32[]{:S(2)}, u32[]{:S(2)}) collective-permute-start(bf16[2,192,1280]{2,1,0:T(8,128)(2,1)S(1)} %collective-permute-done.4.refs_1_), channel_id=1, source_target_pairs={{0,8},{1,9},{2,10},{3,11},{8,16},{9,17},{10,18},{11,19},{12,4},{13... | collective-permute-start | bytes 2949128 | tf_op jit(solution)/shard_map/ppermute | solution.py:195
  49.9 55.0 %copy-start.4 = (bf16[2,128,1280]{2,1,0:T(8,128)(2,1)}, bf16[2,128,1280]{2,1,0:T(8,128)(2,1)S(1)}, u32[]{:S(2)}) copy-start(bf16[2,128,1280]{2,1,0:T(8,128)(2,1)S(1)} %collective-permute-done.6.refs_4_) | copy-start | bytes 1966084
  49.9 13.0 %collective-permute-start.10 = (bf16[2,64,1280]{2,1,0:T(8,128)(2,1)}, bf16[2,64,1280]{2,1,0:T(8,128)(2,1)S(1)}, u32[]{:S(2)}, u32[]{:S(2)}) collective-permute-start(bf16[2,64,1280]{2,1,0:T(8,128)(2,1)} %get-tuple-element.16), channel_id=1, source_target_pairs={{0,4},{1,5},{2,6},{3,7},{4,0},{5,1},{6,2},{7,3},{8,12},{9,13},{10,... | collective-permute-start | bytes 983048 | tf_op jit(solution)/shard_map/ppermute | solution.py:195
  49.9 14.3 %collective-permute-start.7 = (bf16[2,64,1280]{2,1,0:T(8,128)(2,1)S(1)}, bf16[2,64,1280]{2,1,0:T(8,128)(2,1)}, u32[]{:S(2)}, u32[]{:S(2)}) collective-permute-start(bf16[2,64,1280]{2,1,0:T(8,128)(2,1)S(1)} %slice.9), channel_id=1, source_target_pairs={{0,4},{1,5},{2,6},{3,7},{8,12},{9,13},{10,14},{11,15},{12,8},{13,9... | collective-permute-start | bytes 983048 | tf_op jit(solution)/shard_map/ppermute | solution.py:195
  61.5 43.4 %copy-start.3 = (bf16[2,128,1280]{2,1,0:T(8,128)(2,1)}, bf16[2,128,1280]{2,1,0:T(8,128)(2,1)S(1)}, u32[]{:S(2)}) copy-start(bf16[2,128,1280]{2,1,0:T(8,128)(2,1)S(1)} %collective-permute-done.refs_1_) | copy-start | bytes 1966084
  61.5 56.7 %collective-permute-start.9 = (bf16[2,128,1280]{2,1,0:T(8,128)(2,1)}, bf16[2,128,1280]{2,1,0:T(8,128)(2,1)}, u32[]{:S(2)}, u32[]{:S(2)}) collective-permute-start(bf16[2,128,1280]{2,1,0:T(8,128)(2,1)} %collective-permute-done.8.refs_3_), channel_id=1, source_target_pairs={{4,0},{5,1},{6,2},{7,3},{8,12},{9,13},{10,14},{11,15},{12,8},{13,9... | collective-permute-start | bytes 1966088 | tf_op jit(solution)/shard_map/ppermute | solution.py:195
  62.9 11.3 %collective-permute-start.2 = (bf16[2,64,1280]{2,1,0:T(8,128)(2,1)S(1)}, bf16[2,64,1280]{2,1,0:T(8,128)(2,1)}, u32[]{:S(2)}, u32[]{:S(2)}) collective-permute-start(bf16[2,64,1280]{2,1,0:T(8,128)(2,1)S(1)} %slice.8), channel_id=1, source_target_pairs={{8,0},{9,1},{10,2},{11,3},{12,4},{13,5},{14,6},{15,7},{16,24},{17,... | collective-permute-start | bytes 983048 | tf_op jit(solution)/shard_map/ppermute | solution.py:195
  64.2 68.2 %collective-permute-start.1 = (bf16[2,128,1280]{2,1,0:T(8,128)(2,1)S(1)}, bf16[2,128,1280]{2,1,0:T(8,128)(2,1)}, u32[]{:S(2)}, u32[]{:S(2)}) collective-permute-start(bf16[2,128,1280]{2,1,0:T(8,128)(2,1)S(1)} %collective-permute-done.refs_1_), channel_id=1, source_target_pairs={{0,4},{1,5},{2,6},{3,7},{4,0},{5,1},{6,2},{7,3},{8,12},{9,13},{10,... | collective-permute-start | bytes 1966088 | tf_op jit(solution)/shard_map/ppermute | solution.py:195
  74.2 58.2 %collective-permute-start.3 = (bf16[2,64,1280]{2,1,0:T(8,128)(2,1)}, bf16[2,64,1280]{2,1,0:T(8,128)(2,1)}, u32[]{:S(2)}, u32[]{:S(2)}) collective-permute-start(bf16[2,64,1280]{2,1,0:T(8,128)(2,1)} %collective-permute-done.2.refs_2_), channel_id=1, source_target_pairs={{0,4},{1,5},{2,6},{3,7},{4,0},{5,1},{6,2},{7,3},{24,28},{25,29},{2... | collective-permute-start | bytes 983048 | tf_op jit(solution)/shard_map/ppermute | solution.py:195
  144.5 3.2 %collective-permute-start.11 = (bf16[512,1280]{1,0:T(8,128)(2,1)}, bf16[512,1280]{1,0:T(8,128)(2,1)S(1)}, u32[]{:S(2)}, u32[]{:S(2)}) collective-permute-start(bf16[512,1280]{1,0:T(8,128)(2,1)} %stage2.1.mine_ref), channel_id=1, source_target_pairs={{0,1},{1,0},{2,3},{3,2},{4,5},{5,4},{6,7},{7,6},{8,9},{9,8},{10,11... | collective-permute-start | bytes 3932168 | tf_op jit(solution)/shard_map/ppermute | solution.py:195
  157.1 31.0 %collective-permute-start.13 = (bf16[512,1280]{1,0:T(8,128)(2,1)}, bf16[512,1280]{1,0:T(8,128)(2,1)S(1)}, u32[]{:S(2)}, u32[]{:S(2)}) collective-permute-start(bf16[512,1280]{1,0:T(8,128)(2,1)} %away.1), channel_id=1, source_target_pairs={{0,2},{1,3},{2,0},{3,1},{4,6},{5,7},{6,4},{7,5},{8,10},{9,11},{10,... | collective-permute-start | bytes 3932168 | tf_op jit(solution)/shard_map/ppermute | solution.py:195
  158.6 32.7 %copy-start.1 = (s32[8,8]{1,0:T(8,128)S(1)}, s32[8,8]{1,0:T(8,128)}, u32[]{:S(2)}) copy-start(s32[8,8]{1,0:T(8,128)} %param.15) | copy-start | bytes 772
  (4 other events, 20.9 us)
where the time goes:
time: 193 us; the launch traced here: 191 us
  Pallas kernels  71.9 us (37%)
  waiting for transfers between devices  54.1 us (28%)
  starting transfers between devices  50.1 us (26%)
  other arithmetic  9.42 us (5%)
  local copies, waits for them, and re-layouts  5.45 us (3%)
    ppermute x14, waiting for transfers between devices, move(): return lax.ppermute(array, AXES, route)  54.1 us
    ppermute x14, starting transfers between devices, move(): return lax.ppermute(array, AXES, route)  50.1 us
    pallas_call x4, Pallas kernels, attend(): pl.pallas_call(lambda *refs: attend_kernel(*refs, buffers=len(buffers), o...  50 us
    pallas_call x2, Pallas kernels, project(): pl.pallas_call(project_kernel, grid_spec=pltpu.PrefetchScalarGridSpec(num...  16.8 us
    pallas_call x1, Pallas kernels, pack(): pl.pallas_call(lambda *refs: pack_kernel(*refs, cuts=cuts), grid=(width /...  5.09 us
  transfers between devices with their start and end apart: 14, of which 5 were waited for; matrix products, arithmetic and copies ran while one was open for 2% of the time, Pallas kernels for 33%

commit v1 on v0

v1 whole, which is shorter than its diff:
```python
import math

import jax
import jax.numpy as jnp
import numpy as np
from jax import lax
from jax.experimental import pallas as pl
from jax.experimental.pallas import tpu as pltpu
from jax.sharding import PartitionSpec as P

HEAD_DIM = 128
MASKED = -1e30
AXES = ("tm", "head")
F32 = jnp.float32
BF16 = jnp.bfloat16


def prefix_order(row_count):
    rows = np.arange(0, row_count, 2)
    zeros = [(r & -r).bit_length() if r else 64 for r in rows.tolist()]
    return rows[np.argsort([-z for z in zeros], kind="stable")]


def pack_kernel(order_ref, key_ref, value_ref, *out_refs, cuts):
    picks = order_ref.shape[0]
    row_count = key_ref.shape[0]
    column = lax.broadcasted_iota(jnp.int32, (picks, row_count), 1)
    choose = jnp.where(order_ref[...] == column, 1.0, 0.0).astype(BF16)
    for plane, source in enumerate((key_ref, value_ref)):
        picked = jnp.dot(choose, source[...], preferred_element_type=F32).astype(BF16)
        for out_ref, (low, high) in zip(out_refs, cuts):
            out_ref[plane] = picked[low:high]


def pack(key_vectors, value_vectors, order, cuts):
    row_count, width = key_vectors.shape
    tile = width // 2
    picks = len(order)
    rows = jnp.asarray(order.astype(np.int32)[:, None])
    return pl.pallas_call(
        lambda *refs: pack_kernel(*refs, cuts=cuts),
        grid=(width // tile,),
        in_specs=[
            pl.BlockSpec((picks, 1), lambda j: (0, 0)),
            pl.BlockSpec((row_count, tile), lambda j: (0, j)),
            pl.BlockSpec((row_count, tile), lambda j: (0, j)),
        ],
        out_specs=[
            pl.BlockSpec((2, high - low, tile), lambda j: (0, 0, j)) for low, high in cuts
        ],
        out_shape=[jax.ShapeDtypeStruct((2, high - low, width), BF16) for low, high in cuts],
        name="pack",
        compiler_params=pltpu.CompilerParams(vmem_limit_bytes=48 << 20),
        cost_estimate=pl.CostEstimate(
            flops=4 * picks * row_count * width, bytes_accessed=8 * row_count * width, transcendentals=0
        ),
    )(rows, key_vectors, value_vectors)


def attend_kernel(*refs, buffers, own, first, last, heads):
    refs = list(refs)
    query_ref = refs.pop(0)
    own_refs = [refs.pop(0), refs.pop(0)] if own else None
    packed_refs = [refs.pop(0) for _ in range(buffers)]
    bias_ref = refs.pop(0)
    state_in, accum_in = (None, None) if first else (refs.pop(0), refs.pop(0))
    query_count = query_ref.shape[0]
    factor = math.log2(math.e) / math.sqrt(HEAD_DIM)
    bias = jnp.concatenate([bias_ref[...]] * (query_count // HEAD_DIM), axis=1)
    for head in range(heads):
        span = slice(head * HEAD_DIM, (head + 1) * HEAD_DIM)
        keys = [ref[0, :, span] for ref in packed_refs]
        values = [ref[1, :, span] for ref in packed_refs]
        key = keys[0] if len(keys) == 1 else jnp.concatenate(keys, axis=0)
        value = values[0] if len(values) == 1 else jnp.concatenate(values, axis=0)
        query = query_ref[:, span]
        by_last = (((1,), (1,)), ((), ()))
        scores = lax.dot_general(key, query, by_last, preferred_element_type=F32) + bias
        top = jnp.max(scores, axis=0, keepdims=True)
        if own:
            own_scores = lax.dot_general(
                own_refs[0][:, span], query, by_last, preferred_element_type=F32
            )
            top = jnp.maximum(top, jnp.max(own_scores, axis=0, keepdims=True))
        if not first:
            top_in = state_in[head, 0:1, :]
            top = jnp.maximum(top, top_in)
            shrink = jnp.exp2((top_in - top) * factor)
        level = top * factor
        weights = jnp.exp2(scores * factor - level)
        total = jnp.sum(weights, axis=0, keepdims=True)
        accum = jnp.dot(value.T, weights.astype(BF16), preferred_element_type=F32)
        if own:
            own_weights = jnp.exp2(own_scores * factor - level)
            total = total + jnp.sum(own_weights, axis=0, keepdims=True)
            accum = accum + jnp.dot(
                own_refs[1][:, span].T, own_weights.astype(BF16), preferred_element_type=F32
            )
        if not first:
            total = total + shrink * state_in[head, 1:2, :]
            accum = accum + shrink * accum_in[head]
        if last:
            refs[0][:, span] = (accum / total).T.astype(BF16)
        else:
            refs[0][head, 0:1, :] = top
            refs[0][head, 1:2, :] = total
            refs[1][head] = accum


def attend(query_vectors, own_pair, buffers, bias, carry, last, heads, name):
    row_count, width = query_vectors.shape
    head_count = width // HEAD_DIM
    span = heads * HEAD_DIM
    whole = pl.BlockSpec((row_count, span), lambda h: (0, h))
    state = pl.BlockSpec((heads, 8, row_count), lambda h: (h, 0, 0))
    accum = pl.BlockSpec((heads, HEAD_DIM, row_count), lambda h: (h, 0, 0))
    operands, specs = ([query_vectors], [whole])
    own = own_pair is not None
    count = bias.shape[0]
    if own:
        operands += list(own_pair)
        specs += [whole, whole]
    for buffer in buffers:
        operands.append(buffer)
        specs.append(pl.BlockSpec((2, buffer.shape[1], span), lambda h: (0, 0, h)))
    operands.append(bias)
    specs.append(pl.BlockSpec((count, HEAD_DIM), lambda h: (0, 0)))
    first = carry is None
    if not first:
        operands += list(carry)
        specs += [state, accum]
    if last:
        shapes = [jax.ShapeDtypeStruct((row_count, width), BF16)]
        out_specs = [whole]
    else:
        shapes = [
            jax.ShapeDtypeStruct((head_count, 8, row_count), F32),
            jax.ShapeDtypeStruct((head_count, HEAD_DIM, row_count), F32),
        ]
        out_specs = [state, accum]
    total = count + (row_count if own else 0)
    return pl.pallas_call(
        lambda *refs: attend_kernel(
            *refs, buffers=len(buffers), own=own, first=first, last=last, heads=heads
        ),
        grid=(head_count // heads,),
        in_specs=specs,
        out_specs=out_specs,
        out_shape=shapes,
        name=name,
        compiler_params=pltpu.CompilerParams(vmem_limit_bytes=48 << 20),
        cost_estimate=pl.CostEstimate(
            flops=4 * row_count * total * width,
            bytes_accessed=8 * row_count * width,
            transcendentals=row_count * total * head_count,
        ),
    )(*operands)


def per_device(query_vectors, key_vectors, value_vectors, band_table, out_weight):
    row_count, width = query_vectors.shape
    block_count = lax.axis_size("tm")
    group_count = lax.axis_size("head")
    my_block = lax.axis_index("tm")
    my_group = lax.axis_index("head")
    table_row = lax.dynamic_index_in_dim(band_table, my_block, 0, keepdims=False)

    def move(array, block_to, group_to=lambda h: h):
        route = []
        for t in range(block_count):
            for h in range(group_count):
                to = block_to(t)
                if to is not None and 0 <= to < block_count:
                    route.append((t * group_count + h, to * group_count + group_to(h)))
        return lax.ppermute(array, AXES, route)

    def bias_of(pieces):
        blocks = jnp.stack([jnp.asarray(block, jnp.int32) for block, _, _ in pieces])
        number = np.concatenate([np.full(n, i) for i, (_, _, n) in enumerate(pieces)])
        rank = np.concatenate([np.arange(a, a + n) for _, a, n in pieces]).astype(np.int32)
        member = jnp.asarray(number[None, :] == np.arange(len(pieces))[:, None])
        here = jnp.arange(block_count, dtype=jnp.int32)[None, :] == blocks[:, None]
        band = jnp.sum(jnp.where(here, table_row[None, :], 0), axis=1)
        kept = jnp.where(jnp.any(here, axis=1), jnp.right_shift(jnp.int32(row_count), band), 0)
        limit = jnp.sum(jnp.where(member, kept[:, None], 0), axis=0)
        bias = jnp.where(jnp.asarray(rank) < limit, 0.0, MASKED).astype(F32)
        return jnp.broadcast_to(bias[:, None], (rank.size, HEAD_DIM))

    order = prefix_order(row_count)
    near = row_count // 2
    if block_count == 8:
        a, ab = (row_count // 8, row_count // 4)
        side = jnp.where(my_block % 2 == 0, 1, -1)
        far_way = lambda t: t + 2 if t % 2 == 0 else t - 2
        near_way = lambda t: t - 2 if t % 2 == 0 else t + 2
        partner = my_block ^ 1
        far_block, near_block = (my_block - 2 * side, my_block + 2 * side)
        two, opposite = (my_block ^ 4, my_block ^ 6)
        adjacent, far_cross = (my_block - side, my_block + 3 * side)
        at_end = (my_block < 2) | (my_block >= block_count - 2)
        sent, sent_ab, sent_a = pack(key_vectors, value_vectors, order, [(0, near), (0, ab), (0, a)])
        x_rows = move(sent, lambda t: t ^ 1)
        z_far = move(sent_ab, far_way)
        z_near = move(sent_ab, near_way)
        z_two = move(sent_a, lambda t: t ^ 4)
        z_three = move(sent_a, lambda t: t ^ 6 if t in (0, 1, 6, 7) else None)
        x_rows, z_far, z_near, z_two, z_three, out_weight = lax.optimization_barrier(
            (x_rows, z_far, z_near, z_two, z_three, out_weight)
        )
        behind = x_rows[:, a:]
        has_far = (far_block >= 0) & (far_block < block_count)
        has_near = (near_block >= 0) & (near_block < block_count)
        slot_far = jnp.where(has_far, z_far[:, :a], z_three)
        slot_near = jnp.where(has_near, z_near[:, :a], z_three)
        relayed = jnp.concatenate([slot_far, z_far[:, a:], slot_near, z_two], axis=1)
        near_bc = move(behind, far_way)
        crossed = move(relayed, lambda t: t ^ 1)
        none = jnp.int32(-1)
        three = jnp.where(at_end, opposite, none)
        three_cross = jnp.where(at_end, opposite ^ 1, none)
        has_far_cross = (far_cross >= 0) & (far_cross < block_count)
        has_adjacent = (adjacent >= 0) & (adjacent < block_count)
        stages = [
            (
                [x_rows, z_far, z_near, z_two, z_three],
                [
                    (partner, 0, near),
                    (far_block, 0, ab),
                    (near_block, 0, ab),
                    (two, 0, a),
                    (three, 0, a),
                ],
            ),
            (
                [near_bc, crossed],
                [
                    (adjacent, a, near - a),
                    (jnp.where(has_far_cross, far_cross, three_cross), 0, a),
                    (far_cross, a, ab - a),
                    (jnp.where(has_adjacent, adjacent, three_cross), 0, a),
                    (two ^ 1, 0, a),
                    (my_block - 3 * side, a, ab - a),
                ],
            ),
        ]
    else:
        (packed,) = pack(key_vectors, value_vectors, order, [(0, near)])
        received, blocks = ([], [])
        for distance in range(1, block_count):
            rows = row_count >> distance.bit_length()
            for sign in (1, -1):
                received.append(move(packed[:, :rows], lambda t: t + sign * distance))
                blocks.append((my_block - sign * distance, 0, rows))
        stages = [
            ([jnp.concatenate(received[:2], axis=1)], blocks[:2]),
            ([jnp.concatenate(received[2:], axis=1)], blocks[2:]),
        ]

    own_pair = (key_vectors, value_vectors)
    buffers, pieces = stages[0]
    bias = bias_of(pieces)
    carry = attend(query_vectors, own_pair, buffers, bias, None, False, 2, "first")
    buffers, pieces = stages[1]
    if block_count == 8:
        near_bc, crossed = buffers
        near_bc, state = lax.optimization_barrier((near_bc, carry[0]))
        carry = (state, carry[1])
        buffers = [near_bc, crossed, move(near_bc[:, :a], far_way)]

    core = lambda h: h ^ 1
    same = lambda t: t
    mine = my_group % 2
    level = my_group // 2
    out_width = out_weight.shape[1] // group_count
    columns = lambda number: lax.dynamic_slice_in_dim(out_weight, number * out_width, out_width, 1)
    away, home = (2 * (1 - level) + mine, 2 * level + mine)
    moved = move(out_weight, same, core)

    carry = attend(query_vectors, None, buffers, bias_of(pieces), carry, True, 2, "second")
    attention = carry[0]
    other = move(attention, same, core)

    def project(number, low, span):
        start = number * out_width + low
        own_weight = lax.dynamic_slice_in_dim(out_weight, start, span, 1)
        other_weight = lax.dynamic_slice_in_dim(moved, start, span, 1)
        total = jnp.dot(attention, own_weight, preferred_element_type=F32)
        return total + jnp.dot(other, other_weight, preferred_element_type=F32)

    half = out_width // 2
    arrived = [
        move(project(away, low, half).astype(BF16), same, lambda h: h ^ 2) for low in (0, half)
    ]
    kept = project(home, 0, out_width)
    return (kept + jnp.concatenate(arrived, axis=1).astype(F32)).astype(BF16)


def solution(mesh):
    in_specs = (P("tm", "head"), P("tm", "head"), P("tm", "head"), P(), P("head", None))
    out_specs = P("tm", "head")
    return jax.shard_map(
        per_device, mesh=mesh, in_specs=in_specs, out_specs=out_specs, check_vma=False
    )
```

time: 193 us -> 142 us (0.74)
  the two profiles are of different devices: /device:TPU:0 before, /device:TPU:2 now
where the time goes in v1:
time: 142 us
  waiting for transfers between devices  70.3 us (50%)
  Pallas kernels  23 us (16%)
  starting transfers between devices  22 us (15%)
  matrix products  21.1 us (15%)
  local copies, waits for them, and re-layouts  4.12 us (3%)
    ppermute x12, waiting for transfers between devices, move(): return lax.ppermute(array, AXES, route)  70.3 us
    ppermute x12, starting transfers between devices, move(): return lax.ppermute(array, AXES, route)  22 us
    pallas_call x2, Pallas kernels, attend(): pl.pallas_call(lambda *refs: attend_kernel(*refs, buffers=len(buffers), o...  21.3 us
    dot_general x3, matrix products, project(): total = jnp.dot(attention, own_weight, preferred_element_type=F32)  12.1 us
    dot_general x3, matrix products, project(): return total + jnp.dot(other, other_weight, preferred_element_type=F32)  9.03 us
    unnamed x22, local copies, waits for them, and re-layouts  3.6 us
  transfers between devices with their start and end apart: 12, of which 7 were waited for; matrix products, arithmetic and copies ran while one was open for 8% of the time, Pallas kernels for 15%

profile of v1, /device:TPU:2, one launch (start us, length us, event | category | flops | bytes accessed | tf_op | source)
XLA Modules:
  0.0 142.0 jit_solution(11821349475754080351)
XLA Ops:
  0.0 1.3 copy-done.2
  1.3 1.3 copy-done.4
  3.6 1.7 %pack.1 = (bf16[2,256,1280]{2,1,0:T(8,128)(2,1)S(1)}, bf16[2,128,1280]{2,1,0:T(8,128)(2,1)S(1)}, bf16[2,64,1280]{2,1,0:T(8,128)(2,1)S(1)}) custom-call(s32[256,1]{1,0:T(8,128)S(1)} %copy-done.5, bf16[512,1280]{1,0:T(8,128)(2,1)S(1)} %copy-done.2, bf16[512,1280]{1,0:T(8,128)(2,1)S(1)} %copy-done.4), custom_call_target="tpu_custom_call" | custom-call | flops 671088640 | bytes 5242880 | tf_op jit(solution)/shard_map/pack/pallas_call | solution.py:40
  6.6 4.7 %collective-permute-start.2 = (bf16[2,128,1280]{2,1,0:T(8,128)(2,1)S(1)}, bf16[2,128,1280]{2,1,0:T(8,128)(2,1)S(1)}, u32[]{:S(2)}, u32[]{:S(2)}) collective-permute-start(bf16[2,128,1280]{2,1,0:T(8,128)(2,1)S(1)} %get-tuple-element.19), channel_id=1, source_target_pairs={{4,12},{5,13},{6,14},{7,15},{8,0},{9,1},{10,2},{11,3},{12,20},{13,... | collective-permute-start | bytes 1966088 | tf_op jit(solution)/shard_map/ppermute | solution.py:175
  11.3 3.1 %collective-permute-start.3 = (bf16[2,64,1280]{2,1,0:T(8,128)(2,1)S(1)}, bf16[2,64,1280]{2,1,0:T(8,128)(2,1)S(1)}, u32[]{:S(2)}, u32[]{:S(2)}) collective-permute-start(bf16[2,64,1280]{2,1,0:T(8,128)(2,1)S(1)} %get-tuple-element.20), channel_id=1, source_target_pairs={{0,16},{1,17},{2,18},{3,19},{4,20},{5,21},{6,22},{7,23},{8,24},{9,... | collective-permute-start | bytes 983048 | tf_op jit(solution)/shard_map/ppermute | solution.py:175
  14.4 3.2 %collective-permute-start.4 = (bf16[2,64,1280]{2,1,0:T(8,128)(2,1)S(1)}, bf16[2,64,1280]{2,1,0:T(8,128)(2,1)S(1)}, u32[]{:S(2)}, u32[]{:S(2)}) collective-permute-start(bf16[2,64,1280]{2,1,0:T(8,128)(2,1)S(1)} %get-tuple-element.20), channel_id=1, source_target_pairs={{0,24},{1,25},{2,26},{3,27},{4,28},{5,29},{6,30},{7,31},{24,0},{25... | collective-permute-start | bytes 983048 | tf_op jit(solution)/shard_map/ppermute | solution.py:175
  17.6 28.4 %collective-permute-done.3.refs_6_ = bf16[2,64,1280]{2,1,0:T(8,128)(2,1)S(1)} collective-permute-done((bf16[2,64,1280]{2,1,0:T(8,128)(2,1)S(1)}, bf16[2,64,1280]{2,1,0:T(8,128)(2,1)S(1)}, u32[]{:S(2)}, u32[]{:S(2)}) %collective-permute-start.3) | collective-permute-done | bytes 327712 | tf_op jit(solution)/shard_map/ppermute | solution.py:175
  47.0 4.8 %collective-permute-start.6 = (bf16[2,256,1280]{2,1,0:T(8,128)(2,1)S(1)}, bf16[2,256,1280]{2,1,0:T(8,128)(2,1)S(1)}, u32[]{:S(2)}, u32[]{:S(2)}) collective-permute-start(bf16[2,256,1280]{2,1,0:T(8,128)(2,1)S(1)} %pad_maximum_fusion), channel_id=1, source_target_pairs={{0,4},{1,5},{2,6},{3,7},{4,0},{5,1},{6,2},{7,3},{8,12},{9,13},{10,... | collective-permute-start | bytes 3932168 | tf_op jit(solution)/shard_map/ppermute | solution.py:175
  53.8 13.3 %first.1 = (f32[10,8,512]{2,1,0:T(8,128)S(1)}, f32[10,128,512]{2,1,0:T(8,128)}) custom-call(bf16[512,1280]{1,0:T(8,128)(2,1)S(1)} %copy-done.1, bf16[512,1280]{1,0:T(8,128)(2,1)S(1)} %copy-done.3, bf16[512,1280]{1,0:T(8,128)(2,1)} %refs_2_.3, bf16[2,256,1280]{2,1,0:T(8,128)(2,1)} %copy-done.6, bf16[2,128,1280]{2,1,0:T(8,128)(2,1)S(1)} %collective-permute-done.1.refs_4_, ...), custom_call_target="tpu_custom_call" | custom-call | flops 3019898880 | bytes 5242880 | tf_op jit(solution)/shard_map/first/pallas_call | solution.py:142
  67.1 10.4 %collective-permute-done.5.refs_1_ = bf16[2,192,1280]{2,1,0:T(8,128)(2,1)S(1)} collective-permute-done((bf16[2,192,1280]{2,1,0:T(8,128)(2,1)S(1)}, bf16[2,192,1280]{2,1,0:T(8,128)(2,1)S(1)}, u32[]{:S(2)}, u32[]{:S(2)}) %collective-permute-start.5) | collective-permute-done | bytes 983072 | tf_op jit(solution)/shard_map/ppermute | solution.py:175
  77.6 1.5 %collective-permute-start.7 = (bf16[2,64,1280]{2,1,0:T(8,128)(2,1)S(1)}, bf16[2,64,1280]{2,1,0:T(8,128)(2,1)S(1)}, u32[]{:S(2)}, u32[]{:S(2)}) collective-permute-start(bf16[2,64,1280]{2,1,0:T(8,128)(2,1)S(1)} %slice.19), channel_id=1, source_target_pairs={{0,8},{1,9},{2,10},{3,11},{8,16},{9,17},{10,18},{11,19},{12,4},{13... | collective-permute-start | bytes 983048 | tf_op jit(solution)/shard_map/ppermute | solution.py:175
  79.2 2.0 %collective-permute-done.6.refs_2_ = bf16[2,256,1280]{2,1,0:T(8,128)(2,1)S(1)} collective-permute-done((bf16[2,256,1280]{2,1,0:T(8,128)(2,1)S(1)}, bf16[2,256,1280]{2,1,0:T(8,128)(2,1)S(1)}, u32[]{:S(2)}, u32[]{:S(2)}) %collective-permute-start.6) | collective-permute-done | bytes 1310752 | tf_op jit(solution)/shard_map/ppermute | solution.py:175
  81.1 7.3 %collective-permute-done.7.refs_3_ = bf16[2,64,1280]{2,1,0:T(8,128)(2,1)S(1)} collective-permute-done((bf16[2,64,1280]{2,1,0:T(8,128)(2,1)S(1)}, bf16[2,64,1280]{2,1,0:T(8,128)(2,1)S(1)}, u32[]{:S(2)}, u32[]{:S(2)}) %collective-permute-start.7) | collective-permute-done | bytes 327712 | tf_op jit(solution)/shard_map/ppermute | solution.py:175
  88.5 8.0 %second.1 = bf16[512,1280]{1,0:T(8,128)(2,1)S(1)} custom-call(bf16[512,1280]{1,0:T(8,128)(2,1)S(1)} %copy-done.1, bf16[2,192,1280]{2,1,0:T(8,128)(2,1)S(1)} %collective-permute-done.5.refs_1_, bf16[2,256,1280]{2,1,0:T(8,128)(2,1)S(1)} %collective-permute-done.6.refs_2_, bf16[2,64,1280]{2,1,0:T(8,128)(2,1)S(1)} %collective-permute-done.7.refs_3_, ...), custom_call_target="tpu_custom_call" | custom-call | flops 1342177280 | bytes 5242880 | tf_op jit(solution)/shard_map/second/pallas_call | solution.py:142
  96.6 3.0 %collective-permute-done.8 = bf16[512,1280]{1,0:T(8,128)(2,1)S(1)} collective-permute-done((bf16[512,1280]{1,0:T(8,128)(2,1)S(1)}, bf16[512,1280]{1,0:T(8,128)(2,1)S(1)}, u32[]{:S(2)}, u32[]{:S(2)}) %collective-permute-start.8) | collective-permute-done | bytes 1310752 | tf_op jit(solution)/shard_map/ppermute | solution.py:175
  99.6 2.6 %fusion.11 = f32[512,640]{1,0:T(8,128)S(1)} fusion(bf16[512,1280]{1,0:T(8,128)(2,1)S(1)} %collective-permute-done.8, bf16[1280,5120]{1,0:T(8,128)(2,1)} %collective-permute-done.9, s32[]{:T(128)S(6)} %select_n.123), kind=kOutput, calls=%fused_computation.10 | convolution fusion | flops 838860800 | bytes 4259844 | tf_op jit(solution)/shard_map/dot_general | solution.py:288
  102.3 3.5 %fusion.24 = bf16[512,640]{1,0:T(8,128)(2,1)} fusion(f32[512,640]{1,0:T(8,128)S(1)} %fusion.11, bf16[512,1280]{1,0:T(8,128)(2,1)S(1)} %second.1, bf16[1280,5120]{1,0:T(8,128)(2,1)} %param.14, s32[]{:T(128)S(6)} %select_n.123), kind=kOutput, calls=%fused_computation.17 | convolution fusion | flops 839516160 | bytes 4915204 | tf_op jit(solution)/shard_map/dot_general | solution.py:287
  105.8 1.5 %collective-permute-start.10 = (bf16[512,640]{1,0:T(8,128)(2,1)}, bf16[512,640]{1,0:T(8,128)(2,1)S(1)}, u32[]{:S(2)}, u32[]{:S(2)}) collective-permute-start(bf16[512,640]{1,0:T(8,128)(2,1)} %fusion.24), channel_id=1, source_target_pairs={{0,2},{1,3},{2,0},{3,1},{4,6},{5,7},{6,4},{7,5},{8,10},{9,11},{10,... | collective-permute-start | bytes 1966088 | tf_op jit(solution)/shard_map/ppermute | solution.py:175
  107.3 2.6 %fusion.7 = f32[512,640]{1,0:T(8,128)S(1)} fusion(bf16[512,1280]{1,0:T(8,128)(2,1)S(1)} %collective-permute-done.8, bf16[1280,5120]{1,0:T(8,128)(2,1)} %collective-permute-done.9, s32[]{:T(128)S(6)} %select_n.124), kind=kOutput, calls=%fused_computation.6 | convolution fusion | flops 838860800 | bytes 4259844 | tf_op jit(solution)/shard_map/dot_general | solution.py:288
  109.9 3.5 %fusion.21 = bf16[512,640]{1,0:T(8,128)(2,1)} fusion(f32[512,640]{1,0:T(8,128)S(1)} %fusion.7, bf16[512,1280]{1,0:T(8,128)(2,1)S(1)} %second.1, bf16[1280,5120]{1,0:T(8,128)(2,1)} %param.14, s32[]{:T(128)S(6)} %select_n.124), kind=kOutput, calls=%fused_computation.16 | convolution fusion | flops 839516160 | bytes 4915204 | tf_op jit(solution)/shard_map/dot_general | solution.py:287
  113.9 3.8 %fusion.1 = f32[512,1280]{1,0:T(8,128)S(1)} fusion(bf16[512,1280]{1,0:T(8,128)(2,1)S(1)} %collective-permute-done.8, bf16[1280,5120]{1,0:T(8,128)(2,1)} %collective-permute-done.9, s32[]{:T(128)S(6)} %select_n.122), kind=kOutput, calls=%fused_computation.2 | convolution fusion | flops 1677721600 | bytes 7208964 | tf_op jit(solution)/shard_map/dot_general | solution.py:288
  117.7 5.8 %collective-permute-done.10 = bf16[512,640]{1,0:T(8,128)(2,1)S(1)} collective-permute-done((bf16[512,640]{1,0:T(8,128)(2,1)}, bf16[512,640]{1,0:T(8,128)(2,1)S(1)}, u32[]{:S(2)}, u32[]{:S(2)}) %collective-permute-start.10) | collective-permute-done | bytes 655392 | tf_op jit(solution)/shard_map/ppermute | solution.py:175
  123.6 13.3 %collective-permute-done.11 = bf16[512,640]{1,0:T(8,128)(2,1)} collective-permute-done((bf16[512,640]{1,0:T(8,128)(2,1)}, bf16[512,640]{1,0:T(8,128)(2,1)}, u32[]{:S(2)}, u32[]{:S(2)}) %collective-permute-start.11) | collective-permute-done | bytes 655392 | tf_op jit(solution)/shard_map/ppermute | solution.py:175
  136.9 5.1 %fusion.4 = bf16[512,1280]{1,0:T(8,128)(2,1)} fusion(f32[512,1280]{1,0:T(8,128)S(1)} %fusion.1, bf16[512,1280]{1,0:T(8,128)(2,1)S(1)} %second.1, bf16[1280,5120]{1,0:T(8,128)(2,1)} %param.14, s32[]{:T(128)S(6)} %select_n.122, bf16[512,640]{1,0:T(8,128)(2,1)} %collective-permute-done.11, bf16[512,640]{1,0:T(8,128)(2,1)S(1)} %collective-permute-done.10), kind=kOutput, calls=%fused_computation.5 | convolution fusion | flops 1682309120 | bytes 9830404 | tf_op jit(solution)/shard_map/dot_general | solution.py:287
  (50 shorter events, 5.9 us)
Async XLA Ops:
  0.0 46.4 %copy-start = (s32[8,8]{1,0:T(8,128)S(1)}, s32[8,8]{1,0:T(8,128)}, u32[]{:S(2)}) copy-start(s32[8,8]{1,0:T(8,128)} %param.13) | copy-start | bytes 772
  0.0 1.3 copy-start.2
  1.3 1.3 copy-start.4
  2.7 0.9 copy-start.5
  5.3 40.8 %collective-permute-start = (bf16[2,256,1280]{2,1,0:T(8,128)(2,1)S(1)}, bf16[2,256,1280]{2,1,0:T(8,128)(2,1)S(1)}, u32[]{:S(2)}, u32[]{:S(2)}) collective-permute-start(bf16[2,256,1280]{2,1,0:T(8,128)(2,1)S(1)} %get-tuple-element.18), channel_id=1, source_target_pairs={{0,4},{1,5},{2,6},{3,7},{4,0},{5,1},{6,2},{7,3},{8,12},{9,13},{10,... | collective-permute-start | bytes 3932168 | tf_op jit(solution)/shard_map/ppermute | solution.py:175
  5.3 40.7 %collective-permute-start.1 = (bf16[2,128,1280]{2,1,0:T(8,128)(2,1)S(1)}, bf16[2,128,1280]{2,1,0:T(8,128)(2,1)S(1)}, u32[]{:S(2)}, u32[]{:S(2)}) collective-permute-start(bf16[2,128,1280]{2,1,0:T(8,128)(2,1)S(1)} %get-tuple-element.19), channel_id=1, source_target_pairs={{0,8},{1,9},{2,10},{3,11},{8,16},{9,17},{10,18},{11,19},{12,4},{13... | collective-permute-start | bytes 1966088 | tf_op jit(solution)/shard_map/ppermute | solution.py:175
  6.6 39.4 %collective-permute-start.2 = (bf16[2,128,1280]{2,1,0:T(8,128)(2,1)S(1)}, bf16[2,128,1280]{2,1,0:T(8,128)(2,1)S(1)}, u32[]{:S(2)}, u32[]{:S(2)}) collective-permute-start(bf16[2,128,1280]{2,1,0:T(8,128)(2,1)S(1)} %get-tuple-element.19), channel_id=1, source_target_pairs={{4,12},{5,13},{6,14},{7,15},{8,0},{9,1},{10,2},{11,3},{12,20},{13,... | collective-permute-start | bytes 1966088 | tf_op jit(solution)/shard_map/ppermute | solution.py:175
  11.3 34.7 %collective-permute-start.3 = (bf16[2,64,1280]{2,1,0:T(8,128)(2,1)S(1)}, bf16[2,64,1280]{2,1,0:T(8,128)(2,1)S(1)}, u32[]{:S(2)}, u32[]{:S(2)}) collective-permute-start(bf16[2,64,1280]{2,1,0:T(8,128)(2,1)S(1)} %get-tuple-element.20), channel_id=1, source_target_pairs={{0,16},{1,17},{2,18},{3,19},{4,20},{5,21},{6,22},{7,23},{8,24},{9,... | collective-permute-start | bytes 983048 | tf_op jit(solution)/shard_map/ppermute | solution.py:175
  14.4 31.6 %collective-permute-start.4 = (bf16[2,64,1280]{2,1,0:T(8,128)(2,1)S(1)}, bf16[2,64,1280]{2,1,0:T(8,128)(2,1)S(1)}, u32[]{:S(2)}, u32[]{:S(2)}) collective-permute-start(bf16[2,64,1280]{2,1,0:T(8,128)(2,1)S(1)} %get-tuple-element.20), channel_id=1, source_target_pairs={{0,24},{1,25},{2,26},{3,27},{4,28},{5,29},{6,30},{7,31},{24,0},{25... | collective-permute-start | bytes 983048 | tf_op jit(solution)/shard_map/ppermute | solution.py:175
  46.0 5.7 %copy-start.6 = (bf16[2,256,1280]{2,1,0:T(8,128)(2,1)}, bf16[2,256,1280]{2,1,0:T(8,128)(2,1)S(1)}, u32[]{:S(2)}) copy-start(bf16[2,256,1280]{2,1,0:T(8,128)(2,1)S(1)} %collective-permute-done.refs_3_) | copy-start | bytes 3932164
  46.1 53.6 %collective-permute-start.9 = (bf16[1280,5120]{1,0:T(8,128)(2,1)}, bf16[1280,5120]{1,0:T(8,128)(2,1)}, u32[]{:S(2)}, u32[]{:S(2)}) collective-permute-start(bf16[1280,5120]{1,0:T(8,128)(2,1)} %param.14), channel_id=1, source_target_pairs={{0,1},{1,0},{2,3},{3,2},{4,5},{5,4},{6,7},{7,6},{8,9},{9,8},{10,11... | collective-permute-start | bytes 39321608 | tf_op jit(solution)/shard_map/ppermute | solution.py:175
  46.8 6.9 %copy-start.3 = (bf16[512,1280]{1,0:T(8,128)(2,1)S(1)}, bf16[512,1280]{1,0:T(8,128)(2,1)}, u32[]{:S(2)}) copy-start(bf16[512,1280]{1,0:T(8,128)(2,1)} %refs_1_.3) | copy-start | bytes 3932164
  47.0 6.5 %copy-start.7 = (pred[5,640]{1,0:T(8,128)(4,1)S(1)}, pred[5,640]{1,0:T(8,128)(4,1)}, u32[]{:S(2)}) copy-start(pred[5,640]{1,0:T(8,128)(4,1)} %constant.80.clone) | copy-start | bytes 9604
  47.0 6.6 %copy-start.8 = (s32[640]{0:T(1024)S(1)}, s32[640]{0:T(1024)}, u32[]{:S(2)}) copy-start(s32[640]{0:T(1024)} %constant.81.clone) | copy-start | bytes 7684
  47.0 6.8 %copy-start.1 = (bf16[512,1280]{1,0:T(8,128)(2,1)S(1)}, bf16[512,1280]{1,0:T(8,128)(2,1)}, u32[]{:S(2)}) copy-start(bf16[512,1280]{1,0:T(8,128)(2,1)} %refs_0_.4) | copy-start | bytes 3932164
  47.0 34.1 %collective-permute-start.6 = (bf16[2,256,1280]{2,1,0:T(8,128)(2,1)S(1)}, bf16[2,256,1280]{2,1,0:T(8,128)(2,1)S(1)}, u32[]{:S(2)}, u32[]{:S(2)}) collective-permute-start(bf16[2,256,1280]{2,1,0:T(8,128)(2,1)S(1)} %pad_maximum_fusion), channel_id=1, source_target_pairs={{0,4},{1,5},{2,6},{3,7},{4,0},{5,1},{6,2},{7,3},{8,12},{9,13},{10,... | collective-permute-start | bytes 3932168 | tf_op jit(solution)/shard_map/ppermute | solution.py:175
  51.8 25.7 %collective-permute-start.5 = (bf16[2,192,1280]{2,1,0:T(8,128)(2,1)S(1)}, bf16[2,192,1280]{2,1,0:T(8,128)(2,1)S(1)}, u32[]{:S(2)}, u32[]{:S(2)}) collective-permute-start(bf16[2,192,1280]{2,1,0:T(8,128)(2,1)S(1)} %slice.15), channel_id=1, source_target_pairs={{0,8},{1,9},{2,10},{3,11},{8,16},{9,17},{10,18},{11,19},{12,4},{13... | collective-permute-start | bytes 2949128 | tf_op jit(solution)/shard_map/ppermute | solution.py:175
  53.8 25.3 %copy-start.9 = (pred[6,512]{1,0:T(8,128)(4,1)S(1)}, pred[6,512]{1,0:T(8,128)(4,1)}, u32[]{:S(2)}) copy-start(pred[6,512]{1,0:T(8,128)(4,1)} %constant.82.clone) | copy-start | bytes 9220
  53.8 25.3 %copy-start.10 = (s32[512]{0:T(512)S(1)}, s32[512]{0:T(512)}, u32[]{:S(2)}) copy-start(s32[512]{0:T(512)} %constant.83.clone) | copy-start | bytes 6148
  77.6 10.8 %collective-permute-start.7 = (bf16[2,64,1280]{2,1,0:T(8,128)(2,1)S(1)}, bf16[2,64,1280]{2,1,0:T(8,128)(2,1)S(1)}, u32[]{:S(2)}, u32[]{:S(2)}) collective-permute-start(bf16[2,64,1280]{2,1,0:T(8,128)(2,1)S(1)} %slice.19), channel_id=1, source_target_pairs={{0,8},{1,9},{2,10},{3,11},{8,16},{9,17},{10,18},{11,19},{12,4},{13... | collective-permute-start | bytes 983048 | tf_op jit(solution)/shard_map/ppermute | solution.py:175
  96.5 3.1 %collective-permute-start.8 = (bf16[512,1280]{1,0:T(8,128)(2,1)S(1)}, bf16[512,1280]{1,0:T(8,128)(2,1)S(1)}, u32[]{:S(2)}, u32[]{:S(2)}) collective-permute-start(bf16[512,1280]{1,0:T(8,128)(2,1)S(1)} %second.1), channel_id=1, source_target_pairs={{0,1},{1,0},{2,3},{3,2},{4,5},{5,4},{6,7},{7,6},{8,9},{9,8},{10,11... | collective-permute-start | bytes 3932168 | tf_op jit(solution)/shard_map/ppermute | solution.py:175
  105.8 17.8 %collective-permute-start.10 = (bf16[512,640]{1,0:T(8,128)(2,1)}, bf16[512,640]{1,0:T(8,128)(2,1)S(1)}, u32[]{:S(2)}, u32[]{:S(2)}) collective-permute-start(bf16[512,640]{1,0:T(8,128)(2,1)} %fusion.24), channel_id=1, source_target_pairs={{0,2},{1,3},{2,0},{3,1},{4,6},{5,7},{6,4},{7,5},{8,10},{9,11},{10,... | collective-permute-start | bytes 1966088 | tf_op jit(solution)/shard_map/ppermute | solution.py:175
  113.4 23.5 %collective-permute-start.11 = (bf16[512,640]{1,0:T(8,128)(2,1)}, bf16[512,640]{1,0:T(8,128)(2,1)}, u32[]{:S(2)}, u32[]{:S(2)}) collective-permute-start(bf16[512,640]{1,0:T(8,128)(2,1)} %fusion.21), channel_id=1, source_target_pairs={{0,2},{1,3},{2,0},{3,1},{4,6},{5,7},{6,4},{7,5},{8,10},{9,11},{10,... | collective-permute-start | bytes 1966088 | tf_op jit(solution)/shard_map/ppermute | solution.py:175

commit v2 on v1

v2 whole, which is shorter than its diff:
```python
import math

import jax
import jax.numpy as jnp
import numpy as np
from jax import lax
from jax.experimental import pallas as pl
from jax.experimental.pallas import tpu as pltpu
from jax.sharding import PartitionSpec as P

HEAD_DIM = 128
MASKED = -1e30
AXES = ("tm", "head")
F32 = jnp.float32
BF16 = jnp.bfloat16


def pack_kernel(key_ref, value_ref, *out_refs, cuts):
    row_count = key_ref.shape[0]
    picks = row_count // 2
    rank = lax.broadcasted_iota(jnp.int32, (picks, 1), 0)
    place = jnp.zeros_like(rank)
    step = 1
    while step < picks:
        stride = row_count // (2 * step)
        place = jnp.where(rank >= step, (2 * (rank - step) + 1) * stride, place)
        step *= 2
    column = lax.broadcasted_iota(jnp.int32, (picks, row_count), 1)
    choose = jnp.where(place == column, 1.0, 0.0).astype(BF16)
    for plane, source in enumerate((key_ref, value_ref)):
        picked = jnp.dot(choose, source[...], preferred_element_type=F32).astype(BF16)
        for out_ref, (low, high) in zip(out_refs, cuts):
            out_ref[plane] = picked[low:high]


def pack(key_vectors, value_vectors, cuts):
    row_count, width = key_vectors.shape
    tile = width // 2
    return pl.pallas_call(
        lambda *refs: pack_kernel(*refs, cuts=cuts),
        grid=(width // tile,),
        in_specs=[pl.BlockSpec((row_count, tile), lambda j: (0, j))] * 2,
        out_specs=[
            pl.BlockSpec((2, high - low, tile), lambda j: (0, 0, j)) for low, high in cuts
        ],
        out_shape=[jax.ShapeDtypeStruct((2, high - low, width), BF16) for low, high in cuts],
        name="pack",
        compiler_params=pltpu.CompilerParams(vmem_limit_bytes=48 << 20),
        cost_estimate=pl.CostEstimate(
            flops=2 * row_count * row_count * width,
            bytes_accessed=8 * row_count * width,
            transcendentals=0,
        ),
    )(key_vectors, value_vectors)


def attend_kernel(*refs, buffers, own, first, last, heads):
    refs = list(refs)
    query_ref = refs.pop(0)
    own_refs = [refs.pop(0), refs.pop(0)] if own else None
    packed_refs = [refs.pop(0) for _ in range(buffers)]
    bias_ref = refs.pop(0) if buffers else None
    state_in, accum_in = (None, None) if first else (refs.pop(0), refs.pop(0))
    query_count = query_ref.shape[0]
    factor = math.log2(math.e) / math.sqrt(HEAD_DIM)
    if buffers:
        bias = jnp.concatenate([bias_ref[...]] * (query_count // HEAD_DIM), axis=1)
    for head in range(heads):
        span = slice(head * HEAD_DIM, (head + 1) * HEAD_DIM)
        if own:
            key, value = (own_refs[0][:, span], own_refs[1][:, span])
        else:
            key = jnp.concatenate([ref[0, :, span] for ref in packed_refs], axis=0)
            value = jnp.concatenate([ref[1, :, span] for ref in packed_refs], axis=0)
        scores = lax.dot_general(
            key, query_ref[:, span], (((1,), (1,)), ((), ())), preferred_element_type=F32
        )
        if buffers:
            scores = scores + bias
        top = jnp.max(scores, axis=0, keepdims=True)
        if not first:
            top_in = state_in[head, 0:1, :]
            top = jnp.maximum(top, top_in)
            shrink = jnp.exp2((top_in - top) * factor)
        level = top * factor
        weights = jnp.exp2(scores * factor - level)
        total = jnp.sum(weights, axis=0, keepdims=True)
        accum = jnp.dot(value.T, weights.astype(BF16), preferred_element_type=F32)
        if not first:
            total = total + shrink * state_in[head, 1:2, :]
            accum = accum + shrink * accum_in[head]
        if last:
            refs[0][:, span] = (accum / total).T.astype(BF16)
        else:
            refs[0][head, 0:1, :] = top
            refs[0][head, 1:2, :] = total
            refs[1][head] = accum


def attend(query_vectors, own_pair, buffers, bias, carry, last, low, high, name):
    row_count = query_vectors.shape[0]
    heads = 5 if (high - low) % 5 == 0 else 1
    span = heads * HEAD_DIM
    skip = low // heads
    assert low % heads == 0
    whole = pl.BlockSpec((row_count, span), lambda h: (0, h + skip))
    state = pl.BlockSpec((heads, 8, row_count), lambda h: (h, 0, 0))
    accum = pl.BlockSpec((heads, HEAD_DIM, row_count), lambda h: (h, 0, 0))
    state_in = pl.BlockSpec((heads, 8, row_count), lambda h: (h + skip, 0, 0))
    accum_in = pl.BlockSpec((heads, HEAD_DIM, row_count), lambda h: (h + skip, 0, 0))
    operands, specs = ([query_vectors], [whole])
    own = own_pair is not None
    count = row_count if own else bias.shape[0]
    if own:
        operands += list(own_pair)
        specs += [whole, whole]
    for buffer in buffers:
        operands.append(buffer)
        specs.append(pl.BlockSpec((2, buffer.shape[1], span), lambda h: (0, 0, h + skip)))
    if buffers:
        operands.append(bias)
        specs.append(pl.BlockSpec((count, HEAD_DIM), lambda h: (0, 0)))
    first = carry is None
    if not first:
        operands += list(carry)
        specs += [state_in, accum_in]
    width = (high - low) * HEAD_DIM
    if last:
        shapes = [jax.ShapeDtypeStruct((row_count, width), BF16)]
        out_specs = [pl.BlockSpec((row_count, span), lambda h: (0, h))]
    else:
        shapes = [
            jax.ShapeDtypeStruct((high - low, 8, row_count), F32),
            jax.ShapeDtypeStruct((high - low, HEAD_DIM, row_count), F32),
        ]
        out_specs = [state, accum]
    return pl.pallas_call(
        lambda *refs: attend_kernel(
            *refs, buffers=len(buffers), own=own, first=first, last=last, heads=heads
        ),
        grid=((high - low) // heads,),
        in_specs=specs,
        out_specs=out_specs,
        out_shape=shapes,
        name=name,
        compiler_params=pltpu.CompilerParams(vmem_limit_bytes=48 << 20),
        cost_estimate=pl.CostEstimate(
            flops=4 * row_count * count * width,
            bytes_accessed=8 * row_count * width,
            transcendentals=row_count * count * (high - low),
        ),
    )(*operands)


def per_device(query_vectors, key_vectors, value_vectors, band_table, out_weight):
    row_count, width = query_vectors.shape
    block_count = lax.axis_size("tm")
    group_count = lax.axis_size("head")
    my_block = lax.axis_index("tm")
    my_group = lax.axis_index("head")
    table_row = lax.dynamic_index_in_dim(band_table, my_block, 0, keepdims=False)

    def move(array, block_to, group_to=lambda h: h):
        route = []
        for t in range(block_count):
            for h in range(group_count):
                to = block_to(t)
                if to is not None and 0 <= to < block_count:
                    route.append((t * group_count + h, to * group_count + group_to(h)))
        return lax.ppermute(array, AXES, route)

    def bias_of(pieces):
        blocks = jnp.stack([jnp.asarray(block, jnp.int32) for block, _, _ in pieces])
        number = np.concatenate([np.full(n, i) for i, (_, _, n) in enumerate(pieces)])
        rank = np.concatenate([np.arange(a, a + n) for _, a, n in pieces]).astype(np.int32)
        member = jnp.asarray(number[None, :] == np.arange(len(pieces))[:, None])
        here = jnp.arange(block_count, dtype=jnp.int32)[None, :] == blocks[:, None]
        band = jnp.sum(jnp.where(here, table_row[None, :], 0), axis=1)
        kept = jnp.where(jnp.any(here, axis=1), jnp.right_shift(jnp.int32(row_count), band), 0)
        limit = jnp.sum(jnp.where(member, kept[:, None], 0), axis=0)
        bias = jnp.where(jnp.asarray(rank) < limit, 0.0, MASKED).astype(F32)
        return jnp.broadcast_to(bias[:, None], (rank.size, HEAD_DIM))

    def within(block):
        return (block >= 0) & (block < block_count)

    head_count = width // HEAD_DIM
    core = lambda h: h ^ 1
    same = lambda t: t
    mine = my_group % 2
    level = my_group // 2
    out_width = out_weight.shape[1] // group_count
    away, home = (2 * (1 - level) + mine, 2 * level + mine)
    moved = move(out_weight, same, core)
    near = row_count // 2
    own_pair = (key_vectors, value_vectors)

    def further(buffers, pieces, carry, name):
        return attend(
            query_vectors, None, buffers, bias_of(pieces), carry, False, 0, head_count, name
        )

    if block_count == 8:
        a, ab = (row_count // 8, row_count // 4)
        side = jnp.where(my_block % 2 == 0, 1, -1)
        far_way = lambda t: t + 2 if t % 2 == 0 else t - 2
        near_way = lambda t: t - 2 if t % 2 == 0 else t + 2
        partner, two, opposite = (my_block ^ 1, my_block ^ 4, my_block ^ 6)
        far_block, near_block = (my_block - 2 * side, my_block + 2 * side)
        adjacent, far_cross = (my_block - side, my_block + 3 * side)
        at_end = (my_block < 2) | (my_block >= block_count - 2)
        none = jnp.int32(-1)
        three = jnp.where(at_end, opposite, none)

        sent, sent_ab, sent_a = pack(key_vectors, value_vectors, [(0, near), (0, ab), (0, a)])
        x_rows = move(sent, lambda t: t ^ 1)
        z_far = move(sent_ab, far_way)
        z_near = move(sent_ab, near_way)
        z_two = move(sent_a, lambda t: t ^ 4)
        carry = attend(query_vectors, own_pair, [], None, None, False, 0, head_count, "own")
        x_rows, z_far, z_near, state = lax.optimization_barrier((x_rows, z_far, z_near, carry[0]))
        carry = (state, carry[1])
        near_b = move(x_rows[:, a:ab], far_way)
        near_c = move(x_rows[:, ab:], far_way)
        slot_far = jnp.where(within(far_block), z_far[:, :a], z_two)
        slot_near = jnp.where(within(near_block), z_near[:, :a], z_two)
        crossed = move(
            jnp.concatenate([slot_far, z_far[:, a:], slot_near], axis=1), lambda t: t ^ 1
        )
        z_three = move(z_two, lambda t: {4: 6, 5: 7, 2: 0, 3: 1}.get(t))
        carry = further(
            [x_rows, z_far, z_near, z_two],
            [(partner, 0, near), (far_block, 0, ab), (near_block, 0, ab), (two, 0, a)],
            carry,
            "first",
        )
        near_b, z_three, state, out_weight, moved = lax.optimization_barrier(
            (near_b, z_three, carry[0], out_weight, moved)
        )
        carry = (state, carry[1])
        cross_last = move(jnp.where(at_end, z_three, z_two), lambda t: t ^ 1)
        chain_b = move(near_b, far_way)
        carry = further(
            [near_b, near_c, z_three],
            [(adjacent, a, ab - a), (adjacent, ab, near - ab), (three, 0, a)],
            carry,
            "middle",
        )
        buffers = [crossed, cross_last, chain_b]
        pieces = [
            (jnp.where(within(far_cross), far_cross, two ^ 1), 0, a),
            (far_cross, a, ab - a),
            (jnp.where(within(adjacent), adjacent, two ^ 1), 0, a),
            (jnp.where(at_end, opposite ^ 1, two ^ 1), 0, a),
            (my_block - 3 * side, a, ab - a),
        ]
    else:
        (packed,) = pack(key_vectors, value_vectors, [(0, near)])
        received, pieces = ([], [])
        for distance in range(1, block_count):
            rows = row_count >> distance.bit_length()
            for sign in (1, -1):
                received.append(move(packed[:, :rows], lambda t: t + sign * distance))
                pieces.append((my_block - sign * distance, 0, rows))
        carry = attend(query_vectors, own_pair, [], None, None, False, 0, head_count, "own")
        carry = further([jnp.concatenate(received[:2], axis=1)], pieces[:2], carry, "first")
        buffers, pieces = ([jnp.concatenate(received[2:], axis=1)], pieces[2:])

    def block_of(weight, number):
        return lax.dynamic_slice_in_dim(weight, number * out_width, out_width, 1)

    weights = lax.optimization_barrier(
        [block_of(weight, number) for weight in (out_weight, moved) for number in (away, home)]
    )
    bias = bias_of(pieces)
    cut = head_count // 2
    parts = []
    for low, high in ((0, cut), (cut, head_count)):
        (part,) = attend(
            query_vectors, None, buffers, bias, carry, True, low, high, f"last{low}"
        )
        parts.append((part, move(part, same, core), low * HEAD_DIM, high * HEAD_DIM))

    def project(index, first, last):
        total = 0.0
        for part, other, low, high in parts:
            total = total + jnp.dot(
                part, weights[index][low:high, first:last], preferred_element_type=F32
            )
            total = total + jnp.dot(
                other, weights[index + 2][low:high, first:last], preferred_element_type=F32
            )
        return total

    half = out_width // 2
    arrived = [
        move(project(0, first, first + half).astype(BF16), same, lambda h: h ^ 2)
        for first in (0, half)
    ]
    kept, arrived[0] = lax.optimization_barrier((project(1, 0, out_width), arrived[0]))
    return (kept + jnp.concatenate(arrived, axis=1).astype(F32)).astype(BF16)


def solution(mesh):
    in_specs = (P("tm", "head"), P("tm", "head"), P("tm", "head"), P(), P("head", None))
    out_specs = P("tm", "head")
    return jax.shard_map(
        per_device, mesh=mesh, in_specs=in_specs, out_specs=out_specs, check_vma=False
    )
```

time: 142 us -> 139 us (0.979); the launches traced: 142 us -> 137 us
  waiting for transfers between devices: 70.3 us -> 53.5 us
  local copies, waits for them, and re-layouts: 4.12 us -> 16 us
  matrix products: 21.1 us -> 10.9 us
  Pallas kernels: 23 us -> 31.7 us
  other arithmetic: 1.09 us -> 4.2 us
  starting transfers between devices: 22 us -> 20.4 us
    ppermute x12 -> x15, waiting for transfers between devices: 70.3 us -> 53.5 us  [move(): return lax.ppermute(array, AXES, route)]
    dot_general x6 -> x12, matrix products: 21.1 us -> 10.9 us  [the longest x6 5.56 us: project(): jnp.dot(part, weights[index][low:high, first:last], preferred_element_typ...]
    dynamic_slice x0 -> x1, local copies, waits for them, and re-layouts: none -> 8.12 us  [block_of(): return lax.dynamic_slice_in_dim(weight, number * out_width, out_width, 1)]
    pallas_call x2 -> x5, Pallas kernels: 21.3 us -> 29.3 us  [attend(): pl.pallas_call(lambda *refs: attend_kernel(*refs, buffers=len(buffers), o...]
    unnamed x22 -> x32, local copies, waits for them, and re-layouts: 3.6 us -> 7.45 us
    ppermute x12 -> x15, starting transfers between devices: 22 us -> 20.4 us  [move(): return lax.ppermute(array, AXES, route)]
  transfers between devices with their start and end apart: 12 -> 15, of which waited for: 7 -> 6; matrix products, arithmetic and copies ran while one was open for 8% -> 15% of each run, Pallas kernels for 15% -> 20%
where the time goes in v2:
time: 139 us; the launch traced here: 137 us
  waiting for transfers between devices  53.5 us (38%)
  Pallas kernels  31.7 us (23%)
  starting transfers between devices  20.4 us (15%)
  local copies, waits for them, and re-layouts  16 us (12%)
  matrix products  10.9 us (8%)
  other arithmetic  4.2 us (3%)
    ppermute x15, waiting for transfers between devices, move(): return lax.ppermute(array, AXES, route)  53.5 us
    pallas_call x5, Pallas kernels, attend(): pl.pallas_call(lambda *refs: attend_kernel(*refs, buffers=len(buffers), o...  29.3 us
    ppermute x15, starting transfers between devices, move(): return lax.ppermute(array, AXES, route)  20.4 us
    dynamic_slice x1, local copies, waits for them, and re-layouts, block_of(): return lax.dynamic_slice_in_dim(weight, number * out_width, out_width, 1)  8.12 us
    unnamed x32, local copies, waits for them, and re-layouts  7.45 us
    dot_general x6, matrix products, project(): jnp.dot(part, weights[index][low:high, first:last], preferred_element_typ...  5.56 us
    dot_general x6, matrix products, project(): jnp.dot(other, weights[index + 2][low:high, first:last], preferred_elemen...  5.38 us
  transfers between devices with their start and end apart: 15, of which 6 were waited for; matrix products, arithmetic and copies ran while one was open for 15% of the time, Pallas kernels for 20%

profile of v2, /device:TPU:2, one launch (start us, length us, event | category | flops | bytes accessed | tf_op | source)
XLA Modules:
  0.0 137.2 jit_solution(1653749505990850473)
XLA Ops:
  0.1 1.4 %copy-done.4 = bf16[512,1280]{1,0:T(8,128)(2,1)S(1)} copy-done((bf16[512,1280]{1,0:T(8,128)(2,1)S(1)}, bf16[512,1280]{1,0:T(8,128)(2,1)}, u32[]{:S(2)}) %copy-start.4) | copy-done | bytes 1310744
  1.5 1.3 copy-done.6
  2.8 2.4 %pack.1 = (bf16[2,256,1280]{2,1,0:T(8,128)(2,1)}, bf16[2,128,1280]{2,1,0:T(8,128)(2,1)}, bf16[2,64,1280]{2,1,0:T(8,128)(2,1)}) custom-call(bf16[512,1280]{1,0:T(8,128)(2,1)S(1)} %copy-done.4, bf16[512,1280]{1,0:T(8,128)(2,1)S(1)} %copy-done.6), custom_call_target="tpu_custom_call" | custom-call | flops 671088640 | bytes 5242880 | tf_op jit(solution)/shard_map/pack/pallas_call | solution.py:39
  5.3 4.5 %collective-permute-start.2 = (bf16[2,128,1280]{2,1,0:T(8,128)(2,1)}, bf16[2,128,1280]{2,1,0:T(8,128)(2,1)}, u32[]{:S(2)}, u32[]{:S(2)}) collective-permute-start(bf16[2,128,1280]{2,1,0:T(8,128)(2,1)} %get-tuple-element.30), channel_id=1, source_target_pairs={{4,12},{5,13},{6,14},{7,15},{8,0},{9,1},{10,2},{11,3},{12,20},{13,... | collective-permute-start | bytes 1966088 | tf_op jit(solution)/shard_map/ppermute | solution.py:170
  11.0 2.9 %collective-permute-start.3 = (bf16[2,64,1280]{2,1,0:T(8,128)(2,1)}, bf16[2,64,1280]{2,1,0:T(8,128)(2,1)}, u32[]{:S(2)}, u32[]{:S(2)}) collective-permute-start(bf16[2,64,1280]{2,1,0:T(8,128)(2,1)} %get-tuple-element.33), channel_id=1, source_target_pairs={{0,16},{1,17},{2,18},{3,19},{4,20},{5,21},{6,22},{7,23},{8,24},{9,... | collective-permute-start | bytes 983048 | tf_op jit(solution)/shard_map/ppermute | solution.py:170
  13.9 1.4 %collective-permute-start = (bf16[2,256,1280]{2,1,0:T(8,128)(2,1)}, bf16[2,256,1280]{2,1,0:T(8,128)(2,1)S(1)}, u32[]{:S(2)}, u32[]{:S(2)}) collective-permute-start(bf16[2,256,1280]{2,1,0:T(8,128)(2,1)} %get-tuple-element.29), channel_id=1, source_target_pairs={{0,4},{1,5},{2,6},{3,7},{4,0},{5,1},{6,2},{7,3},{8,12},{9,13},{10,... | collective-permute-start | bytes 3932168 | tf_op jit(solution)/shard_map/ppermute | solution.py:170
  16.8 1.3 copy-done.5
  18.1 1.3 copy-done.7
  19.4 7.1 %own.1 = (f32[10,8,512]{2,1,0:T(8,128)S(1)}, f32[10,128,512]{2,1,0:T(8,128)}) custom-call(bf16[512,1280]{1,0:T(8,128)(2,1)S(1)} %copy-done.2, bf16[512,1280]{1,0:T(8,128)(2,1)S(1)} %copy-done.5, bf16[512,1280]{1,0:T(8,128)(2,1)S(1)} %copy-done.7), custom_call_target="tpu_custom_call" | custom-call | flops 1342177280 | bytes 5242880 | tf_op jit(solution)/shard_map/own/pallas_call | solution.py:137
  26.8 16.1 %collective-permute-done.3.refs_4_ = bf16[2,64,1280]{2,1,0:T(8,128)(2,1)} collective-permute-done((bf16[2,64,1280]{2,1,0:T(8,128)(2,1)}, bf16[2,64,1280]{2,1,0:T(8,128)(2,1)}, u32[]{:S(2)}, u32[]{:S(2)}) %collective-permute-start.3) | collective-permute-done | bytes 327712 | tf_op jit(solution)/shard_map/ppermute | solution.py:170
  44.4 1.3 collective-permute-start.5
  45.8 1.3 collective-permute-start.10
  47.2 9.2 %first.1 = (f32[10,8,512]{2,1,0:T(8,128)S(1)}, f32[10,128,512]{2,1,0:T(8,128)}) custom-call(bf16[512,1280]{1,0:T(8,128)(2,1)S(1)} %copy-done.2, bf16[2,256,1280]{2,1,0:T(8,128)(2,1)S(1)} %collective-permute-done.refs_1_, bf16[2,128,1280]{2,1,0:T(8,128)(2,1)S(1)} %collective-permute-done.1.refs_2_, bf16[2,128,1280]{2,1,0:T(8,128)(2,1)} %collective-permute-done.2.refs_3_, ...), custom_call_target="tpu_custom_call" | custom-call | flops 1509949440 | bytes 5242880 | tf_op jit(solution)/shard_map/first/pallas_call | solution.py:137
  56.4 6.3 %collective-permute-done.5.refs_1_ = bf16[2,64,1280]{2,1,0:T(8,128)(2,1)S(1)} collective-permute-done((bf16[2,64,1280]{2,1,0:T(8,128)(2,1)S(1)}, bf16[2,64,1280]{2,1,0:T(8,128)(2,1)S(1)}, u32[]{:S(2)}, u32[]{:S(2)}) %collective-permute-start.5) | collective-permute-done | bytes 327712 | tf_op jit(solution)/shard_map/ppermute | solution.py:170
  65.4 2.2 %collective-permute-start.4 = (bf16[2,192,1280]{2,1,0:T(8,128)(2,1)S(1)}, bf16[2,192,1280]{2,1,0:T(8,128)(2,1)S(1)}, u32[]{:S(2)}, u32[]{:S(2)}) collective-permute-start(bf16[2,192,1280]{2,1,0:T(8,128)(2,1)S(1)} %pad_maximum_fusion), channel_id=1, source_target_pairs={{0,4},{1,5},{2,6},{3,7},{4,0},{5,1},{6,2},{7,3},{8,12},{9,13},{10,... | collective-permute-start | bytes 2949128 | tf_op jit(solution)/shard_map/ppermute | solution.py:170
  67.6 8.1 %constant_dynamic-slice_fusion = (bf16[1280,1280]{1,0:T(8,128)(2,1)}, bf16[1280,1280]{1,0:T(8,128)(2,1)S(1)}, bf16[1280,1280]{1,0:T(8,128)(2,1)S(1)}, bf16[1280,1280]{1,0:T(8,128)(2,1)}) fusion(bf16[1280,5120]{1,0:T(8,128)(2,1)} %collective-permute-done.7, s32[]{:T(128)S(6)} %select_n.151, s32[]{:T(128)S(6)} %select_n.150, bf16[1280,5120]{1,0:T(8,128)(2,1)} %param.15), kind=kLoop, calls=%fused_computation.52 | loop fusion | bytes 26214408 | tf_op jit(solution)/shard_map/dynamic_slice | solution.py:270
  76.8 5.4 %middle.1 = (f32[10,8,512]{2,1,0:T(8,128)S(1)}, f32[10,128,512]{2,1,0:T(8,128)S(1)}) custom-call(bf16[512,1280]{1,0:T(8,128)(2,1)S(1)} %copy-done.2, bf16[2,64,1280]{2,1,0:T(8,128)(2,1)S(1)} %collective-permute-done.5.refs_1_, bf16[2,128,1280]{2,1,0:T(8,128)(2,1)S(1)} %collective-permute-done.10.refs_2_, ...), custom_call_target="tpu_custom_call" | custom-call | flops 671088640 | bytes 5242880 | tf_op jit(solution)/shard_map/middle/pallas_call | solution.py:137
  82.3 1.5 %copy-done.3 = f32[10,128,512]{2,1,0:T(8,128)} copy-done((f32[10,128,512]{2,1,0:T(8,128)}, f32[10,128,512]{2,1,0:T(8,128)S(1)}, u32[]{:S(2)}) %copy-start.3) | copy-done | bytes 2621464
  83.8 7.6 %collective-permute-done.4.refs_1_ = bf16[2,192,1280]{2,1,0:T(8,128)(2,1)S(1)} collective-permute-done((bf16[2,192,1280]{2,1,0:T(8,128)(2,1)S(1)}, bf16[2,192,1280]{2,1,0:T(8,128)(2,1)S(1)}, u32[]{:S(2)}, u32[]{:S(2)}) %collective-permute-start.4) | collective-permute-done | bytes 983072 | tf_op jit(solution)/shard_map/ppermute | solution.py:170
  91.5 3.8 %last0.1 = bf16[512,640]{1,0:T(8,128)(2,1)S(1)} custom-call(bf16[512,1280]{1,0:T(8,128)(2,1)S(1)} %copy-done.2, bf16[2,192,1280]{2,1,0:T(8,128)(2,1)S(1)} %collective-permute-done.4.refs_1_, bf16[2,64,1280]{2,1,0:T(8,128)(2,1)S(1)} %collective-permute-done.8.refs_2_, bf16[2,64,1280]{2,1,0:T(8,128)(2,1)S(1)} %collective-permute-done.9.refs_3_, ...), custom_call_target="tpu_custom_call" | custom-call | flops 419430400 | bytes 2621440 | tf_op jit(solution)/shard_map/last0/pallas_call | solution.py:137
  95.3 3.8 %last5.1 = bf16[512,640]{1,0:T(8,128)(2,1)S(1)} custom-call(bf16[512,1280]{1,0:T(8,128)(2,1)S(1)} %copy-done.2, bf16[2,192,1280]{2,1,0:T(8,128)(2,1)S(1)} %collective-permute-done.4.refs_1_, bf16[2,64,1280]{2,1,0:T(8,128)(2,1)S(1)} %collective-permute-done.8.refs_2_, bf16[2,64,1280]{2,1,0:T(8,128)(2,1)S(1)} %collective-permute-done.9.refs_3_, ...), custom_call_target="tpu_custom_call" | custom-call | flops 419430400 | bytes 2621440 | tf_op jit(solution)/shard_map/last5/pallas_call | solution.py:137
  104.7 1.6 %collective-permute-start.14 = (bf16[512,640]{1,0:T(8,128)(2,1)S(1)}, bf16[512,640]{1,0:T(8,128)(2,1)S(1)}, u32[]{:S(2)}, u32[]{:S(2)}) collective-permute-start(bf16[512,640]{1,0:T(8,128)(2,1)S(1)} %fusion.13), channel_id=1, source_target_pairs={{0,2},{1,3},{2,0},{3,1},{4,6},{5,7},{6,4},{7,5},{8,10},{9,11},{10,... | collective-permute-start | bytes 1966088 | tf_op jit(solution)/shard_map/ppermute | solution.py:170
  113.4 22.4 %collective-permute-done.13 = bf16[512,640]{1,0:T(8,128)(2,1)S(1)} collective-permute-done((bf16[512,640]{1,0:T(8,128)(2,1)S(1)}, bf16[512,640]{1,0:T(8,128)(2,1)S(1)}, u32[]{:S(2)}, u32[]{:S(2)}) %collective-permute-start.13) | collective-permute-done | bytes 655392 | tf_op jit(solution)/shard_map/ppermute | solution.py:170
  135.8 1.4 add_convert_fusion
  (84 shorter events, 21.2 us)
Async XLA Ops:
  0.0 15.5 %copy-start = (s32[8,8]{1,0:T(8,128)S(1)}, s32[8,8]{1,0:T(8,128)}, u32[]{:S(2)}) copy-start(s32[8,8]{1,0:T(8,128)} %param.14) | copy-start | bytes 772
  0.0 16.5 %copy-start.11 = (pred[5,320]{1,0:T(8,128)(4,1)S(1)}, pred[5,320]{1,0:T(8,128)(4,1)}, u32[]{:S(2)}) copy-start(pred[5,320]{1,0:T(8,128)(4,1)} %constant.82.clone) | copy-start | bytes 4804
  0.0 16.8 %copy-start.2 = (bf16[512,1280]{1,0:T(8,128)(2,1)S(1)}, bf16[512,1280]{1,0:T(8,128)(2,1)}, u32[]{:S(2)}) copy-start(bf16[512,1280]{1,0:T(8,128)(2,1)} %refs_0_.11) | copy-start | bytes 3932164
  0.0 62.7 %collective-permute-start.7 = (bf16[1280,5120]{1,0:T(8,128)(2,1)}, bf16[1280,5120]{1,0:T(8,128)(2,1)}, u32[]{:S(2)}, u32[]{:S(2)}) collective-permute-start(bf16[1280,5120]{1,0:T(8,128)(2,1)} %param.15), channel_id=1, source_target_pairs={{0,1},{1,0},{2,3},{3,2},{4,5},{5,4},{6,7},{7,6},{8,9},{9,8},{10,11... | collective-permute-start | bytes 39321608 | tf_op jit(solution)/shard_map/ppermute | solution.py:170
  5.2 21.4 %copy-start.12 = (pred[4,576]{1,0:T(4,128)(4,1)S(1)}, pred[4,576]{1,0:T(4,128)(4,1)}, u32[]{:S(2)}) copy-start(pred[4,576]{1,0:T(4,128)(4,1)} %constant.78.clone) | copy-start | bytes 6916
  5.2 21.4 %copy-start.13 = (s32[320]{0:T(512)S(1)}, s32[320]{0:T(512)}, u32[]{:S(2)}) copy-start(s32[320]{0:T(512)} %constant.83.clone) | copy-start | bytes 3844
  5.2 21.5 %copy-start.15 = (pred[3,256]{1,0:T(4,128)(4,1)S(1)}, pred[3,256]{1,0:T(4,128)(4,1)}, u32[]{:S(2)}) copy-start(pred[3,256]{1,0:T(4,128)(4,1)} %constant.80.clone) | copy-start | bytes 2308
  5.2 21.6 %copy-start.10 = (s32[576]{0:T(1024)S(1)}, s32[576]{0:T(1024)}, u32[]{:S(2)}) copy-start(s32[576]{0:T(1024)} %constant.79.clone) | copy-start | bytes 6916
  5.3 39.0 %collective-permute-start.2 = (bf16[2,128,1280]{2,1,0:T(8,128)(2,1)}, bf16[2,128,1280]{2,1,0:T(8,128)(2,1)}, u32[]{:S(2)}, u32[]{:S(2)}) collective-permute-start(bf16[2,128,1280]{2,1,0:T(8,128)(2,1)} %get-tuple-element.30), channel_id=1, source_target_pairs={{4,12},{5,13},{6,14},{7,15},{8,0},{9,1},{10,2},{11,3},{12,20},{13,... | collective-permute-start | bytes 1966088 | tf_op jit(solution)/shard_map/ppermute | solution.py:170
  9.7 34.5 %collective-permute-start.1 = (bf16[2,128,1280]{2,1,0:T(8,128)(2,1)}, bf16[2,128,1280]{2,1,0:T(8,128)(2,1)S(1)}, u32[]{:S(2)}, u32[]{:S(2)}) collective-permute-start(bf16[2,128,1280]{2,1,0:T(8,128)(2,1)} %get-tuple-element.30), channel_id=1, source_target_pairs={{0,8},{1,9},{2,10},{3,11},{8,16},{9,17},{10,18},{11,19},{12,4},{13... | collective-permute-start | bytes 1966088 | tf_op jit(solution)/shard_map/ppermute | solution.py:170
  11.0 31.9 %collective-permute-start.3 = (bf16[2,64,1280]{2,1,0:T(8,128)(2,1)}, bf16[2,64,1280]{2,1,0:T(8,128)(2,1)}, u32[]{:S(2)}, u32[]{:S(2)}) collective-permute-start(bf16[2,64,1280]{2,1,0:T(8,128)(2,1)} %get-tuple-element.33), channel_id=1, source_target_pairs={{0,16},{1,17},{2,18},{3,19},{4,20},{5,21},{6,22},{7,23},{8,24},{9,... | collective-permute-start | bytes 983048 | tf_op jit(solution)/shard_map/ppermute | solution.py:170
  13.9 30.5 %collective-permute-start = (bf16[2,256,1280]{2,1,0:T(8,128)(2,1)}, bf16[2,256,1280]{2,1,0:T(8,128)(2,1)S(1)}, u32[]{:S(2)}, u32[]{:S(2)}) collective-permute-start(bf16[2,256,1280]{2,1,0:T(8,128)(2,1)} %get-tuple-element.29), channel_id=1, source_target_pairs={{0,4},{1,5},{2,6},{3,7},{4,0},{5,1},{6,2},{7,3},{8,12},{9,13},{10,... | collective-permute-start | bytes 3932168 | tf_op jit(solution)/shard_map/ppermute | solution.py:170
  19.4 26.3 %copy-start.14 = (s32[256]{0:T(256)S(1)}, s32[256]{0:T(256)}, u32[]{:S(2)}) copy-start(s32[256]{0:T(256)} %constant.81.clone) | copy-start | bytes 3076
  42.9 13.5 %collective-permute-start.6 = (bf16[2,64,1280]{2,1,0:T(8,128)(2,1)}, bf16[2,64,1280]{2,1,0:T(8,128)(2,1)S(1)}, u32[]{:S(2)}, u32[]{:S(2)}) collective-permute-start(bf16[2,64,1280]{2,1,0:T(8,128)(2,1)} %collective-permute-done.3.refs_4_), channel_id=1, source_target_pairs={{8,0},{9,1},{10,2},{11,3},{12,4},{13,5},{14,6},{15,7},{16,24},{17,... | collective-permute-start | bytes 983048 | tf_op jit(solution)/shard_map/ppermute | solution.py:170
  44.4 18.3 %collective-permute-start.5 = (bf16[2,64,1280]{2,1,0:T(8,128)(2,1)S(1)}, bf16[2,64,1280]{2,1,0:T(8,128)(2,1)S(1)}, u32[]{:S(2)}, u32[]{:S(2)}) collective-permute-start(bf16[2,64,1280]{2,1,0:T(8,128)(2,1)S(1)} %slice.54), channel_id=1, source_target_pairs={{0,8},{1,9},{2,10},{3,11},{8,16},{9,17},{10,18},{11,19},{12,4},{13... | collective-permute-start | bytes 983048 | tf_op jit(solution)/shard_map/ppermute | solution.py:170
  45.8 31.0 %collective-permute-start.10 = (bf16[2,128,1280]{2,1,0:T(8,128)(2,1)S(1)}, bf16[2,128,1280]{2,1,0:T(8,128)(2,1)S(1)}, u32[]{:S(2)}, u32[]{:S(2)}) collective-permute-start(bf16[2,128,1280]{2,1,0:T(8,128)(2,1)S(1)} %slice.55), channel_id=1, source_target_pairs={{0,8},{1,9},{2,10},{3,11},{8,16},{9,17},{10,18},{11,19},{12,4},{13... | collective-permute-start | bytes 1966088 | tf_op jit(solution)/shard_map/ppermute | solution.py:170
  63.9 19.9 %collective-permute-start.8 = (bf16[2,64,1280]{2,1,0:T(8,128)(2,1)S(1)}, bf16[2,64,1280]{2,1,0:T(8,128)(2,1)S(1)}, u32[]{:S(2)}, u32[]{:S(2)}) collective-permute-start(bf16[2,64,1280]{2,1,0:T(8,128)(2,1)S(1)} %get-tuple-element.59), channel_id=1, source_target_pairs={{0,4},{1,5},{2,6},{3,7},{4,0},{5,1},{6,2},{7,3},{8,12},{9,13},{10,... | collective-permute-start | bytes 983048 | tf_op jit(solution)/shard_map/ppermute | solution.py:170
  64.0 19.8 %collective-permute-start.9 = (bf16[2,64,1280]{2,1,0:T(8,128)(2,1)S(1)}, bf16[2,64,1280]{2,1,0:T(8,128)(2,1)S(1)}, u32[]{:S(2)}, u32[]{:S(2)}) collective-permute-start(bf16[2,64,1280]{2,1,0:T(8,128)(2,1)S(1)} %collective-permute-done.5.refs_1_), channel_id=1, source_target_pairs={{0,8},{1,9},{2,10},{3,11},{8,16},{9,17},{10,18},{11,19},{12,4},{13... | collective-permute-start | bytes 983048 | tf_op jit(solution)/shard_map/ppermute | solution.py:170
  65.4 26.0 %collective-permute-start.4 = (bf16[2,192,1280]{2,1,0:T(8,128)(2,1)S(1)}, bf16[2,192,1280]{2,1,0:T(8,128)(2,1)S(1)}, u32[]{:S(2)}, u32[]{:S(2)}) collective-permute-start(bf16[2,192,1280]{2,1,0:T(8,128)(2,1)S(1)} %pad_maximum_fusion), channel_id=1, source_target_pairs={{0,4},{1,5},{2,6},{3,7},{4,0},{5,1},{6,2},{7,3},{8,12},{9,13},{10,... | collective-permute-start | bytes 2949128 | tf_op jit(solution)/shard_map/ppermute | solution.py:170
  95.2 7.9 %collective-permute-start.11 = (bf16[512,640]{1,0:T(8,128)(2,1)S(1)}, bf16[512,640]{1,0:T(8,128)(2,1)S(1)}, u32[]{:S(2)}, u32[]{:S(2)}) collective-permute-start(bf16[512,640]{1,0:T(8,128)(2,1)S(1)} %last0.1), channel_id=1, source_target_pairs={{0,1},{1,0},{2,3},{3,2},{4,5},{5,4},{6,7},{7,6},{8,9},{9,8},{10,11... | collective-permute-start | bytes 1966088 | tf_op jit(solution)/shard_map/ppermute | solution.py:170
  99.1 3.3 %collective-permute-start.12 = (bf16[512,640]{1,0:T(8,128)(2,1)S(1)}, bf16[512,640]{1,0:T(8,128)(2,1)S(1)}, u32[]{:S(2)}, u32[]{:S(2)}) collective-permute-start(bf16[512,640]{1,0:T(8,128)(2,1)S(1)} %last5.1), channel_id=1, source_target_pairs={{0,1},{1,0},{2,3},{3,2},{4,5},{5,4},{6,7},{7,6},{8,9},{9,8},{10,11... | collective-permute-start | bytes 1966088 | tf_op jit(solution)/shard_map/ppermute | solution.py:170
  104.7 31.1 %collective-permute-start.14 = (bf16[512,640]{1,0:T(8,128)(2,1)S(1)}, bf16[512,640]{1,0:T(8,128)(2,1)S(1)}, u32[]{:S(2)}, u32[]{:S(2)}) collective-permute-start(bf16[512,640]{1,0:T(8,128)(2,1)S(1)} %fusion.13), channel_id=1, source_target_pairs={{0,2},{1,3},{2,0},{3,1},{4,6},{5,7},{6,4},{7,5},{8,10},{9,11},{10,... | collective-permute-start | bytes 1966088 | tf_op jit(solution)/shard_map/ppermute | solution.py:170
  108.6 27.2 %collective-permute-start.13 = (bf16[512,640]{1,0:T(8,128)(2,1)S(1)}, bf16[512,640]{1,0:T(8,128)(2,1)S(1)}, u32[]{:S(2)}, u32[]{:S(2)}) collective-permute-start(bf16[512,640]{1,0:T(8,128)(2,1)S(1)} %fusion.14), channel_id=1, source_target_pairs={{0,2},{1,3},{2,0},{3,1},{4,6},{5,7},{6,4},{7,5},{8,10},{9,11},{10,... | collective-permute-start | bytes 1966088 | tf_op jit(solution)/shard_map/ppermute | solution.py:170
  112.1 25.0 %copy-start.1 = (s32[8,8]{1,0:T(8,128)S(1)}, s32[8,8]{1,0:T(8,128)}, u32[]{:S(2)}) copy-start(s32[8,8]{1,0:T(8,128)} %param.14) | copy-start | bytes 772
  (7 other events, 10.9 us)

commit v3 on v2

--- a/solution.py
+++ b/solution.py
@@ -52,6 +52,38 @@
             transcendentals=0,
         ),
     )(key_vectors, value_vectors)
+
+
+def gather_kernel(flag_ref, far_ref, near_ref, two_ref, out_ref):
+    a = two_ref.shape[1]
+    ab = far_ref.shape[1]
+    far_here, near_here = (flag_ref[0] != 0, flag_ref[1] != 0)
+    for plane in range(2):
+        two = two_ref[plane]
+        out_ref[plane, :a] = jnp.where(far_here, far_ref[plane, :a], two)
+        out_ref[plane, a:ab] = far_ref[plane, a:]
+        out_ref[plane, ab:] = jnp.where(near_here, near_ref[plane, :a], two)
+
+
+def gather(flags, far, near, two):
+    rows = far.shape[1] + two.shape[1]
+    width = two.shape[2]
+    tile = width // 2
+    spec = lambda count: pl.BlockSpec((2, count, tile), lambda j, flags: (0, 0, j))
+    return pl.pallas_call(
+        gather_kernel,
+        grid_spec=pltpu.PrefetchScalarGridSpec(
+            num_scalar_prefetch=1,
+            grid=(width // tile,),
+            in_specs=[spec(far.shape[1]), spec(near.shape[1]), spec(two.shape[1])],
+            out_specs=spec(rows),
+        ),
+        out_shape=jax.ShapeDtypeStruct((2, rows, width), BF16),
+        name="gather",
+        cost_estimate=pl.CostEstimate(
+            flops=0, bytes_accessed=8 * rows * width, transcendentals=0
+        ),
+    )(flags, far, near, two)
 
 
 def attend_kernel(*refs, buffers, own, first, last, heads):
@@ -222,11 +254,8 @@
         carry = (state, carry[1])
         near_b = move(x_rows[:, a:ab], far_way)
         near_c = move(x_rows[:, ab:], far_way)
-        slot_far = jnp.where(within(far_block), z_far[:, :a], z_two)
-        slot_near = jnp.where(within(near_block), z_near[:, :a], z_two)
-        crossed = move(
-            jnp.concatenate([slot_far, z_far[:, a:], slot_near], axis=1), lambda t: t ^ 1
-        )
+        flags = jnp.stack([within(far_block), within(near_block)]).astype(jnp.int32)
+        crossed = move(gather(flags, z_far, z_near, z_two), lambda t: t ^ 1)
         z_three = move(z_two, lambda t: {4: 6, 5: 7, 2: 0, 3: 1}.get(t))
         carry = further(
             [x_rows, z_far, z_near, z_two],

time: 139 us -> 134 us (0.964)
  the two profiles are of different devices: /device:TPU:2 before, /device:TPU:0 now
where the time goes in v3:
time: 134 us; the launch traced here: 133 us
  waiting for transfers between devices  39.1 us (29%)
  Pallas kernels  34.6 us (26%)
  starting transfers between devices  26 us (19%)
  local copies, waits for them, and re-layouts  18.4 us (14%)
  matrix products  10.9 us (8%)
  other arithmetic  3.56 us (3%)
    ppermute x15, waiting for transfers between devices, move(): return lax.ppermute(array, AXES, route)  39.1 us
    pallas_call x5, Pallas kernels, attend(): pl.pallas_call(lambda *refs: attend_kernel(*refs, buffers=len(buffers), o...  29.4 us
    ppermute x15, starting transfers between devices, move(): return lax.ppermute(array, AXES, route)  26 us
    unnamed x36, local copies, waits for them, and re-layouts  8.22 us
    dynamic_slice x1, local copies, waits for them, and re-layouts, block_of(): return lax.dynamic_slice_in_dim(weight, number * out_width, out_width, 1)  8.16 us
    dot_general x6, matrix products, project(): jnp.dot(part, weights[index][low:high, first:last], preferred_element_typ...  5.56 us
    dot_general x6, matrix products, project(): jnp.dot(other, weights[index + 2][low:high, first:last], preferred_elemen...  5.38 us
    pallas_call x1, Pallas kernels, gather(): pl.pallas_call(gather_kernel, grid_spec=pltpu.PrefetchScalarGridSpec(num_...  2.86 us
  transfers between devices with their start and end apart: 15, of which 4 were waited for; matrix products, arithmetic and copies ran while one was open for 16% of the time, Pallas kernels for 23%

profile of v3, /device:TPU:0, one launch (start us, length us, event | category | flops | bytes accessed | tf_op | source)
XLA Modules:
  0.0 133.0 jit_solution(10779481042516693148)
XLA Ops:
  0.5 1.3 copy-done.6
  1.9 1.3 copy-done.8
  3.2 2.4 %pack.1 = (bf16[2,256,1280]{2,1,0:T(8,128)(2,1)}, bf16[2,128,1280]{2,1,0:T(8,128)(2,1)}, bf16[2,64,1280]{2,1,0:T(8,128)(2,1)S(1)}) custom-call(bf16[512,1280]{1,0:T(8,128)(2,1)S(1)} %copy-done.6, bf16[512,1280]{1,0:T(8,128)(2,1)S(1)} %copy-done.8), custom_call_target="tpu_custom_call" | custom-call | flops 671088640 | bytes 5242880 | tf_op jit(solution)/shard_map/pack/pallas_call | solution.py:39
  5.5 1.4 %collective-permute-start.2 = (bf16[2,128,1280]{2,1,0:T(8,128)(2,1)}, bf16[2,128,1280]{2,1,0:T(8,128)(2,1)}, u32[]{:S(2)}, u32[]{:S(2)}) collective-permute-start(bf16[2,128,1280]{2,1,0:T(8,128)(2,1)} %get-tuple-element.30), channel_id=1, source_target_pairs={{4,12},{5,13},{6,14},{7,15},{8,0},{9,1},{10,2},{11,3},{12,20},{13,... | collective-permute-start | bytes 1966088 | tf_op jit(solution)/shard_map/ppermute | solution.py:202
  7.0 6.1 %collective-permute-start.1 = (bf16[2,128,1280]{2,1,0:T(8,128)(2,1)}, bf16[2,128,1280]{2,1,0:T(8,128)(2,1)}, u32[]{:S(2)}, u32[]{:S(2)}) collective-permute-start(bf16[2,128,1280]{2,1,0:T(8,128)(2,1)} %get-tuple-element.30), channel_id=1, source_target_pairs={{0,8},{1,9},{2,10},{3,11},{8,16},{9,17},{10,18},{11,19},{12,4},{13... | collective-permute-start | bytes 1966088 | tf_op jit(solution)/shard_map/ppermute | solution.py:202
  13.1 3.1 %collective-permute-start.3 = (bf16[2,64,1280]{2,1,0:T(8,128)(2,1)S(1)}, bf16[2,64,1280]{2,1,0:T(8,128)(2,1)S(1)}, u32[]{:S(2)}, u32[]{:S(2)}) collective-permute-start(bf16[2,64,1280]{2,1,0:T(8,128)(2,1)S(1)} %get-tuple-element.34), channel_id=1, source_target_pairs={{0,16},{1,17},{2,18},{3,19},{4,20},{5,21},{6,22},{7,23},{8,24},{9,... | collective-permute-start | bytes 983048 | tf_op jit(solution)/shard_map/ppermute | solution.py:202
  18.4 1.3 copy-done.7
  19.7 1.3 copy-done.9
  21.0 7.1 %own.1 = (f32[10,8,512]{2,1,0:T(8,128)S(1)}, f32[10,128,512]{2,1,0:T(8,128)}) custom-call(bf16[512,1280]{1,0:T(8,128)(2,1)S(1)} %copy-done.2, bf16[512,1280]{1,0:T(8,128)(2,1)S(1)} %copy-done.7, bf16[512,1280]{1,0:T(8,128)(2,1)S(1)} %copy-done.9), custom_call_target="tpu_custom_call" | custom-call | flops 1342177280 | bytes 5242880 | tf_op jit(solution)/shard_map/own/pallas_call | solution.py:169
  28.9 12.1 %collective-permute-done.3.two_ref.refs_4_ = bf16[2,64,1280]{2,1,0:T(8,128)(2,1)S(1)} collective-permute-done((bf16[2,64,1280]{2,1,0:T(8,128)(2,1)S(1)}, bf16[2,64,1280]{2,1,0:T(8,128)(2,1)S(1)}, u32[]{:S(2)}, u32[]{:S(2)}) %collective-permute-start.3) | collective-permute-done | bytes 327712 | tf_op jit(solution)/shard_map/ppermute | solution.py:202
  42.3 4.3 %collective-permute-done.refs_1_ = bf16[2,256,1280]{2,1,0:T(8,128)(2,1)S(1)} collective-permute-done((bf16[2,256,1280]{2,1,0:T(8,128)(2,1)}, bf16[2,256,1280]{2,1,0:T(8,128)(2,1)S(1)}, u32[]{:S(2)}, u32[]{:S(2)}) %collective-permute-start) | collective-permute-done | bytes 1310752 | tf_op jit(solution)/shard_map/ppermute | solution.py:202
  47.4 3.9 %collective-permute-start.5 = (bf16[2,64,1280]{2,1,0:T(8,128)(2,1)}, bf16[2,64,1280]{2,1,0:T(8,128)(2,1)}, u32[]{:S(2)}, u32[]{:S(2)}) collective-permute-start(bf16[2,64,1280]{2,1,0:T(8,128)(2,1)} %slice.42), channel_id=1, source_target_pairs={{0,8},{1,9},{2,10},{3,11},{8,16},{9,17},{10,18},{11,19},{12,4},{13... | collective-permute-start | bytes 983048 | tf_op jit(solution)/shard_map/ppermute | solution.py:202
  52.2 2.8 %collective-permute-start.10 = (bf16[2,128,1280]{2,1,0:T(8,128)(2,1)}, bf16[2,128,1280]{2,1,0:T(8,128)(2,1)}, u32[]{:S(2)}, u32[]{:S(2)}) collective-permute-start(bf16[2,128,1280]{2,1,0:T(8,128)(2,1)} %slice.43), channel_id=1, source_target_pairs={{0,8},{1,9},{2,10},{3,11},{8,16},{9,17},{10,18},{11,19},{12,4},{13... | collective-permute-start | bytes 1966088 | tf_op jit(solution)/shard_map/ppermute | solution.py:202
  55.0 2.9 %gather.1 = bf16[2,192,1280]{2,1,0:T(8,128)(2,1)} custom-call(s32[2]{0:T(128)} %add_convert_fusion.1.flag_ref, bf16[2,128,1280]{2,1,0:T(8,128)(2,1)} %collective-permute-done.1.far_ref.refs_2_, bf16[2,128,1280]{2,1,0:T(8,128)(2,1)} %collective-permute-done.2.near_ref.refs_3_, bf16[2,64,1280]{2,1,0:T(8,128)(2,1)} %copy-done.4), custom_call_target="tpu_custom_call" | custom-call | bytes 1966080 | tf_op jit(solution)/shard_map/gather/pallas_call | solution.py:73
  58.9 9.2 %first.1 = (f32[10,8,512]{2,1,0:T(8,128)S(1)}, f32[10,128,512]{2,1,0:T(8,128)}) custom-call(bf16[512,1280]{1,0:T(8,128)(2,1)S(1)} %copy-done.2, bf16[2,256,1280]{2,1,0:T(8,128)(2,1)S(1)} %collective-permute-done.refs_1_, bf16[2,128,1280]{2,1,0:T(8,128)(2,1)} %collective-permute-done.1.far_ref.refs_2_, ...), custom_call_target="tpu_custom_call" | custom-call | flops 1509949440 | bytes 5242880 | tf_op jit(solution)/shard_map/first/pallas_call | solution.py:169
  68.2 2.1 %collective-permute-start.8 = (bf16[2,64,1280]{2,1,0:T(8,128)(2,1)S(1)}, bf16[2,64,1280]{2,1,0:T(8,128)(2,1)S(1)}, u32[]{:S(2)}, u32[]{:S(2)}) collective-permute-start(bf16[2,64,1280]{2,1,0:T(8,128)(2,1)S(1)} %broadcast_select_fusion), channel_id=1, source_target_pairs={{0,4},{1,5},{2,6},{3,7},{4,0},{5,1},{6,2},{7,3},{8,12},{9,13},{10,... | collective-permute-start | bytes 983048 | tf_op jit(solution)/shard_map/ppermute | solution.py:202
  71.6 8.2 %constant_dynamic-slice_fusion = (bf16[1280,1280]{1,0:T(8,128)(2,1)}, bf16[1280,1280]{1,0:T(8,128)(2,1)S(1)}, bf16[1280,1280]{1,0:T(8,128)(2,1)S(1)}, bf16[1280,1280]{1,0:T(8,128)(2,1)}) fusion(bf16[1280,5120]{1,0:T(8,128)(2,1)} %collective-permute-done.7, s32[]{:T(128)S(6)} %select_n.135, s32[]{:T(128)S(6)} %select_n.134, bf16[1280,5120]{1,0:T(8,128)(2,1)} %param.15), kind=kLoop, calls=%fused_computation.50 | loop fusion | bytes 26214408 | tf_op jit(solution)/shard_map/dynamic_slice | solution.py:299
  79.8 5.6 %middle.1 = (f32[10,8,512]{2,1,0:T(8,128)S(1)}, f32[10,128,512]{2,1,0:T(8,128)S(1)}) custom-call(bf16[512,1280]{1,0:T(8,128)(2,1)S(1)} %copy-done.2, bf16[2,64,1280]{2,1,0:T(8,128)(2,1)} %collective-permute-done.5.refs_1_, bf16[2,128,1280]{2,1,0:T(8,128)(2,1)} %collective-permute-done.10.refs_2_, bf16[2,64,1280]{2,1,0:T(8,128)(2,1)S(1)} %collective-permute-done.6.refs_3_, ...), custom_call_target="tpu_custom_call" | custom-call | flops 671088640 | bytes 5242880 | tf_op jit(solution)/shard_map/middle/pallas_call | solution.py:169
  85.4 1.5 %copy-done.3 = f32[10,128,512]{2,1,0:T(8,128)} copy-done((f32[10,128,512]{2,1,0:T(8,128)}, f32[10,128,512]{2,1,0:T(8,128)S(1)}, u32[]{:S(2)}) %copy-start.3) | copy-done | bytes 2621464
  87.3 3.8 %last0.1 = bf16[512,640]{1,0:T(8,128)(2,1)S(1)} custom-call(bf16[512,1280]{1,0:T(8,128)(2,1)S(1)} %copy-done.2, bf16[2,192,1280]{2,1,0:T(8,128)(2,1)S(1)} %collective-permute-done.4.refs_1_, bf16[2,64,1280]{2,1,0:T(8,128)(2,1)S(1)} %collective-permute-done.8.refs_2_, bf16[2,64,1280]{2,1,0:T(8,128)(2,1)S(1)} %collective-permute-done.9.refs_3_, ...), custom_call_target="tpu_custom_call" | custom-call | flops 419430400 | bytes 2621440 | tf_op jit(solution)/shard_map/last0/pallas_call | solution.py:169
  91.2 3.8 %last5.1 = bf16[512,640]{1,0:T(8,128)(2,1)S(1)} custom-call(bf16[512,1280]{1,0:T(8,128)(2,1)S(1)} %copy-done.2, bf16[2,192,1280]{2,1,0:T(8,128)(2,1)S(1)} %collective-permute-done.4.refs_1_, bf16[2,64,1280]{2,1,0:T(8,128)(2,1)S(1)} %collective-permute-done.8.refs_2_, bf16[2,64,1280]{2,1,0:T(8,128)(2,1)S(1)} %collective-permute-done.9.refs_3_, ...), custom_call_target="tpu_custom_call" | custom-call | flops 419430400 | bytes 2621440 | tf_op jit(solution)/shard_map/last5/pallas_call | solution.py:169
  100.6 1.5 %collective-permute-start.14 = (bf16[512,640]{1,0:T(8,128)(2,1)S(1)}, bf16[512,640]{1,0:T(8,128)(2,1)S(1)}, u32[]{:S(2)}, u32[]{:S(2)}) collective-permute-start(bf16[512,640]{1,0:T(8,128)(2,1)S(1)} %fusion.13), channel_id=1, source_target_pairs={{0,2},{1,3},{2,0},{3,1},{4,6},{5,7},{6,4},{7,5},{8,10},{9,11},{10,... | collective-permute-start | bytes 1966088 | tf_op jit(solution)/shard_map/ppermute | solution.py:202
  109.2 22.5 %collective-permute-done.13 = bf16[512,640]{1,0:T(8,128)(2,1)S(1)} collective-permute-done((bf16[512,640]{1,0:T(8,128)(2,1)S(1)}, bf16[512,640]{1,0:T(8,128)(2,1)S(1)}, u32[]{:S(2)}, u32[]{:S(2)}) %collective-permute-start.13) | collective-permute-done | bytes 655392 | tf_op jit(solution)/shard_map/ppermute | solution.py:202
  131.6 1.3 %add_convert_fusion = bf16[512,1280]{1,0:T(8,128)(2,1)} fusion(f32[512,1280]{1,0:T(8,128)S(1)} %fusion.1, bf16[512,640]{1,0:T(8,128)(2,1)S(1)} %collective-permute-done.14, bf16[512,640]{1,0:T(8,128)(2,1)S(1)} %collective-permute-done.13), kind=kLoop, calls=%fused_computation.3 | loop fusion | flops 3932160 | bytes 5242880 | tf_op jit(solution)/shard_map/convert_element_type | solution.py:330
  (89 shorter events, 22.1 us)
Async XLA Ops:
  0.0 17.0 %copy-start = (s32[8,8]{1,0:T(8,128)S(1)}, s32[8,8]{1,0:T(8,128)}, u32[]{:S(2)}) copy-start(s32[8,8]{1,0:T(8,128)} %param.14) | copy-start | bytes 772
  0.0 18.2 %copy-start.14 = (pred[4,576]{1,0:T(4,128)(4,1)S(1)}, pred[4,576]{1,0:T(4,128)(4,1)}, u32[]{:S(2)}) copy-start(pred[4,576]{1,0:T(4,128)(4,1)} %constant.78.clone) | copy-start | bytes 6916
  0.0 18.3 %copy-start.13 = (pred[5,320]{1,0:T(8,128)(4,1)S(1)}, pred[5,320]{1,0:T(8,128)(4,1)}, u32[]{:S(2)}) copy-start(pred[5,320]{1,0:T(8,128)(4,1)} %constant.82.clone) | copy-start | bytes 4804
  0.0 18.4 %copy-start.2 = (bf16[512,1280]{1,0:T(8,128)(2,1)S(1)}, bf16[512,1280]{1,0:T(8,128)(2,1)}, u32[]{:S(2)}) copy-start(bf16[512,1280]{1,0:T(8,128)(2,1)} %refs_0_.11) | copy-start | bytes 3932164
  0.0 68.1 %collective-permute-start.7 = (bf16[1280,5120]{1,0:T(8,128)(2,1)}, bf16[1280,5120]{1,0:T(8,128)(2,1)}, u32[]{:S(2)}, u32[]{:S(2)}) collective-permute-start(bf16[1280,5120]{1,0:T(8,128)(2,1)} %param.15), channel_id=1, source_target_pairs={{0,1},{1,0},{2,3},{3,2},{4,5},{5,4},{6,7},{7,6},{8,9},{9,8},{10,11... | collective-permute-start | bytes 39321608 | tf_op jit(solution)/shard_map/ppermute | solution.py:202
  5.5 22.7 %copy-start.17 = (pred[3,256]{1,0:T(4,128)(4,1)S(1)}, pred[3,256]{1,0:T(4,128)(4,1)}, u32[]{:S(2)}) copy-start(pred[3,256]{1,0:T(4,128)(4,1)} %constant.80.clone) | copy-start | bytes 2308
  5.5 22.7 %copy-start.15 = (s32[320]{0:T(512)S(1)}, s32[320]{0:T(512)}, u32[]{:S(2)}) copy-start(s32[320]{0:T(512)} %constant.83.clone) | copy-start | bytes 3844
  5.5 23.4 %copy-start.12 = (s32[576]{0:T(1024)S(1)}, s32[576]{0:T(1024)}, u32[]{:S(2)}) copy-start(s32[576]{0:T(1024)} %constant.79.clone) | copy-start | bytes 6916
  5.5 36.8 %collective-permute-start.2 = (bf16[2,128,1280]{2,1,0:T(8,128)(2,1)}, bf16[2,128,1280]{2,1,0:T(8,128)(2,1)}, u32[]{:S(2)}, u32[]{:S(2)}) collective-permute-start(bf16[2,128,1280]{2,1,0:T(8,128)(2,1)} %get-tuple-element.30), channel_id=1, source_target_pairs={{4,12},{5,13},{6,14},{7,15},{8,0},{9,1},{10,2},{11,3},{12,20},{13,... | collective-permute-start | bytes 1966088 | tf_op jit(solution)/shard_map/ppermute | solution.py:202
  7.0 35.3 %collective-permute-start.1 = (bf16[2,128,1280]{2,1,0:T(8,128)(2,1)}, bf16[2,128,1280]{2,1,0:T(8,128)(2,1)}, u32[]{:S(2)}, u32[]{:S(2)}) collective-permute-start(bf16[2,128,1280]{2,1,0:T(8,128)(2,1)} %get-tuple-element.30), channel_id=1, source_target_pairs={{0,8},{1,9},{2,10},{3,11},{8,16},{9,17},{10,18},{11,19},{12,4},{13... | collective-permute-start | bytes 1966088 | tf_op jit(solution)/shard_map/ppermute | solution.py:202
  13.1 27.9 %collective-permute-start.3 = (bf16[2,64,1280]{2,1,0:T(8,128)(2,1)S(1)}, bf16[2,64,1280]{2,1,0:T(8,128)(2,1)S(1)}, u32[]{:S(2)}, u32[]{:S(2)}) collective-permute-start(bf16[2,64,1280]{2,1,0:T(8,128)(2,1)S(1)} %get-tuple-element.34), channel_id=1, source_target_pairs={{0,16},{1,17},{2,18},{3,19},{4,20},{5,21},{6,22},{7,23},{8,24},{9,... | collective-permute-start | bytes 983048 | tf_op jit(solution)/shard_map/ppermute | solution.py:202
  16.1 30.5 %collective-permute-start = (bf16[2,256,1280]{2,1,0:T(8,128)(2,1)}, bf16[2,256,1280]{2,1,0:T(8,128)(2,1)S(1)}, u32[]{:S(2)}, u32[]{:S(2)}) collective-permute-start(bf16[2,256,1280]{2,1,0:T(8,128)(2,1)} %get-tuple-element.29), channel_id=1, source_target_pairs={{0,4},{1,5},{2,6},{3,7},{4,0},{5,1},{6,2},{7,3},{8,12},{9,13},{10,... | collective-permute-start | bytes 3932168 | tf_op jit(solution)/shard_map/ppermute | solution.py:202
  21.0 30.2 %copy-start.16 = (s32[256]{0:T(256)S(1)}, s32[256]{0:T(256)}, u32[]{:S(2)}) copy-start(s32[256]{0:T(256)} %constant.81.clone) | copy-start | bytes 3076
  41.0 27.1 %collective-permute-start.6 = (bf16[2,64,1280]{2,1,0:T(8,128)(2,1)S(1)}, bf16[2,64,1280]{2,1,0:T(8,128)(2,1)S(1)}, u32[]{:S(2)}, u32[]{:S(2)}) collective-permute-start(bf16[2,64,1280]{2,1,0:T(8,128)(2,1)S(1)} %collective-permute-done.3.two_ref.refs_4_), channel_id=1, source_target_pairs={{8,0},{9,1},{10,2},{11,3},{12,4},{13,5},{14,6},{15,7},{16,24},{17,... | collective-permute-start | bytes 983048 | tf_op jit(solution)/shard_map/ppermute | solution.py:202
  47.4 20.8 %collective-permute-start.5 = (bf16[2,64,1280]{2,1,0:T(8,128)(2,1)}, bf16[2,64,1280]{2,1,0:T(8,128)(2,1)}, u32[]{:S(2)}, u32[]{:S(2)}) collective-permute-start(bf16[2,64,1280]{2,1,0:T(8,128)(2,1)} %slice.42), channel_id=1, source_target_pairs={{0,8},{1,9},{2,10},{3,11},{8,16},{9,17},{10,18},{11,19},{12,4},{13... | collective-permute-start | bytes 983048 | tf_op jit(solution)/shard_map/ppermute | solution.py:202
  52.2 27.6 %collective-permute-start.10 = (bf16[2,128,1280]{2,1,0:T(8,128)(2,1)}, bf16[2,128,1280]{2,1,0:T(8,128)(2,1)}, u32[]{:S(2)}, u32[]{:S(2)}) collective-permute-start(bf16[2,128,1280]{2,1,0:T(8,128)(2,1)} %slice.43), channel_id=1, source_target_pairs={{0,8},{1,9},{2,10},{3,11},{8,16},{9,17},{10,18},{11,19},{12,4},{13... | collective-permute-start | bytes 1966088 | tf_op jit(solution)/shard_map/ppermute | solution.py:202
  57.8 29.1 %collective-permute-start.4 = (bf16[2,192,1280]{2,1,0:T(8,128)(2,1)}, bf16[2,192,1280]{2,1,0:T(8,128)(2,1)S(1)}, u32[]{:S(2)}, u32[]{:S(2)}) collective-permute-start(bf16[2,192,1280]{2,1,0:T(8,128)(2,1)} %gather.1), channel_id=1, source_target_pairs={{0,4},{1,5},{2,6},{3,7},{4,0},{5,1},{6,2},{7,3},{8,12},{9,13},{10,... | collective-permute-start | bytes 2949128 | tf_op jit(solution)/shard_map/ppermute | solution.py:202
  68.2 19.0 %collective-permute-start.8 = (bf16[2,64,1280]{2,1,0:T(8,128)(2,1)S(1)}, bf16[2,64,1280]{2,1,0:T(8,128)(2,1)S(1)}, u32[]{:S(2)}, u32[]{:S(2)}) collective-permute-start(bf16[2,64,1280]{2,1,0:T(8,128)(2,1)S(1)} %broadcast_select_fusion), channel_id=1, source_target_pairs={{0,4},{1,5},{2,6},{3,7},{4,0},{5,1},{6,2},{7,3},{8,12},{9,13},{10,... | collective-permute-start | bytes 983048 | tf_op jit(solution)/shard_map/ppermute | solution.py:202
  70.3 16.9 %collective-permute-start.9 = (bf16[2,64,1280]{2,1,0:T(8,128)(2,1)}, bf16[2,64,1280]{2,1,0:T(8,128)(2,1)S(1)}, u32[]{:S(2)}, u32[]{:S(2)}) collective-permute-start(bf16[2,64,1280]{2,1,0:T(8,128)(2,1)} %collective-permute-done.5.refs_1_), channel_id=1, source_target_pairs={{0,8},{1,9},{2,10},{3,11},{8,16},{9,17},{10,18},{11,19},{12,4},{13... | collective-permute-start | bytes 983048 | tf_op jit(solution)/shard_map/ppermute | solution.py:202
  91.1 7.9 %collective-permute-start.11 = (bf16[512,640]{1,0:T(8,128)(2,1)S(1)}, bf16[512,640]{1,0:T(8,128)(2,1)S(1)}, u32[]{:S(2)}, u32[]{:S(2)}) collective-permute-start(bf16[512,640]{1,0:T(8,128)(2,1)S(1)} %last0.1), channel_id=1, source_target_pairs={{0,1},{1,0},{2,3},{3,2},{4,5},{5,4},{6,7},{7,6},{8,9},{9,8},{10,11... | collective-permute-start | bytes 1966088 | tf_op jit(solution)/shard_map/ppermute | solution.py:202
  94.9 3.3 %collective-permute-start.12 = (bf16[512,640]{1,0:T(8,128)(2,1)S(1)}, bf16[512,640]{1,0:T(8,128)(2,1)S(1)}, u32[]{:S(2)}, u32[]{:S(2)}) collective-permute-start(bf16[512,640]{1,0:T(8,128)(2,1)S(1)} %last5.1), channel_id=1, source_target_pairs={{0,1},{1,0},{2,3},{3,2},{4,5},{5,4},{6,7},{7,6},{8,9},{9,8},{10,11... | collective-permute-start | bytes 1966088 | tf_op jit(solution)/shard_map/ppermute | solution.py:202
  100.6 31.1 %collective-permute-start.14 = (bf16[512,640]{1,0:T(8,128)(2,1)S(1)}, bf16[512,640]{1,0:T(8,128)(2,1)S(1)}, u32[]{:S(2)}, u32[]{:S(2)}) collective-permute-start(bf16[512,640]{1,0:T(8,128)(2,1)S(1)} %fusion.13), channel_id=1, source_target_pairs={{0,2},{1,3},{2,0},{3,1},{4,6},{5,7},{6,4},{7,5},{8,10},{9,11},{10,... | collective-permute-start | bytes 1966088 | tf_op jit(solution)/shard_map/ppermute | solution.py:202
  104.4 27.3 %collective-permute-start.13 = (bf16[512,640]{1,0:T(8,128)(2,1)S(1)}, bf16[512,640]{1,0:T(8,128)(2,1)S(1)}, u32[]{:S(2)}, u32[]{:S(2)}) collective-permute-start(bf16[512,640]{1,0:T(8,128)(2,1)S(1)} %fusion.14), channel_id=1, source_target_pairs={{0,2},{1,3},{2,0},{3,1},{4,6},{5,7},{6,4},{7,5},{8,10},{9,11},{10,... | collective-permute-start | bytes 1966088 | tf_op jit(solution)/shard_map/ppermute | solution.py:202
  107.9 25.1 %copy-start.1 = (s32[8,8]{1,0:T(8,128)S(1)}, s32[8,8]{1,0:T(8,128)}, u32[]{:S(2)}) copy-start(s32[8,8]{1,0:T(8,128)} %param.14) | copy-start | bytes 772
  (9 other events, 25.7 us)

commit v4 on v2

--- a/solution.py
+++ b/solution.py
@@ -54,7 +54,7 @@
     )(key_vectors, value_vectors)
 
 
-def attend_kernel(*refs, buffers, own, first, last, heads):
+def attend_kernel(*refs, buffers, own, first, last, low, high):
     refs = list(refs)
     query_ref = refs.pop(0)
     own_refs = [refs.pop(0), refs.pop(0)] if own else None
@@ -63,10 +63,10 @@
     state_in, accum_in = (None, None) if first else (refs.pop(0), refs.pop(0))
     query_count = query_ref.shape[0]
     factor = math.log2(math.e) / math.sqrt(HEAD_DIM)
-    if buffers:
-        bias = jnp.concatenate([bias_ref[...]] * (query_count // HEAD_DIM), axis=1)
-    for head in range(heads):
-        span = slice(head * HEAD_DIM, (head + 1) * HEAD_DIM)
+    together = 2
+
+    def one(head):
+        span = pl.ds(pl.multiple_of((head + low) * HEAD_DIM, HEAD_DIM), HEAD_DIM)
         if own:
             key, value = (own_refs[0][:, span], own_refs[1][:, span])
         else:
@@ -76,74 +76,59 @@
             key, query_ref[:, span], (((1,), (1,)), ((), ())), preferred_element_type=F32
         )
         if buffers:
-            scores = scores + bias
+            scores = scores + jnp.concatenate([bias_ref[...]] * (query_count // HEAD_DIM), axis=1)
         top = jnp.max(scores, axis=0, keepdims=True)
         if not first:
-            top_in = state_in[head, 0:1, :]
-            top = jnp.maximum(top, top_in)
-            shrink = jnp.exp2((top_in - top) * factor)
-        level = top * factor
-        weights = jnp.exp2(scores * factor - level)
+            state = state_in[head + low]
+            top = jnp.maximum(top, state[0:1])
+            shrink = jnp.exp2((state[0:1] - top) * factor)
+        weights = jnp.exp2(scores * factor - top * factor)
         total = jnp.sum(weights, axis=0, keepdims=True)
         accum = jnp.dot(value.T, weights.astype(BF16), preferred_element_type=F32)
         if not first:
-            total = total + shrink * state_in[head, 1:2, :]
-            accum = accum + shrink * accum_in[head]
+            total = total + shrink * state[1:2]
+            accum = accum + shrink * accum_in[head + low]
         if last:
-            refs[0][:, span] = (accum / total).T.astype(BF16)
+            out = pl.ds(pl.multiple_of(head * HEAD_DIM, HEAD_DIM), HEAD_DIM)
+            refs[0][:, out] = (accum / total).T.astype(BF16)
         else:
             refs[0][head, 0:1, :] = top
             refs[0][head, 1:2, :] = total
             refs[1][head] = accum
 
+    def several(step, nothing):
+        for member in range(together):
+            one(step * together + member)
+        return nothing
+
+    lax.fori_loop(0, (high - low) // together, several, 0)
+
 
 def attend(query_vectors, own_pair, buffers, bias, carry, last, low, high, name):
     row_count = query_vectors.shape[0]
-    heads = 5 if (high - low) % 5 == 0 else 1
-    span = heads * HEAD_DIM
-    skip = low // heads
-    assert low % heads == 0
-    whole = pl.BlockSpec((row_count, span), lambda h: (0, h + skip))
-    state = pl.BlockSpec((heads, 8, row_count), lambda h: (h, 0, 0))
-    accum = pl.BlockSpec((heads, HEAD_DIM, row_count), lambda h: (h, 0, 0))
-    state_in = pl.BlockSpec((heads, 8, row_count), lambda h: (h + skip, 0, 0))
-    accum_in = pl.BlockSpec((heads, HEAD_DIM, row_count), lambda h: (h + skip, 0, 0))
-    operands, specs = ([query_vectors], [whole])
     own = own_pair is not None
+    first = carry is None
+    operands = [query_vectors] + (list(own_pair) if own else list(buffers) + [bias])
+    operands += [] if first else list(carry)
     count = row_count if own else bias.shape[0]
-    if own:
-        operands += list(own_pair)
-        specs += [whole, whole]
-    for buffer in buffers:
-        operands.append(buffer)
-        specs.append(pl.BlockSpec((2, buffer.shape[1], span), lambda h: (0, 0, h + skip)))
-    if buffers:
-        operands.append(bias)
-        specs.append(pl.BlockSpec((count, HEAD_DIM), lambda h: (0, 0)))
-    first = carry is None
-    if not first:
-        operands += list(carry)
-        specs += [state_in, accum_in]
     width = (high - low) * HEAD_DIM
     if last:
         shapes = [jax.ShapeDtypeStruct((row_count, width), BF16)]
-        out_specs = [pl.BlockSpec((row_count, span), lambda h: (0, h))]
     else:
         shapes = [
             jax.ShapeDtypeStruct((high - low, 8, row_count), F32),
             jax.ShapeDtypeStruct((high - low, HEAD_DIM, row_count), F32),
         ]
-        out_specs = [state, accum]
+    held = pl.BlockSpec(memory_space=pltpu.VMEM)
     return pl.pallas_call(
         lambda *refs: attend_kernel(
-            *refs, buffers=len(buffers), own=own, first=first, last=last, heads=heads
+            *refs, buffers=len(buffers), own=own, first=first, last=last, low=low, high=high
         ),
-        grid=((high - low) // heads,),
-        in_specs=specs,
-        out_specs=out_specs,
+        in_specs=[held] * len(operands),
+        out_specs=[held] * len(shapes),
         out_shape=shapes,
         name=name,
-        compiler_params=pltpu.CompilerParams(vmem_limit_bytes=48 << 20),
+        compiler_params=pltpu.CompilerParams(vmem_limit_bytes=16 << 20),
         cost_estimate=pl.CostEstimate(
             flops=4 * row_count * count * width,
             bytes_accessed=8 * row_count * width,
@@ -200,58 +185,64 @@
             query_vectors, None, buffers, bias_of(pieces), carry, False, 0, head_count, name
         )
 
+    def blocks_of(*sources):
+        return [
+            lax.dynamic_slice_in_dim(source, number * out_width, out_width, 1)
+            for source in sources
+            for number in (away, home)
+        ]
+
     if block_count == 8:
         a, ab = (row_count // 8, row_count // 4)
         side = jnp.where(my_block % 2 == 0, 1, -1)
-        far_way = lambda t: t + 2 if t % 2 == 0 else t - 2
-        near_way = lambda t: t - 2 if t % 2 == 0 else t + 2
+        far_of = lambda t: t - 2 if t % 2 == 0 else t + 2
+        near_of = lambda t: t + 2 if t % 2 == 0 else t - 2
+        twin_if = lambda source: lambda t: t ^ 1 if 0 <= source(t) < block_count else None
+        ends = (0, 1, block_count - 2, block_count - 1)
         partner, two, opposite = (my_block ^ 1, my_block ^ 4, my_block ^ 6)
         far_block, near_block = (my_block - 2 * side, my_block + 2 * side)
         adjacent, far_cross = (my_block - side, my_block + 3 * side)
         at_end = (my_block < 2) | (my_block >= block_count - 2)
-        none = jnp.int32(-1)
-        three = jnp.where(at_end, opposite, none)
+        three = jnp.where(at_end, opposite, -1)
 
         sent, sent_ab, sent_a = pack(key_vectors, value_vectors, [(0, near), (0, ab), (0, a)])
         x_rows = move(sent, lambda t: t ^ 1)
-        z_far = move(sent_ab, far_way)
-        z_near = move(sent_ab, near_way)
+        z_far = move(sent_ab, near_of)
+        z_near = move(sent_ab, far_of)
         z_two = move(sent_a, lambda t: t ^ 4)
         carry = attend(query_vectors, own_pair, [], None, None, False, 0, head_count, "own")
-        x_rows, z_far, z_near, state = lax.optimization_barrier((x_rows, z_far, z_near, carry[0]))
-        carry = (state, carry[1])
-        near_b = move(x_rows[:, a:ab], far_way)
-        near_c = move(x_rows[:, ab:], far_way)
-        slot_far = jnp.where(within(far_block), z_far[:, :a], z_two)
-        slot_near = jnp.where(within(near_block), z_near[:, :a], z_two)
-        crossed = move(
-            jnp.concatenate([slot_far, z_far[:, a:], slot_near], axis=1), lambda t: t ^ 1
-        )
+        z_far, z_near, state, out_weight, moved = lax.optimization_barrier(
+            (z_far, z_near, carry[0], out_weight, moved)
+        )
+        cross_far = move(z_far, twin_if(far_of))
+        cross_near = move(z_near[:, :a], twin_if(near_of))
+        weights = blocks_of(out_weight, moved)
+        x_rows, z_two, state, weights = lax.optimization_barrier((x_rows, z_two, state, weights))
+        near_bc = move(x_rows[:, a:], near_of)
+        cross_two = move(z_two, lambda t: t ^ 1)
         z_three = move(z_two, lambda t: {4: 6, 5: 7, 2: 0, 3: 1}.get(t))
         carry = further(
             [x_rows, z_far, z_near, z_two],
             [(partner, 0, near), (far_block, 0, ab), (near_block, 0, ab), (two, 0, a)],
-            carry,
+            (state, carry[1]),
             "first",
         )
-        near_b, z_three, state, out_weight, moved = lax.optimization_barrier(
-            (near_b, z_three, carry[0], out_weight, moved)
-        )
-        carry = (state, carry[1])
-        cross_last = move(jnp.where(at_end, z_three, z_two), lambda t: t ^ 1)
-        chain_b = move(near_b, far_way)
+        z_three, state = lax.optimization_barrier((z_three, carry[0]))
+        cross_three = move(z_three, lambda t: t ^ 1 if t in ends else None)
+        near_bc, state = lax.optimization_barrier((near_bc, state))
+        chain_b = move(near_bc[:, : ab - a], near_of)
         carry = further(
-            [near_b, near_c, z_three],
-            [(adjacent, a, ab - a), (adjacent, ab, near - ab), (three, 0, a)],
-            carry,
+            [near_bc, z_three],
+            [(adjacent, a, near - a), (three, 0, a)],
+            (state, carry[1]),
             "middle",
         )
-        buffers = [crossed, cross_last, chain_b]
+        buffers = [cross_far, cross_near, cross_two, cross_three, chain_b]
         pieces = [
-            (jnp.where(within(far_cross), far_cross, two ^ 1), 0, a),
-            (far_cross, a, ab - a),
-            (jnp.where(within(adjacent), adjacent, two ^ 1), 0, a),
-            (jnp.where(at_end, opposite ^ 1, two ^ 1), 0, a),
+            (far_cross, 0, ab),
+            (adjacent, 0, a),
+            (two ^ 1, 0, a),
+            (jnp.where(at_end, opposite ^ 1, -1), 0, a),
             (my_block - 3 * side, a, ab - a),
         ]
     else:
@@ -265,15 +256,10 @@
         carry = attend(query_vectors, own_pair, [], None, None, False, 0, head_count, "own")
         carry = further([jnp.concatenate(received[:2], axis=1)], pieces[:2], carry, "first")
         buffers, pieces = ([jnp.concatenate(received[2:], axis=1)], pieces[2:])
-
-    def block_of(weight, number):
-        return lax.dynamic_slice_in_dim(weight, number * out_width, out_width, 1)
-
-    weights = lax.optimization_barrier(
-        [block_of(weight, number) for weight in (out_weight, moved) for number in (away, home)]
-    )
+        weights = lax.optimization_barrier(blocks_of(out_weight, moved))
+
     bias = bias_of(pieces)
-    cut = head_count // 2
+    cut = 2 * ((head_count + 2) // 4)
     parts = []
     for low, high in ((0, cut), (cut, head_count)):
         (part,) = attend(
@@ -293,10 +279,10 @@
         return total
 
     half = out_width // 2
-    arrived = [
-        move(project(0, first, first + half).astype(BF16), same, lambda h: h ^ 2)
-        for first in (0, half)
-    ]
+    sent = [project(0, first, first + half).astype(BF16) for first in (0, half)]
+    sent[1], held = lax.optimization_barrier((sent[1], [part[:2] for part in parts]))
+    parts = [kept + part[2:] for kept, part in zip(held, parts)]
+    arrived = [move(block, same, lambda h: h ^ 2) for block in sent]
     kept, arrived[0] = lax.optimization_barrier((project(1, 0, out_width), arrived[0]))
     return (kept + jnp.concatenate(arrived, axis=1).astype(F32)).astype(BF16)
 

time: 139 us -> 129 us (0.928)
  starting transfers between devices: 20.4 us -> 25.2 us
  Pallas kernels: 31.7 us -> 27.2 us
  local copies, waits for them, and re-layouts: 16 us -> 12.7 us
  waiting for transfers between devices: 53.5 us -> 50.3 us
    ppermute x15 -> x16, starting transfers between devices: 20.4 us -> 25.2 us  [move(): return lax.ppermute(array, AXES, route)]
    pallas_call x5, Pallas kernels: 29.3 us -> 24.8 us  [attend(): pl.pallas_call(lambda *refs: attend_kernel(*refs, buffers=len(buffers), o...]
    ppermute x15 -> x16, waiting for transfers between devices: 53.5 us -> 50.3 us  [move(): return lax.ppermute(array, AXES, route)]
    dynamic_slice x1, local copies, waits for them, and re-layouts: 8.12 us -> 5.3 us  [blocks_of(): lax.dynamic_slice_in_dim(source, number * out_width, out_width, 1)]
    unnamed x32 -> x30, local copies, waits for them, and re-layouts: 7.45 us -> 6.85 us
  transfers between devices with their start and end apart: 15 -> 16, of which waited for: 6 -> 9; matrix products, arithmetic and copies ran while one was open for 15% -> 12% of each run, Pallas kernels for 20% -> 18%
where the time goes in v4:
time: 129 us; the launch traced here: 128 us
  waiting for transfers between devices  50.3 us (39%)
  Pallas kernels  27.2 us (21%)
  starting transfers between devices  25.2 us (20%)
  local copies, waits for them, and re-layouts  12.7 us (10%)
  matrix products  9.67 us (7%)
  other arithmetic  2.86 us (2%)
    ppermute x16, waiting for transfers between devices, move(): return lax.ppermute(array, AXES, route)  50.3 us
    ppermute x16, starting transfers between devices, move(): return lax.ppermute(array, AXES, route)  25.2 us
    pallas_call x5, Pallas kernels, attend(): pl.pallas_call(lambda *refs: attend_kernel(*refs, buffers=len(buffers), o...  24.8 us
    unnamed x30, local copies, waits for them, and re-layouts  6.85 us
    dynamic_slice x1, local copies, waits for them, and re-layouts, blocks_of(): lax.dynamic_slice_in_dim(source, number * out_width, out_width, 1)  5.3 us
    dot_general x6, matrix products, project(): jnp.dot(part, weights[index][low:high, first:last], preferred_element_typ...  4.94 us
    dot_general x6, matrix products, project(): jnp.dot(other, weights[index + 2][low:high, first:last], preferred_elemen...  4.73 us
  transfers between devices with their start and end apart: 16, of which 9 were waited for; matrix products, arithmetic and copies ran while one was open for 12% of the time, Pallas kernels for 18%

profile of v4, /device:TPU:2, one launch (start us, length us, event | category | flops | bytes accessed | tf_op | source)
XLA Modules:
  0.0 128.3 jit_solution(8761264470361942799)
XLA Ops:
  0.1 1.4 %copy-done.5 = bf16[512,1280]{1,0:T(8,128)(2,1)S(1)} copy-done((bf16[512,1280]{1,0:T(8,128)(2,1)S(1)}, bf16[512,1280]{1,0:T(8,128)(2,1)}, u32[]{:S(2)}) %copy-start.5) | copy-done | bytes 1310744
  2.8 2.4 %pack.1 = (bf16[2,256,1280]{2,1,0:T(8,128)(2,1)}, bf16[2,128,1280]{2,1,0:T(8,128)(2,1)}, bf16[2,64,1280]{2,1,0:T(8,128)(2,1)}) custom-call(bf16[512,1280]{1,0:T(8,128)(2,1)S(1)} %copy-done.5, bf16[512,1280]{1,0:T(8,128)(2,1)S(1)} %copy-done.7), custom_call_target="tpu_custom_call" | custom-call | flops 671088640 | bytes 5242880 | tf_op jit(solution)/shard_map/pack/pallas_call | solution.py:39
  6.5 4.6 %collective-permute-start.1 = (bf16[2,128,1280]{2,1,0:T(8,128)(2,1)}, bf16[2,128,1280]{2,1,0:T(8,128)(2,1)S(1)}, u32[]{:S(2)}, u32[]{:S(2)}) collective-permute-start(bf16[2,128,1280]{2,1,0:T(8,128)(2,1)} %get-tuple-element.37), channel_id=1, source_target_pairs={{4,12},{5,13},{6,14},{7,15},{8,0},{9,1},{10,2},{11,3},{12,20},{13,... | collective-permute-start | bytes 1966088 | tf_op jit(solution)/shard_map/ppermute | solution.py:155
  11.5 3.2 %collective-permute-start.6 = (bf16[2,64,1280]{2,1,0:T(8,128)(2,1)}, bf16[2,64,1280]{2,1,0:T(8,128)(2,1)}, u32[]{:S(2)}, u32[]{:S(2)}) collective-permute-start(bf16[2,64,1280]{2,1,0:T(8,128)(2,1)} %get-tuple-element.42), channel_id=1, source_target_pairs={{0,16},{1,17},{2,18},{3,19},{4,20},{5,21},{6,22},{7,23},{8,24},{9,... | collective-permute-start | bytes 983048 | tf_op jit(solution)/shard_map/ppermute | solution.py:155
  15.7 1.3 %copy-done.6 = bf16[512,1280]{1,0:T(8,128)(2,1)S(1)} copy-done((bf16[512,1280]{1,0:T(8,128)(2,1)S(1)}, bf16[512,1280]{1,0:T(8,128)(2,1)}, u32[]{:S(2)}) %copy-start.6) | copy-done | bytes 1310744
  18.4 6.4 %own.1 = (f32[10,8,512]{2,1,0:T(8,128)S(1)}, f32[10,128,512]{2,1,0:T(8,128)S(1)}) custom-call(bf16[512,1280]{1,0:T(8,128)(2,1)S(1)} %copy-done.2, bf16[512,1280]{1,0:T(8,128)(2,1)S(1)} %copy-done.6, bf16[512,1280]{1,0:T(8,128)(2,1)S(1)} %copy-done.8), custom_call_target="tpu_custom_call" | custom-call | flops 1342177280 | bytes 5242880 | tf_op jit(solution)/shard_map/own/pallas_call | solution.py:123
  24.8 1.4 %copy-done.3 = f32[10,128,512]{2,1,0:T(8,128)} copy-done((f32[10,128,512]{2,1,0:T(8,128)}, f32[10,128,512]{2,1,0:T(8,128)S(1)}, u32[]{:S(2)}) %copy-start.3) | copy-done | bytes 2621464
  26.5 5.3 %constant_dynamic-slice_fusion.1 = (bf16[1280,1280]{1,0:T(8,128)(2,1)S(1)}, bf16[1280,1280]{1,0:T(8,128)(2,1)S(1)}, bf16[1280,1280]{1,0:T(8,128)(2,1)S(1)}, bf16[1280,1280]{1,0:T(8,128)(2,1)S(1)}) fusion(bf16[1280,5120]{1,0:T(8,128)(2,1)} %collective-permute-done.2, s32[]{:T(128)S(6)} %select_n.101, s32[]{:T(128)S(6)} %select_n.100, bf16[1280,5120]{1,0:T(8,128)(2,1)} %param.15), kind=kLoop, calls=%fused_computation.46 | loop fusion | bytes 26214408 | tf_op jit(solution)/shard_map/dynamic_slice | solution.py:190
  31.8 7.7 %collective-permute-done.6.refs_4_ = bf16[2,64,1280]{2,1,0:T(8,128)(2,1)} collective-permute-done((bf16[2,64,1280]{2,1,0:T(8,128)(2,1)}, bf16[2,64,1280]{2,1,0:T(8,128)(2,1)}, u32[]{:S(2)}, u32[]{:S(2)}) %collective-permute-start.6) | collective-permute-done | bytes 327712 | tf_op jit(solution)/shard_map/ppermute | solution.py:155
  39.5 2.4 %collective-permute-done.5.refs_1_ = bf16[2,256,1280]{2,1,0:T(8,128)(2,1)S(1)} collective-permute-done((bf16[2,256,1280]{2,1,0:T(8,128)(2,1)}, bf16[2,256,1280]{2,1,0:T(8,128)(2,1)S(1)}, u32[]{:S(2)}, u32[]{:S(2)}) %collective-permute-start.5) | collective-permute-done | bytes 1310752 | tf_op jit(solution)/shard_map/ppermute | solution.py:155
  44.9 5.6 %collective-permute-start.3 = (bf16[2,128,1280]{2,1,0:T(8,128)(2,1)}, bf16[2,128,1280]{2,1,0:T(8,128)(2,1)S(1)}, u32[]{:S(2)}, u32[]{:S(2)}) collective-permute-start(bf16[2,128,1280]{2,1,0:T(8,128)(2,1)} %collective-permute-done.refs_2_), channel_id=1, source_target_pairs={{4,0},{5,1},{6,2},{7,3},{8,12},{9,13},{10,14},{11,15},{12,8},{13,9... | collective-permute-start | bytes 1966088 | tf_op jit(solution)/shard_map/ppermute | solution.py:155
  52.0 8.3 %first.1 = (f32[10,8,512]{2,1,0:T(8,128)S(1)}, f32[10,128,512]{2,1,0:T(8,128)S(1)}) custom-call(bf16[512,1280]{1,0:T(8,128)(2,1)S(1)} %copy-done.2, bf16[2,256,1280]{2,1,0:T(8,128)(2,1)S(1)} %collective-permute-done.5.refs_1_, bf16[2,128,1280]{2,1,0:T(8,128)(2,1)} %collective-permute-done.refs_2_, bf16[2,128,1280]{2,1,0:T(8,128)(2,1)S(1)} %collective-permute-done.1.refs_3_, ...), custom_call_target="tpu_custom_call" | custom-call | flops 1509949440 | bytes 5242880 | tf_op jit(solution)/shard_map/first/pallas_call | solution.py:123
  60.4 13.1 %collective-permute-done.8.refs_2_ = bf16[2,64,1280]{2,1,0:T(8,128)(2,1)S(1)} collective-permute-done((bf16[2,64,1280]{2,1,0:T(8,128)(2,1)}, bf16[2,64,1280]{2,1,0:T(8,128)(2,1)S(1)}, u32[]{:S(2)}, u32[]{:S(2)}) %collective-permute-start.8) | collective-permute-done | bytes 327712 | tf_op jit(solution)/shard_map/ppermute | solution.py:155
  73.5 1.9 %collective-permute-start.9 = (bf16[2,64,1280]{2,1,0:T(8,128)(2,1)S(1)}, bf16[2,64,1280]{2,1,0:T(8,128)(2,1)S(1)}, u32[]{:S(2)}, u32[]{:S(2)}) collective-permute-start(bf16[2,64,1280]{2,1,0:T(8,128)(2,1)S(1)} %collective-permute-done.8.refs_2_), channel_id=1, source_target_pairs={{0,4},{1,5},{2,6},{3,7},{4,0},{5,1},{6,2},{7,3},{24,28},{25,29},{2... | collective-permute-start | bytes 983048 | tf_op jit(solution)/shard_map/ppermute | solution.py:155
  75.4 1.5 %collective-permute-start.11 = (bf16[2,64,1280]{2,1,0:T(8,128)(2,1)S(1)}, bf16[2,64,1280]{2,1,0:T(8,128)(2,1)S(1)}, u32[]{:S(2)}, u32[]{:S(2)}) collective-permute-start(bf16[2,64,1280]{2,1,0:T(8,128)(2,1)S(1)} %slice.47), channel_id=1, source_target_pairs={{0,8},{1,9},{2,10},{3,11},{8,16},{9,17},{10,18},{11,19},{12,4},{13... | collective-permute-start | bytes 983048 | tf_op jit(solution)/shard_map/ppermute | solution.py:155
  77.1 4.3 %middle.1 = (f32[10,8,512]{2,1,0:T(8,128)S(1)}, f32[10,128,512]{2,1,0:T(8,128)S(1)}) custom-call(bf16[512,1280]{1,0:T(8,128)(2,1)S(1)} %copy-done.2, bf16[2,192,1280]{2,1,0:T(8,128)(2,1)S(1)} %collective-permute-done.10.refs_1_, bf16[2,64,1280]{2,1,0:T(8,128)(2,1)S(1)} %collective-permute-done.8.refs_2_, f32[256,128]{1,0:T(8,128)S(1)} %broadcast_in_dim.164.refs_3_, ...), custom_call_target="tpu_custom_call" | custom-call | flops 671088640 | bytes 5242880 | tf_op jit(solution)/shard_map/middle/pallas_call | solution.py:123
  81.4 1.5 %collective-permute-done.9.refs_4_ = bf16[2,64,1280]{2,1,0:T(8,128)(2,1)S(1)} collective-permute-done((bf16[2,64,1280]{2,1,0:T(8,128)(2,1)S(1)}, bf16[2,64,1280]{2,1,0:T(8,128)(2,1)S(1)}, u32[]{:S(2)}, u32[]{:S(2)}) %collective-permute-start.9) | collective-permute-done | bytes 327712 | tf_op jit(solution)/shard_map/ppermute | solution.py:155
  83.0 2.0 %collective-permute-done.11.refs_5_ = bf16[2,64,1280]{2,1,0:T(8,128)(2,1)S(1)} collective-permute-done((bf16[2,64,1280]{2,1,0:T(8,128)(2,1)S(1)}, bf16[2,64,1280]{2,1,0:T(8,128)(2,1)S(1)}, u32[]{:S(2)}, u32[]{:S(2)}) %collective-permute-start.11) | collective-permute-done | bytes 327712 | tf_op jit(solution)/shard_map/ppermute | solution.py:155
  85.1 3.5 %last0.1 = bf16[512,768]{1,0:T(8,128)(2,1)S(1)} custom-call(bf16[512,1280]{1,0:T(8,128)(2,1)S(1)} %copy-done.2, bf16[2,128,1280]{2,1,0:T(8,128)(2,1)S(1)} %collective-permute-done.3.refs_1_, bf16[2,64,1280]{2,1,0:T(8,128)(2,1)S(1)} %collective-permute-done.4.refs_2_, bf16[2,64,1280]{2,1,0:T(8,128)(2,1)S(1)} %collective-permute-done.7.refs_3_, ...), custom_call_target="tpu_custom_call" | custom-call | flops 603979776 | bytes 3145728 | tf_op jit(solution)/shard_map/last0/pallas_call | solution.py:123
  88.7 2.3 %last6.1 = bf16[512,512]{1,0:T(8,128)(2,1)S(1)} custom-call(bf16[512,1280]{1,0:T(8,128)(2,1)S(1)} %copy-done.2, bf16[2,128,1280]{2,1,0:T(8,128)(2,1)S(1)} %collective-permute-done.3.refs_1_, bf16[2,64,1280]{2,1,0:T(8,128)(2,1)S(1)} %collective-permute-done.4.refs_2_, bf16[2,64,1280]{2,1,0:T(8,128)(2,1)S(1)} %collective-permute-done.7.refs_3_, ...), custom_call_target="tpu_custom_call" | custom-call | flops 402653184 | bytes 2097152 | tf_op jit(solution)/shard_map/last6/pallas_call | solution.py:123
  95.9 1.8 %collective-permute-start.14 = (bf16[512,640]{1,0:T(8,128)(2,1)S(1)}, bf16[512,640]{1,0:T(8,128)(2,1)S(1)}, u32[]{:S(2)}, u32[]{:S(2)}) collective-permute-start(bf16[512,640]{1,0:T(8,128)(2,1)S(1)} %fusion.9), channel_id=1, source_target_pairs={{0,2},{1,3},{2,0},{3,1},{4,6},{5,7},{6,4},{7,5},{8,10},{9,11},{10,... | collective-permute-start | bytes 1966088 | tf_op jit(solution)/shard_map/ppermute | solution.py:155
  103.9 9.6 %collective-permute-done.14 = bf16[512,640]{1,0:T(8,128)(2,1)S(1)} collective-permute-done((bf16[512,640]{1,0:T(8,128)(2,1)S(1)}, bf16[512,640]{1,0:T(8,128)(2,1)S(1)}, u32[]{:S(2)}, u32[]{:S(2)}) %collective-permute-start.14) | collective-permute-done | bytes 655392 | tf_op jit(solution)/shard_map/ppermute | solution.py:155
  113.5 13.5 %collective-permute-done.15 = bf16[512,640]{1,0:T(8,128)(2,1)S(1)} collective-permute-done((bf16[512,640]{1,0:T(8,128)(2,1)S(1)}, bf16[512,640]{1,0:T(8,128)(2,1)S(1)}, u32[]{:S(2)}, u32[]{:S(2)}) %collective-permute-start.15) | collective-permute-done | bytes 655392 | tf_op jit(solution)/shard_map/ppermute | solution.py:155
  127.0 1.3 %add_convert_fusion = bf16[512,1280]{1,0:T(8,128)(2,1)} fusion(f32[512,1280]{1,0:T(8,128)S(1)} %fusion.1, bf16[512,640]{1,0:T(8,128)(2,1)S(1)} %collective-permute-done.15, bf16[512,640]{1,0:T(8,128)(2,1)S(1)} %collective-permute-done.14), kind=kLoop, calls=%fused_computation.3 | loop fusion | flops 3932160 | bytes 5242880 | tf_op jit(solution)/shard_map/convert_element_type | solution.py:287
  (83 shorter events, 21.6 us)
Async XLA Ops:
  0.0 15.7 %copy-start.2 = (bf16[512,1280]{1,0:T(8,128)(2,1)S(1)}, bf16[512,1280]{1,0:T(8,128)(2,1)}, u32[]{:S(2)}) copy-start(bf16[512,1280]{1,0:T(8,128)(2,1)} %refs_0_.11) | copy-start | bytes 3932164
  0.0 26.5 %collective-permute-start.2 = (bf16[1280,5120]{1,0:T(8,128)(2,1)}, bf16[1280,5120]{1,0:T(8,128)(2,1)}, u32[]{:S(2)}, u32[]{:S(2)}) collective-permute-start(bf16[1280,5120]{1,0:T(8,128)(2,1)} %param.15), channel_id=1, source_target_pairs={{0,1},{1,0},{2,3},{3,2},{4,5},{5,4},{6,7},{7,6},{8,9},{9,8},{10,11... | collective-permute-start | bytes 39321608 | tf_op jit(solution)/shard_map/ppermute | solution.py:155
  5.2 21.2 %collective-permute-start = (bf16[2,128,1280]{2,1,0:T(8,128)(2,1)}, bf16[2,128,1280]{2,1,0:T(8,128)(2,1)}, u32[]{:S(2)}, u32[]{:S(2)}) collective-permute-start(bf16[2,128,1280]{2,1,0:T(8,128)(2,1)} %get-tuple-element.37), channel_id=1, source_target_pairs={{0,8},{1,9},{2,10},{3,11},{8,16},{9,17},{10,18},{11,19},{12,4},{13... | collective-permute-start | bytes 1966088 | tf_op jit(solution)/shard_map/ppermute | solution.py:155
  6.5 20.0 %collective-permute-start.1 = (bf16[2,128,1280]{2,1,0:T(8,128)(2,1)}, bf16[2,128,1280]{2,1,0:T(8,128)(2,1)S(1)}, u32[]{:S(2)}, u32[]{:S(2)}) collective-permute-start(bf16[2,128,1280]{2,1,0:T(8,128)(2,1)} %get-tuple-element.37), channel_id=1, source_target_pairs={{4,12},{5,13},{6,14},{7,15},{8,0},{9,1},{10,2},{11,3},{12,20},{13,... | collective-permute-start | bytes 1966088 | tf_op jit(solution)/shard_map/ppermute | solution.py:155
  11.1 30.8 %collective-permute-start.5 = (bf16[2,256,1280]{2,1,0:T(8,128)(2,1)}, bf16[2,256,1280]{2,1,0:T(8,128)(2,1)S(1)}, u32[]{:S(2)}, u32[]{:S(2)}) collective-permute-start(bf16[2,256,1280]{2,1,0:T(8,128)(2,1)} %get-tuple-element.41), channel_id=1, source_target_pairs={{0,4},{1,5},{2,6},{3,7},{4,0},{5,1},{6,2},{7,3},{8,12},{9,13},{10,... | collective-permute-start | bytes 3932168 | tf_op jit(solution)/shard_map/ppermute | solution.py:155
  11.5 28.0 %collective-permute-start.6 = (bf16[2,64,1280]{2,1,0:T(8,128)(2,1)}, bf16[2,64,1280]{2,1,0:T(8,128)(2,1)}, u32[]{:S(2)}, u32[]{:S(2)}) collective-permute-start(bf16[2,64,1280]{2,1,0:T(8,128)(2,1)} %get-tuple-element.42), channel_id=1, source_target_pairs={{0,16},{1,17},{2,18},{3,19},{4,20},{5,21},{6,22},{7,23},{8,24},{9,... | collective-permute-start | bytes 983048 | tf_op jit(solution)/shard_map/ppermute | solution.py:155
  26.5 16.9 %copy-start.11 = (pred[4,576]{1,0:T(4,128)(4,1)S(1)}, pred[4,576]{1,0:T(4,128)(4,1)}, u32[]{:S(2)}) copy-start(pred[4,576]{1,0:T(4,128)(4,1)} %constant.77.clone) | copy-start | bytes 6916
  26.5 17.0 %copy-start.13 = (s32[256]{0:T(256)S(1)}, s32[256]{0:T(256)}, u32[]{:S(2)}) copy-start(s32[256]{0:T(256)} %constant.80.clone) | copy-start | bytes 3076
  26.5 17.1 %copy-start.9 = (s32[576]{0:T(1024)S(1)}, s32[576]{0:T(1024)}, u32[]{:S(2)}) copy-start(s32[576]{0:T(1024)} %constant.78.clone) | copy-start | bytes 6916
  31.8 20.2 %copy-start.4 = (f32[10,128,512]{2,1,0:T(8,128)S(1)}, f32[10,128,512]{2,1,0:T(8,128)}, u32[]{:S(2)}) copy-start(f32[10,128,512]{2,1,0:T(8,128)} %copy-done.3) | copy-start | bytes 7864324
  42.0 33.4 %collective-permute-start.10 = (bf16[2,192,1280]{2,1,0:T(8,128)(2,1)S(1)}, bf16[2,192,1280]{2,1,0:T(8,128)(2,1)S(1)}, u32[]{:S(2)}, u32[]{:S(2)}) collective-permute-start(bf16[2,192,1280]{2,1,0:T(8,128)(2,1)S(1)} %slice.46), channel_id=1, source_target_pairs={{0,8},{1,9},{2,10},{3,11},{8,16},{9,17},{10,18},{11,19},{12,4},{13... | collective-permute-start | bytes 2949128 | tf_op jit(solution)/shard_map/ppermute | solution.py:155
  43.6 29.9 %collective-permute-start.8 = (bf16[2,64,1280]{2,1,0:T(8,128)(2,1)}, bf16[2,64,1280]{2,1,0:T(8,128)(2,1)S(1)}, u32[]{:S(2)}, u32[]{:S(2)}) collective-permute-start(bf16[2,64,1280]{2,1,0:T(8,128)(2,1)} %collective-permute-done.6.refs_4_), channel_id=1, source_target_pairs={{8,0},{9,1},{10,2},{11,3},{12,4},{13,5},{14,6},{15,7},{16,24},{17,... | collective-permute-start | bytes 983048 | tf_op jit(solution)/shard_map/ppermute | solution.py:155
  44.9 38.1 %collective-permute-start.3 = (bf16[2,128,1280]{2,1,0:T(8,128)(2,1)}, bf16[2,128,1280]{2,1,0:T(8,128)(2,1)S(1)}, u32[]{:S(2)}, u32[]{:S(2)}) collective-permute-start(bf16[2,128,1280]{2,1,0:T(8,128)(2,1)} %collective-permute-done.refs_2_), channel_id=1, source_target_pairs={{4,0},{5,1},{6,2},{7,3},{8,12},{9,13},{10,14},{11,15},{12,8},{13,9... | collective-permute-start | bytes 1966088 | tf_op jit(solution)/shard_map/ppermute | solution.py:155
  50.5 31.0 %collective-permute-start.7 = (bf16[2,64,1280]{2,1,0:T(8,128)(2,1)}, bf16[2,64,1280]{2,1,0:T(8,128)(2,1)S(1)}, u32[]{:S(2)}, u32[]{:S(2)}) collective-permute-start(bf16[2,64,1280]{2,1,0:T(8,128)(2,1)} %collective-permute-done.6.refs_4_), channel_id=1, source_target_pairs={{0,4},{1,5},{2,6},{3,7},{4,0},{5,1},{6,2},{7,3},{8,12},{9,13},{10,... | collective-permute-start | bytes 983048 | tf_op jit(solution)/shard_map/ppermute | solution.py:155
  50.6 30.9 %collective-permute-start.4 = (bf16[2,64,1280]{2,1,0:T(8,128)(2,1)S(1)}, bf16[2,64,1280]{2,1,0:T(8,128)(2,1)S(1)}, u32[]{:S(2)}, u32[]{:S(2)}) collective-permute-start(bf16[2,64,1280]{2,1,0:T(8,128)(2,1)S(1)} %slice.45), channel_id=1, source_target_pairs={{0,4},{1,5},{2,6},{3,7},{8,12},{9,13},{10,14},{11,15},{12,8},{13,9... | collective-permute-start | bytes 983048 | tf_op jit(solution)/shard_map/ppermute | solution.py:155
  52.0 24.9 %copy-start.10 = (pred[5,384]{1,0:T(8,128)(4,1)S(1)}, pred[5,384]{1,0:T(8,128)(4,1)}, u32[]{:S(2)}) copy-start(pred[5,384]{1,0:T(8,128)(4,1)} %constant.81.clone) | copy-start | bytes 5764
  52.0 25.0 %copy-start.12 = (s32[384]{0:T(512)S(1)}, s32[384]{0:T(512)}, u32[]{:S(2)}) copy-start(s32[384]{0:T(512)} %constant.82.clone) | copy-start | bytes 4612
  73.5 9.5 %collective-permute-start.9 = (bf16[2,64,1280]{2,1,0:T(8,128)(2,1)S(1)}, bf16[2,64,1280]{2,1,0:T(8,128)(2,1)S(1)}, u32[]{:S(2)}, u32[]{:S(2)}) collective-permute-start(bf16[2,64,1280]{2,1,0:T(8,128)(2,1)S(1)} %collective-permute-done.8.refs_2_), channel_id=1, source_target_pairs={{0,4},{1,5},{2,6},{3,7},{4,0},{5,1},{6,2},{7,3},{24,28},{25,29},{2... | collective-permute-start | bytes 983048 | tf_op jit(solution)/shard_map/ppermute | solution.py:155
  75.4 9.5 %collective-permute-start.11 = (bf16[2,64,1280]{2,1,0:T(8,128)(2,1)S(1)}, bf16[2,64,1280]{2,1,0:T(8,128)(2,1)S(1)}, u32[]{:S(2)}, u32[]{:S(2)}) collective-permute-start(bf16[2,64,1280]{2,1,0:T(8,128)(2,1)S(1)} %slice.47), channel_id=1, source_target_pairs={{0,8},{1,9},{2,10},{3,11},{8,16},{9,17},{10,18},{11,19},{12,4},{13... | collective-permute-start | bytes 983048 | tf_op jit(solution)/shard_map/ppermute | solution.py:155
  88.6 5.7 %collective-permute-start.12 = (bf16[512,768]{1,0:T(8,128)(2,1)S(1)}, bf16[512,768]{1,0:T(8,128)(2,1)S(1)}, u32[]{:S(2)}, u32[]{:S(2)}) collective-permute-start(bf16[512,768]{1,0:T(8,128)(2,1)S(1)} %last0.1), channel_id=1, source_target_pairs={{0,1},{1,0},{2,3},{3,2},{4,5},{5,4},{6,7},{7,6},{8,9},{9,8},{10,11... | collective-permute-start | bytes 2359304 | tf_op jit(solution)/shard_map/ppermute | solution.py:155
  91.0 2.1 %collective-permute-start.13 = (bf16[512,512]{1,0:T(8,128)(2,1)S(1)}, bf16[512,512]{1,0:T(8,128)(2,1)S(1)}, u32[]{:S(2)}, u32[]{:S(2)}) collective-permute-start(bf16[512,512]{1,0:T(8,128)(2,1)S(1)} %last6.1), channel_id=1, source_target_pairs={{0,1},{1,0},{2,3},{3,2},{4,5},{5,4},{6,7},{7,6},{8,9},{9,8},{10,11... | collective-permute-start | bytes 1572872 | tf_op jit(solution)/shard_map/ppermute | solution.py:155
  95.9 17.6 %collective-permute-start.14 = (bf16[512,640]{1,0:T(8,128)(2,1)S(1)}, bf16[512,640]{1,0:T(8,128)(2,1)S(1)}, u32[]{:S(2)}, u32[]{:S(2)}) collective-permute-start(bf16[512,640]{1,0:T(8,128)(2,1)S(1)} %fusion.9), channel_id=1, source_target_pairs={{0,2},{1,3},{2,0},{3,1},{4,6},{5,7},{6,4},{7,5},{8,10},{9,11},{10,... | collective-permute-start | bytes 1966088 | tf_op jit(solution)/shard_map/ppermute | solution.py:155
  101.3 25.7 %collective-permute-start.15 = (bf16[512,640]{1,0:T(8,128)(2,1)S(1)}, bf16[512,640]{1,0:T(8,128)(2,1)S(1)}, u32[]{:S(2)}, u32[]{:S(2)}) collective-permute-start(bf16[512,640]{1,0:T(8,128)(2,1)S(1)} %fusion.10), channel_id=1, source_target_pairs={{0,2},{1,3},{2,0},{3,1},{4,6},{5,7},{6,4},{7,5},{8,10},{9,11},{10,... | collective-permute-start | bytes 1966088 | tf_op jit(solution)/shard_map/ppermute | solution.py:155
  102.5 25.8 %copy-start.1 = (s32[8,8]{1,0:T(8,128)S(1)}, s32[8,8]{1,0:T(8,128)}, u32[]{:S(2)}) copy-start(s32[8,8]{1,0:T(8,128)} %param.14) | copy-start | bytes 772
  (7 other events, 37.3 us)

commit v5 on v4

--- a/solution.py
+++ b/solution.py
@@ -52,6 +52,31 @@
             transcendentals=0,
         ),
     )(key_vectors, value_vectors)
+
+
+def gather_kernel(flag_ref, far_ref, near_ref, two_ref, out_ref):
+    a = two_ref.shape[1]
+    ab = far_ref.shape[1]
+    far_here, near_here = (flag_ref[0] != 0, flag_ref[1] != 0)
+    for plane in range(2):
+        two = two_ref[plane]
+        out_ref[plane, :a] = jnp.where(far_here, far_ref[plane, :a], two)
+        out_ref[plane, a:ab] = far_ref[plane, a:]
+        out_ref[plane, ab:] = jnp.where(near_here, near_ref[plane, :a], two)
+
+
+def gather(flags, far, near, two):
+    rows = far.shape[1] + two.shape[1]
+    width = two.shape[2]
+    held = pl.BlockSpec(memory_space=pltpu.VMEM)
+    return pl.pallas_call(
+        gather_kernel,
+        in_specs=[pl.BlockSpec(memory_space=pltpu.SMEM), held, held, held],
+        out_specs=held,
+        out_shape=jax.ShapeDtypeStruct((2, rows, width), BF16),
+        name="gather",
+        cost_estimate=pl.CostEstimate(flops=0, bytes_accessed=8 * rows * width, transcendentals=0),
+    )(flags, far, near, two)
 
 
 def attend_kernel(*refs, buffers, own, first, last, low, high):
@@ -176,7 +201,6 @@
     level = my_group // 2
     out_width = out_weight.shape[1] // group_count
     away, home = (2 * (1 - level) + mine, 2 * level + mine)
-    moved = move(out_weight, same, core)
     near = row_count // 2
     own_pair = (key_vectors, value_vectors)
 
@@ -197,7 +221,6 @@
         side = jnp.where(my_block % 2 == 0, 1, -1)
         far_of = lambda t: t - 2 if t % 2 == 0 else t + 2
         near_of = lambda t: t + 2 if t % 2 == 0 else t - 2
-        twin_if = lambda source: lambda t: t ^ 1 if 0 <= source(t) < block_count else None
         ends = (0, 1, block_count - 2, block_count - 1)
         partner, two, opposite = (my_block ^ 1, my_block ^ 4, my_block ^ 6)
         far_block, near_block = (my_block - 2 * side, my_block + 2 * side)
@@ -210,39 +233,44 @@
         z_far = move(sent_ab, near_of)
         z_near = move(sent_ab, far_of)
         z_two = move(sent_a, lambda t: t ^ 4)
+        z_three = move(sent_a, lambda t: t ^ 6 if t in ends else None)
         carry = attend(query_vectors, own_pair, [], None, None, False, 0, head_count, "own")
-        z_far, z_near, state, out_weight, moved = lax.optimization_barrier(
-            (z_far, z_near, carry[0], out_weight, moved)
-        )
-        cross_far = move(z_far, twin_if(far_of))
-        cross_near = move(z_near[:, :a], twin_if(near_of))
-        weights = blocks_of(out_weight, moved)
-        x_rows, z_two, state, weights = lax.optimization_barrier((x_rows, z_two, state, weights))
-        near_bc = move(x_rows[:, a:], near_of)
-        cross_two = move(z_two, lambda t: t ^ 1)
-        z_three = move(z_two, lambda t: {4: 6, 5: 7, 2: 0, 3: 1}.get(t))
+        x_rows, z_far, z_near, z_two, state, out_weight = lax.optimization_barrier(
+            (x_rows, z_far, z_near, z_two, carry[0], out_weight)
+        )
+        near_b = move(x_rows[:, a:ab], near_of)
+        near_c = move(x_rows[:, ab:], near_of)
+        flags = jnp.stack([within(far_block), within(near_block)]).astype(jnp.int32)
+        crossed = move(gather(flags, z_far, z_near, z_two), lambda t: t ^ 1)
+        cross_last = move(jnp.where(at_end, z_three, z_two), lambda t: t ^ 1)
+        moved = move(out_weight, same, core)
         carry = further(
-            [x_rows, z_far, z_near, z_two],
-            [(partner, 0, near), (far_block, 0, ab), (near_block, 0, ab), (two, 0, a)],
+            [x_rows, z_far, z_near, z_two, z_three],
+            [
+                (partner, 0, near),
+                (far_block, 0, ab),
+                (near_block, 0, ab),
+                (two, 0, a),
+                (three, 0, a),
+            ],
             (state, carry[1]),
             "first",
         )
-        z_three, state = lax.optimization_barrier((z_three, carry[0]))
-        cross_three = move(z_three, lambda t: t ^ 1 if t in ends else None)
-        near_bc, state = lax.optimization_barrier((near_bc, state))
-        chain_b = move(near_bc[:, : ab - a], near_of)
+        near_b, state, moved = lax.optimization_barrier((near_b, carry[0], moved))
+        chain_b = move(near_b, near_of)
+        weights = lax.optimization_barrier(blocks_of(out_weight, moved))
         carry = further(
-            [near_bc, z_three],
-            [(adjacent, a, near - a), (three, 0, a)],
+            [near_b, near_c],
+            [(adjacent, a, ab - a), (adjacent, ab, near - ab)],
             (state, carry[1]),
             "middle",
         )
-        buffers = [cross_far, cross_near, cross_two, cross_three, chain_b]
+        buffers = [crossed, cross_last, chain_b]
         pieces = [
-            (far_cross, 0, ab),
-            (adjacent, 0, a),
-            (two ^ 1, 0, a),
-            (jnp.where(at_end, opposite ^ 1, -1), 0, a),
+            (jnp.where(within(far_cross), far_cross, two ^ 1), 0, a),
+            (far_cross, a, ab - a),
+            (jnp.where(within(adjacent), adjacent, two ^ 1), 0, a),
+            (jnp.where(at_end, opposite ^ 1, two ^ 1), 0, a),
             (my_block - 3 * side, a, ab - a),
         ]
     else:
@@ -256,6 +284,7 @@
         carry = attend(query_vectors, own_pair, [], None, None, False, 0, head_count, "own")
         carry = further([jnp.concatenate(received[:2], axis=1)], pieces[:2], carry, "first")
         buffers, pieces = ([jnp.concatenate(received[2:], axis=1)], pieces[2:])
+        moved = move(out_weight, same, core)
         weights = lax.optimization_barrier(blocks_of(out_weight, moved))
 
     bias = bias_of(pieces)

time: 129 us -> 133 us (1.031)
  the two profiles are of different devices: /device:TPU:2 before, /device:TPU:12 now
where the time goes in v5:
time: 133 us
  waiting for transfers between devices  44 us (33%)
  starting transfers between devices  31.3 us (24%)
  Pallas kernels  28.9 us (22%)
  local copies, waits for them, and re-layouts  14.2 us (11%)
  matrix products  9.77 us (7%)
  other arithmetic  4.28 us (3%)
    ppermute x15, waiting for transfers between devices, move(): return lax.ppermute(array, AXES, route)  44 us
    ppermute x15, starting transfers between devices, move(): return lax.ppermute(array, AXES, route)  31.3 us
    pallas_call x5, Pallas kernels, attend(): pl.pallas_call(lambda *refs: attend_kernel(*refs, buffers=len(buffers), o...  24.3 us
    dynamic_slice x2, local copies, waits for them, and re-layouts, blocks_of(): lax.dynamic_slice_in_dim(source, number * out_width, out_width, 1)  6.72 us
    unnamed x38, local copies, waits for them, and re-layouts  5.32 us
    dot_general x6, matrix products, project(): jnp.dot(part, weights[index][low:high, first:last], preferred_element_typ...  5.02 us
    dot_general x6, matrix products, project(): jnp.dot(other, weights[index + 2][low:high, first:last], preferred_elemen...  4.74 us
  transfers between devices with their start and end apart: 15, of which 5 were waited for; matrix products, arithmetic and copies ran while one was open for 15% of the time, Pallas kernels for 18%

profile of v5, /device:TPU:12, one launch (start us, length us, event | category | flops | bytes accessed | tf_op | source)
XLA Modules:
  0.0 133.0 jit_solution(1374069358544047761)
XLA Ops:
  0.0 1.4 %copy-done.11 = bf16[512,1280]{1,0:T(8,128)(2,1)S(1)} copy-done((bf16[512,1280]{1,0:T(8,128)(2,1)S(1)}, bf16[512,1280]{1,0:T(8,128)(2,1)}, u32[]{:S(2)}) %copy-start.11) | copy-done | bytes 1310744
  2.7 2.2 %pack.1 = (bf16[2,256,1280]{2,1,0:T(8,128)(2,1)S(1)}, bf16[2,128,1280]{2,1,0:T(8,128)(2,1)S(1)}, bf16[2,64,1280]{2,1,0:T(8,128)(2,1)}) custom-call(bf16[512,1280]{1,0:T(8,128)(2,1)S(1)} %copy-done.11, bf16[512,1280]{1,0:T(8,128)(2,1)S(1)} %copy-done.12), custom_call_target="tpu_custom_call" | custom-call | flops 671088640 | bytes 5242880 | tf_op jit(solution)/shard_map/pack/pallas_call | solution.py:39
  5.0 1.6 %collective-permute-start = (bf16[2,256,1280]{2,1,0:T(8,128)(2,1)S(1)}, bf16[2,256,1280]{2,1,0:T(8,128)(2,1)S(1)}, u32[]{:S(2)}, u32[]{:S(2)}) collective-permute-start(bf16[2,256,1280]{2,1,0:T(8,128)(2,1)S(1)} %get-tuple-element.34), channel_id=1, source_target_pairs={{0,4},{1,5},{2,6},{3,7},{4,0},{5,1},{6,2},{7,3},{8,12},{9,13},{10,... | collective-permute-start | bytes 3932168 | tf_op jit(solution)/shard_map/ppermute | solution.py:180
  6.6 3.5 %collective-permute-start.1 = (bf16[2,128,1280]{2,1,0:T(8,128)(2,1)S(1)}, bf16[2,128,1280]{2,1,0:T(8,128)(2,1)S(1)}, u32[]{:S(2)}, u32[]{:S(2)}) collective-permute-start(bf16[2,128,1280]{2,1,0:T(8,128)(2,1)S(1)} %get-tuple-element.35), channel_id=1, source_target_pairs={{0,8},{1,9},{2,10},{3,11},{8,16},{9,17},{10,18},{11,19},{12,4},{13... | collective-permute-start | bytes 1966088 | tf_op jit(solution)/shard_map/ppermute | solution.py:180
  10.0 2.4 %collective-permute-start.2 = (bf16[2,128,1280]{2,1,0:T(8,128)(2,1)S(1)}, bf16[2,128,1280]{2,1,0:T(8,128)(2,1)S(1)}, u32[]{:S(2)}, u32[]{:S(2)}) collective-permute-start(bf16[2,128,1280]{2,1,0:T(8,128)(2,1)S(1)} %get-tuple-element.35), channel_id=1, source_target_pairs={{4,12},{5,13},{6,14},{7,15},{8,0},{9,1},{10,2},{11,3},{12,20},{13,... | collective-permute-start | bytes 1966088 | tf_op jit(solution)/shard_map/ppermute | solution.py:180
  12.5 2.6 %collective-permute-start.3 = (bf16[2,64,1280]{2,1,0:T(8,128)(2,1)}, bf16[2,64,1280]{2,1,0:T(8,128)(2,1)S(1)}, u32[]{:S(2)}, u32[]{:S(2)}) collective-permute-start(bf16[2,64,1280]{2,1,0:T(8,128)(2,1)} %get-tuple-element.36), channel_id=1, source_target_pairs={{0,16},{1,17},{2,18},{3,19},{4,20},{5,21},{6,22},{7,23},{8,24},{9,... | collective-permute-start | bytes 983048 | tf_op jit(solution)/shard_map/ppermute | solution.py:180
  15.1 6.4 %own.1 = (f32[10,8,512]{2,1,0:T(8,128)S(1)}, f32[10,128,512]{2,1,0:T(8,128)S(1)}) custom-call(bf16[512,1280]{1,0:T(8,128)(2,1)S(1)} %copy-done.2, bf16[512,1280]{1,0:T(8,128)(2,1)S(1)} %copy-done.11, bf16[512,1280]{1,0:T(8,128)(2,1)S(1)} %copy-done.12), custom_call_target="tpu_custom_call" | custom-call | flops 1342177280 | bytes 5242880 | tf_op jit(solution)/shard_map/own/pallas_call | solution.py:148
  21.5 1.5 %copy-done.5 = f32[10,128,512]{2,1,0:T(8,128)} copy-done((f32[10,128,512]{2,1,0:T(8,128)}, f32[10,128,512]{2,1,0:T(8,128)S(1)}, u32[]{:S(2)}) %copy-start.5) | copy-done | bytes 2621464
  22.9 14.9 %collective-permute-done.3.two_ref.refs_4_ = bf16[2,64,1280]{2,1,0:T(8,128)(2,1)S(1)} collective-permute-done((bf16[2,64,1280]{2,1,0:T(8,128)(2,1)}, bf16[2,64,1280]{2,1,0:T(8,128)(2,1)S(1)}, u32[]{:S(2)}, u32[]{:S(2)}) %collective-permute-start.3) | collective-permute-done | bytes 327712 | tf_op jit(solution)/shard_map/ppermute | solution.py:180
  43.6 5.6 %collective-permute-start.7 = (bf16[2,64,1280]{2,1,0:T(8,128)(2,1)}, bf16[2,64,1280]{2,1,0:T(8,128)(2,1)}, u32[]{:S(2)}, u32[]{:S(2)}) collective-permute-start(bf16[2,64,1280]{2,1,0:T(8,128)(2,1)} %slice.42), channel_id=1, source_target_pairs={{0,8},{1,9},{2,10},{3,11},{8,16},{9,17},{10,18},{11,19},{12,4},{13... | collective-permute-start | bytes 983048 | tf_op jit(solution)/shard_map/ppermute | solution.py:180
  49.1 7.9 %collective-permute-start.10 = (bf16[2,128,1280]{2,1,0:T(8,128)(2,1)}, bf16[2,128,1280]{2,1,0:T(8,128)(2,1)}, u32[]{:S(2)}, u32[]{:S(2)}) collective-permute-start(bf16[2,128,1280]{2,1,0:T(8,128)(2,1)} %slice.43), channel_id=1, source_target_pairs={{0,8},{1,9},{2,10},{3,11},{8,16},{9,17},{10,18},{11,19},{12,4},{13... | collective-permute-start | bytes 1966088 | tf_op jit(solution)/shard_map/ppermute | solution.py:180
  57.0 2.4 %gather.1 = bf16[2,192,1280]{2,1,0:T(8,128)(2,1)} custom-call(s32[2]{0:T(128)} %add_convert_fusion.1.flag_ref, bf16[2,128,1280]{2,1,0:T(8,128)(2,1)} %copy-done.7, bf16[2,128,1280]{2,1,0:T(8,128)(2,1)} %copy-done.9, bf16[2,64,1280]{2,1,0:T(8,128)(2,1)} %copy-done.3), custom_call_target="tpu_custom_call" | custom-call | bytes 1966080 | tf_op jit(solution)/shard_map/gather/pallas_call | solution.py:72
  60.5 2.1 %collective-permute-start.6 = (bf16[2,64,1280]{2,1,0:T(8,128)(2,1)S(1)}, bf16[2,64,1280]{2,1,0:T(8,128)(2,1)S(1)}, u32[]{:S(2)}, u32[]{:S(2)}) collective-permute-start(bf16[2,64,1280]{2,1,0:T(8,128)(2,1)S(1)} %broadcast_select_fusion), channel_id=1, source_target_pairs={{0,4},{1,5},{2,6},{3,7},{4,0},{5,1},{6,2},{7,3},{8,12},{9,13},{10,... | collective-permute-start | bytes 983048 | tf_op jit(solution)/shard_map/ppermute | solution.py:180
  62.6 3.4 %constant_dynamic-slice_fusion.1 = (bf16[1280,1280]{1,0:T(8,128)(2,1)S(1)}, bf16[1280,1280]{1,0:T(8,128)(2,1)S(1)}) fusion(bf16[1280,5120]{1,0:T(8,128)(2,1)} %param.15, s32[]{:T(128)S(6)} %select_n.134, s32[]{:T(128)S(6)} %select_n.133), kind=kLoop, calls=%fused_computation.48 | loop fusion | bytes 13107208 | tf_op jit(solution)/shard_map/dynamic_slice | solution.py:214
  66.1 7.5 %first.1 = (f32[10,8,512]{2,1,0:T(8,128)S(1)}, f32[10,128,512]{2,1,0:T(8,128)S(1)}) custom-call(bf16[512,1280]{1,0:T(8,128)(2,1)S(1)} %copy-done.2, bf16[2,256,1280]{2,1,0:T(8,128)(2,1)S(1)} %collective-permute-done.refs_1_, bf16[2,128,1280]{2,1,0:T(8,128)(2,1)S(1)} %copy-done.8, bf16[2,128,1280]{2,1,0:T(8,128)(2,1)S(1)} %copy-done.10, ...), custom_call_target="tpu_custom_call" | custom-call | flops 1677721600 | bytes 5242880 | tf_op jit(solution)/shard_map/first/pallas_call | solution.py:148
  73.6 2.2 %collective-permute-start.9 = (bf16[2,64,1280]{2,1,0:T(8,128)(2,1)}, bf16[2,64,1280]{2,1,0:T(8,128)(2,1)S(1)}, u32[]{:S(2)}, u32[]{:S(2)}) collective-permute-start(bf16[2,64,1280]{2,1,0:T(8,128)(2,1)} %collective-permute-done.7.refs_1_), channel_id=1, source_target_pairs={{0,8},{1,9},{2,10},{3,11},{8,16},{9,17},{10,18},{11,19},{12,4},{13... | collective-permute-start | bytes 983048 | tf_op jit(solution)/shard_map/ppermute | solution.py:180
  75.9 3.4 %constant_dynamic-slice_fusion.3 = (bf16[1280,1280]{1,0:T(8,128)(2,1)S(1)}, bf16[1280,1280]{1,0:T(8,128)(2,1)S(1)}) fusion(bf16[1280,5120]{1,0:T(8,128)(2,1)} %collective-permute-done.8, s32[]{:T(128)S(6)} %select_n.134, s32[]{:T(128)S(6)} %select_n.133), kind=kLoop, calls=%fused_computation.50 | loop fusion | bytes 13107208 | tf_op jit(solution)/shard_map/dynamic_slice | solution.py:214
  79.3 5.0 %middle.1 = (f32[10,8,512]{2,1,0:T(8,128)S(1)}, f32[10,128,512]{2,1,0:T(8,128)S(1)}) custom-call(bf16[512,1280]{1,0:T(8,128)(2,1)S(1)} %copy-done.2, bf16[2,64,1280]{2,1,0:T(8,128)(2,1)} %collective-permute-done.7.refs_1_, bf16[2,128,1280]{2,1,0:T(8,128)(2,1)} %collective-permute-done.10.refs_2_, f32[192,128]{1,0:T(8,128)S(1)} %broadcast_in_dim.150.refs_3_, ...), custom_call_target="tpu_custom_call" | custom-call | flops 503316480 | bytes 5242880 | tf_op jit(solution)/shard_map/middle/pallas_call | solution.py:148
  84.3 5.6 %collective-permute-done.6.refs_2_ = bf16[2,64,1280]{2,1,0:T(8,128)(2,1)S(1)} collective-permute-done((bf16[2,64,1280]{2,1,0:T(8,128)(2,1)S(1)}, bf16[2,64,1280]{2,1,0:T(8,128)(2,1)S(1)}, u32[]{:S(2)}, u32[]{:S(2)}) %collective-permute-start.6) | collective-permute-done | bytes 327712 | tf_op jit(solution)/shard_map/ppermute | solution.py:180
  90.1 3.3 %last0.1 = bf16[512,768]{1,0:T(8,128)(2,1)S(1)} custom-call(bf16[512,1280]{1,0:T(8,128)(2,1)S(1)} %copy-done.2, bf16[2,192,1280]{2,1,0:T(8,128)(2,1)S(1)} %collective-permute-done.4.refs_1_, bf16[2,64,1280]{2,1,0:T(8,128)(2,1)S(1)} %collective-permute-done.6.refs_2_, bf16[2,64,1280]{2,1,0:T(8,128)(2,1)S(1)} %collective-permute-done.9.refs_3_, ...), custom_call_target="tpu_custom_call" | custom-call | flops 503316480 | bytes 3145728 | tf_op jit(solution)/shard_map/last0/pallas_call | solution.py:148
  93.4 2.2 %last6.1 = bf16[512,512]{1,0:T(8,128)(2,1)S(1)} custom-call(bf16[512,1280]{1,0:T(8,128)(2,1)S(1)} %copy-done.2, bf16[2,192,1280]{2,1,0:T(8,128)(2,1)S(1)} %collective-permute-done.4.refs_1_, bf16[2,64,1280]{2,1,0:T(8,128)(2,1)S(1)} %collective-permute-done.6.refs_2_, bf16[2,64,1280]{2,1,0:T(8,128)(2,1)S(1)} %collective-permute-done.9.refs_3_, ...), custom_call_target="tpu_custom_call" | custom-call | flops 335544320 | bytes 2097152 | tf_op jit(solution)/shard_map/last6/pallas_call | solution.py:148
  104.7 1.6 %collective-permute-start.14 = (bf16[512,640]{1,0:T(8,128)(2,1)S(1)}, bf16[512,640]{1,0:T(8,128)(2,1)S(1)}, u32[]{:S(2)}, u32[]{:S(2)}) collective-permute-start(bf16[512,640]{1,0:T(8,128)(2,1)S(1)} %fusion.10), channel_id=1, source_target_pairs={{0,2},{1,3},{2,0},{3,1},{4,6},{5,7},{6,4},{7,5},{8,10},{9,11},{10,... | collective-permute-start | bytes 1966088 | tf_op jit(solution)/shard_map/ppermute | solution.py:180
  108.6 9.5 %collective-permute-done.13 = bf16[512,640]{1,0:T(8,128)(2,1)S(1)} collective-permute-done((bf16[512,640]{1,0:T(8,128)(2,1)S(1)}, bf16[512,640]{1,0:T(8,128)(2,1)S(1)}, u32[]{:S(2)}, u32[]{:S(2)}) %collective-permute-start.13) | collective-permute-done | bytes 655392 | tf_op jit(solution)/shard_map/ppermute | solution.py:180
  118.1 13.5 %collective-permute-done.14 = bf16[512,640]{1,0:T(8,128)(2,1)S(1)} collective-permute-done((bf16[512,640]{1,0:T(8,128)(2,1)S(1)}, bf16[512,640]{1,0:T(8,128)(2,1)S(1)}, u32[]{:S(2)}, u32[]{:S(2)}) %collective-permute-start.14) | collective-permute-done | bytes 655392 | tf_op jit(solution)/shard_map/ppermute | solution.py:180
  (90 shorter events, 20.9 us)
Async XLA Ops:
  0.0 40.0 %copy-start = (s32[8,8]{1,0:T(8,128)S(1)}, s32[8,8]{1,0:T(8,128)}, u32[]{:S(2)}) copy-start(s32[8,8]{1,0:T(8,128)} %param.14) | copy-start | bytes 772
  5.0 35.8 %copy-start.18 = (pred[2,192]{1,0:T(4,128)(4,1)S(1)}, pred[2,192]{1,0:T(4,128)(4,1)}, u32[]{:S(2)}) copy-start(pred[2,192]{1,0:T(4,128)(4,1)} %constant.79.clone) | copy-start | bytes 1156
  5.0 36.1 %copy-start.15 = (pred[5,320]{1,0:T(8,128)(4,1)S(1)}, pred[5,320]{1,0:T(8,128)(4,1)}, u32[]{:S(2)}) copy-start(pred[5,320]{1,0:T(8,128)(4,1)} %constant.81.clone) | copy-start | bytes 4804
  5.0 36.2 %copy-start.13 = (pred[5,640]{1,0:T(8,128)(4,1)S(1)}, pred[5,640]{1,0:T(8,128)(4,1)}, u32[]{:S(2)}) copy-start(pred[5,640]{1,0:T(8,128)(4,1)} %constant.77.clone) | copy-start | bytes 9604
  5.0 36.3 %copy-start.17 = (s32[192]{0:T(256)S(1)}, s32[192]{0:T(256)}, u32[]{:S(2)}) copy-start(s32[192]{0:T(256)} %constant.80.clone) | copy-start | bytes 2308
  5.0 36.3 %copy-start.16 = (s32[320]{0:T(512)S(1)}, s32[320]{0:T(512)}, u32[]{:S(2)}) copy-start(s32[320]{0:T(512)} %constant.82.clone) | copy-start | bytes 3844
  5.0 36.9 %copy-start.14 = (s32[640]{0:T(1024)S(1)}, s32[640]{0:T(1024)}, u32[]{:S(2)}) copy-start(s32[640]{0:T(1024)} %constant.78.clone) | copy-start | bytes 7684
  5.0 32.9 %collective-permute-start = (bf16[2,256,1280]{2,1,0:T(8,128)(2,1)S(1)}, bf16[2,256,1280]{2,1,0:T(8,128)(2,1)S(1)}, u32[]{:S(2)}, u32[]{:S(2)}) collective-permute-start(bf16[2,256,1280]{2,1,0:T(8,128)(2,1)S(1)} %get-tuple-element.34), channel_id=1, source_target_pairs={{0,4},{1,5},{2,6},{3,7},{4,0},{5,1},{6,2},{7,3},{8,12},{9,13},{10,... | collective-permute-start | bytes 3932168 | tf_op jit(solution)/shard_map/ppermute | solution.py:180
  6.6 31.3 %collective-permute-start.1 = (bf16[2,128,1280]{2,1,0:T(8,128)(2,1)S(1)}, bf16[2,128,1280]{2,1,0:T(8,128)(2,1)S(1)}, u32[]{:S(2)}, u32[]{:S(2)}) collective-permute-start(bf16[2,128,1280]{2,1,0:T(8,128)(2,1)S(1)} %get-tuple-element.35), channel_id=1, source_target_pairs={{0,8},{1,9},{2,10},{3,11},{8,16},{9,17},{10,18},{11,19},{12,4},{13... | collective-permute-start | bytes 1966088 | tf_op jit(solution)/shard_map/ppermute | solution.py:180
  10.0 27.8 %collective-permute-start.2 = (bf16[2,128,1280]{2,1,0:T(8,128)(2,1)S(1)}, bf16[2,128,1280]{2,1,0:T(8,128)(2,1)S(1)}, u32[]{:S(2)}, u32[]{:S(2)}) collective-permute-start(bf16[2,128,1280]{2,1,0:T(8,128)(2,1)S(1)} %get-tuple-element.35), channel_id=1, source_target_pairs={{4,12},{5,13},{6,14},{7,15},{8,0},{9,1},{10,2},{11,3},{12,20},{13,... | collective-permute-start | bytes 1966088 | tf_op jit(solution)/shard_map/ppermute | solution.py:180
  12.5 25.4 %collective-permute-start.3 = (bf16[2,64,1280]{2,1,0:T(8,128)(2,1)}, bf16[2,64,1280]{2,1,0:T(8,128)(2,1)S(1)}, u32[]{:S(2)}, u32[]{:S(2)}) collective-permute-start(bf16[2,64,1280]{2,1,0:T(8,128)(2,1)} %get-tuple-element.36), channel_id=1, source_target_pairs={{0,16},{1,17},{2,18},{3,19},{4,20},{5,21},{6,22},{7,23},{8,24},{9,... | collective-permute-start | bytes 983048 | tf_op jit(solution)/shard_map/ppermute | solution.py:180
  37.9 19.1 %copy-start.3 = (bf16[2,64,1280]{2,1,0:T(8,128)(2,1)}, bf16[2,64,1280]{2,1,0:T(8,128)(2,1)S(1)}, u32[]{:S(2)}) copy-start(bf16[2,64,1280]{2,1,0:T(8,128)(2,1)S(1)} %collective-permute-done.3.two_ref.refs_4_) | copy-start | bytes 983044
  39.0 34.6 %collective-permute-start.8 = (bf16[1280,5120]{1,0:T(8,128)(2,1)}, bf16[1280,5120]{1,0:T(8,128)(2,1)}, u32[]{:S(2)}, u32[]{:S(2)}) collective-permute-start(bf16[1280,5120]{1,0:T(8,128)(2,1)} %param.15), channel_id=1, source_target_pairs={{0,1},{1,0},{2,3},{3,2},{4,5},{5,4},{6,7},{7,6},{8,9},{9,8},{10,11... | collective-permute-start | bytes 39321608 | tf_op jit(solution)/shard_map/ppermute | solution.py:180
  39.0 20.4 %collective-permute-start.5 = (bf16[2,64,1280]{2,1,0:T(8,128)(2,1)}, bf16[2,64,1280]{2,1,0:T(8,128)(2,1)S(1)}, u32[]{:S(2)}, u32[]{:S(2)}) collective-permute-start(bf16[2,64,1280]{2,1,0:T(8,128)(2,1)} %get-tuple-element.36), channel_id=1, source_target_pairs={{0,24},{1,25},{2,26},{3,27},{4,28},{5,29},{6,30},{7,31},{24,0},{25... | collective-permute-start | bytes 983048 | tf_op jit(solution)/shard_map/ppermute | solution.py:180
  43.6 30.1 %collective-permute-start.7 = (bf16[2,64,1280]{2,1,0:T(8,128)(2,1)}, bf16[2,64,1280]{2,1,0:T(8,128)(2,1)}, u32[]{:S(2)}, u32[]{:S(2)}) collective-permute-start(bf16[2,64,1280]{2,1,0:T(8,128)(2,1)} %slice.42), channel_id=1, source_target_pairs={{0,8},{1,9},{2,10},{3,11},{8,16},{9,17},{10,18},{11,19},{12,4},{13... | collective-permute-start | bytes 983048 | tf_op jit(solution)/shard_map/ppermute | solution.py:180
  49.1 30.1 %collective-permute-start.10 = (bf16[2,128,1280]{2,1,0:T(8,128)(2,1)}, bf16[2,128,1280]{2,1,0:T(8,128)(2,1)}, u32[]{:S(2)}, u32[]{:S(2)}) collective-permute-start(bf16[2,128,1280]{2,1,0:T(8,128)(2,1)} %slice.43), channel_id=1, source_target_pairs={{0,8},{1,9},{2,10},{3,11},{8,16},{9,17},{10,18},{11,19},{12,4},{13... | collective-permute-start | bytes 1966088 | tf_op jit(solution)/shard_map/ppermute | solution.py:180
  59.4 30.6 %collective-permute-start.4 = (bf16[2,192,1280]{2,1,0:T(8,128)(2,1)}, bf16[2,192,1280]{2,1,0:T(8,128)(2,1)S(1)}, u32[]{:S(2)}, u32[]{:S(2)}) collective-permute-start(bf16[2,192,1280]{2,1,0:T(8,128)(2,1)} %gather.1), channel_id=1, source_target_pairs={{0,4},{1,5},{2,6},{3,7},{4,0},{5,1},{6,2},{7,3},{8,12},{9,13},{10,... | collective-permute-start | bytes 2949128 | tf_op jit(solution)/shard_map/ppermute | solution.py:180
  60.5 29.5 %collective-permute-start.6 = (bf16[2,64,1280]{2,1,0:T(8,128)(2,1)S(1)}, bf16[2,64,1280]{2,1,0:T(8,128)(2,1)S(1)}, u32[]{:S(2)}, u32[]{:S(2)}) collective-permute-start(bf16[2,64,1280]{2,1,0:T(8,128)(2,1)S(1)} %broadcast_select_fusion), channel_id=1, source_target_pairs={{0,4},{1,5},{2,6},{3,7},{4,0},{5,1},{6,2},{7,3},{8,12},{9,13},{10,... | collective-permute-start | bytes 983048 | tf_op jit(solution)/shard_map/ppermute | solution.py:180
  73.6 16.3 %collective-permute-start.9 = (bf16[2,64,1280]{2,1,0:T(8,128)(2,1)}, bf16[2,64,1280]{2,1,0:T(8,128)(2,1)S(1)}, u32[]{:S(2)}, u32[]{:S(2)}) collective-permute-start(bf16[2,64,1280]{2,1,0:T(8,128)(2,1)} %collective-permute-done.7.refs_1_), channel_id=1, source_target_pairs={{0,8},{1,9},{2,10},{3,11},{8,16},{9,17},{10,18},{11,19},{12,4},{13... | collective-permute-start | bytes 983048 | tf_op jit(solution)/shard_map/ppermute | solution.py:180
  93.3 5.5 %collective-permute-start.11 = (bf16[512,768]{1,0:T(8,128)(2,1)S(1)}, bf16[512,768]{1,0:T(8,128)(2,1)S(1)}, u32[]{:S(2)}, u32[]{:S(2)}) collective-permute-start(bf16[512,768]{1,0:T(8,128)(2,1)S(1)} %last0.1), channel_id=1, source_target_pairs={{0,1},{1,0},{2,3},{3,2},{4,5},{5,4},{6,7},{7,6},{8,9},{9,8},{10,11... | collective-permute-start | bytes 2359304 | tf_op jit(solution)/shard_map/ppermute | solution.py:180
  95.6 2.1 %collective-permute-start.12 = (bf16[512,512]{1,0:T(8,128)(2,1)S(1)}, bf16[512,512]{1,0:T(8,128)(2,1)S(1)}, u32[]{:S(2)}, u32[]{:S(2)}) collective-permute-start(bf16[512,512]{1,0:T(8,128)(2,1)S(1)} %last6.1), channel_id=1, source_target_pairs={{0,1},{1,0},{2,3},{3,2},{4,5},{5,4},{6,7},{7,6},{8,9},{9,8},{10,11... | collective-permute-start | bytes 1572872 | tf_op jit(solution)/shard_map/ppermute | solution.py:180
  100.5 17.6 %collective-permute-start.13 = (bf16[512,640]{1,0:T(8,128)(2,1)S(1)}, bf16[512,640]{1,0:T(8,128)(2,1)S(1)}, u32[]{:S(2)}, u32[]{:S(2)}) collective-permute-start(bf16[512,640]{1,0:T(8,128)(2,1)S(1)} %fusion.9), channel_id=1, source_target_pairs={{0,2},{1,3},{2,0},{3,1},{4,6},{5,7},{6,4},{7,5},{8,10},{9,11},{10,... | collective-permute-start | bytes 1966088 | tf_op jit(solution)/shard_map/ppermute | solution.py:180
  104.7 26.9 %collective-permute-start.14 = (bf16[512,640]{1,0:T(8,128)(2,1)S(1)}, bf16[512,640]{1,0:T(8,128)(2,1)S(1)}, u32[]{:S(2)}, u32[]{:S(2)}) collective-permute-start(bf16[512,640]{1,0:T(8,128)(2,1)S(1)} %fusion.10), channel_id=1, source_target_pairs={{0,2},{1,3},{2,0},{3,1},{4,6},{5,7},{6,4},{7,5},{8,10},{9,11},{10,... | collective-permute-start | bytes 1966088 | tf_op jit(solution)/shard_map/ppermute | solution.py:180
  107.1 25.8 %copy-start.1 = (s32[8,8]{1,0:T(8,128)S(1)}, s32[8,8]{1,0:T(8,128)}, u32[]{:S(2)}) copy-start(s32[8,8]{1,0:T(8,128)} %param.14) | copy-start | bytes 772
  (10 other events, 43.8 us)

commit v6 on v4

--- a/solution.py
+++ b/solution.py
@@ -130,9 +130,9 @@
         name=name,
         compiler_params=pltpu.CompilerParams(vmem_limit_bytes=16 << 20),
         cost_estimate=pl.CostEstimate(
-            flops=4 * row_count * count * width,
-            bytes_accessed=8 * row_count * width,
-            transcendentals=row_count * count * (high - low),
+            flops=0 if own else 4 * row_count * count * width,
+            bytes_accessed=0 if own else 8 * row_count * width,
+            transcendentals=0 if own else row_count * count * (high - low),
         ),
     )(*operands)
 
@@ -205,19 +205,19 @@
         at_end = (my_block < 2) | (my_block >= block_count - 2)
         three = jnp.where(at_end, opposite, -1)
 
-        sent, sent_ab, sent_a = pack(key_vectors, value_vectors, [(0, near), (0, ab), (0, a)])
+        sent, sent_ab, sent_ba, sent_a = pack(
+            key_vectors, value_vectors, [(0, near), (0, ab), (0, ab), (0, a)]
+        )
         x_rows = move(sent, lambda t: t ^ 1)
         z_far = move(sent_ab, near_of)
-        z_near = move(sent_ab, far_of)
+        z_near = move(sent_ba, far_of)
         z_two = move(sent_a, lambda t: t ^ 4)
         carry = attend(query_vectors, own_pair, [], None, None, False, 0, head_count, "own")
-        z_far, z_near, state, out_weight, moved = lax.optimization_barrier(
-            (z_far, z_near, carry[0], out_weight, moved)
+        x_rows, z_far, z_near, z_two, state, moved = lax.optimization_barrier(
+            (x_rows, z_far, z_near, z_two, carry[0], moved)
         )
         cross_far = move(z_far, twin_if(far_of))
         cross_near = move(z_near[:, :a], twin_if(near_of))
-        weights = blocks_of(out_weight, moved)
-        x_rows, z_two, state, weights = lax.optimization_barrier((x_rows, z_two, state, weights))
         near_bc = move(x_rows[:, a:], near_of)
         cross_two = move(z_two, lambda t: t ^ 1)
         z_three = move(z_two, lambda t: {4: 6, 5: 7, 2: 0, 3: 1}.get(t))
@@ -229,7 +229,9 @@
         )
         z_three, state = lax.optimization_barrier((z_three, carry[0]))
         cross_three = move(z_three, lambda t: t ^ 1 if t in ends else None)
-        near_bc, state = lax.optimization_barrier((near_bc, state))
+        state, out_weight, moved = lax.optimization_barrier((state, out_weight, moved))
+        weights = blocks_of(out_weight, moved)
+        near_bc, state, weights = lax.optimization_barrier((near_bc, state, weights))
         chain_b = move(near_bc[:, : ab - a], near_of)
         carry = further(
             [near_bc, z_three],
@@ -265,6 +267,7 @@
         (part,) = attend(
             query_vectors, None, buffers, bias, carry, True, low, high, f"last{low}"
         )
+        bias, part = lax.optimization_barrier((bias, part))
         parts.append((part, move(part, same, core), low * HEAD_DIM, high * HEAD_DIM))
 
     def project(index, first, last):

time: 129 us -> 134 us (1.039)
  starting transfers between devices: 25.2 us -> 32.6 us
  waiting for transfers between devices: 50.3 us -> 47.4 us
    ppermute x16, starting transfers between devices: 25.2 us -> 32.6 us  [move(): return lax.ppermute(array, AXES, route)]
    ppermute x16, waiting for transfers between devices: 50.3 us -> 47.4 us  [move(): return lax.ppermute(array, AXES, route)]
  transfers between devices with their start and end apart: 16 -> 16, of which waited for: 9 -> 6; matrix products, arithmetic and copies ran while one was open for 12% -> 10% of each run, Pallas kernels for 18% -> 16%
where the time goes in v6:
time: 134 us; the launch traced here: 133 us
  waiting for transfers between devices  47.4 us (35%)
  starting transfers between devices  32.6 us (24%)
  Pallas kernels  27.7 us (21%)
  local copies, waits for them, and re-layouts  12.6 us (9%)
  matrix products  9.72 us (7%)
  other arithmetic  2.87 us (2%)
    ppermute x16, waiting for transfers between devices, move(): return lax.ppermute(array, AXES, route)  47.4 us
    ppermute x16, starting transfers between devices, move(): return lax.ppermute(array, AXES, route)  32.6 us
    pallas_call x5, Pallas kernels, attend(): pl.pallas_call(lambda *refs: attend_kernel(*refs, buffers=len(buffers), o...  25.2 us
    unnamed x30, local copies, waits for them, and re-layouts  5.55 us
    dynamic_slice x1, local copies, waits for them, and re-layouts, blocks_of(): lax.dynamic_slice_in_dim(source, number * out_width, out_width, 1)  5.28 us
    dot_general x6, matrix products, project(): jnp.dot(part, weights[index][low:high, first:last], preferred_element_typ...  4.97 us
    dot_general x6, matrix products, project(): jnp.dot(other, weights[index + 2][low:high, first:last], preferred_elemen...  4.75 us
  transfers between devices with their start and end apart: 16, of which 6 were waited for; matrix products, arithmetic and copies ran while one was open for 10% of the time, Pallas kernels for 16%

profile of v6, /device:TPU:2, one launch (start us, length us, event | category | flops | bytes accessed | tf_op | source)
XLA Modules:
  0.0 133.2 jit_solution(12647645685784971434)
XLA Ops:
  0.0 1.4 %copy-done.3 = bf16[512,1280]{1,0:T(8,128)(2,1)S(1)} copy-done((bf16[512,1280]{1,0:T(8,128)(2,1)S(1)}, bf16[512,1280]{1,0:T(8,128)(2,1)}, u32[]{:S(2)}) %copy-start.3) | copy-done | bytes 1310744
  1.4 1.3 copy-done.5
  2.8 2.5 %pack.1 = (bf16[2,256,1280]{2,1,0:T(8,128)(2,1)}, bf16[2,128,1280]{2,1,0:T(8,128)(2,1)}, bf16[2,128,1280]{2,1,0:T(8,128)(2,1)}, bf16[2,64,1280]{2,1,0:T(8,128)(2,1)}) custom-call(bf16[512,1280]{1,0:T(8,128)(2,1)S(1)} %copy-done.3, bf16[512,1280]{1,0:T(8,128)(2,1)S(1)} %copy-done.5), custom_call_target="tpu_custom_call" | custom-call | flops 671088640 | bytes 5242880 | tf_op jit(solution)/shard_map/pack/pallas_call | solution.py:39
  6.7 4.7 %collective-permute-start.2 = (bf16[2,128,1280]{2,1,0:T(8,128)(2,1)}, bf16[2,128,1280]{2,1,0:T(8,128)(2,1)S(1)}, u32[]{:S(2)}, u32[]{:S(2)}) collective-permute-start(bf16[2,128,1280]{2,1,0:T(8,128)(2,1)} %get-tuple-element.44), channel_id=1, source_target_pairs={{4,12},{5,13},{6,14},{7,15},{8,0},{9,1},{10,2},{11,3},{12,20},{13,... | collective-permute-start | bytes 1966088 | tf_op jit(solution)/shard_map/ppermute | solution.py:155
  11.3 3.9 %collective-permute-start.3 = (bf16[2,64,1280]{2,1,0:T(8,128)(2,1)}, bf16[2,64,1280]{2,1,0:T(8,128)(2,1)}, u32[]{:S(2)}, u32[]{:S(2)}) collective-permute-start(bf16[2,64,1280]{2,1,0:T(8,128)(2,1)} %get-tuple-element.45), channel_id=1, source_target_pairs={{0,16},{1,17},{2,18},{3,19},{4,20},{5,21},{6,22},{7,23},{8,24},{9,... | collective-permute-start | bytes 983048 | tf_op jit(solution)/shard_map/ppermute | solution.py:155
  15.3 1.3 copy-done.6
  16.6 6.4 %own.1 = (f32[10,8,512]{2,1,0:T(8,128)S(1)}, f32[10,128,512]{2,1,0:T(8,128)S(1)}) custom-call(bf16[512,1280]{1,0:T(8,128)(2,1)S(1)} %copy-done.2, bf16[512,1280]{1,0:T(8,128)(2,1)S(1)} %copy-done.4, bf16[512,1280]{1,0:T(8,128)(2,1)S(1)} %copy-done.6), custom_call_target="tpu_custom_call" | custom-call | tf_op jit(solution)/shard_map/own/pallas_call | solution.py:123
  23.0 1.4 %copy-done.7 = f32[10,128,512]{2,1,0:T(8,128)} copy-done((f32[10,128,512]{2,1,0:T(8,128)}, f32[10,128,512]{2,1,0:T(8,128)S(1)}, u32[]{:S(2)}) %copy-start.7) | copy-done | bytes 2621464
  26.0 13.9 %collective-permute-done.3.refs_4_ = bf16[2,64,1280]{2,1,0:T(8,128)(2,1)} collective-permute-done((bf16[2,64,1280]{2,1,0:T(8,128)(2,1)}, bf16[2,64,1280]{2,1,0:T(8,128)(2,1)}, u32[]{:S(2)}, u32[]{:S(2)}) %collective-permute-start.3) | collective-permute-done | bytes 327712 | tf_op jit(solution)/shard_map/ppermute | solution.py:155
  41.3 4.8 %collective-permute-start.7 = (bf16[2,64,1280]{2,1,0:T(8,128)(2,1)}, bf16[2,64,1280]{2,1,0:T(8,128)(2,1)S(1)}, u32[]{:S(2)}, u32[]{:S(2)}) collective-permute-start(bf16[2,64,1280]{2,1,0:T(8,128)(2,1)} %collective-permute-done.3.refs_4_), channel_id=1, source_target_pairs={{0,4},{1,5},{2,6},{3,7},{4,0},{5,1},{6,2},{7,3},{8,12},{9,13},{10,... | collective-permute-start | bytes 983048 | tf_op jit(solution)/shard_map/ppermute | solution.py:155
  46.0 2.0 %collective-permute-start.5 = (bf16[2,128,1280]{2,1,0:T(8,128)(2,1)}, bf16[2,128,1280]{2,1,0:T(8,128)(2,1)S(1)}, u32[]{:S(2)}, u32[]{:S(2)}) collective-permute-start(bf16[2,128,1280]{2,1,0:T(8,128)(2,1)} %collective-permute-done.1.refs_2_), channel_id=1, source_target_pairs={{4,0},{5,1},{6,2},{7,3},{8,12},{9,13},{10,14},{11,15},{12,8},{13,9... | collective-permute-start | bytes 1966088 | tf_op jit(solution)/shard_map/ppermute | solution.py:155
  52.1 8.7 %first.1 = (f32[10,8,512]{2,1,0:T(8,128)S(1)}, f32[10,128,512]{2,1,0:T(8,128)S(1)}) custom-call(bf16[512,1280]{1,0:T(8,128)(2,1)S(1)} %copy-done.2, bf16[2,256,1280]{2,1,0:T(8,128)(2,1)} %collective-permute-done.refs_1_, bf16[2,128,1280]{2,1,0:T(8,128)(2,1)} %collective-permute-done.1.refs_2_, bf16[2,128,1280]{2,1,0:T(8,128)(2,1)S(1)} %collective-permute-done.2.refs_3_, ...), custom_call_target="tpu_custom_call" | custom-call | flops 1509949440 | bytes 5242880 | tf_op jit(solution)/shard_map/first/pallas_call | solution.py:123
  60.8 7.9 %collective-permute-start.9 = (bf16[2,64,1280]{2,1,0:T(8,128)(2,1)S(1)}, bf16[2,64,1280]{2,1,0:T(8,128)(2,1)S(1)}, u32[]{:S(2)}, u32[]{:S(2)}) collective-permute-start(bf16[2,64,1280]{2,1,0:T(8,128)(2,1)S(1)} %collective-permute-done.8.refs_2_), channel_id=1, source_target_pairs={{0,4},{1,5},{2,6},{3,7},{4,0},{5,1},{6,2},{7,3},{24,28},{25,29},{2... | collective-permute-start | bytes 983048 | tf_op jit(solution)/shard_map/ppermute | solution.py:155
  68.7 5.3 %constant_dynamic-slice_fusion = (bf16[1280,1280]{1,0:T(8,128)(2,1)S(1)}, bf16[1280,1280]{1,0:T(8,128)(2,1)S(1)}, bf16[1280,1280]{1,0:T(8,128)(2,1)S(1)}, bf16[1280,1280]{1,0:T(8,128)(2,1)S(1)}) fusion(bf16[1280,5120]{1,0:T(8,128)(2,1)} %collective-permute-done.4, s32[]{:T(128)S(6)} %select_n.113, s32[]{:T(128)S(6)} %select_n.112, bf16[1280,5120]{1,0:T(8,128)(2,1)} %param.15), kind=kLoop, calls=%fused_computation.45 | loop fusion | bytes 26214408 | tf_op jit(solution)/shard_map/dynamic_slice | solution.py:190
  74.0 3.6 %collective-permute-done.10.refs_1_ = bf16[2,192,1280]{2,1,0:T(8,128)(2,1)S(1)} collective-permute-done((bf16[2,192,1280]{2,1,0:T(8,128)(2,1)S(1)}, bf16[2,192,1280]{2,1,0:T(8,128)(2,1)S(1)}, u32[]{:S(2)}, u32[]{:S(2)}) %collective-permute-start.10) | collective-permute-done | bytes 983072 | tf_op jit(solution)/shard_map/ppermute | solution.py:155
  77.6 1.5 %collective-permute-start.11 = (bf16[2,64,1280]{2,1,0:T(8,128)(2,1)S(1)}, bf16[2,64,1280]{2,1,0:T(8,128)(2,1)S(1)}, u32[]{:S(2)}, u32[]{:S(2)}) collective-permute-start(bf16[2,64,1280]{2,1,0:T(8,128)(2,1)S(1)} %slice.47), channel_id=1, source_target_pairs={{0,8},{1,9},{2,10},{3,11},{8,16},{9,17},{10,18},{11,19},{12,4},{13... | collective-permute-start | bytes 983048 | tf_op jit(solution)/shard_map/ppermute | solution.py:155
  79.3 4.3 %middle.1 = (f32[10,8,512]{2,1,0:T(8,128)S(1)}, f32[10,128,512]{2,1,0:T(8,128)S(1)}) custom-call(bf16[512,1280]{1,0:T(8,128)(2,1)S(1)} %copy-done.2, bf16[2,192,1280]{2,1,0:T(8,128)(2,1)S(1)} %collective-permute-done.10.refs_1_, bf16[2,64,1280]{2,1,0:T(8,128)(2,1)S(1)} %collective-permute-done.8.refs_2_, f32[256,128]{1,0:T(8,128)S(1)} %broadcast_in_dim.164.refs_3_, ...), custom_call_target="tpu_custom_call" | custom-call | flops 671088640 | bytes 5242880 | tf_op jit(solution)/shard_map/middle/pallas_call | solution.py:123
  83.6 2.9 %collective-permute-done.11.refs_5_ = bf16[2,64,1280]{2,1,0:T(8,128)(2,1)S(1)} collective-permute-done((bf16[2,64,1280]{2,1,0:T(8,128)(2,1)S(1)}, bf16[2,64,1280]{2,1,0:T(8,128)(2,1)S(1)}, u32[]{:S(2)}, u32[]{:S(2)}) %collective-permute-start.11) | collective-permute-done | bytes 327712 | tf_op jit(solution)/shard_map/ppermute | solution.py:155
  86.7 3.5 %last0.1 = bf16[512,768]{1,0:T(8,128)(2,1)S(1)} custom-call(bf16[512,1280]{1,0:T(8,128)(2,1)S(1)} %copy-done.2, bf16[2,128,1280]{2,1,0:T(8,128)(2,1)S(1)} %collective-permute-done.5.refs_1_, bf16[2,64,1280]{2,1,0:T(8,128)(2,1)S(1)} %collective-permute-done.6.refs_2_, bf16[2,64,1280]{2,1,0:T(8,128)(2,1)S(1)} %collective-permute-done.7.refs_3_, ...), custom_call_target="tpu_custom_call" | custom-call | flops 603979776 | bytes 3145728 | tf_op jit(solution)/shard_map/last0/pallas_call | solution.py:123
  90.2 2.3 %last6.1 = bf16[512,512]{1,0:T(8,128)(2,1)S(1)} custom-call(bf16[512,1280]{1,0:T(8,128)(2,1)S(1)} %copy-done.2, bf16[2,128,1280]{2,1,0:T(8,128)(2,1)S(1)} %collective-permute-done.5.refs_1_, bf16[2,64,1280]{2,1,0:T(8,128)(2,1)S(1)} %collective-permute-done.6.refs_2_, bf16[2,64,1280]{2,1,0:T(8,128)(2,1)S(1)} %collective-permute-done.7.refs_3_, ...), custom_call_target="tpu_custom_call" | custom-call | flops 402653184 | bytes 2097152 | tf_op jit(solution)/shard_map/last6/pallas_call | solution.py:123
  101.0 1.5 %collective-permute-start.14 = (bf16[512,640]{1,0:T(8,128)(2,1)S(1)}, bf16[512,640]{1,0:T(8,128)(2,1)S(1)}, u32[]{:S(2)}, u32[]{:S(2)}) collective-permute-start(bf16[512,640]{1,0:T(8,128)(2,1)S(1)} %fusion.9), channel_id=1, source_target_pairs={{0,2},{1,3},{2,0},{3,1},{4,6},{5,7},{6,4},{7,5},{8,10},{9,11},{10,... | collective-permute-start | bytes 1966088 | tf_op jit(solution)/shard_map/ppermute | solution.py:155
  105.2 13.4 %collective-permute-done.14 = bf16[512,640]{1,0:T(8,128)(2,1)S(1)} collective-permute-done((bf16[512,640]{1,0:T(8,128)(2,1)S(1)}, bf16[512,640]{1,0:T(8,128)(2,1)S(1)}, u32[]{:S(2)}, u32[]{:S(2)}) %collective-permute-start.14) | collective-permute-done | bytes 655392 | tf_op jit(solution)/shard_map/ppermute | solution.py:155
  118.7 13.2 %collective-permute-done.15 = bf16[512,640]{1,0:T(8,128)(2,1)S(1)} collective-permute-done((bf16[512,640]{1,0:T(8,128)(2,1)S(1)}, bf16[512,640]{1,0:T(8,128)(2,1)S(1)}, u32[]{:S(2)}, u32[]{:S(2)}) %collective-permute-start.15) | collective-permute-done | bytes 655392 | tf_op jit(solution)/shard_map/ppermute | solution.py:155
  131.9 1.3 %add_convert_fusion = bf16[512,1280]{1,0:T(8,128)(2,1)} fusion(f32[512,1280]{1,0:T(8,128)S(1)} %fusion.1, bf16[512,640]{1,0:T(8,128)(2,1)S(1)} %collective-permute-done.15, bf16[512,640]{1,0:T(8,128)(2,1)S(1)} %collective-permute-done.14), kind=kLoop, calls=%fused_computation.3 | loop fusion | flops 3932160 | bytes 5242880 | tf_op jit(solution)/shard_map/convert_element_type | solution.py:290
  (83 shorter events, 19.8 us)
Async XLA Ops:
  0.0 24.6 %copy-start = (s32[8,8]{1,0:T(8,128)S(1)}, s32[8,8]{1,0:T(8,128)}, u32[]{:S(2)}) copy-start(s32[8,8]{1,0:T(8,128)} %param.14) | copy-start | bytes 772
  0.0 39.9 %collective-permute-start.4 = (bf16[1280,5120]{1,0:T(8,128)(2,1)}, bf16[1280,5120]{1,0:T(8,128)(2,1)}, u32[]{:S(2)}, u32[]{:S(2)}) collective-permute-start(bf16[1280,5120]{1,0:T(8,128)(2,1)} %param.15), channel_id=1, source_target_pairs={{0,1},{1,0},{2,3},{3,2},{4,5},{5,4},{6,7},{7,6},{8,9},{9,8},{10,11... | collective-permute-start | bytes 39321608 | tf_op jit(solution)/shard_map/ppermute | solution.py:155
  5.3 20.2 %copy-start.14 = (pred[2,256]{1,0:T(4,128)(4,1)S(1)}, pred[2,256]{1,0:T(4,128)(4,1)}, u32[]{:S(2)}) copy-start(pred[2,256]{1,0:T(4,128)(4,1)} %constant.79.clone) | copy-start | bytes 1540
  5.3 20.3 %copy-start.11 = (pred[4,576]{1,0:T(4,128)(4,1)S(1)}, pred[4,576]{1,0:T(4,128)(4,1)}, u32[]{:S(2)}) copy-start(pred[4,576]{1,0:T(4,128)(4,1)} %constant.77.clone) | copy-start | bytes 6916
  5.3 20.5 %copy-start.13 = (s32[256]{0:T(256)S(1)}, s32[256]{0:T(256)}, u32[]{:S(2)}) copy-start(s32[256]{0:T(256)} %constant.80.clone) | copy-start | bytes 3076
  5.3 20.7 %copy-start.9 = (s32[576]{0:T(1024)S(1)}, s32[576]{0:T(1024)}, u32[]{:S(2)}) copy-start(s32[576]{0:T(1024)} %constant.78.clone) | copy-start | bytes 6916
  5.3 34.7 %collective-permute-start = (bf16[2,256,1280]{2,1,0:T(8,128)(2,1)}, bf16[2,256,1280]{2,1,0:T(8,128)(2,1)}, u32[]{:S(2)}, u32[]{:S(2)}) collective-permute-start(bf16[2,256,1280]{2,1,0:T(8,128)(2,1)} %get-tuple-element.42), channel_id=1, source_target_pairs={{0,4},{1,5},{2,6},{3,7},{4,0},{5,1},{6,2},{7,3},{8,12},{9,13},{10,... | collective-permute-start | bytes 3932168 | tf_op jit(solution)/shard_map/ppermute | solution.py:155
  5.4 34.6 %collective-permute-start.1 = (bf16[2,128,1280]{2,1,0:T(8,128)(2,1)}, bf16[2,128,1280]{2,1,0:T(8,128)(2,1)}, u32[]{:S(2)}, u32[]{:S(2)}) collective-permute-start(bf16[2,128,1280]{2,1,0:T(8,128)(2,1)} %get-tuple-element.43), channel_id=1, source_target_pairs={{0,8},{1,9},{2,10},{3,11},{8,16},{9,17},{10,18},{11,19},{12,4},{13... | collective-permute-start | bytes 1966088 | tf_op jit(solution)/shard_map/ppermute | solution.py:155
  6.7 33.3 %collective-permute-start.2 = (bf16[2,128,1280]{2,1,0:T(8,128)(2,1)}, bf16[2,128,1280]{2,1,0:T(8,128)(2,1)S(1)}, u32[]{:S(2)}, u32[]{:S(2)}) collective-permute-start(bf16[2,128,1280]{2,1,0:T(8,128)(2,1)} %get-tuple-element.44), channel_id=1, source_target_pairs={{4,12},{5,13},{6,14},{7,15},{8,0},{9,1},{10,2},{11,3},{12,20},{13,... | collective-permute-start | bytes 1966088 | tf_op jit(solution)/shard_map/ppermute | solution.py:155
  11.3 28.6 %collective-permute-start.3 = (bf16[2,64,1280]{2,1,0:T(8,128)(2,1)}, bf16[2,64,1280]{2,1,0:T(8,128)(2,1)}, u32[]{:S(2)}, u32[]{:S(2)}) collective-permute-start(bf16[2,64,1280]{2,1,0:T(8,128)(2,1)} %get-tuple-element.45), channel_id=1, source_target_pairs={{0,16},{1,17},{2,18},{3,19},{4,20},{5,21},{6,22},{7,23},{8,24},{9,... | collective-permute-start | bytes 983048 | tf_op jit(solution)/shard_map/ppermute | solution.py:155
  24.5 27.6 %copy-start.8 = (f32[10,128,512]{2,1,0:T(8,128)S(1)}, f32[10,128,512]{2,1,0:T(8,128)}, u32[]{:S(2)}) copy-start(f32[10,128,512]{2,1,0:T(8,128)} %copy-done.7) | copy-start | bytes 7864324
  40.0 20.8 %collective-permute-start.8 = (bf16[2,64,1280]{2,1,0:T(8,128)(2,1)}, bf16[2,64,1280]{2,1,0:T(8,128)(2,1)S(1)}, u32[]{:S(2)}, u32[]{:S(2)}) collective-permute-start(bf16[2,64,1280]{2,1,0:T(8,128)(2,1)} %collective-permute-done.3.refs_4_), channel_id=1, source_target_pairs={{8,0},{9,1},{10,2},{11,3},{12,4},{13,5},{14,6},{15,7},{16,24},{17,... | collective-permute-start | bytes 983048 | tf_op jit(solution)/shard_map/ppermute | solution.py:155
  41.3 42.3 %collective-permute-start.7 = (bf16[2,64,1280]{2,1,0:T(8,128)(2,1)}, bf16[2,64,1280]{2,1,0:T(8,128)(2,1)S(1)}, u32[]{:S(2)}, u32[]{:S(2)}) collective-permute-start(bf16[2,64,1280]{2,1,0:T(8,128)(2,1)} %collective-permute-done.3.refs_4_), channel_id=1, source_target_pairs={{0,4},{1,5},{2,6},{3,7},{4,0},{5,1},{6,2},{7,3},{8,12},{9,13},{10,... | collective-permute-start | bytes 983048 | tf_op jit(solution)/shard_map/ppermute | solution.py:155
  46.0 37.6 %collective-permute-start.5 = (bf16[2,128,1280]{2,1,0:T(8,128)(2,1)}, bf16[2,128,1280]{2,1,0:T(8,128)(2,1)S(1)}, u32[]{:S(2)}, u32[]{:S(2)}) collective-permute-start(bf16[2,128,1280]{2,1,0:T(8,128)(2,1)} %collective-permute-done.1.refs_2_), channel_id=1, source_target_pairs={{4,0},{5,1},{6,2},{7,3},{8,12},{9,13},{10,14},{11,15},{12,8},{13,9... | collective-permute-start | bytes 1966088 | tf_op jit(solution)/shard_map/ppermute | solution.py:155
  48.0 35.5 %collective-permute-start.6 = (bf16[2,64,1280]{2,1,0:T(8,128)(2,1)S(1)}, bf16[2,64,1280]{2,1,0:T(8,128)(2,1)S(1)}, u32[]{:S(2)}, u32[]{:S(2)}) collective-permute-start(bf16[2,64,1280]{2,1,0:T(8,128)(2,1)S(1)} %slice.45), channel_id=1, source_target_pairs={{0,4},{1,5},{2,6},{3,7},{8,12},{9,13},{10,14},{11,15},{12,8},{13,9... | collective-permute-start | bytes 983048 | tf_op jit(solution)/shard_map/ppermute | solution.py:155
  50.6 26.9 %collective-permute-start.10 = (bf16[2,192,1280]{2,1,0:T(8,128)(2,1)S(1)}, bf16[2,192,1280]{2,1,0:T(8,128)(2,1)S(1)}, u32[]{:S(2)}, u32[]{:S(2)}) collective-permute-start(bf16[2,192,1280]{2,1,0:T(8,128)(2,1)S(1)} %slice.46), channel_id=1, source_target_pairs={{0,8},{1,9},{2,10},{3,11},{8,16},{9,17},{10,18},{11,19},{12,4},{13... | collective-permute-start | bytes 2949128 | tf_op jit(solution)/shard_map/ppermute | solution.py:155
  60.8 18.4 %copy-start.12 = (s32[384]{0:T(512)S(1)}, s32[384]{0:T(512)}, u32[]{:S(2)}) copy-start(s32[384]{0:T(512)} %constant.82.clone) | copy-start | bytes 4612
  60.8 22.8 %collective-permute-start.9 = (bf16[2,64,1280]{2,1,0:T(8,128)(2,1)S(1)}, bf16[2,64,1280]{2,1,0:T(8,128)(2,1)S(1)}, u32[]{:S(2)}, u32[]{:S(2)}) collective-permute-start(bf16[2,64,1280]{2,1,0:T(8,128)(2,1)S(1)} %collective-permute-done.8.refs_2_), channel_id=1, source_target_pairs={{0,4},{1,5},{2,6},{3,7},{4,0},{5,1},{6,2},{7,3},{24,28},{25,29},{2... | collective-permute-start | bytes 983048 | tf_op jit(solution)/shard_map/ppermute | solution.py:155
  77.6 9.0 %collective-permute-start.11 = (bf16[2,64,1280]{2,1,0:T(8,128)(2,1)S(1)}, bf16[2,64,1280]{2,1,0:T(8,128)(2,1)S(1)}, u32[]{:S(2)}, u32[]{:S(2)}) collective-permute-start(bf16[2,64,1280]{2,1,0:T(8,128)(2,1)S(1)} %slice.47), channel_id=1, source_target_pairs={{0,8},{1,9},{2,10},{3,11},{8,16},{9,17},{10,18},{11,19},{12,4},{13... | collective-permute-start | bytes 983048 | tf_op jit(solution)/shard_map/ppermute | solution.py:155
  92.5 2.0 %collective-permute-start.13 = (bf16[512,512]{1,0:T(8,128)(2,1)S(1)}, bf16[512,512]{1,0:T(8,128)(2,1)S(1)}, u32[]{:S(2)}, u32[]{:S(2)}) collective-permute-start(bf16[512,512]{1,0:T(8,128)(2,1)S(1)} %last6.1), channel_id=1, source_target_pairs={{0,1},{1,0},{2,3},{3,2},{4,5},{5,4},{6,7},{7,6},{8,9},{9,8},{10,11... | collective-permute-start | bytes 1572872 | tf_op jit(solution)/shard_map/ppermute | solution.py:155
  92.6 3.0 %collective-permute-start.12 = (bf16[512,768]{1,0:T(8,128)(2,1)S(1)}, bf16[512,768]{1,0:T(8,128)(2,1)S(1)}, u32[]{:S(2)}, u32[]{:S(2)}) collective-permute-start(bf16[512,768]{1,0:T(8,128)(2,1)S(1)} %last0.1), channel_id=1, source_target_pairs={{0,1},{1,0},{2,3},{3,2},{4,5},{5,4},{6,7},{7,6},{8,9},{9,8},{10,11... | collective-permute-start | bytes 2359304 | tf_op jit(solution)/shard_map/ppermute | solution.py:155
  101.0 17.6 %collective-permute-start.14 = (bf16[512,640]{1,0:T(8,128)(2,1)S(1)}, bf16[512,640]{1,0:T(8,128)(2,1)S(1)}, u32[]{:S(2)}, u32[]{:S(2)}) collective-permute-start(bf16[512,640]{1,0:T(8,128)(2,1)S(1)} %fusion.9), channel_id=1, source_target_pairs={{0,2},{1,3},{2,0},{3,1},{4,6},{5,7},{6,4},{7,5},{8,10},{9,11},{10,... | collective-permute-start | bytes 1966088 | tf_op jit(solution)/shard_map/ppermute | solution.py:155
  102.5 29.4 %collective-permute-start.15 = (bf16[512,640]{1,0:T(8,128)(2,1)S(1)}, bf16[512,640]{1,0:T(8,128)(2,1)S(1)}, u32[]{:S(2)}, u32[]{:S(2)}) collective-permute-start(bf16[512,640]{1,0:T(8,128)(2,1)S(1)} %fusion.10), channel_id=1, source_target_pairs={{0,2},{1,3},{2,0},{3,1},{4,6},{5,7},{6,4},{7,5},{8,10},{9,11},{10,... | collective-permute-start | bytes 1966088 | tf_op jit(solution)/shard_map/ppermute | solution.py:155
  104.0 29.3 %copy-start.1 = (s32[8,8]{1,0:T(8,128)S(1)}, s32[8,8]{1,0:T(8,128)}, u32[]{:S(2)}) copy-start(s32[8,8]{1,0:T(8,128)} %param.14) | copy-start | bytes 772
  (7 other events, 51.6 us)

commit v7 on v6

--- a/solution.py
+++ b/solution.py
@@ -216,10 +216,10 @@
         x_rows, z_far, z_near, z_two, state, moved = lax.optimization_barrier(
             (x_rows, z_far, z_near, z_two, carry[0], moved)
         )
+        near_b = move(x_rows[:, a:ab], near_of)
+        near_c = move(x_rows[:, ab:], near_of)
         cross_far = move(z_far, twin_if(far_of))
-        cross_near = move(z_near[:, :a], twin_if(near_of))
-        near_bc = move(x_rows[:, a:], near_of)
-        cross_two = move(z_two, lambda t: t ^ 1)
+        cross_two = move(jnp.concatenate([z_near[:, :a], z_two], axis=1), lambda t: t ^ 1)
         z_three = move(z_two, lambda t: {4: 6, 5: 7, 2: 0, 3: 1}.get(t))
         carry = further(
             [x_rows, z_far, z_near, z_two],
@@ -227,19 +227,20 @@
             (state, carry[1]),
             "first",
         )
-        z_three, state = lax.optimization_barrier((z_three, carry[0]))
+        near_b, z_three, state, out_weight, moved = lax.optimization_barrier(
+            (near_b, z_three, carry[0], out_weight, moved)
+        )
+        chain_b = move(near_b, near_of)
         cross_three = move(z_three, lambda t: t ^ 1 if t in ends else None)
-        state, out_weight, moved = lax.optimization_barrier((state, out_weight, moved))
         weights = blocks_of(out_weight, moved)
-        near_bc, state, weights = lax.optimization_barrier((near_bc, state, weights))
-        chain_b = move(near_bc[:, : ab - a], near_of)
+        near_c, state, weights = lax.optimization_barrier((near_c, state, weights))
         carry = further(
-            [near_bc, z_three],
-            [(adjacent, a, near - a), (three, 0, a)],
+            [near_b, near_c, z_three],
+            [(adjacent, a, ab - a), (adjacent, ab, near - ab), (three, 0, a)],
             (state, carry[1]),
             "middle",
         )
-        buffers = [cross_far, cross_near, cross_two, cross_three, chain_b]
+        buffers = [cross_far, cross_two, cross_three, chain_b]
         pieces = [
             (far_cross, 0, ab),
             (adjacent, 0, a),
@@ -261,13 +262,12 @@
         weights = lax.optimization_barrier(blocks_of(out_weight, moved))
 
     bias = bias_of(pieces)
-    cut = 2 * ((head_count + 2) // 4)
+    cut = 2 * (head_count // 4)
     parts = []
     for low, high in ((0, cut), (cut, head_count)):
         (part,) = attend(
             query_vectors, None, buffers, bias, carry, True, low, high, f"last{low}"
         )
-        bias, part = lax.optimization_barrier((bias, part))
         parts.append((part, move(part, same, core), low * HEAD_DIM, high * HEAD_DIM))
 
     def project(index, first, last):
@@ -282,9 +282,11 @@
         return total
 
     half = out_width // 2
-    sent = [project(0, first, first + half).astype(BF16) for first in (0, half)]
-    sent[1], held = lax.optimization_barrier((sent[1], [part[:2] for part in parts]))
-    parts = [kept + part[2:] for kept, part in zip(held, parts)]
+    sent = []
+    for first in (0, half):
+        sent.append(project(0, first, first + half).astype(BF16))
+        _, held = lax.optimization_barrier((sent[-1], [part[:2] for part in parts]))
+        parts = [kept + part[2:] for kept, part in zip(held, parts)]
     arrived = [move(block, same, lambda h: h ^ 2) for block in sent]
     kept, arrived[0] = lax.optimization_barrier((project(1, 0, out_width), arrived[0]))
     return (kept + jnp.concatenate(arrived, axis=1).astype(F32)).astype(BF16)

time: 134 us -> 130 us (0.970)
  starting transfers between devices: 32.6 us -> 26.7 us
    ppermute x16, starting transfers between devices: 32.6 us -> 26.7 us  [move(): return lax.ppermute(array, AXES, route)]
  transfers between devices with their start and end apart: 16 -> 16, of which waited for: 6 -> 7; matrix products, arithmetic and copies ran while one was open for 10% -> 13% of each run, Pallas kernels for 16% -> 20%
where the time goes in v7:
time: 130 us
  waiting for transfers between devices  47.7 us (37%)
  Pallas kernels  27.8 us (21%)
  starting transfers between devices  26.7 us (21%)
  local copies, waits for them, and re-layouts  13.4 us (10%)
  matrix products  9.61 us (7%)
  other arithmetic  3.93 us (3%)
    ppermute x16, waiting for transfers between devices, move(): return lax.ppermute(array, AXES, route)  47.7 us
    ppermute x16, starting transfers between devices, move(): return lax.ppermute(array, AXES, route)  26.7 us
    pallas_call x5, Pallas kernels, attend(): pl.pallas_call(lambda *refs: attend_kernel(*refs, buffers=len(buffers), o...  25.3 us
    unnamed x30, local copies, waits for them, and re-layouts  5.55 us
    dynamic_slice x1, local copies, waits for them, and re-layouts, blocks_of(): lax.dynamic_slice_in_dim(source, number * out_width, out_width, 1)  5.28 us
    dot_general x6, matrix products, project(): jnp.dot(part, weights[index][low:high, first:last], preferred_element_typ...  4.87 us
    dot_general x6, matrix products, project(): jnp.dot(other, weights[index + 2][low:high, first:last], preferred_elemen...  4.74 us
  transfers between devices with their start and end apart: 16, of which 7 were waited for; matrix products, arithmetic and copies ran while one was open for 13% of the time, Pallas kernels for 20%

profile of v7, /device:TPU:2, one launch (start us, length us, event | category | flops | bytes accessed | tf_op | source)
XLA Modules:
  0.0 129.6 jit_solution(13977557184462227622)
XLA Ops:
  0.0 1.4 %copy-done.3 = bf16[512,1280]{1,0:T(8,128)(2,1)S(1)} copy-done((bf16[512,1280]{1,0:T(8,128)(2,1)S(1)}, bf16[512,1280]{1,0:T(8,128)(2,1)}, u32[]{:S(2)}) %copy-start.3) | copy-done | bytes 1310744
  1.4 1.3 %copy-done.5 = bf16[512,1280]{1,0:T(8,128)(2,1)S(1)} copy-done((bf16[512,1280]{1,0:T(8,128)(2,1)S(1)}, bf16[512,1280]{1,0:T(8,128)(2,1)}, u32[]{:S(2)}) %copy-start.5) | copy-done | bytes 1310744
  2.8 2.5 %pack.1 = (bf16[2,256,1280]{2,1,0:T(8,128)(2,1)}, bf16[2,128,1280]{2,1,0:T(8,128)(2,1)}, bf16[2,128,1280]{2,1,0:T(8,128)(2,1)}, bf16[2,64,1280]{2,1,0:T(8,128)(2,1)}) custom-call(bf16[512,1280]{1,0:T(8,128)(2,1)S(1)} %copy-done.3, bf16[512,1280]{1,0:T(8,128)(2,1)S(1)} %copy-done.5), custom_call_target="tpu_custom_call" | custom-call | flops 671088640 | bytes 5242880 | tf_op jit(solution)/shard_map/pack/pallas_call | solution.py:39
  6.7 4.7 %collective-permute-start.2 = (bf16[2,128,1280]{2,1,0:T(8,128)(2,1)}, bf16[2,128,1280]{2,1,0:T(8,128)(2,1)S(1)}, u32[]{:S(2)}, u32[]{:S(2)}) collective-permute-start(bf16[2,128,1280]{2,1,0:T(8,128)(2,1)} %get-tuple-element.44), channel_id=1, source_target_pairs={{4,12},{5,13},{6,14},{7,15},{8,0},{9,1},{10,2},{11,3},{12,20},{13,... | collective-permute-start | bytes 1966088 | tf_op jit(solution)/shard_map/ppermute | solution.py:155
  11.4 3.9 %collective-permute-start.3 = (bf16[2,64,1280]{2,1,0:T(8,128)(2,1)}, bf16[2,64,1280]{2,1,0:T(8,128)(2,1)}, u32[]{:S(2)}, u32[]{:S(2)}) collective-permute-start(bf16[2,64,1280]{2,1,0:T(8,128)(2,1)} %get-tuple-element.45), channel_id=1, source_target_pairs={{0,16},{1,17},{2,18},{3,19},{4,20},{5,21},{6,22},{7,23},{8,24},{9,... | collective-permute-start | bytes 983048 | tf_op jit(solution)/shard_map/ppermute | solution.py:155
  15.3 1.3 %copy-done.6 = bf16[512,1280]{1,0:T(8,128)(2,1)S(1)} copy-done((bf16[512,1280]{1,0:T(8,128)(2,1)S(1)}, bf16[512,1280]{1,0:T(8,128)(2,1)}, u32[]{:S(2)}) %copy-start.6) | copy-done | bytes 1310744
  16.6 6.4 %own.1 = (f32[10,8,512]{2,1,0:T(8,128)S(1)}, f32[10,128,512]{2,1,0:T(8,128)S(1)}) custom-call(bf16[512,1280]{1,0:T(8,128)(2,1)S(1)} %copy-done.2, bf16[512,1280]{1,0:T(8,128)(2,1)S(1)} %copy-done.4, bf16[512,1280]{1,0:T(8,128)(2,1)S(1)} %copy-done.6), custom_call_target="tpu_custom_call" | custom-call | tf_op jit(solution)/shard_map/own/pallas_call | solution.py:123
  23.0 1.4 %copy-done.7 = f32[10,128,512]{2,1,0:T(8,128)} copy-done((f32[10,128,512]{2,1,0:T(8,128)}, f32[10,128,512]{2,1,0:T(8,128)S(1)}, u32[]{:S(2)}) %copy-start.7) | copy-done | bytes 2621464
  26.2 13.8 %collective-permute-done.3.refs_4_ = bf16[2,64,1280]{2,1,0:T(8,128)(2,1)} collective-permute-done((bf16[2,64,1280]{2,1,0:T(8,128)(2,1)}, bf16[2,64,1280]{2,1,0:T(8,128)(2,1)}, u32[]{:S(2)}, u32[]{:S(2)}) %collective-permute-start.3) | collective-permute-done | bytes 327712 | tf_op jit(solution)/shard_map/ppermute | solution.py:155
  42.1 6.7 %collective-permute-start.5 = (bf16[2,128,1280]{2,1,0:T(8,128)(2,1)}, bf16[2,128,1280]{2,1,0:T(8,128)(2,1)S(1)}, u32[]{:S(2)}, u32[]{:S(2)}) collective-permute-start(bf16[2,128,1280]{2,1,0:T(8,128)(2,1)} %collective-permute-done.1.refs_2_), channel_id=1, source_target_pairs={{4,0},{5,1},{6,2},{7,3},{8,12},{9,13},{10,14},{11,15},{12,8},{13,9... | collective-permute-start | bytes 1966088 | tf_op jit(solution)/shard_map/ppermute | solution.py:155
  52.5 1.3 collective-permute-start.11
  54.0 8.7 %first.1 = (f32[10,8,512]{2,1,0:T(8,128)S(1)}, f32[10,128,512]{2,1,0:T(8,128)S(1)}) custom-call(bf16[512,1280]{1,0:T(8,128)(2,1)S(1)} %copy-done.2, bf16[2,256,1280]{2,1,0:T(8,128)(2,1)} %collective-permute-done.refs_1_, bf16[2,128,1280]{2,1,0:T(8,128)(2,1)} %collective-permute-done.1.refs_2_, bf16[2,128,1280]{2,1,0:T(8,128)(2,1)S(1)} %collective-permute-done.2.refs_3_, ...), custom_call_target="tpu_custom_call" | custom-call | flops 1509949440 | bytes 5242880 | tf_op jit(solution)/shard_map/first/pallas_call | solution.py:123
  62.7 5.7 %collective-permute-done.8.refs_3_ = bf16[2,64,1280]{2,1,0:T(8,128)(2,1)S(1)} collective-permute-done((bf16[2,64,1280]{2,1,0:T(8,128)(2,1)}, bf16[2,64,1280]{2,1,0:T(8,128)(2,1)S(1)}, u32[]{:S(2)}, u32[]{:S(2)}) %collective-permute-start.8) | collective-permute-done | bytes 327712 | tf_op jit(solution)/shard_map/ppermute | solution.py:155
  68.4 1.9 %collective-permute-start.9 = (bf16[2,64,1280]{2,1,0:T(8,128)(2,1)S(1)}, bf16[2,64,1280]{2,1,0:T(8,128)(2,1)S(1)}, u32[]{:S(2)}, u32[]{:S(2)}) collective-permute-start(bf16[2,64,1280]{2,1,0:T(8,128)(2,1)S(1)} %collective-permute-done.8.refs_3_), channel_id=1, source_target_pairs={{0,4},{1,5},{2,6},{3,7},{4,0},{5,1},{6,2},{7,3},{24,28},{25,29},{2... | collective-permute-start | bytes 983048 | tf_op jit(solution)/shard_map/ppermute | solution.py:155
  70.3 1.5 %collective-permute-start.10 = (bf16[2,64,1280]{2,1,0:T(8,128)(2,1)S(1)}, bf16[2,64,1280]{2,1,0:T(8,128)(2,1)S(1)}, u32[]{:S(2)}, u32[]{:S(2)}) collective-permute-start(bf16[2,64,1280]{2,1,0:T(8,128)(2,1)S(1)} %collective-permute-done.7.refs_1_), channel_id=1, source_target_pairs={{0,8},{1,9},{2,10},{3,11},{8,16},{9,17},{10,18},{11,19},{12,4},{13... | collective-permute-start | bytes 983048 | tf_op jit(solution)/shard_map/ppermute | solution.py:155
  71.8 5.3 %constant_dynamic-slice_fusion = (bf16[1280,1280]{1,0:T(8,128)(2,1)S(1)}, bf16[1280,1280]{1,0:T(8,128)(2,1)S(1)}, bf16[1280,1280]{1,0:T(8,128)(2,1)S(1)}, bf16[1280,1280]{1,0:T(8,128)(2,1)S(1)}) fusion(bf16[1280,5120]{1,0:T(8,128)(2,1)} %collective-permute-done.4, s32[]{:T(128)S(6)} %select_n.113, s32[]{:T(128)S(6)} %select_n.112, bf16[1280,5120]{1,0:T(8,128)(2,1)} %param.15), kind=kLoop, calls=%fused_computation.49 | loop fusion | bytes 26214408 | tf_op jit(solution)/shard_map/dynamic_slice | solution.py:190
  77.1 5.4 %collective-permute-done.11.refs_2_ = bf16[2,128,1280]{2,1,0:T(8,128)(2,1)S(1)} collective-permute-done((bf16[2,128,1280]{2,1,0:T(8,128)(2,1)S(1)}, bf16[2,128,1280]{2,1,0:T(8,128)(2,1)S(1)}, u32[]{:S(2)}, u32[]{:S(2)}) %collective-permute-start.11) | collective-permute-done | bytes 655392 | tf_op jit(solution)/shard_map/ppermute | solution.py:155
  82.5 4.3 %middle.1 = (f32[10,8,512]{2,1,0:T(8,128)S(1)}, f32[10,128,512]{2,1,0:T(8,128)S(1)}) custom-call(bf16[512,1280]{1,0:T(8,128)(2,1)S(1)} %copy-done.2, bf16[2,64,1280]{2,1,0:T(8,128)(2,1)S(1)} %collective-permute-done.7.refs_1_, bf16[2,128,1280]{2,1,0:T(8,128)(2,1)S(1)} %collective-permute-done.11.refs_2_, ...), custom_call_target="tpu_custom_call" | custom-call | flops 671088640 | bytes 5242880 | tf_op jit(solution)/shard_map/middle/pallas_call | solution.py:123
  87.3 2.4 %last0.1 = bf16[512,512]{1,0:T(8,128)(2,1)S(1)} custom-call(bf16[512,1280]{1,0:T(8,128)(2,1)S(1)} %copy-done.2, bf16[2,128,1280]{2,1,0:T(8,128)(2,1)S(1)} %collective-permute-done.5.refs_1_, bf16[2,128,1280]{2,1,0:T(8,128)(2,1)S(1)} %collective-permute-done.6.refs_2_, bf16[2,64,1280]{2,1,0:T(8,128)(2,1)S(1)} %collective-permute-done.9.refs_3_, ...), custom_call_target="tpu_custom_call" | custom-call | flops 402653184 | bytes 2097152 | tf_op jit(solution)/shard_map/last0/pallas_call | solution.py:123
  89.7 3.5 %last4.1 = bf16[512,768]{1,0:T(8,128)(2,1)S(1)} custom-call(bf16[512,1280]{1,0:T(8,128)(2,1)S(1)} %copy-done.2, bf16[2,128,1280]{2,1,0:T(8,128)(2,1)S(1)} %collective-permute-done.5.refs_1_, bf16[2,128,1280]{2,1,0:T(8,128)(2,1)S(1)} %collective-permute-done.6.refs_2_, bf16[2,64,1280]{2,1,0:T(8,128)(2,1)S(1)} %collective-permute-done.9.refs_3_, ...), custom_call_target="tpu_custom_call" | custom-call | flops 603979776 | bytes 3145728 | tf_op jit(solution)/shard_map/last4/pallas_call | solution.py:123
  97.1 1.5 %collective-permute-start.14 = (bf16[512,640]{1,0:T(8,128)(2,1)S(1)}, bf16[512,640]{1,0:T(8,128)(2,1)S(1)}, u32[]{:S(2)}, u32[]{:S(2)}) collective-permute-start(bf16[512,640]{1,0:T(8,128)(2,1)S(1)} %fusion.10), channel_id=1, source_target_pairs={{0,2},{1,3},{2,0},{3,1},{4,6},{5,7},{6,4},{7,5},{8,10},{9,11},{10,... | collective-permute-start | bytes 1966088 | tf_op jit(solution)/shard_map/ppermute | solution.py:155
  106.2 8.5 %collective-permute-done.14 = bf16[512,640]{1,0:T(8,128)(2,1)S(1)} collective-permute-done((bf16[512,640]{1,0:T(8,128)(2,1)S(1)}, bf16[512,640]{1,0:T(8,128)(2,1)S(1)}, u32[]{:S(2)}, u32[]{:S(2)}) %collective-permute-start.14) | collective-permute-done | bytes 655392 | tf_op jit(solution)/shard_map/ppermute | solution.py:155
  114.7 13.5 %collective-permute-done.15 = bf16[512,640]{1,0:T(8,128)(2,1)S(1)} collective-permute-done((bf16[512,640]{1,0:T(8,128)(2,1)S(1)}, bf16[512,640]{1,0:T(8,128)(2,1)S(1)}, u32[]{:S(2)}, u32[]{:S(2)}) %collective-permute-start.15) | collective-permute-done | bytes 655392 | tf_op jit(solution)/shard_map/ppermute | solution.py:155
  128.2 1.4 %add_convert_fusion = bf16[512,1280]{1,0:T(8,128)(2,1)} fusion(f32[512,1280]{1,0:T(8,128)S(1)} %fusion.1, bf16[512,640]{1,0:T(8,128)(2,1)S(1)} %collective-permute-done.15, bf16[512,640]{1,0:T(8,128)(2,1)S(1)} %collective-permute-done.14), kind=kLoop, calls=%fused_computation.3 | loop fusion | flops 3932160 | bytes 5242880 | tf_op jit(solution)/shard_map/convert_element_type | solution.py:292
  (84 shorter events, 21.0 us)
Async XLA Ops:
  0.0 24.6 %copy-start = (s32[8,8]{1,0:T(8,128)S(1)}, s32[8,8]{1,0:T(8,128)}, u32[]{:S(2)}) copy-start(s32[8,8]{1,0:T(8,128)} %param.14) | copy-start | bytes 772
  0.0 40.0 %collective-permute-start.4 = (bf16[1280,5120]{1,0:T(8,128)(2,1)}, bf16[1280,5120]{1,0:T(8,128)(2,1)}, u32[]{:S(2)}, u32[]{:S(2)}) collective-permute-start(bf16[1280,5120]{1,0:T(8,128)(2,1)} %param.15), channel_id=1, source_target_pairs={{0,1},{1,0},{2,3},{3,2},{4,5},{5,4},{6,7},{7,6},{8,9},{9,8},{10,11... | collective-permute-start | bytes 39321608 | tf_op jit(solution)/shard_map/ppermute | solution.py:155
  5.3 20.7 %copy-start.13 = (s32[256]{0:T(256)S(1)}, s32[256]{0:T(256)}, u32[]{:S(2)}) copy-start(s32[256]{0:T(256)} %constant.80.clone) | copy-start | bytes 3076
  5.3 20.7 %copy-start.10 = (pred[5,384]{1,0:T(8,128)(4,1)S(1)}, pred[5,384]{1,0:T(8,128)(4,1)}, u32[]{:S(2)}) copy-start(pred[5,384]{1,0:T(8,128)(4,1)} %constant.81.clone) | copy-start | bytes 5764
  5.3 20.8 %copy-start.12 = (s32[384]{0:T(512)S(1)}, s32[384]{0:T(512)}, u32[]{:S(2)}) copy-start(s32[384]{0:T(512)} %constant.82.clone) | copy-start | bytes 4612
  5.3 20.8 %copy-start.11 = (pred[4,576]{1,0:T(4,128)(4,1)S(1)}, pred[4,576]{1,0:T(4,128)(4,1)}, u32[]{:S(2)}) copy-start(pred[4,576]{1,0:T(4,128)(4,1)} %constant.77.clone) | copy-start | bytes 6916
  5.3 20.8 %copy-start.9 = (s32[576]{0:T(1024)S(1)}, s32[576]{0:T(1024)}, u32[]{:S(2)}) copy-start(s32[576]{0:T(1024)} %constant.78.clone) | copy-start | bytes 6916
  5.3 34.7 %collective-permute-start = (bf16[2,256,1280]{2,1,0:T(8,128)(2,1)}, bf16[2,256,1280]{2,1,0:T(8,128)(2,1)}, u32[]{:S(2)}, u32[]{:S(2)}) collective-permute-start(bf16[2,256,1280]{2,1,0:T(8,128)(2,1)} %get-tuple-element.42), channel_id=1, source_target_pairs={{0,4},{1,5},{2,6},{3,7},{4,0},{5,1},{6,2},{7,3},{8,12},{9,13},{10,... | collective-permute-start | bytes 3932168 | tf_op jit(solution)/shard_map/ppermute | solution.py:155
  5.4 34.6 %collective-permute-start.1 = (bf16[2,128,1280]{2,1,0:T(8,128)(2,1)}, bf16[2,128,1280]{2,1,0:T(8,128)(2,1)}, u32[]{:S(2)}, u32[]{:S(2)}) collective-permute-start(bf16[2,128,1280]{2,1,0:T(8,128)(2,1)} %get-tuple-element.43), channel_id=1, source_target_pairs={{0,8},{1,9},{2,10},{3,11},{8,16},{9,17},{10,18},{11,19},{12,4},{13... | collective-permute-start | bytes 1966088 | tf_op jit(solution)/shard_map/ppermute | solution.py:155
  6.7 33.3 %collective-permute-start.2 = (bf16[2,128,1280]{2,1,0:T(8,128)(2,1)}, bf16[2,128,1280]{2,1,0:T(8,128)(2,1)S(1)}, u32[]{:S(2)}, u32[]{:S(2)}) collective-permute-start(bf16[2,128,1280]{2,1,0:T(8,128)(2,1)} %get-tuple-element.44), channel_id=1, source_target_pairs={{4,12},{5,13},{6,14},{7,15},{8,0},{9,1},{10,2},{11,3},{12,20},{13,... | collective-permute-start | bytes 1966088 | tf_op jit(solution)/shard_map/ppermute | solution.py:155
  11.4 28.6 %collective-permute-start.3 = (bf16[2,64,1280]{2,1,0:T(8,128)(2,1)}, bf16[2,64,1280]{2,1,0:T(8,128)(2,1)}, u32[]{:S(2)}, u32[]{:S(2)}) collective-permute-start(bf16[2,64,1280]{2,1,0:T(8,128)(2,1)} %get-tuple-element.45), channel_id=1, source_target_pairs={{0,16},{1,17},{2,18},{3,19},{4,20},{5,21},{6,22},{7,23},{8,24},{9,... | collective-permute-start | bytes 983048 | tf_op jit(solution)/shard_map/ppermute | solution.py:155
  24.5 29.4 %copy-start.8 = (f32[10,128,512]{2,1,0:T(8,128)S(1)}, f32[10,128,512]{2,1,0:T(8,128)}, u32[]{:S(2)}) copy-start(f32[10,128,512]{2,1,0:T(8,128)} %copy-done.7) | copy-start | bytes 7864324
  42.1 45.0 %collective-permute-start.5 = (bf16[2,128,1280]{2,1,0:T(8,128)(2,1)}, bf16[2,128,1280]{2,1,0:T(8,128)(2,1)S(1)}, u32[]{:S(2)}, u32[]{:S(2)}) collective-permute-start(bf16[2,128,1280]{2,1,0:T(8,128)(2,1)} %collective-permute-done.1.refs_2_), channel_id=1, source_target_pairs={{4,0},{5,1},{6,2},{7,3},{8,12},{9,13},{10,14},{11,15},{12,8},{13,9... | collective-permute-start | bytes 1966088 | tf_op jit(solution)/shard_map/ppermute | solution.py:155
  48.8 13.9 %collective-permute-start.7 = (bf16[2,64,1280]{2,1,0:T(8,128)(2,1)S(1)}, bf16[2,64,1280]{2,1,0:T(8,128)(2,1)S(1)}, u32[]{:S(2)}, u32[]{:S(2)}) collective-permute-start(bf16[2,64,1280]{2,1,0:T(8,128)(2,1)S(1)} %slice.46), channel_id=1, source_target_pairs={{0,8},{1,9},{2,10},{3,11},{8,16},{9,17},{10,18},{11,19},{12,4},{13... | collective-permute-start | bytes 983048 | tf_op jit(solution)/shard_map/ppermute | solution.py:155
  50.1 18.3 %collective-permute-start.8 = (bf16[2,64,1280]{2,1,0:T(8,128)(2,1)}, bf16[2,64,1280]{2,1,0:T(8,128)(2,1)S(1)}, u32[]{:S(2)}, u32[]{:S(2)}) collective-permute-start(bf16[2,64,1280]{2,1,0:T(8,128)(2,1)} %collective-permute-done.3.refs_4_), channel_id=1, source_target_pairs={{8,0},{9,1},{10,2},{11,3},{12,4},{13,5},{14,6},{15,7},{16,24},{17,... | collective-permute-start | bytes 983048 | tf_op jit(solution)/shard_map/ppermute | solution.py:155
  52.4 34.7 %collective-permute-start.6 = (bf16[2,128,1280]{2,1,0:T(8,128)(2,1)S(1)}, bf16[2,128,1280]{2,1,0:T(8,128)(2,1)S(1)}, u32[]{:S(2)}, u32[]{:S(2)}) collective-permute-start(bf16[2,128,1280]{2,1,0:T(8,128)(2,1)S(1)} %pad_maximum_fusion), channel_id=1, source_target_pairs={{0,4},{1,5},{2,6},{3,7},{4,0},{5,1},{6,2},{7,3},{8,12},{9,13},{10,... | collective-permute-start | bytes 1966088 | tf_op jit(solution)/shard_map/ppermute | solution.py:155
  52.5 29.9 %collective-permute-start.11 = (bf16[2,128,1280]{2,1,0:T(8,128)(2,1)S(1)}, bf16[2,128,1280]{2,1,0:T(8,128)(2,1)S(1)}, u32[]{:S(2)}, u32[]{:S(2)}) collective-permute-start(bf16[2,128,1280]{2,1,0:T(8,128)(2,1)S(1)} %slice.47), channel_id=1, source_target_pairs={{0,8},{1,9},{2,10},{3,11},{8,16},{9,17},{10,18},{11,19},{12,4},{13... | collective-permute-start | bytes 1966088 | tf_op jit(solution)/shard_map/ppermute | solution.py:155
  68.4 18.4 %collective-permute-start.9 = (bf16[2,64,1280]{2,1,0:T(8,128)(2,1)S(1)}, bf16[2,64,1280]{2,1,0:T(8,128)(2,1)S(1)}, u32[]{:S(2)}, u32[]{:S(2)}) collective-permute-start(bf16[2,64,1280]{2,1,0:T(8,128)(2,1)S(1)} %collective-permute-done.8.refs_3_), channel_id=1, source_target_pairs={{0,4},{1,5},{2,6},{3,7},{4,0},{5,1},{6,2},{7,3},{24,28},{25,29},{2... | collective-permute-start | bytes 983048 | tf_op jit(solution)/shard_map/ppermute | solution.py:155
  70.3 16.8 %collective-permute-start.10 = (bf16[2,64,1280]{2,1,0:T(8,128)(2,1)S(1)}, bf16[2,64,1280]{2,1,0:T(8,128)(2,1)S(1)}, u32[]{:S(2)}, u32[]{:S(2)}) collective-permute-start(bf16[2,64,1280]{2,1,0:T(8,128)(2,1)S(1)} %collective-permute-done.7.refs_1_), channel_id=1, source_target_pairs={{0,8},{1,9},{2,10},{3,11},{8,16},{9,17},{10,18},{11,19},{12,4},{13... | collective-permute-start | bytes 983048 | tf_op jit(solution)/shard_map/ppermute | solution.py:155
  89.6 4.9 %collective-permute-start.12 = (bf16[512,512]{1,0:T(8,128)(2,1)S(1)}, bf16[512,512]{1,0:T(8,128)(2,1)S(1)}, u32[]{:S(2)}, u32[]{:S(2)}) collective-permute-start(bf16[512,512]{1,0:T(8,128)(2,1)S(1)} %last0.1), channel_id=1, source_target_pairs={{0,1},{1,0},{2,3},{3,2},{4,5},{5,4},{6,7},{7,6},{8,9},{9,8},{10,11... | collective-permute-start | bytes 1572872 | tf_op jit(solution)/shard_map/ppermute | solution.py:155
  93.2 2.5 %collective-permute-start.13 = (bf16[512,768]{1,0:T(8,128)(2,1)S(1)}, bf16[512,768]{1,0:T(8,128)(2,1)S(1)}, u32[]{:S(2)}, u32[]{:S(2)}) collective-permute-start(bf16[512,768]{1,0:T(8,128)(2,1)S(1)} %last4.1), channel_id=1, source_target_pairs={{0,1},{1,0},{2,3},{3,2},{4,5},{5,4},{6,7},{7,6},{8,9},{9,8},{10,11... | collective-permute-start | bytes 2359304 | tf_op jit(solution)/shard_map/ppermute | solution.py:155
  97.1 17.6 %collective-permute-start.14 = (bf16[512,640]{1,0:T(8,128)(2,1)S(1)}, bf16[512,640]{1,0:T(8,128)(2,1)S(1)}, u32[]{:S(2)}, u32[]{:S(2)}) collective-permute-start(bf16[512,640]{1,0:T(8,128)(2,1)S(1)} %fusion.10), channel_id=1, source_target_pairs={{0,2},{1,3},{2,0},{3,1},{4,6},{5,7},{6,4},{7,5},{8,10},{9,11},{10,... | collective-permute-start | bytes 1966088 | tf_op jit(solution)/shard_map/ppermute | solution.py:155
  101.3 26.9 %collective-permute-start.15 = (bf16[512,640]{1,0:T(8,128)(2,1)S(1)}, bf16[512,640]{1,0:T(8,128)(2,1)S(1)}, u32[]{:S(2)}, u32[]{:S(2)}) collective-permute-start(bf16[512,640]{1,0:T(8,128)(2,1)S(1)} %fusion.11), channel_id=1, source_target_pairs={{0,2},{1,3},{2,0},{3,1},{4,6},{5,7},{6,4},{7,5},{8,10},{9,11},{10,... | collective-permute-start | bytes 1966088 | tf_op jit(solution)/shard_map/ppermute | solution.py:155
  105.2 24.3 %copy-start.1 = (s32[8,8]{1,0:T(8,128)S(1)}, s32[8,8]{1,0:T(8,128)}, u32[]{:S(2)}) copy-start(s32[8,8]{1,0:T(8,128)} %param.14) | copy-start | bytes 772
  (7 other events, 53.9 us)

commit v8 on v7

--- a/solution.py
+++ b/solution.py
@@ -213,8 +213,17 @@
         z_near = move(sent_ba, far_of)
         z_two = move(sent_a, lambda t: t ^ 4)
         carry = attend(query_vectors, own_pair, [], None, None, False, 0, head_count, "own")
-        x_rows, z_far, z_near, z_two, state, moved = lax.optimization_barrier(
-            (x_rows, z_far, z_near, z_two, carry[0], moved)
+        z_far, z_near, state = lax.optimization_barrier((z_far, z_near, carry[0]))
+        carry = further(
+            [z_far, z_near],
+            [(far_block, 0, ab), (near_block, 0, ab)],
+            (state, carry[1]),
+            "early",
+        )
+        state, out_weight, moved = lax.optimization_barrier((carry[0], out_weight, moved))
+        weights = blocks_of(out_weight, moved)
+        x_rows, z_near, z_two, state, weights = lax.optimization_barrier(
+            (x_rows, z_near, z_two, state, weights)
         )
         near_b = move(x_rows[:, a:ab], near_of)
         near_c = move(x_rows[:, ab:], near_of)
@@ -222,27 +231,27 @@
         cross_two = move(jnp.concatenate([z_near[:, :a], z_two], axis=1), lambda t: t ^ 1)
         z_three = move(z_two, lambda t: {4: 6, 5: 7, 2: 0, 3: 1}.get(t))
         carry = further(
-            [x_rows, z_far, z_near, z_two],
-            [(partner, 0, near), (far_block, 0, ab), (near_block, 0, ab), (two, 0, a)],
+            [x_rows, z_two],
+            [(partner, 0, near), (two, 0, a)],
             (state, carry[1]),
             "first",
         )
-        near_b, z_three, state, out_weight, moved = lax.optimization_barrier(
-            (near_b, z_three, carry[0], out_weight, moved)
-        )
+        near_b, z_three, state = lax.optimization_barrier((near_b, z_three, carry[0]))
         chain_b = move(near_b, near_of)
         cross_three = move(z_three, lambda t: t ^ 1 if t in ends else None)
-        weights = blocks_of(out_weight, moved)
-        near_c, state, weights = lax.optimization_barrier((near_c, state, weights))
         carry = further(
-            [near_b, near_c, z_three],
-            [(adjacent, a, ab - a), (adjacent, ab, near - ab), (three, 0, a)],
+            [near_b, near_c, z_three, cross_far],
+            [
+                (adjacent, a, ab - a),
+                (adjacent, ab, near - ab),
+                (three, 0, a),
+                (far_cross, 0, ab),
+            ],
             (state, carry[1]),
             "middle",
         )
-        buffers = [cross_far, cross_two, cross_three, chain_b]
+        buffers = [cross_two, cross_three, chain_b]
         pieces = [
-            (far_cross, 0, ab),
             (adjacent, 0, a),
             (two ^ 1, 0, a),
             (jnp.where(at_end, opposite ^ 1, -1), 0, a),

time: 130 us -> 130 us (level)
  waiting for transfers between devices: 47.7 us -> 31.5 us
  starting transfers between devices: 26.7 us -> 36.2 us
  local copies, waits for them, and re-layouts: 13.4 us -> 16.6 us
  Pallas kernels: 27.8 us -> 30.8 us
    ppermute x16, waiting for transfers between devices: 47.7 us -> 31.5 us  [move(): return lax.ppermute(array, AXES, route)]
    ppermute x16, starting transfers between devices: 26.7 us -> 36.2 us  [move(): return lax.ppermute(array, AXES, route)]
    pallas_call x5 -> x6, Pallas kernels: 25.3 us -> 28.3 us  [attend(): pl.pallas_call(lambda *refs: attend_kernel(*refs, buffers=len(buffers), o...]
    unnamed x30 -> x34, local copies, waits for them, and re-layouts: 5.55 us -> 7.3 us
    dynamic_slice x1 -> x2, local copies, waits for them, and re-layouts: 5.28 us -> 6.72 us  [blocks_of(): lax.dynamic_slice_in_dim(source, number * out_width, out_width, 1)]
  transfers between devices with their start and end apart: 16 -> 16, of which waited for: 7 -> 5; matrix products, arithmetic and copies ran while one was open for 13% -> 16% of each run, Pallas kernels for 20% -> 22%
where the time goes in v8:
time: 130 us; the launch traced here: 129 us
  starting transfers between devices  36.2 us (28%)
  waiting for transfers between devices  31.5 us (24%)
  Pallas kernels  30.8 us (24%)
  local copies, waits for them, and re-layouts  16.6 us (13%)
  matrix products  9.8 us (8%)
  other arithmetic  4.09 us (3%)
    ppermute x16, starting transfers between devices, move(): return lax.ppermute(array, AXES, route)  36.2 us
    ppermute x16, waiting for transfers between devices, move(): return lax.ppermute(array, AXES, route)  31.5 us
    pallas_call x6, Pallas kernels, attend(): pl.pallas_call(lambda *refs: attend_kernel(*refs, buffers=len(buffers), o...  28.3 us
    unnamed x34, local copies, waits for them, and re-layouts  7.3 us
    dynamic_slice x2, local copies, waits for them, and re-layouts, blocks_of(): lax.dynamic_slice_in_dim(source, number * out_width, out_width, 1)  6.72 us
    dot_general x6, matrix products, project(): jnp.dot(part, weights[index][low:high, first:last], preferred_element_typ...  5.05 us
    dot_general x6, matrix products, project(): jnp.dot(other, weights[index + 2][low:high, first:last], preferred_elemen...  4.75 us
  transfers between devices with their start and end apart: 16, of which 5 were waited for; matrix products, arithmetic and copies ran while one was open for 16% of the time, Pallas kernels for 22%

profile of v8, /device:TPU:2, one launch (start us, length us, event | category | flops | bytes accessed | tf_op | source)
XLA Modules:
  0.0 129.4 jit_solution(9114239831393615132)
XLA Ops:
  0.0 1.4 %copy-done.3 = bf16[512,1280]{1,0:T(8,128)(2,1)S(1)} copy-done((bf16[512,1280]{1,0:T(8,128)(2,1)S(1)}, bf16[512,1280]{1,0:T(8,128)(2,1)}, u32[]{:S(2)}) %copy-start.3) | copy-done | bytes 1310744
  2.8 2.5 %pack.1 = (bf16[2,256,1280]{2,1,0:T(8,128)(2,1)}, bf16[2,128,1280]{2,1,0:T(8,128)(2,1)}, bf16[2,128,1280]{2,1,0:T(8,128)(2,1)}, bf16[2,64,1280]{2,1,0:T(8,128)(2,1)}) custom-call(bf16[512,1280]{1,0:T(8,128)(2,1)S(1)} %copy-done.3, bf16[512,1280]{1,0:T(8,128)(2,1)S(1)} %copy-done.5), custom_call_target="tpu_custom_call" | custom-call | flops 671088640 | bytes 5242880 | tf_op jit(solution)/shard_map/pack/pallas_call | solution.py:39
  5.3 1.4 %collective-permute-start.1 = (bf16[2,128,1280]{2,1,0:T(8,128)(2,1)}, bf16[2,128,1280]{2,1,0:T(8,128)(2,1)}, u32[]{:S(2)}, u32[]{:S(2)}) collective-permute-start(bf16[2,128,1280]{2,1,0:T(8,128)(2,1)} %get-tuple-element.45), channel_id=1, source_target_pairs={{0,8},{1,9},{2,10},{3,11},{8,16},{9,17},{10,18},{11,19},{12,4},{13... | collective-permute-start | bytes 1966088 | tf_op jit(solution)/shard_map/ppermute | solution.py:155
  6.7 4.6 %collective-permute-start.2 = (bf16[2,128,1280]{2,1,0:T(8,128)(2,1)}, bf16[2,128,1280]{2,1,0:T(8,128)(2,1)S(1)}, u32[]{:S(2)}, u32[]{:S(2)}) collective-permute-start(bf16[2,128,1280]{2,1,0:T(8,128)(2,1)} %get-tuple-element.46), channel_id=1, source_target_pairs={{4,12},{5,13},{6,14},{7,15},{8,0},{9,1},{10,2},{11,3},{12,20},{13,... | collective-permute-start | bytes 1966088 | tf_op jit(solution)/shard_map/ppermute | solution.py:155
  11.7 3.2 %collective-permute-start.3 = (bf16[2,64,1280]{2,1,0:T(8,128)(2,1)}, bf16[2,64,1280]{2,1,0:T(8,128)(2,1)}, u32[]{:S(2)}, u32[]{:S(2)}) collective-permute-start(bf16[2,64,1280]{2,1,0:T(8,128)(2,1)} %get-tuple-element.49), channel_id=1, source_target_pairs={{0,16},{1,17},{2,18},{3,19},{4,20},{5,21},{6,22},{7,23},{8,24},{9,... | collective-permute-start | bytes 983048 | tf_op jit(solution)/shard_map/ppermute | solution.py:155
  16.2 6.4 %own.1 = (f32[10,8,512]{2,1,0:T(8,128)S(1)}, f32[10,128,512]{2,1,0:T(8,128)S(1)}) custom-call(bf16[512,1280]{1,0:T(8,128)(2,1)S(1)} %copy-done.2, bf16[512,1280]{1,0:T(8,128)(2,1)S(1)} %copy-done.4, bf16[512,1280]{1,0:T(8,128)(2,1)S(1)} %copy-done.6), custom_call_target="tpu_custom_call" | custom-call | tf_op jit(solution)/shard_map/own/pallas_call | solution.py:123
  22.6 1.5 %copy-done.7 = f32[10,128,512]{2,1,0:T(8,128)} copy-done((f32[10,128,512]{2,1,0:T(8,128)}, f32[10,128,512]{2,1,0:T(8,128)S(1)}, u32[]{:S(2)}) %copy-start.7) | copy-done | bytes 2621464
  26.7 5.0 %collective-permute-start.11 = (bf16[2,128,1280]{2,1,0:T(8,128)(2,1)}, bf16[2,128,1280]{2,1,0:T(8,128)(2,1)S(1)}, u32[]{:S(2)}, u32[]{:S(2)}) collective-permute-start(bf16[2,128,1280]{2,1,0:T(8,128)(2,1)} %collective-permute-done.1.refs_1_), channel_id=1, source_target_pairs={{4,0},{5,1},{6,2},{7,3},{8,12},{9,13},{10,14},{11,15},{12,8},{13,9... | collective-permute-start | bytes 1966088 | tf_op jit(solution)/shard_map/ppermute | solution.py:155
  31.9 1.7 %copy-done.8 = f32[10,128,512]{2,1,0:T(8,128)S(1)} copy-done((f32[10,128,512]{2,1,0:T(8,128)S(1)}, f32[10,128,512]{2,1,0:T(8,128)}, u32[]{:S(2)}) %copy-start.8) | copy-done | bytes 2621464
  33.6 5.4 %early.1 = (f32[10,8,512]{2,1,0:T(8,128)S(1)}, f32[10,128,512]{2,1,0:T(8,128)S(1)}) custom-call(bf16[512,1280]{1,0:T(8,128)(2,1)S(1)} %copy-done.2, bf16[2,128,1280]{2,1,0:T(8,128)(2,1)} %collective-permute-done.1.refs_1_, bf16[2,128,1280]{2,1,0:T(8,128)(2,1)S(1)} %collective-permute-done.2.refs_2_, f32[256,128]{1,0:T(8,128)S(1)} %broadcast_in_dim.166.refs_3_, ...), custom_call_target="tpu_custom_call" | custom-call | flops 671088640 | bytes 5242880 | tf_op jit(solution)/shard_map/early/pallas_call | solution.py:123
  39.0 3.4 %constant_dynamic-slice_fusion = (bf16[1280,1280]{1,0:T(8,128)(2,1)S(1)}, bf16[1280,1280]{1,0:T(8,128)(2,1)S(1)}) fusion(bf16[1280,5120]{1,0:T(8,128)(2,1)} %collective-permute-done.4, s32[]{:T(128)S(6)} %select_n.123, s32[]{:T(128)S(6)} %select_n.122), kind=kLoop, calls=%fused_computation.48 | loop fusion | bytes 13107208 | tf_op jit(solution)/shard_map/dynamic_slice | solution.py:190
  42.3 3.4 %constant_dynamic-slice_fusion.2 = (bf16[1280,1280]{1,0:T(8,128)(2,1)S(1)}, bf16[1280,1280]{1,0:T(8,128)(2,1)S(1)}) fusion(bf16[1280,5120]{1,0:T(8,128)(2,1)} %param.17, s32[]{:T(128)S(6)} %select_n.123, s32[]{:T(128)S(6)} %select_n.122), kind=kLoop, calls=%fused_computation.50 | loop fusion | bytes 13107208 | tf_op jit(solution)/shard_map/dynamic_slice | solution.py:190
  52.8 11.5 %collective-permute-start.5 = (bf16[2,128,1280]{2,1,0:T(8,128)(2,1)S(1)}, bf16[2,128,1280]{2,1,0:T(8,128)(2,1)S(1)}, u32[]{:S(2)}, u32[]{:S(2)}) collective-permute-start(bf16[2,128,1280]{2,1,0:T(8,128)(2,1)S(1)} %pad_maximum_fusion), channel_id=1, source_target_pairs={{0,4},{1,5},{2,6},{3,7},{4,0},{5,1},{6,2},{7,3},{8,12},{9,13},{10,... | collective-permute-start | bytes 1966088 | tf_op jit(solution)/shard_map/ppermute | solution.py:155
  64.5 6.4 %first.1 = (f32[10,8,512]{2,1,0:T(8,128)S(1)}, f32[10,128,512]{2,1,0:T(8,128)S(1)}) custom-call(bf16[512,1280]{1,0:T(8,128)(2,1)S(1)} %copy-done.2, bf16[2,256,1280]{2,1,0:T(8,128)(2,1)} %collective-permute-done.refs_1_, bf16[2,64,1280]{2,1,0:T(8,128)(2,1)} %collective-permute-done.3.refs_2_, f32[320,128]{1,0:T(8,128)S(1)} %broadcast_in_dim.171.refs_3_, ...), custom_call_target="tpu_custom_call" | custom-call | flops 838860800 | bytes 5242880 | tf_op jit(solution)/shard_map/first/pallas_call | solution.py:123
  70.9 1.9 %collective-permute-start.8 = (bf16[2,64,1280]{2,1,0:T(8,128)(2,1)S(1)}, bf16[2,64,1280]{2,1,0:T(8,128)(2,1)S(1)}, u32[]{:S(2)}, u32[]{:S(2)}) collective-permute-start(bf16[2,64,1280]{2,1,0:T(8,128)(2,1)S(1)} %collective-permute-done.7.refs_3_), channel_id=1, source_target_pairs={{0,4},{1,5},{2,6},{3,7},{4,0},{5,1},{6,2},{7,3},{24,28},{25,29},{2... | collective-permute-start | bytes 983048 | tf_op jit(solution)/shard_map/ppermute | solution.py:155
  72.9 1.5 %collective-permute-start.9 = (bf16[2,64,1280]{2,1,0:T(8,128)(2,1)S(1)}, bf16[2,64,1280]{2,1,0:T(8,128)(2,1)S(1)}, u32[]{:S(2)}, u32[]{:S(2)}) collective-permute-start(bf16[2,64,1280]{2,1,0:T(8,128)(2,1)S(1)} %collective-permute-done.6.refs_1_), channel_id=1, source_target_pairs={{0,8},{1,9},{2,10},{3,11},{8,16},{9,17},{10,18},{11,19},{12,4},{13... | collective-permute-start | bytes 983048 | tf_op jit(solution)/shard_map/ppermute | solution.py:155
  74.5 8.0 %collective-permute-done.10.refs_2_ = bf16[2,128,1280]{2,1,0:T(8,128)(2,1)S(1)} collective-permute-done((bf16[2,128,1280]{2,1,0:T(8,128)(2,1)S(1)}, bf16[2,128,1280]{2,1,0:T(8,128)(2,1)S(1)}, u32[]{:S(2)}, u32[]{:S(2)}) %collective-permute-start.10) | collective-permute-done | bytes 655392 | tf_op jit(solution)/shard_map/ppermute | solution.py:155
  82.6 5.5 %middle.1 = (f32[10,8,512]{2,1,0:T(8,128)S(1)}, f32[10,128,512]{2,1,0:T(8,128)S(1)}) custom-call(bf16[512,1280]{1,0:T(8,128)(2,1)S(1)} %copy-done.2, bf16[2,64,1280]{2,1,0:T(8,128)(2,1)S(1)} %collective-permute-done.6.refs_1_, bf16[2,128,1280]{2,1,0:T(8,128)(2,1)S(1)} %collective-permute-done.10.refs_2_, ...), custom_call_target="tpu_custom_call" | custom-call | flops 1006632960 | bytes 5242880 | tf_op jit(solution)/shard_map/middle/pallas_call | solution.py:123
  88.2 1.9 %last0.1 = bf16[512,512]{1,0:T(8,128)(2,1)S(1)} custom-call(bf16[512,1280]{1,0:T(8,128)(2,1)S(1)} %copy-done.2, bf16[2,128,1280]{2,1,0:T(8,128)(2,1)S(1)} %collective-permute-done.5.refs_1_, bf16[2,64,1280]{2,1,0:T(8,128)(2,1)S(1)} %collective-permute-done.8.refs_2_, bf16[2,64,1280]{2,1,0:T(8,128)(2,1)S(1)} %collective-permute-done.9.refs_3_, ...), custom_call_target="tpu_custom_call" | custom-call | flops 268435456 | bytes 2097152 | tf_op jit(solution)/shard_map/last0/pallas_call | solution.py:123
  90.2 2.8 %last4.1 = bf16[512,768]{1,0:T(8,128)(2,1)S(1)} custom-call(bf16[512,1280]{1,0:T(8,128)(2,1)S(1)} %copy-done.2, bf16[2,128,1280]{2,1,0:T(8,128)(2,1)S(1)} %collective-permute-done.5.refs_1_, bf16[2,64,1280]{2,1,0:T(8,128)(2,1)S(1)} %collective-permute-done.8.refs_2_, bf16[2,64,1280]{2,1,0:T(8,128)(2,1)S(1)} %collective-permute-done.9.refs_3_, ...), custom_call_target="tpu_custom_call" | custom-call | flops 402653184 | bytes 3145728 | tf_op jit(solution)/shard_map/last4/pallas_call | solution.py:123
  96.9 1.6 %collective-permute-start.14 = (bf16[512,640]{1,0:T(8,128)(2,1)S(1)}, bf16[512,640]{1,0:T(8,128)(2,1)S(1)}, u32[]{:S(2)}, u32[]{:S(2)}) collective-permute-start(bf16[512,640]{1,0:T(8,128)(2,1)S(1)} %fusion.10), channel_id=1, source_target_pairs={{0,2},{1,3},{2,0},{3,1},{4,6},{5,7},{6,4},{7,5},{8,10},{9,11},{10,... | collective-permute-start | bytes 1966088 | tf_op jit(solution)/shard_map/ppermute | solution.py:155
  106.1 8.4 %collective-permute-done.14 = bf16[512,640]{1,0:T(8,128)(2,1)S(1)} collective-permute-done((bf16[512,640]{1,0:T(8,128)(2,1)S(1)}, bf16[512,640]{1,0:T(8,128)(2,1)S(1)}, u32[]{:S(2)}, u32[]{:S(2)}) %collective-permute-start.14) | collective-permute-done | bytes 655392 | tf_op jit(solution)/shard_map/ppermute | solution.py:155
  114.5 13.5 %collective-permute-done.15 = bf16[512,640]{1,0:T(8,128)(2,1)S(1)} collective-permute-done((bf16[512,640]{1,0:T(8,128)(2,1)S(1)}, bf16[512,640]{1,0:T(8,128)(2,1)S(1)}, u32[]{:S(2)}, u32[]{:S(2)}) %collective-permute-start.15) | collective-permute-done | bytes 655392 | tf_op jit(solution)/shard_map/ppermute | solution.py:155
  128.0 1.4 %add_convert_fusion = bf16[512,1280]{1,0:T(8,128)(2,1)} fusion(f32[512,1280]{1,0:T(8,128)S(1)} %fusion.1, bf16[512,640]{1,0:T(8,128)(2,1)S(1)} %collective-permute-done.15, bf16[512,640]{1,0:T(8,128)(2,1)S(1)} %collective-permute-done.14), kind=kLoop, calls=%fused_computation.3 | loop fusion | flops 3932160 | bytes 5242880 | tf_op jit(solution)/shard_map/convert_element_type | solution.py:301
  (93 shorter events, 24.7 us)
Async XLA Ops:
  0.0 24.1 %copy-start = (s32[8,8]{1,0:T(8,128)S(1)}, s32[8,8]{1,0:T(8,128)}, u32[]{:S(2)}) copy-start(s32[8,8]{1,0:T(8,128)} %param.16) | copy-start | bytes 772
  0.0 39.0 %collective-permute-start.4 = (bf16[1280,5120]{1,0:T(8,128)(2,1)}, bf16[1280,5120]{1,0:T(8,128)(2,1)}, u32[]{:S(2)}, u32[]{:S(2)}) collective-permute-start(bf16[1280,5120]{1,0:T(8,128)(2,1)} %param.17), channel_id=1, source_target_pairs={{0,1},{1,0},{2,3},{3,2},{4,5},{5,4},{6,7},{7,6},{8,9},{9,8},{10,11... | collective-permute-start | bytes 39321608 | tf_op jit(solution)/shard_map/ppermute | solution.py:155
  5.3 19.9 %copy-start.16 = (pred[2,256]{1,0:T(4,128)(4,1)S(1)}, pred[2,256]{1,0:T(4,128)(4,1)}, u32[]{:S(2)}) copy-start(pred[2,256]{1,0:T(4,128)(4,1)} %constant.80.clone) | copy-start | bytes 1540
  5.3 20.3 %copy-start.15 = (pred[4,256]{1,0:T(4,128)(4,1)S(1)}, pred[4,256]{1,0:T(4,128)(4,1)}, u32[]{:S(2)}) copy-start(pred[4,256]{1,0:T(4,128)(4,1)} %constant.86.clone) | copy-start | bytes 3076
  5.3 20.3 %copy-start.12 = (pred[2,320]{1,0:T(4,128)(4,1)S(1)}, pred[2,320]{1,0:T(4,128)(4,1)}, u32[]{:S(2)}) copy-start(pred[2,320]{1,0:T(4,128)(4,1)} %constant.82.clone) | copy-start | bytes 1924
  5.3 20.4 %copy-start.14 = (s32[256]{0:T(256)S(1)}, s32[256]{0:T(256)}, u32[]{:S(2)}) copy-start(s32[256]{0:T(256)} %constant.81.clone) | copy-start | bytes 3076
  5.3 20.4 %copy-start.13 = (s32[256]{0:T(256)S(1)}, s32[256]{0:T(256)}, u32[]{:S(2)}) copy-start(s32[256]{0:T(256)} %constant.87.clone) | copy-start | bytes 3076
  5.3 20.4 %copy-start.10 = (s32[320]{0:T(512)S(1)}, s32[320]{0:T(512)}, u32[]{:S(2)}) copy-start(s32[320]{0:T(512)} %constant.83.clone) | copy-start | bytes 3844
  5.3 20.5 %collective-permute-start.1 = (bf16[2,128,1280]{2,1,0:T(8,128)(2,1)}, bf16[2,128,1280]{2,1,0:T(8,128)(2,1)}, u32[]{:S(2)}, u32[]{:S(2)}) collective-permute-start(bf16[2,128,1280]{2,1,0:T(8,128)(2,1)} %get-tuple-element.45), channel_id=1, source_target_pairs={{0,8},{1,9},{2,10},{3,11},{8,16},{9,17},{10,18},{11,19},{12,4},{13... | collective-permute-start | bytes 1966088 | tf_op jit(solution)/shard_map/ppermute | solution.py:155
  6.7 20.0 %collective-permute-start.2 = (bf16[2,128,1280]{2,1,0:T(8,128)(2,1)}, bf16[2,128,1280]{2,1,0:T(8,128)(2,1)S(1)}, u32[]{:S(2)}, u32[]{:S(2)}) collective-permute-start(bf16[2,128,1280]{2,1,0:T(8,128)(2,1)} %get-tuple-element.46), channel_id=1, source_target_pairs={{4,12},{5,13},{6,14},{7,15},{8,0},{9,1},{10,2},{11,3},{12,20},{13,... | collective-permute-start | bytes 1966088 | tf_op jit(solution)/shard_map/ppermute | solution.py:155
  11.4 34.3 %collective-permute-start = (bf16[2,256,1280]{2,1,0:T(8,128)(2,1)}, bf16[2,256,1280]{2,1,0:T(8,128)(2,1)}, u32[]{:S(2)}, u32[]{:S(2)}) collective-permute-start(bf16[2,256,1280]{2,1,0:T(8,128)(2,1)} %get-tuple-element.44), channel_id=1, source_target_pairs={{0,4},{1,5},{2,6},{3,7},{4,0},{5,1},{6,2},{7,3},{8,12},{9,13},{10,... | collective-permute-start | bytes 3932168 | tf_op jit(solution)/shard_map/ppermute | solution.py:155
  11.7 34.0 %collective-permute-start.3 = (bf16[2,64,1280]{2,1,0:T(8,128)(2,1)}, bf16[2,64,1280]{2,1,0:T(8,128)(2,1)}, u32[]{:S(2)}, u32[]{:S(2)}) collective-permute-start(bf16[2,64,1280]{2,1,0:T(8,128)(2,1)} %get-tuple-element.49), channel_id=1, source_target_pairs={{0,16},{1,17},{2,18},{3,19},{4,20},{5,21},{6,22},{7,23},{8,24},{9,... | collective-permute-start | bytes 983048 | tf_op jit(solution)/shard_map/ppermute | solution.py:155
  26.7 47.7 %collective-permute-start.11 = (bf16[2,128,1280]{2,1,0:T(8,128)(2,1)}, bf16[2,128,1280]{2,1,0:T(8,128)(2,1)S(1)}, u32[]{:S(2)}, u32[]{:S(2)}) collective-permute-start(bf16[2,128,1280]{2,1,0:T(8,128)(2,1)} %collective-permute-done.1.refs_1_), channel_id=1, source_target_pairs={{4,0},{5,1},{6,2},{7,3},{8,12},{9,13},{10,14},{11,15},{12,8},{13,9... | collective-permute-start | bytes 1966088 | tf_op jit(solution)/shard_map/ppermute | solution.py:155
  47.9 23.0 %collective-permute-start.6 = (bf16[2,64,1280]{2,1,0:T(8,128)(2,1)S(1)}, bf16[2,64,1280]{2,1,0:T(8,128)(2,1)S(1)}, u32[]{:S(2)}, u32[]{:S(2)}) collective-permute-start(bf16[2,64,1280]{2,1,0:T(8,128)(2,1)S(1)} %slice.46), channel_id=1, source_target_pairs={{0,8},{1,9},{2,10},{3,11},{8,16},{9,17},{10,18},{11,19},{12,4},{13... | collective-permute-start | bytes 983048 | tf_op jit(solution)/shard_map/ppermute | solution.py:155
  49.2 21.8 %collective-permute-start.7 = (bf16[2,64,1280]{2,1,0:T(8,128)(2,1)}, bf16[2,64,1280]{2,1,0:T(8,128)(2,1)S(1)}, u32[]{:S(2)}, u32[]{:S(2)}) collective-permute-start(bf16[2,64,1280]{2,1,0:T(8,128)(2,1)} %collective-permute-done.3.refs_2_), channel_id=1, source_target_pairs={{8,0},{9,1},{10,2},{11,3},{12,4},{13,5},{14,6},{15,7},{16,24},{17,... | collective-permute-start | bytes 983048 | tf_op jit(solution)/shard_map/ppermute | solution.py:155
  50.5 32.0 %collective-permute-start.10 = (bf16[2,128,1280]{2,1,0:T(8,128)(2,1)S(1)}, bf16[2,128,1280]{2,1,0:T(8,128)(2,1)S(1)}, u32[]{:S(2)}, u32[]{:S(2)}) collective-permute-start(bf16[2,128,1280]{2,1,0:T(8,128)(2,1)S(1)} %slice.47), channel_id=1, source_target_pairs={{0,8},{1,9},{2,10},{3,11},{8,16},{9,17},{10,18},{11,19},{12,4},{13... | collective-permute-start | bytes 1966088 | tf_op jit(solution)/shard_map/ppermute | solution.py:155
  52.8 35.3 %collective-permute-start.5 = (bf16[2,128,1280]{2,1,0:T(8,128)(2,1)S(1)}, bf16[2,128,1280]{2,1,0:T(8,128)(2,1)S(1)}, u32[]{:S(2)}, u32[]{:S(2)}) collective-permute-start(bf16[2,128,1280]{2,1,0:T(8,128)(2,1)S(1)} %pad_maximum_fusion), channel_id=1, source_target_pairs={{0,4},{1,5},{2,6},{3,7},{4,0},{5,1},{6,2},{7,3},{8,12},{9,13},{10,... | collective-permute-start | bytes 1966088 | tf_op jit(solution)/shard_map/ppermute | solution.py:155
  70.9 17.2 %collective-permute-start.8 = (bf16[2,64,1280]{2,1,0:T(8,128)(2,1)S(1)}, bf16[2,64,1280]{2,1,0:T(8,128)(2,1)S(1)}, u32[]{:S(2)}, u32[]{:S(2)}) collective-permute-start(bf16[2,64,1280]{2,1,0:T(8,128)(2,1)S(1)} %collective-permute-done.7.refs_3_), channel_id=1, source_target_pairs={{0,4},{1,5},{2,6},{3,7},{4,0},{5,1},{6,2},{7,3},{24,28},{25,29},{2... | collective-permute-start | bytes 983048 | tf_op jit(solution)/shard_map/ppermute | solution.py:155
  72.9 15.2 %collective-permute-start.9 = (bf16[2,64,1280]{2,1,0:T(8,128)(2,1)S(1)}, bf16[2,64,1280]{2,1,0:T(8,128)(2,1)S(1)}, u32[]{:S(2)}, u32[]{:S(2)}) collective-permute-start(bf16[2,64,1280]{2,1,0:T(8,128)(2,1)S(1)} %collective-permute-done.6.refs_1_), channel_id=1, source_target_pairs={{0,8},{1,9},{2,10},{3,11},{8,16},{9,17},{10,18},{11,19},{12,4},{13... | collective-permute-start | bytes 983048 | tf_op jit(solution)/shard_map/ppermute | solution.py:155
  90.1 4.2 %collective-permute-start.12 = (bf16[512,512]{1,0:T(8,128)(2,1)S(1)}, bf16[512,512]{1,0:T(8,128)(2,1)S(1)}, u32[]{:S(2)}, u32[]{:S(2)}) collective-permute-start(bf16[512,512]{1,0:T(8,128)(2,1)S(1)} %last0.1), channel_id=1, source_target_pairs={{0,1},{1,0},{2,3},{3,2},{4,5},{5,4},{6,7},{7,6},{8,9},{9,8},{10,11... | collective-permute-start | bytes 1572872 | tf_op jit(solution)/shard_map/ppermute | solution.py:155
  93.0 2.5 %collective-permute-start.13 = (bf16[512,768]{1,0:T(8,128)(2,1)S(1)}, bf16[512,768]{1,0:T(8,128)(2,1)S(1)}, u32[]{:S(2)}, u32[]{:S(2)}) collective-permute-start(bf16[512,768]{1,0:T(8,128)(2,1)S(1)} %last4.1), channel_id=1, source_target_pairs={{0,1},{1,0},{2,3},{3,2},{4,5},{5,4},{6,7},{7,6},{8,9},{9,8},{10,11... | collective-permute-start | bytes 2359304 | tf_op jit(solution)/shard_map/ppermute | solution.py:155
  96.9 17.6 %collective-permute-start.14 = (bf16[512,640]{1,0:T(8,128)(2,1)S(1)}, bf16[512,640]{1,0:T(8,128)(2,1)S(1)}, u32[]{:S(2)}, u32[]{:S(2)}) collective-permute-start(bf16[512,640]{1,0:T(8,128)(2,1)S(1)} %fusion.10), channel_id=1, source_target_pairs={{0,2},{1,3},{2,0},{3,1},{4,6},{5,7},{6,4},{7,5},{8,10},{9,11},{10,... | collective-permute-start | bytes 1966088 | tf_op jit(solution)/shard_map/ppermute | solution.py:155
  101.4 26.7 %collective-permute-start.15 = (bf16[512,640]{1,0:T(8,128)(2,1)S(1)}, bf16[512,640]{1,0:T(8,128)(2,1)S(1)}, u32[]{:S(2)}, u32[]{:S(2)}) collective-permute-start(bf16[512,640]{1,0:T(8,128)(2,1)S(1)} %fusion.11), channel_id=1, source_target_pairs={{0,2},{1,3},{2,0},{3,1},{4,6},{5,7},{6,4},{7,5},{8,10},{9,11},{10,... | collective-permute-start | bytes 1966088 | tf_op jit(solution)/shard_map/ppermute | solution.py:155
  105.2 24.2 %copy-start.1 = (s32[8,8]{1,0:T(8,128)S(1)}, s32[8,8]{1,0:T(8,128)}, u32[]{:S(2)}) copy-start(s32[8,8]{1,0:T(8,128)} %param.16) | copy-start | bytes 772
  (9 other events, 54.2 us)

commit v9 on v8

--- a/solution.py
+++ b/solution.py
@@ -213,15 +213,17 @@
         z_near = move(sent_ba, far_of)
         z_two = move(sent_a, lambda t: t ^ 4)
         carry = attend(query_vectors, own_pair, [], None, None, False, 0, head_count, "own")
-        z_far, z_near, state = lax.optimization_barrier((z_far, z_near, carry[0]))
+        state, out_weight = lax.optimization_barrier((carry[0], out_weight))
+        weights = blocks_of(out_weight)
+        z_far, z_near, state, weights = lax.optimization_barrier((z_far, z_near, state, weights))
         carry = further(
             [z_far, z_near],
             [(far_block, 0, ab), (near_block, 0, ab)],
             (state, carry[1]),
             "early",
         )
-        state, out_weight, moved = lax.optimization_barrier((carry[0], out_weight, moved))
-        weights = blocks_of(out_weight, moved)
+        state, moved = lax.optimization_barrier((carry[0], moved))
+        weights = weights + blocks_of(moved)
         x_rows, z_near, z_two, state, weights = lax.optimization_barrier(
             (x_rows, z_near, z_two, state, weights)
         )

time: 130 us -> 126 us (0.969)
  starting transfers between devices: 36.2 us -> 34 us
  local copies, waits for them, and re-layouts: 16.6 us -> 15 us
    ppermute x16, starting transfers between devices: 36.2 us -> 34 us  [move(): return lax.ppermute(array, AXES, route)]
    unnamed x34, local copies, waits for them, and re-layouts: 7.3 us -> 5.57 us
  transfers between devices with their start and end apart: 16 -> 16, of which waited for: 5 -> 4; matrix products, arithmetic and copies ran while one was open for 16% -> 16% of each run, Pallas kernels for 22% -> 23%
where the time goes in v9:
time: 126 us; the launch traced here: 125 us
  starting transfers between devices  34 us (27%)
  waiting for transfers between devices  31.1 us (25%)
  Pallas kernels  30.8 us (24%)
  local copies, waits for them, and re-layouts  15 us (12%)
  matrix products  9.86 us (8%)
  other arithmetic  4.05 us (3%)
    ppermute x16, starting transfers between devices, move(): return lax.ppermute(array, AXES, route)  34 us
    ppermute x16, waiting for transfers between devices, move(): return lax.ppermute(array, AXES, route)  31.1 us
    pallas_call x6, Pallas kernels, attend(): pl.pallas_call(lambda *refs: attend_kernel(*refs, buffers=len(buffers), o...  28.3 us
    dynamic_slice x2, local copies, waits for them, and re-layouts, blocks_of(): lax.dynamic_slice_in_dim(source, number * out_width, out_width, 1)  6.87 us
    unnamed x34, local copies, waits for them, and re-layouts  5.57 us
    dot_general x6, matrix products, project(): jnp.dot(part, weights[index][low:high, first:last], preferred_element_typ...  5.11 us
    dot_general x6, matrix products, project(): jnp.dot(other, weights[index + 2][low:high, first:last], preferred_elemen...  4.74 us
  transfers between devices with their start and end apart: 16, of which 4 were waited for; matrix products, arithmetic and copies ran while one was open for 16% of the time, Pallas kernels for 23%

profile of v9, /device:TPU:2, one launch (start us, length us, event | category | flops | bytes accessed | tf_op | source)
XLA Modules:
  0.0 125.3 jit_solution(1456819125902835517)
XLA Ops:
  0.0 1.4 %copy-done.3 = bf16[512,1280]{1,0:T(8,128)(2,1)S(1)} copy-done((bf16[512,1280]{1,0:T(8,128)(2,1)S(1)}, bf16[512,1280]{1,0:T(8,128)(2,1)}, u32[]{:S(2)}) %copy-start.3) | copy-done | bytes 1310744
  1.4 1.3 %copy-done.5 = bf16[512,1280]{1,0:T(8,128)(2,1)S(1)} copy-done((bf16[512,1280]{1,0:T(8,128)(2,1)S(1)}, bf16[512,1280]{1,0:T(8,128)(2,1)}, u32[]{:S(2)}) %copy-start.5) | copy-done | bytes 1310744
  2.8 2.5 %pack.1 = (bf16[2,256,1280]{2,1,0:T(8,128)(2,1)}, bf16[2,128,1280]{2,1,0:T(8,128)(2,1)}, bf16[2,128,1280]{2,1,0:T(8,128)(2,1)}, bf16[2,64,1280]{2,1,0:T(8,128)(2,1)}) custom-call(bf16[512,1280]{1,0:T(8,128)(2,1)S(1)} %copy-done.3, bf16[512,1280]{1,0:T(8,128)(2,1)S(1)} %copy-done.5), custom_call_target="tpu_custom_call" | custom-call | flops 671088640 | bytes 5242880 | tf_op jit(solution)/shard_map/pack/pallas_call | solution.py:39
  6.7 4.7 %collective-permute-start.2 = (bf16[2,128,1280]{2,1,0:T(8,128)(2,1)}, bf16[2,128,1280]{2,1,0:T(8,128)(2,1)S(1)}, u32[]{:S(2)}, u32[]{:S(2)}) collective-permute-start(bf16[2,128,1280]{2,1,0:T(8,128)(2,1)} %get-tuple-element.49), channel_id=1, source_target_pairs={{4,12},{5,13},{6,14},{7,15},{8,0},{9,1},{10,2},{11,3},{12,20},{13,... | collective-permute-start | bytes 1966088 | tf_op jit(solution)/shard_map/ppermute | solution.py:155
  11.3 3.9 %collective-permute-start.3 = (bf16[2,64,1280]{2,1,0:T(8,128)(2,1)}, bf16[2,64,1280]{2,1,0:T(8,128)(2,1)}, u32[]{:S(2)}, u32[]{:S(2)}) collective-permute-start(bf16[2,64,1280]{2,1,0:T(8,128)(2,1)} %get-tuple-element.54), channel_id=1, source_target_pairs={{0,16},{1,17},{2,18},{3,19},{4,20},{5,21},{6,22},{7,23},{8,24},{9,... | collective-permute-start | bytes 983048 | tf_op jit(solution)/shard_map/ppermute | solution.py:155
  15.3 1.3 %copy-done.6 = bf16[512,1280]{1,0:T(8,128)(2,1)S(1)} copy-done((bf16[512,1280]{1,0:T(8,128)(2,1)S(1)}, bf16[512,1280]{1,0:T(8,128)(2,1)}, u32[]{:S(2)}) %copy-start.6) | copy-done | bytes 1310744
  16.6 6.4 %own.1 = (f32[10,8,512]{2,1,0:T(8,128)S(1)}, f32[10,128,512]{2,1,0:T(8,128)S(1)}) custom-call(bf16[512,1280]{1,0:T(8,128)(2,1)S(1)} %copy-done.2, bf16[512,1280]{1,0:T(8,128)(2,1)S(1)} %copy-done.4, bf16[512,1280]{1,0:T(8,128)(2,1)S(1)} %copy-done.6), custom_call_target="tpu_custom_call" | custom-call | tf_op jit(solution)/shard_map/own/pallas_call | solution.py:123
  23.0 1.5 %copy-done.7 = f32[10,128,512]{2,1,0:T(8,128)} copy-done((f32[10,128,512]{2,1,0:T(8,128)}, f32[10,128,512]{2,1,0:T(8,128)S(1)}, u32[]{:S(2)}) %copy-start.7) | copy-done | bytes 2621464
  25.9 3.5 %constant_dynamic-slice_fusion.3 = (bf16[1280,1280]{1,0:T(8,128)(2,1)S(1)}, bf16[1280,1280]{1,0:T(8,128)(2,1)S(1)}) fusion(bf16[1280,5120]{1,0:T(8,128)(2,1)} %param.17, s32[]{:T(128)S(6)} %select_n.116, s32[]{:T(128)S(6)} %select_n.115), kind=kLoop, calls=%fused_computation.51 | loop fusion | bytes 13107208 | tf_op jit(solution)/shard_map/dynamic_slice | solution.py:190
  29.7 3.2 %collective-permute-start.11 = (bf16[2,128,1280]{2,1,0:T(8,128)(2,1)}, bf16[2,128,1280]{2,1,0:T(8,128)(2,1)S(1)}, u32[]{:S(2)}, u32[]{:S(2)}) collective-permute-start(bf16[2,128,1280]{2,1,0:T(8,128)(2,1)} %collective-permute-done.1.refs_1_), channel_id=1, source_target_pairs={{4,0},{5,1},{6,2},{7,3},{8,12},{9,13},{10,14},{11,15},{12,8},{13,9... | collective-permute-start | bytes 1966088 | tf_op jit(solution)/shard_map/ppermute | solution.py:155
  33.0 5.4 %early.1 = (f32[10,8,512]{2,1,0:T(8,128)S(1)}, f32[10,128,512]{2,1,0:T(8,128)S(1)}) custom-call(bf16[512,1280]{1,0:T(8,128)(2,1)S(1)} %copy-done.2, bf16[2,128,1280]{2,1,0:T(8,128)(2,1)} %collective-permute-done.1.refs_1_, bf16[2,128,1280]{2,1,0:T(8,128)(2,1)S(1)} %collective-permute-done.2.refs_2_, f32[256,128]{1,0:T(8,128)S(1)} %broadcast_in_dim.166.refs_3_, ...), custom_call_target="tpu_custom_call" | custom-call | flops 671088640 | bytes 5242880 | tf_op jit(solution)/shard_map/early/pallas_call | solution.py:123
  38.4 3.4 %constant_dynamic-slice_fusion = (bf16[1280,1280]{1,0:T(8,128)(2,1)S(1)}, bf16[1280,1280]{1,0:T(8,128)(2,1)S(1)}) fusion(bf16[1280,5120]{1,0:T(8,128)(2,1)} %collective-permute-done.4, s32[]{:T(128)S(6)} %select_n.116, s32[]{:T(128)S(6)} %select_n.115), kind=kLoop, calls=%fused_computation.48 | loop fusion | bytes 13107208 | tf_op jit(solution)/shard_map/dynamic_slice | solution.py:190
  48.9 10.8 %collective-permute-start.5 = (bf16[2,128,1280]{2,1,0:T(8,128)(2,1)S(1)}, bf16[2,128,1280]{2,1,0:T(8,128)(2,1)S(1)}, u32[]{:S(2)}, u32[]{:S(2)}) collective-permute-start(bf16[2,128,1280]{2,1,0:T(8,128)(2,1)S(1)} %pad_maximum_fusion), channel_id=1, source_target_pairs={{0,4},{1,5},{2,6},{3,7},{4,0},{5,1},{6,2},{7,3},{8,12},{9,13},{10,... | collective-permute-start | bytes 1966088 | tf_op jit(solution)/shard_map/ppermute | solution.py:155
  59.8 6.4 %first.1 = (f32[10,8,512]{2,1,0:T(8,128)S(1)}, f32[10,128,512]{2,1,0:T(8,128)S(1)}) custom-call(bf16[512,1280]{1,0:T(8,128)(2,1)S(1)} %copy-done.2, bf16[2,256,1280]{2,1,0:T(8,128)(2,1)} %collective-permute-done.refs_1_, bf16[2,64,1280]{2,1,0:T(8,128)(2,1)} %collective-permute-done.3.refs_2_, f32[320,128]{1,0:T(8,128)S(1)} %broadcast_in_dim.171.refs_3_, ...), custom_call_target="tpu_custom_call" | custom-call | flops 838860800 | bytes 5242880 | tf_op jit(solution)/shard_map/first/pallas_call | solution.py:123
  66.3 1.9 %collective-permute-start.8 = (bf16[2,64,1280]{2,1,0:T(8,128)(2,1)S(1)}, bf16[2,64,1280]{2,1,0:T(8,128)(2,1)S(1)}, u32[]{:S(2)}, u32[]{:S(2)}) collective-permute-start(bf16[2,64,1280]{2,1,0:T(8,128)(2,1)S(1)} %collective-permute-done.7.refs_3_), channel_id=1, source_target_pairs={{0,4},{1,5},{2,6},{3,7},{4,0},{5,1},{6,2},{7,3},{24,28},{25,29},{2... | collective-permute-start | bytes 983048 | tf_op jit(solution)/shard_map/ppermute | solution.py:155
  68.2 1.5 %collective-permute-start.9 = (bf16[2,64,1280]{2,1,0:T(8,128)(2,1)S(1)}, bf16[2,64,1280]{2,1,0:T(8,128)(2,1)S(1)}, u32[]{:S(2)}, u32[]{:S(2)}) collective-permute-start(bf16[2,64,1280]{2,1,0:T(8,128)(2,1)S(1)} %collective-permute-done.6.refs_1_), channel_id=1, source_target_pairs={{0,8},{1,9},{2,10},{3,11},{8,16},{9,17},{10,18},{11,19},{12,4},{13... | collective-permute-start | bytes 983048 | tf_op jit(solution)/shard_map/ppermute | solution.py:155
  69.8 8.6 %collective-permute-done.10.refs_2_ = bf16[2,128,1280]{2,1,0:T(8,128)(2,1)S(1)} collective-permute-done((bf16[2,128,1280]{2,1,0:T(8,128)(2,1)S(1)}, bf16[2,128,1280]{2,1,0:T(8,128)(2,1)S(1)}, u32[]{:S(2)}, u32[]{:S(2)}) %collective-permute-start.10) | collective-permute-done | bytes 655392 | tf_op jit(solution)/shard_map/ppermute | solution.py:155
  78.5 5.5 %middle.1 = (f32[10,8,512]{2,1,0:T(8,128)S(1)}, f32[10,128,512]{2,1,0:T(8,128)S(1)}) custom-call(bf16[512,1280]{1,0:T(8,128)(2,1)S(1)} %copy-done.2, bf16[2,64,1280]{2,1,0:T(8,128)(2,1)S(1)} %collective-permute-done.6.refs_1_, bf16[2,128,1280]{2,1,0:T(8,128)(2,1)S(1)} %collective-permute-done.10.refs_2_, ...), custom_call_target="tpu_custom_call" | custom-call | flops 1006632960 | bytes 5242880 | tf_op jit(solution)/shard_map/middle/pallas_call | solution.py:123
  84.2 1.9 %last0.1 = bf16[512,512]{1,0:T(8,128)(2,1)S(1)} custom-call(bf16[512,1280]{1,0:T(8,128)(2,1)S(1)} %copy-done.2, bf16[2,128,1280]{2,1,0:T(8,128)(2,1)S(1)} %collective-permute-done.5.refs_1_, bf16[2,64,1280]{2,1,0:T(8,128)(2,1)S(1)} %collective-permute-done.8.refs_2_, bf16[2,64,1280]{2,1,0:T(8,128)(2,1)S(1)} %collective-permute-done.9.refs_3_, ...), custom_call_target="tpu_custom_call" | custom-call | flops 268435456 | bytes 2097152 | tf_op jit(solution)/shard_map/last0/pallas_call | solution.py:123
  86.1 2.8 %last4.1 = bf16[512,768]{1,0:T(8,128)(2,1)S(1)} custom-call(bf16[512,1280]{1,0:T(8,128)(2,1)S(1)} %copy-done.2, bf16[2,128,1280]{2,1,0:T(8,128)(2,1)S(1)} %collective-permute-done.5.refs_1_, bf16[2,64,1280]{2,1,0:T(8,128)(2,1)S(1)} %collective-permute-done.8.refs_2_, bf16[2,64,1280]{2,1,0:T(8,128)(2,1)S(1)} %collective-permute-done.9.refs_3_, ...), custom_call_target="tpu_custom_call" | custom-call | flops 402653184 | bytes 3145728 | tf_op jit(solution)/shard_map/last4/pallas_call | solution.py:123
  92.8 1.6 %collective-permute-start.14 = (bf16[512,640]{1,0:T(8,128)(2,1)S(1)}, bf16[512,640]{1,0:T(8,128)(2,1)S(1)}, u32[]{:S(2)}, u32[]{:S(2)}) collective-permute-start(bf16[512,640]{1,0:T(8,128)(2,1)S(1)} %fusion.10), channel_id=1, source_target_pairs={{0,2},{1,3},{2,0},{3,1},{4,6},{5,7},{6,4},{7,5},{8,10},{9,11},{10,... | collective-permute-start | bytes 1966088 | tf_op jit(solution)/shard_map/ppermute | solution.py:155
  102.1 8.4 %collective-permute-done.14 = bf16[512,640]{1,0:T(8,128)(2,1)S(1)} collective-permute-done((bf16[512,640]{1,0:T(8,128)(2,1)S(1)}, bf16[512,640]{1,0:T(8,128)(2,1)S(1)}, u32[]{:S(2)}, u32[]{:S(2)}) %collective-permute-start.14) | collective-permute-done | bytes 655392 | tf_op jit(solution)/shard_map/ppermute | solution.py:155
  110.5 13.5 %collective-permute-done.15 = bf16[512,640]{1,0:T(8,128)(2,1)S(1)} collective-permute-done((bf16[512,640]{1,0:T(8,128)(2,1)S(1)}, bf16[512,640]{1,0:T(8,128)(2,1)S(1)}, u32[]{:S(2)}, u32[]{:S(2)}) %collective-permute-start.15) | collective-permute-done | bytes 655392 | tf_op jit(solution)/shard_map/ppermute | solution.py:155
  123.9 1.3 %add_convert_fusion = bf16[512,1280]{1,0:T(8,128)(2,1)} fusion(f32[512,1280]{1,0:T(8,128)S(1)} %fusion.1, bf16[512,640]{1,0:T(8,128)(2,1)S(1)} %collective-permute-done.15, bf16[512,640]{1,0:T(8,128)(2,1)S(1)} %collective-permute-done.14), kind=kLoop, calls=%fused_computation.3 | loop fusion | flops 3932160 | bytes 5242880 | tf_op jit(solution)/shard_map/convert_element_type | solution.py:303
  (93 shorter events, 22.3 us)
Async XLA Ops:
  0.0 24.4 %copy-start = (s32[8,8]{1,0:T(8,128)S(1)}, s32[8,8]{1,0:T(8,128)}, u32[]{:S(2)}) copy-start(s32[8,8]{1,0:T(8,128)} %param.16) | copy-start | bytes 772
  0.0 15.3 %copy-start.2 = (bf16[512,1280]{1,0:T(8,128)(2,1)S(1)}, bf16[512,1280]{1,0:T(8,128)(2,1)}, u32[]{:S(2)}) copy-start(bf16[512,1280]{1,0:T(8,128)(2,1)} %refs_0_.13) | copy-start | bytes 3932164
  0.0 38.4 %collective-permute-start.4 = (bf16[1280,5120]{1,0:T(8,128)(2,1)}, bf16[1280,5120]{1,0:T(8,128)(2,1)}, u32[]{:S(2)}, u32[]{:S(2)}) collective-permute-start(bf16[1280,5120]{1,0:T(8,128)(2,1)} %param.17), channel_id=1, source_target_pairs={{0,1},{1,0},{2,3},{3,2},{4,5},{5,4},{6,7},{7,6},{8,9},{9,8},{10,11... | collective-permute-start | bytes 39321608 | tf_op jit(solution)/shard_map/ppermute | solution.py:155
  2.8 12.5 %copy-start.4 = (bf16[512,1280]{1,0:T(8,128)(2,1)S(1)}, bf16[512,1280]{1,0:T(8,128)(2,1)}, u32[]{:S(2)}) copy-start(bf16[512,1280]{1,0:T(8,128)(2,1)} %refs_1_.3) | copy-start | bytes 3932164
  5.3 20.1 %copy-start.16 = (pred[2,256]{1,0:T(4,128)(4,1)S(1)}, pred[2,256]{1,0:T(4,128)(4,1)}, u32[]{:S(2)}) copy-start(pred[2,256]{1,0:T(4,128)(4,1)} %constant.80.clone) | copy-start | bytes 1540
  5.3 20.4 %copy-start.15 = (pred[4,256]{1,0:T(4,128)(4,1)S(1)}, pred[4,256]{1,0:T(4,128)(4,1)}, u32[]{:S(2)}) copy-start(pred[4,256]{1,0:T(4,128)(4,1)} %constant.86.clone) | copy-start | bytes 3076
  5.3 20.5 %copy-start.14 = (s32[256]{0:T(256)S(1)}, s32[256]{0:T(256)}, u32[]{:S(2)}) copy-start(s32[256]{0:T(256)} %constant.81.clone) | copy-start | bytes 3076
  5.3 20.5 %copy-start.13 = (s32[256]{0:T(256)S(1)}, s32[256]{0:T(256)}, u32[]{:S(2)}) copy-start(s32[256]{0:T(256)} %constant.87.clone) | copy-start | bytes 3076
  5.3 36.5 %collective-permute-start = (bf16[2,256,1280]{2,1,0:T(8,128)(2,1)}, bf16[2,256,1280]{2,1,0:T(8,128)(2,1)}, u32[]{:S(2)}, u32[]{:S(2)}) collective-permute-start(bf16[2,256,1280]{2,1,0:T(8,128)(2,1)} %get-tuple-element.47), channel_id=1, source_target_pairs={{0,4},{1,5},{2,6},{3,7},{4,0},{5,1},{6,2},{7,3},{8,12},{9,13},{10,... | collective-permute-start | bytes 3932168 | tf_op jit(solution)/shard_map/ppermute | solution.py:155
  5.4 24.3 %collective-permute-start.1 = (bf16[2,128,1280]{2,1,0:T(8,128)(2,1)}, bf16[2,128,1280]{2,1,0:T(8,128)(2,1)}, u32[]{:S(2)}, u32[]{:S(2)}) collective-permute-start(bf16[2,128,1280]{2,1,0:T(8,128)(2,1)} %get-tuple-element.48), channel_id=1, source_target_pairs={{0,8},{1,9},{2,10},{3,11},{8,16},{9,17},{10,18},{11,19},{12,4},{13... | collective-permute-start | bytes 1966088 | tf_op jit(solution)/shard_map/ppermute | solution.py:155
  6.7 23.0 %collective-permute-start.2 = (bf16[2,128,1280]{2,1,0:T(8,128)(2,1)}, bf16[2,128,1280]{2,1,0:T(8,128)(2,1)S(1)}, u32[]{:S(2)}, u32[]{:S(2)}) collective-permute-start(bf16[2,128,1280]{2,1,0:T(8,128)(2,1)} %get-tuple-element.49), channel_id=1, source_target_pairs={{4,12},{5,13},{6,14},{7,15},{8,0},{9,1},{10,2},{11,3},{12,20},{13,... | collective-permute-start | bytes 1966088 | tf_op jit(solution)/shard_map/ppermute | solution.py:155
  11.3 30.4 %collective-permute-start.3 = (bf16[2,64,1280]{2,1,0:T(8,128)(2,1)}, bf16[2,64,1280]{2,1,0:T(8,128)(2,1)}, u32[]{:S(2)}, u32[]{:S(2)}) collective-permute-start(bf16[2,64,1280]{2,1,0:T(8,128)(2,1)} %get-tuple-element.54), channel_id=1, source_target_pairs={{0,16},{1,17},{2,18},{3,19},{4,20},{5,21},{6,22},{7,23},{8,24},{9,... | collective-permute-start | bytes 983048 | tf_op jit(solution)/shard_map/ppermute | solution.py:155
  29.7 40.1 %collective-permute-start.11 = (bf16[2,128,1280]{2,1,0:T(8,128)(2,1)}, bf16[2,128,1280]{2,1,0:T(8,128)(2,1)S(1)}, u32[]{:S(2)}, u32[]{:S(2)}) collective-permute-start(bf16[2,128,1280]{2,1,0:T(8,128)(2,1)} %collective-permute-done.1.refs_1_), channel_id=1, source_target_pairs={{4,0},{5,1},{6,2},{7,3},{8,12},{9,13},{10,14},{11,15},{12,8},{13,9... | collective-permute-start | bytes 1966088 | tf_op jit(solution)/shard_map/ppermute | solution.py:155
  43.9 22.3 %collective-permute-start.6 = (bf16[2,64,1280]{2,1,0:T(8,128)(2,1)S(1)}, bf16[2,64,1280]{2,1,0:T(8,128)(2,1)S(1)}, u32[]{:S(2)}, u32[]{:S(2)}) collective-permute-start(bf16[2,64,1280]{2,1,0:T(8,128)(2,1)S(1)} %slice.46), channel_id=1, source_target_pairs={{0,8},{1,9},{2,10},{3,11},{8,16},{9,17},{10,18},{11,19},{12,4},{13... | collective-permute-start | bytes 983048 | tf_op jit(solution)/shard_map/ppermute | solution.py:155
  45.2 21.1 %collective-permute-start.7 = (bf16[2,64,1280]{2,1,0:T(8,128)(2,1)}, bf16[2,64,1280]{2,1,0:T(8,128)(2,1)S(1)}, u32[]{:S(2)}, u32[]{:S(2)}) collective-permute-start(bf16[2,64,1280]{2,1,0:T(8,128)(2,1)} %collective-permute-done.3.refs_2_), channel_id=1, source_target_pairs={{8,0},{9,1},{10,2},{11,3},{12,4},{13,5},{14,6},{15,7},{16,24},{17,... | collective-permute-start | bytes 983048 | tf_op jit(solution)/shard_map/ppermute | solution.py:155
  46.5 31.9 %collective-permute-start.10 = (bf16[2,128,1280]{2,1,0:T(8,128)(2,1)S(1)}, bf16[2,128,1280]{2,1,0:T(8,128)(2,1)S(1)}, u32[]{:S(2)}, u32[]{:S(2)}) collective-permute-start(bf16[2,128,1280]{2,1,0:T(8,128)(2,1)S(1)} %slice.47), channel_id=1, source_target_pairs={{0,8},{1,9},{2,10},{3,11},{8,16},{9,17},{10,18},{11,19},{12,4},{13... | collective-permute-start | bytes 1966088 | tf_op jit(solution)/shard_map/ppermute | solution.py:155
  48.9 35.2 %collective-permute-start.5 = (bf16[2,128,1280]{2,1,0:T(8,128)(2,1)S(1)}, bf16[2,128,1280]{2,1,0:T(8,128)(2,1)S(1)}, u32[]{:S(2)}, u32[]{:S(2)}) collective-permute-start(bf16[2,128,1280]{2,1,0:T(8,128)(2,1)S(1)} %pad_maximum_fusion), channel_id=1, source_target_pairs={{0,4},{1,5},{2,6},{3,7},{4,0},{5,1},{6,2},{7,3},{8,12},{9,13},{10,... | collective-permute-start | bytes 1966088 | tf_op jit(solution)/shard_map/ppermute | solution.py:155
  66.3 17.7 %collective-permute-start.8 = (bf16[2,64,1280]{2,1,0:T(8,128)(2,1)S(1)}, bf16[2,64,1280]{2,1,0:T(8,128)(2,1)S(1)}, u32[]{:S(2)}, u32[]{:S(2)}) collective-permute-start(bf16[2,64,1280]{2,1,0:T(8,128)(2,1)S(1)} %collective-permute-done.7.refs_3_), channel_id=1, source_target_pairs={{0,4},{1,5},{2,6},{3,7},{4,0},{5,1},{6,2},{7,3},{24,28},{25,29},{2... | collective-permute-start | bytes 983048 | tf_op jit(solution)/shard_map/ppermute | solution.py:155
  68.2 15.8 %collective-permute-start.9 = (bf16[2,64,1280]{2,1,0:T(8,128)(2,1)S(1)}, bf16[2,64,1280]{2,1,0:T(8,128)(2,1)S(1)}, u32[]{:S(2)}, u32[]{:S(2)}) collective-permute-start(bf16[2,64,1280]{2,1,0:T(8,128)(2,1)S(1)} %collective-permute-done.6.refs_1_), channel_id=1, source_target_pairs={{0,8},{1,9},{2,10},{3,11},{8,16},{9,17},{10,18},{11,19},{12,4},{13... | collective-permute-start | bytes 983048 | tf_op jit(solution)/shard_map/ppermute | solution.py:155
  86.0 4.2 %collective-permute-start.12 = (bf16[512,512]{1,0:T(8,128)(2,1)S(1)}, bf16[512,512]{1,0:T(8,128)(2,1)S(1)}, u32[]{:S(2)}, u32[]{:S(2)}) collective-permute-start(bf16[512,512]{1,0:T(8,128)(2,1)S(1)} %last0.1), channel_id=1, source_target_pairs={{0,1},{1,0},{2,3},{3,2},{4,5},{5,4},{6,7},{7,6},{8,9},{9,8},{10,11... | collective-permute-start | bytes 1572872 | tf_op jit(solution)/shard_map/ppermute | solution.py:155
  88.9 2.5 %collective-permute-start.13 = (bf16[512,768]{1,0:T(8,128)(2,1)S(1)}, bf16[512,768]{1,0:T(8,128)(2,1)S(1)}, u32[]{:S(2)}, u32[]{:S(2)}) collective-permute-start(bf16[512,768]{1,0:T(8,128)(2,1)S(1)} %last4.1), channel_id=1, source_target_pairs={{0,1},{1,0},{2,3},{3,2},{4,5},{5,4},{6,7},{7,6},{8,9},{9,8},{10,11... | collective-permute-start | bytes 2359304 | tf_op jit(solution)/shard_map/ppermute | solution.py:155
  92.8 17.6 %collective-permute-start.14 = (bf16[512,640]{1,0:T(8,128)(2,1)S(1)}, bf16[512,640]{1,0:T(8,128)(2,1)S(1)}, u32[]{:S(2)}, u32[]{:S(2)}) collective-permute-start(bf16[512,640]{1,0:T(8,128)(2,1)S(1)} %fusion.10), channel_id=1, source_target_pairs={{0,2},{1,3},{2,0},{3,1},{4,6},{5,7},{6,4},{7,5},{8,10},{9,11},{10,... | collective-permute-start | bytes 1966088 | tf_op jit(solution)/shard_map/ppermute | solution.py:155
  97.2 26.7 %collective-permute-start.15 = (bf16[512,640]{1,0:T(8,128)(2,1)S(1)}, bf16[512,640]{1,0:T(8,128)(2,1)S(1)}, u32[]{:S(2)}, u32[]{:S(2)}) collective-permute-start(bf16[512,640]{1,0:T(8,128)(2,1)S(1)} %fusion.11), channel_id=1, source_target_pairs={{0,2},{1,3},{2,0},{3,1},{4,6},{5,7},{6,4},{7,5},{8,10},{9,11},{10,... | collective-permute-start | bytes 1966088 | tf_op jit(solution)/shard_map/ppermute | solution.py:155
  101.1 24.2 %copy-start.1 = (s32[8,8]{1,0:T(8,128)S(1)}, s32[8,8]{1,0:T(8,128)}, u32[]{:S(2)}) copy-start(s32[8,8]{1,0:T(8,128)} %param.16) | copy-start | bytes 772
  (9 other events, 40.1 us)

commit v10 on v9

--- a/solution.py
+++ b/solution.py
@@ -120,6 +120,7 @@
             jax.ShapeDtypeStruct((high - low, HEAD_DIM, row_count), F32),
         ]
     held = pl.BlockSpec(memory_space=pltpu.VMEM)
+    scale = {"own": 0, "early": 1, "first": 1}.get(name, 1)
     return pl.pallas_call(
         lambda *refs: attend_kernel(
             *refs, buffers=len(buffers), own=own, first=first, last=last, low=low, high=high
@@ -130,9 +131,9 @@
         name=name,
         compiler_params=pltpu.CompilerParams(vmem_limit_bytes=16 << 20),
         cost_estimate=pl.CostEstimate(
-            flops=0 if own else 4 * row_count * count * width,
-            bytes_accessed=0 if own else 8 * row_count * width,
-            transcendentals=0 if own else row_count * count * (high - low),
+            flops=scale * 4 * row_count * count * width,
+            bytes_accessed=scale * 8 * row_count * width,
+            transcendentals=scale * row_count * count * (high - low),
         ),
     )(*operands)
 
@@ -222,10 +223,8 @@
             (state, carry[1]),
             "early",
         )
-        state, moved = lax.optimization_barrier((carry[0], moved))
-        weights = weights + blocks_of(moved)
-        x_rows, z_near, z_two, state, weights = lax.optimization_barrier(
-            (x_rows, z_near, z_two, state, weights)
+        x_rows, z_near, z_two, state, weights, moved = lax.optimization_barrier(
+            (x_rows, z_near, z_two, carry[0], weights, moved)
         )
         near_b = move(x_rows[:, a:ab], near_of)
         near_c = move(x_rows[:, ab:], near_of)
@@ -238,9 +237,13 @@
             (state, carry[1]),
             "first",
         )
-        near_b, z_three, state = lax.optimization_barrier((near_b, z_three, carry[0]))
+        near_b, z_three, state, moved = lax.optimization_barrier(
+            (near_b, z_three, carry[0], moved)
+        )
+        weights = weights + blocks_of(moved)
         chain_b = move(near_b, near_of)
         cross_three = move(z_three, lambda t: t ^ 1 if t in ends else None)
+        near_c, state, weights = lax.optimization_barrier((near_c, state, weights))
         carry = further(
             [near_b, near_c, z_three, cross_far],
             [

time: 126 us -> 125 us (level)
  starting transfers between devices: 34 us -> 29.1 us
  waiting for transfers between devices: 31.1 us -> 35 us
    ppermute x16, starting transfers between devices: 34 us -> 29.1 us  [move(): return lax.ppermute(array, AXES, route)]
    ppermute x16, waiting for transfers between devices: 31.1 us -> 35 us  [move(): return lax.ppermute(array, AXES, route)]
  transfers between devices with their start and end apart: 16 -> 16, of which waited for: 4 -> 6; matrix products, arithmetic and copies ran while one was open for 16% -> 16% of each run, Pallas kernels for 23% -> 23%
where the time goes in v10:
time: 125 us; the launch traced here: 124 us
  waiting for transfers between devices  35 us (28%)
  Pallas kernels  30.8 us (25%)
  starting transfers between devices  29.1 us (23%)
  local copies, waits for them, and re-layouts  15 us (12%)
  matrix products  9.67 us (8%)
  other arithmetic  4.01 us (3%)
    ppermute x16, waiting for transfers between devices, move(): return lax.ppermute(array, AXES, route)  35 us
    ppermute x16, starting transfers between devices, move(): return lax.ppermute(array, AXES, route)  29.1 us
    pallas_call x6, Pallas kernels, attend(): pl.pallas_call(lambda *refs: attend_kernel(*refs, buffers=len(buffers), o...  28.3 us
    dynamic_slice x2, local copies, waits for them, and re-layouts, blocks_of(): lax.dynamic_slice_in_dim(source, number * out_width, out_width, 1)  6.87 us
    unnamed x34, local copies, waits for them, and re-layouts  5.57 us
    dot_general x6, matrix products, project(): jnp.dot(part, weights[index][low:high, first:last], preferred_element_typ...  4.92 us
    dot_general x6, matrix products, project(): jnp.dot(other, weights[index + 2][low:high, first:last], preferred_elemen...  4.75 us
  transfers between devices with their start and end apart: 16, of which 6 were waited for; matrix products, arithmetic and copies ran while one was open for 16% of the time, Pallas kernels for 23%

profile of v10, /device:TPU:2, one launch (start us, length us, event | category | flops | bytes accessed | tf_op | source)
XLA Modules:
  0.0 124.0 jit_solution(3626708604718121591)
XLA Ops:
  0.0 1.4 %copy-done.3 = bf16[512,1280]{1,0:T(8,128)(2,1)S(1)} copy-done((bf16[512,1280]{1,0:T(8,128)(2,1)S(1)}, bf16[512,1280]{1,0:T(8,128)(2,1)}, u32[]{:S(2)}) %copy-start.3) | copy-done | bytes 1310744
  2.8 2.5 %pack.1 = (bf16[2,256,1280]{2,1,0:T(8,128)(2,1)}, bf16[2,128,1280]{2,1,0:T(8,128)(2,1)}, bf16[2,128,1280]{2,1,0:T(8,128)(2,1)}, bf16[2,64,1280]{2,1,0:T(8,128)(2,1)}) custom-call(bf16[512,1280]{1,0:T(8,128)(2,1)S(1)} %copy-done.3, bf16[512,1280]{1,0:T(8,128)(2,1)S(1)} %copy-done.5), custom_call_target="tpu_custom_call" | custom-call | flops 671088640 | bytes 5242880 | tf_op jit(solution)/shard_map/pack/pallas_call | solution.py:39
  6.7 4.7 %collective-permute-start.2 = (bf16[2,128,1280]{2,1,0:T(8,128)(2,1)}, bf16[2,128,1280]{2,1,0:T(8,128)(2,1)S(1)}, u32[]{:S(2)}, u32[]{:S(2)}) collective-permute-start(bf16[2,128,1280]{2,1,0:T(8,128)(2,1)} %get-tuple-element.53), channel_id=1, source_target_pairs={{4,12},{5,13},{6,14},{7,15},{8,0},{9,1},{10,2},{11,3},{12,20},{13,... | collective-permute-start | bytes 1966088 | tf_op jit(solution)/shard_map/ppermute | solution.py:156
  11.3 3.9 %collective-permute-start.3 = (bf16[2,64,1280]{2,1,0:T(8,128)(2,1)}, bf16[2,64,1280]{2,1,0:T(8,128)(2,1)}, u32[]{:S(2)}, u32[]{:S(2)}) collective-permute-start(bf16[2,64,1280]{2,1,0:T(8,128)(2,1)} %get-tuple-element.58), channel_id=1, source_target_pairs={{0,16},{1,17},{2,18},{3,19},{4,20},{5,21},{6,22},{7,23},{8,24},{9,... | collective-permute-start | bytes 983048 | tf_op jit(solution)/shard_map/ppermute | solution.py:156
  15.3 1.3 %copy-done.6 = bf16[512,1280]{1,0:T(8,128)(2,1)S(1)} copy-done((bf16[512,1280]{1,0:T(8,128)(2,1)S(1)}, bf16[512,1280]{1,0:T(8,128)(2,1)}, u32[]{:S(2)}) %copy-start.6) | copy-done | bytes 1310744
  16.6 6.4 %own.1 = (f32[10,8,512]{2,1,0:T(8,128)S(1)}, f32[10,128,512]{2,1,0:T(8,128)S(1)}) custom-call(bf16[512,1280]{1,0:T(8,128)(2,1)S(1)} %copy-done.2, bf16[512,1280]{1,0:T(8,128)(2,1)S(1)} %copy-done.4, bf16[512,1280]{1,0:T(8,128)(2,1)S(1)} %copy-done.6), custom_call_target="tpu_custom_call" | custom-call | tf_op jit(solution)/shard_map/own/pallas_call | solution.py:124
  23.0 1.5 %copy-done.7 = f32[10,128,512]{2,1,0:T(8,128)} copy-done((f32[10,128,512]{2,1,0:T(8,128)}, f32[10,128,512]{2,1,0:T(8,128)S(1)}, u32[]{:S(2)}) %copy-start.7) | copy-done | bytes 2621464
  26.1 3.5 %constant_dynamic-slice_fusion.3 = (bf16[1280,1280]{1,0:T(8,128)(2,1)S(1)}, bf16[1280,1280]{1,0:T(8,128)(2,1)S(1)}) fusion(bf16[1280,5120]{1,0:T(8,128)(2,1)} %param.17, s32[]{:T(128)S(6)} %select_n.116, s32[]{:T(128)S(6)} %select_n.115), kind=kLoop, calls=%fused_computation.51 | loop fusion | bytes 13107208 | tf_op jit(solution)/shard_map/dynamic_slice | solution.py:191
  29.9 3.0 %collective-permute-start.11 = (bf16[2,128,1280]{2,1,0:T(8,128)(2,1)}, bf16[2,128,1280]{2,1,0:T(8,128)(2,1)S(1)}, u32[]{:S(2)}, u32[]{:S(2)}) collective-permute-start(bf16[2,128,1280]{2,1,0:T(8,128)(2,1)} %collective-permute-done.1.refs_1_), channel_id=1, source_target_pairs={{4,0},{5,1},{6,2},{7,3},{8,12},{9,13},{10,14},{11,15},{12,8},{13,9... | collective-permute-start | bytes 1966088 | tf_op jit(solution)/shard_map/ppermute | solution.py:156
  33.0 5.4 %early.1 = (f32[10,8,512]{2,1,0:T(8,128)S(1)}, f32[10,128,512]{2,1,0:T(8,128)S(1)}) custom-call(bf16[512,1280]{1,0:T(8,128)(2,1)S(1)} %copy-done.2, bf16[2,128,1280]{2,1,0:T(8,128)(2,1)} %collective-permute-done.1.refs_1_, bf16[2,128,1280]{2,1,0:T(8,128)(2,1)S(1)} %collective-permute-done.2.refs_2_, f32[256,128]{1,0:T(8,128)S(1)} %broadcast_in_dim.166.refs_3_, ...), custom_call_target="tpu_custom_call" | custom-call | flops 671088640 | bytes 5242880 | tf_op jit(solution)/shard_map/early/pallas_call | solution.py:124
  38.4 1.6 %collective-permute-done.3.refs_2_ = bf16[2,64,1280]{2,1,0:T(8,128)(2,1)} collective-permute-done((bf16[2,64,1280]{2,1,0:T(8,128)(2,1)}, bf16[2,64,1280]{2,1,0:T(8,128)(2,1)}, u32[]{:S(2)}, u32[]{:S(2)}) %collective-permute-start.3) | collective-permute-done | bytes 327712 | tf_op jit(solution)/shard_map/ppermute | solution.py:156
  45.7 6.0 %collective-permute-start.5 = (bf16[2,128,1280]{2,1,0:T(8,128)(2,1)S(1)}, bf16[2,128,1280]{2,1,0:T(8,128)(2,1)S(1)}, u32[]{:S(2)}, u32[]{:S(2)}) collective-permute-start(bf16[2,128,1280]{2,1,0:T(8,128)(2,1)S(1)} %pad_maximum_fusion), channel_id=1, source_target_pairs={{0,4},{1,5},{2,6},{3,7},{4,0},{5,1},{6,2},{7,3},{8,12},{9,13},{10,... | collective-permute-start | bytes 1966088 | tf_op jit(solution)/shard_map/ppermute | solution.py:156
  53.1 6.4 %first.1 = (f32[10,8,512]{2,1,0:T(8,128)S(1)}, f32[10,128,512]{2,1,0:T(8,128)S(1)}) custom-call(bf16[512,1280]{1,0:T(8,128)(2,1)S(1)} %copy-done.2, bf16[2,256,1280]{2,1,0:T(8,128)(2,1)} %collective-permute-done.refs_1_, bf16[2,64,1280]{2,1,0:T(8,128)(2,1)} %collective-permute-done.3.refs_2_, f32[320,128]{1,0:T(8,128)S(1)} %broadcast_in_dim.171.refs_3_, ...), custom_call_target="tpu_custom_call" | custom-call | flops 838860800 | bytes 5242880 | tf_op jit(solution)/shard_map/first/pallas_call | solution.py:124
  59.5 3.4 %collective-permute-done.7.refs_3_ = bf16[2,64,1280]{2,1,0:T(8,128)(2,1)S(1)} collective-permute-done((bf16[2,64,1280]{2,1,0:T(8,128)(2,1)}, bf16[2,64,1280]{2,1,0:T(8,128)(2,1)S(1)}, u32[]{:S(2)}, u32[]{:S(2)}) %collective-permute-start.7) | collective-permute-done | bytes 327712 | tf_op jit(solution)/shard_map/ppermute | solution.py:156
  62.9 1.9 %collective-permute-start.8 = (bf16[2,64,1280]{2,1,0:T(8,128)(2,1)S(1)}, bf16[2,64,1280]{2,1,0:T(8,128)(2,1)S(1)}, u32[]{:S(2)}, u32[]{:S(2)}) collective-permute-start(bf16[2,64,1280]{2,1,0:T(8,128)(2,1)S(1)} %collective-permute-done.7.refs_3_), channel_id=1, source_target_pairs={{0,4},{1,5},{2,6},{3,7},{4,0},{5,1},{6,2},{7,3},{24,28},{25,29},{2... | collective-permute-start | bytes 983048 | tf_op jit(solution)/shard_map/ppermute | solution.py:156
  64.8 1.5 %collective-permute-start.9 = (bf16[2,64,1280]{2,1,0:T(8,128)(2,1)S(1)}, bf16[2,64,1280]{2,1,0:T(8,128)(2,1)S(1)}, u32[]{:S(2)}, u32[]{:S(2)}) collective-permute-start(bf16[2,64,1280]{2,1,0:T(8,128)(2,1)S(1)} %collective-permute-done.6.refs_1_), channel_id=1, source_target_pairs={{0,8},{1,9},{2,10},{3,11},{8,16},{9,17},{10,18},{11,19},{12,4},{13... | collective-permute-start | bytes 983048 | tf_op jit(solution)/shard_map/ppermute | solution.py:156
  66.3 3.4 %constant_dynamic-slice_fusion = (bf16[1280,1280]{1,0:T(8,128)(2,1)S(1)}, bf16[1280,1280]{1,0:T(8,128)(2,1)S(1)}) fusion(bf16[1280,5120]{1,0:T(8,128)(2,1)} %collective-permute-done.4, s32[]{:T(128)S(6)} %select_n.116, s32[]{:T(128)S(6)} %select_n.115), kind=kLoop, calls=%fused_computation.48 | loop fusion | bytes 13107208 | tf_op jit(solution)/shard_map/dynamic_slice | solution.py:191
  69.7 7.3 %collective-permute-done.10.refs_2_ = bf16[2,128,1280]{2,1,0:T(8,128)(2,1)S(1)} collective-permute-done((bf16[2,128,1280]{2,1,0:T(8,128)(2,1)S(1)}, bf16[2,128,1280]{2,1,0:T(8,128)(2,1)S(1)}, u32[]{:S(2)}, u32[]{:S(2)}) %collective-permute-start.10) | collective-permute-done | bytes 655392 | tf_op jit(solution)/shard_map/ppermute | solution.py:156
  77.1 5.5 %middle.1 = (f32[10,8,512]{2,1,0:T(8,128)S(1)}, f32[10,128,512]{2,1,0:T(8,128)S(1)}) custom-call(bf16[512,1280]{1,0:T(8,128)(2,1)S(1)} %copy-done.2, bf16[2,64,1280]{2,1,0:T(8,128)(2,1)S(1)} %collective-permute-done.6.refs_1_, bf16[2,128,1280]{2,1,0:T(8,128)(2,1)S(1)} %collective-permute-done.10.refs_2_, ...), custom_call_target="tpu_custom_call" | custom-call | flops 1006632960 | bytes 5242880 | tf_op jit(solution)/shard_map/middle/pallas_call | solution.py:124
  82.7 1.9 %last0.1 = bf16[512,512]{1,0:T(8,128)(2,1)S(1)} custom-call(bf16[512,1280]{1,0:T(8,128)(2,1)S(1)} %copy-done.2, bf16[2,128,1280]{2,1,0:T(8,128)(2,1)S(1)} %collective-permute-done.5.refs_1_, bf16[2,64,1280]{2,1,0:T(8,128)(2,1)S(1)} %collective-permute-done.8.refs_2_, bf16[2,64,1280]{2,1,0:T(8,128)(2,1)S(1)} %collective-permute-done.9.refs_3_, ...), custom_call_target="tpu_custom_call" | custom-call | flops 268435456 | bytes 2097152 | tf_op jit(solution)/shard_map/last0/pallas_call | solution.py:124
  84.6 2.8 %last4.1 = bf16[512,768]{1,0:T(8,128)(2,1)S(1)} custom-call(bf16[512,1280]{1,0:T(8,128)(2,1)S(1)} %copy-done.2, bf16[2,128,1280]{2,1,0:T(8,128)(2,1)S(1)} %collective-permute-done.5.refs_1_, bf16[2,64,1280]{2,1,0:T(8,128)(2,1)S(1)} %collective-permute-done.8.refs_2_, bf16[2,64,1280]{2,1,0:T(8,128)(2,1)S(1)} %collective-permute-done.9.refs_3_, ...), custom_call_target="tpu_custom_call" | custom-call | flops 402653184 | bytes 3145728 | tf_op jit(solution)/shard_map/last4/pallas_call | solution.py:124
  91.3 2.2 %collective-permute-start.14 = (bf16[512,640]{1,0:T(8,128)(2,1)S(1)}, bf16[512,640]{1,0:T(8,128)(2,1)S(1)}, u32[]{:S(2)}, u32[]{:S(2)}) collective-permute-start(bf16[512,640]{1,0:T(8,128)(2,1)S(1)} %fusion.10), channel_id=1, source_target_pairs={{0,2},{1,3},{2,0},{3,1},{4,6},{5,7},{6,4},{7,5},{8,10},{9,11},{10,... | collective-permute-start | bytes 1966088 | tf_op jit(solution)/shard_map/ppermute | solution.py:156
  100.5 8.5 %collective-permute-done.14 = bf16[512,640]{1,0:T(8,128)(2,1)S(1)} collective-permute-done((bf16[512,640]{1,0:T(8,128)(2,1)S(1)}, bf16[512,640]{1,0:T(8,128)(2,1)S(1)}, u32[]{:S(2)}, u32[]{:S(2)}) %collective-permute-start.14) | collective-permute-done | bytes 655392 | tf_op jit(solution)/shard_map/ppermute | solution.py:156
  109.0 13.7 %collective-permute-done.15 = bf16[512,640]{1,0:T(8,128)(2,1)S(1)} collective-permute-done((bf16[512,640]{1,0:T(8,128)(2,1)S(1)}, bf16[512,640]{1,0:T(8,128)(2,1)S(1)}, u32[]{:S(2)}, u32[]{:S(2)}) %collective-permute-start.15) | collective-permute-done | bytes 655392 | tf_op jit(solution)/shard_map/ppermute | solution.py:156
  (93 shorter events, 24.1 us)
Async XLA Ops:
  0.0 24.4 %copy-start = (s32[8,8]{1,0:T(8,128)S(1)}, s32[8,8]{1,0:T(8,128)}, u32[]{:S(2)}) copy-start(s32[8,8]{1,0:T(8,128)} %param.16) | copy-start | bytes 772
  0.0 15.3 %copy-start.2 = (bf16[512,1280]{1,0:T(8,128)(2,1)S(1)}, bf16[512,1280]{1,0:T(8,128)(2,1)}, u32[]{:S(2)}) copy-start(bf16[512,1280]{1,0:T(8,128)(2,1)} %refs_0_.13) | copy-start | bytes 3932164
  0.0 39.9 %collective-permute-start.4 = (bf16[1280,5120]{1,0:T(8,128)(2,1)}, bf16[1280,5120]{1,0:T(8,128)(2,1)}, u32[]{:S(2)}, u32[]{:S(2)}) collective-permute-start(bf16[1280,5120]{1,0:T(8,128)(2,1)} %param.17), channel_id=1, source_target_pairs={{0,1},{1,0},{2,3},{3,2},{4,5},{5,4},{6,7},{7,6},{8,9},{9,8},{10,11... | collective-permute-start | bytes 39321608 | tf_op jit(solution)/shard_map/ppermute | solution.py:156
  2.8 12.5 %copy-start.4 = (bf16[512,1280]{1,0:T(8,128)(2,1)S(1)}, bf16[512,1280]{1,0:T(8,128)(2,1)}, u32[]{:S(2)}) copy-start(bf16[512,1280]{1,0:T(8,128)(2,1)} %refs_1_.3) | copy-start | bytes 3932164
  5.3 20.3 %copy-start.16 = (pred[2,256]{1,0:T(4,128)(4,1)S(1)}, pred[2,256]{1,0:T(4,128)(4,1)}, u32[]{:S(2)}) copy-start(pred[2,256]{1,0:T(4,128)(4,1)} %constant.80.clone) | copy-start | bytes 1540
  5.3 20.6 %copy-start.15 = (pred[4,256]{1,0:T(4,128)(4,1)S(1)}, pred[4,256]{1,0:T(4,128)(4,1)}, u32[]{:S(2)}) copy-start(pred[4,256]{1,0:T(4,128)(4,1)} %constant.86.clone) | copy-start | bytes 3076
  5.3 20.7 %copy-start.14 = (s32[256]{0:T(256)S(1)}, s32[256]{0:T(256)}, u32[]{:S(2)}) copy-start(s32[256]{0:T(256)} %constant.81.clone) | copy-start | bytes 3076
  5.3 20.7 %copy-start.13 = (s32[256]{0:T(256)S(1)}, s32[256]{0:T(256)}, u32[]{:S(2)}) copy-start(s32[256]{0:T(256)} %constant.87.clone) | copy-start | bytes 3076
  5.3 34.6 %collective-permute-start = (bf16[2,256,1280]{2,1,0:T(8,128)(2,1)}, bf16[2,256,1280]{2,1,0:T(8,128)(2,1)}, u32[]{:S(2)}, u32[]{:S(2)}) collective-permute-start(bf16[2,256,1280]{2,1,0:T(8,128)(2,1)} %get-tuple-element.51), channel_id=1, source_target_pairs={{0,4},{1,5},{2,6},{3,7},{4,0},{5,1},{6,2},{7,3},{8,12},{9,13},{10,... | collective-permute-start | bytes 3932168 | tf_op jit(solution)/shard_map/ppermute | solution.py:156
  5.4 24.5 %collective-permute-start.1 = (bf16[2,128,1280]{2,1,0:T(8,128)(2,1)}, bf16[2,128,1280]{2,1,0:T(8,128)(2,1)}, u32[]{:S(2)}, u32[]{:S(2)}) collective-permute-start(bf16[2,128,1280]{2,1,0:T(8,128)(2,1)} %get-tuple-element.52), channel_id=1, source_target_pairs={{0,8},{1,9},{2,10},{3,11},{8,16},{9,17},{10,18},{11,19},{12,4},{13... | collective-permute-start | bytes 1966088 | tf_op jit(solution)/shard_map/ppermute | solution.py:156
  6.7 23.2 %collective-permute-start.2 = (bf16[2,128,1280]{2,1,0:T(8,128)(2,1)}, bf16[2,128,1280]{2,1,0:T(8,128)(2,1)S(1)}, u32[]{:S(2)}, u32[]{:S(2)}) collective-permute-start(bf16[2,128,1280]{2,1,0:T(8,128)(2,1)} %get-tuple-element.53), channel_id=1, source_target_pairs={{4,12},{5,13},{6,14},{7,15},{8,0},{9,1},{10,2},{11,3},{12,20},{13,... | collective-permute-start | bytes 1966088 | tf_op jit(solution)/shard_map/ppermute | solution.py:156
  11.3 28.6 %collective-permute-start.3 = (bf16[2,64,1280]{2,1,0:T(8,128)(2,1)}, bf16[2,64,1280]{2,1,0:T(8,128)(2,1)}, u32[]{:S(2)}, u32[]{:S(2)}) collective-permute-start(bf16[2,64,1280]{2,1,0:T(8,128)(2,1)} %get-tuple-element.58), channel_id=1, source_target_pairs={{0,16},{1,17},{2,18},{3,19},{4,20},{5,21},{6,22},{7,23},{8,24},{9,... | collective-permute-start | bytes 983048 | tf_op jit(solution)/shard_map/ppermute | solution.py:156
  29.9 47.1 %collective-permute-start.11 = (bf16[2,128,1280]{2,1,0:T(8,128)(2,1)}, bf16[2,128,1280]{2,1,0:T(8,128)(2,1)S(1)}, u32[]{:S(2)}, u32[]{:S(2)}) collective-permute-start(bf16[2,128,1280]{2,1,0:T(8,128)(2,1)} %collective-permute-done.1.refs_1_), channel_id=1, source_target_pairs={{4,0},{5,1},{6,2},{7,3},{8,12},{9,13},{10,14},{11,15},{12,8},{13,9... | collective-permute-start | bytes 1966088 | tf_op jit(solution)/shard_map/ppermute | solution.py:156
  42.1 17.4 %collective-permute-start.6 = (bf16[2,64,1280]{2,1,0:T(8,128)(2,1)S(1)}, bf16[2,64,1280]{2,1,0:T(8,128)(2,1)S(1)}, u32[]{:S(2)}, u32[]{:S(2)}) collective-permute-start(bf16[2,64,1280]{2,1,0:T(8,128)(2,1)S(1)} %slice.46), channel_id=1, source_target_pairs={{0,8},{1,9},{2,10},{3,11},{8,16},{9,17},{10,18},{11,19},{12,4},{13... | collective-permute-start | bytes 983048 | tf_op jit(solution)/shard_map/ppermute | solution.py:156
  43.4 19.5 %collective-permute-start.7 = (bf16[2,64,1280]{2,1,0:T(8,128)(2,1)}, bf16[2,64,1280]{2,1,0:T(8,128)(2,1)S(1)}, u32[]{:S(2)}, u32[]{:S(2)}) collective-permute-start(bf16[2,64,1280]{2,1,0:T(8,128)(2,1)} %collective-permute-done.3.refs_2_), channel_id=1, source_target_pairs={{8,0},{9,1},{10,2},{11,3},{12,4},{13,5},{14,6},{15,7},{16,24},{17,... | collective-permute-start | bytes 983048 | tf_op jit(solution)/shard_map/ppermute | solution.py:156
  45.7 36.9 %collective-permute-start.5 = (bf16[2,128,1280]{2,1,0:T(8,128)(2,1)S(1)}, bf16[2,128,1280]{2,1,0:T(8,128)(2,1)S(1)}, u32[]{:S(2)}, u32[]{:S(2)}) collective-permute-start(bf16[2,128,1280]{2,1,0:T(8,128)(2,1)S(1)} %pad_maximum_fusion), channel_id=1, source_target_pairs={{0,4},{1,5},{2,6},{3,7},{4,0},{5,1},{6,2},{7,3},{8,12},{9,13},{10,... | collective-permute-start | bytes 1966088 | tf_op jit(solution)/shard_map/ppermute | solution.py:156
  51.7 25.3 %collective-permute-start.10 = (bf16[2,128,1280]{2,1,0:T(8,128)(2,1)S(1)}, bf16[2,128,1280]{2,1,0:T(8,128)(2,1)S(1)}, u32[]{:S(2)}, u32[]{:S(2)}) collective-permute-start(bf16[2,128,1280]{2,1,0:T(8,128)(2,1)S(1)} %slice.47), channel_id=1, source_target_pairs={{0,8},{1,9},{2,10},{3,11},{8,16},{9,17},{10,18},{11,19},{12,4},{13... | collective-permute-start | bytes 1966088 | tf_op jit(solution)/shard_map/ppermute | solution.py:156
  62.9 19.7 %collective-permute-start.8 = (bf16[2,64,1280]{2,1,0:T(8,128)(2,1)S(1)}, bf16[2,64,1280]{2,1,0:T(8,128)(2,1)S(1)}, u32[]{:S(2)}, u32[]{:S(2)}) collective-permute-start(bf16[2,64,1280]{2,1,0:T(8,128)(2,1)S(1)} %collective-permute-done.7.refs_3_), channel_id=1, source_target_pairs={{0,4},{1,5},{2,6},{3,7},{4,0},{5,1},{6,2},{7,3},{24,28},{25,29},{2... | collective-permute-start | bytes 983048 | tf_op jit(solution)/shard_map/ppermute | solution.py:156
  64.8 17.8 %collective-permute-start.9 = (bf16[2,64,1280]{2,1,0:T(8,128)(2,1)S(1)}, bf16[2,64,1280]{2,1,0:T(8,128)(2,1)S(1)}, u32[]{:S(2)}, u32[]{:S(2)}) collective-permute-start(bf16[2,64,1280]{2,1,0:T(8,128)(2,1)S(1)} %collective-permute-done.6.refs_1_), channel_id=1, source_target_pairs={{0,8},{1,9},{2,10},{3,11},{8,16},{9,17},{10,18},{11,19},{12,4},{13... | collective-permute-start | bytes 983048 | tf_op jit(solution)/shard_map/ppermute | solution.py:156
  84.6 4.2 %collective-permute-start.12 = (bf16[512,512]{1,0:T(8,128)(2,1)S(1)}, bf16[512,512]{1,0:T(8,128)(2,1)S(1)}, u32[]{:S(2)}, u32[]{:S(2)}) collective-permute-start(bf16[512,512]{1,0:T(8,128)(2,1)S(1)} %last0.1), channel_id=1, source_target_pairs={{0,1},{1,0},{2,3},{3,2},{4,5},{5,4},{6,7},{7,6},{8,9},{9,8},{10,11... | collective-permute-start | bytes 1572872 | tf_op jit(solution)/shard_map/ppermute | solution.py:156
  87.4 2.5 %collective-permute-start.13 = (bf16[512,768]{1,0:T(8,128)(2,1)S(1)}, bf16[512,768]{1,0:T(8,128)(2,1)S(1)}, u32[]{:S(2)}, u32[]{:S(2)}) collective-permute-start(bf16[512,768]{1,0:T(8,128)(2,1)S(1)} %last4.1), channel_id=1, source_target_pairs={{0,1},{1,0},{2,3},{3,2},{4,5},{5,4},{6,7},{7,6},{8,9},{9,8},{10,11... | collective-permute-start | bytes 2359304 | tf_op jit(solution)/shard_map/ppermute | solution.py:156
  91.3 17.7 %collective-permute-start.14 = (bf16[512,640]{1,0:T(8,128)(2,1)S(1)}, bf16[512,640]{1,0:T(8,128)(2,1)S(1)}, u32[]{:S(2)}, u32[]{:S(2)}) collective-permute-start(bf16[512,640]{1,0:T(8,128)(2,1)S(1)} %fusion.10), channel_id=1, source_target_pairs={{0,2},{1,3},{2,0},{3,1},{4,6},{5,7},{6,4},{7,5},{8,10},{9,11},{10,... | collective-permute-start | bytes 1966088 | tf_op jit(solution)/shard_map/ppermute | solution.py:156
  96.2 26.6 %collective-permute-start.15 = (bf16[512,640]{1,0:T(8,128)(2,1)S(1)}, bf16[512,640]{1,0:T(8,128)(2,1)S(1)}, u32[]{:S(2)}, u32[]{:S(2)}) collective-permute-start(bf16[512,640]{1,0:T(8,128)(2,1)S(1)} %fusion.11), channel_id=1, source_target_pairs={{0,2},{1,3},{2,0},{3,1},{4,6},{5,7},{6,4},{7,5},{8,10},{9,11},{10,... | collective-permute-start | bytes 1966088 | tf_op jit(solution)/shard_map/ppermute | solution.py:156
  99.5 24.5 %copy-start.1 = (s32[8,8]{1,0:T(8,128)S(1)}, s32[8,8]{1,0:T(8,128)}, u32[]{:S(2)}) copy-start(s32[8,8]{1,0:T(8,128)} %param.16) | copy-start | bytes 772
  (9 other events, 27.0 us)

commit v11 on v10

--- a/solution.py
+++ b/solution.py
@@ -243,22 +243,22 @@
         weights = weights + blocks_of(moved)
         chain_b = move(near_b, near_of)
         cross_three = move(z_three, lambda t: t ^ 1 if t in ends else None)
-        near_c, state, weights = lax.optimization_barrier((near_c, state, weights))
+        state, weights = lax.optimization_barrier((state, weights))
         carry = further(
-            [near_b, near_c, z_three, cross_far],
+            [near_b, z_three, cross_far, cross_two],
             [
                 (adjacent, a, ab - a),
-                (adjacent, ab, near - ab),
                 (three, 0, a),
                 (far_cross, 0, ab),
+                (adjacent, 0, a),
+                (two ^ 1, 0, a),
             ],
             (state, carry[1]),
             "middle",
         )
-        buffers = [cross_two, cross_three, chain_b]
+        buffers = [near_c, cross_three, chain_b]
         pieces = [
-            (adjacent, 0, a),
-            (two ^ 1, 0, a),
+            (adjacent, ab, near - ab),
             (jnp.where(at_end, opposite ^ 1, -1), 0, a),
             (my_block - 3 * side, a, ab - a),
         ]

time: 125 us -> 129 us (1.032)
  starting transfers between devices: 29.1 us -> 33.5 us
  waiting for transfers between devices: 35 us -> 33.6 us
    ppermute x16, starting transfers between devices: 29.1 us -> 33.5 us  [move(): return lax.ppermute(array, AXES, route)]
    ppermute x16, waiting for transfers between devices: 35 us -> 33.6 us  [move(): return lax.ppermute(array, AXES, route)]
  transfers between devices with their start and end apart: 16 -> 16, of which waited for: 6 -> 7; matrix products, arithmetic and copies ran while one was open for 16% -> 16% of each run, Pallas kernels for 23% -> 23%
where the time goes in v11:
time: 129 us; the launch traced here: 127 us
  waiting for transfers between devices  33.6 us (26%)
  starting transfers between devices  33.5 us (26%)
  Pallas kernels  30.8 us (24%)
  local copies, waits for them, and re-layouts  15.1 us (12%)
  matrix products  9.64 us (7%)
  other arithmetic  4.2 us (3%)
    ppermute x16, waiting for transfers between devices, move(): return lax.ppermute(array, AXES, route)  33.6 us
    ppermute x16, starting transfers between devices, move(): return lax.ppermute(array, AXES, route)  33.5 us
    pallas_call x6, Pallas kernels, attend(): pl.pallas_call(lambda *refs: attend_kernel(*refs, buffers=len(buffers), o...  28.3 us
    dynamic_slice x2, local copies, waits for them, and re-layouts, blocks_of(): lax.dynamic_slice_in_dim(source, number * out_width, out_width, 1)  6.87 us
    unnamed x34, local copies, waits for them, and re-layouts  5.58 us
    dot_general x6, matrix products, project(): jnp.dot(other, weights[index + 2][low:high, first:last], preferred_elemen...  4.87 us
    dot_general x6, matrix products, project(): jnp.dot(part, weights[index][low:high, first:last], preferred_element_typ...  4.78 us
  transfers between devices with their start and end apart: 16, of which 7 were waited for; matrix products, arithmetic and copies ran while one was open for 16% of the time, Pallas kernels for 23%

profile of v11, /device:TPU:2, one launch (start us, length us, event | category | flops | bytes accessed | tf_op | source)
XLA Modules:
  0.0 127.3 jit_solution(10205127935924421240)
XLA Ops:
  0.0 1.4 %copy-done.3 = bf16[512,1280]{1,0:T(8,128)(2,1)S(1)} copy-done((bf16[512,1280]{1,0:T(8,128)(2,1)S(1)}, bf16[512,1280]{1,0:T(8,128)(2,1)}, u32[]{:S(2)}) %copy-start.3) | copy-done | bytes 1310744
  2.8 2.5 %pack.1 = (bf16[2,256,1280]{2,1,0:T(8,128)(2,1)}, bf16[2,128,1280]{2,1,0:T(8,128)(2,1)}, bf16[2,128,1280]{2,1,0:T(8,128)(2,1)}, bf16[2,64,1280]{2,1,0:T(8,128)(2,1)}) custom-call(bf16[512,1280]{1,0:T(8,128)(2,1)S(1)} %copy-done.3, bf16[512,1280]{1,0:T(8,128)(2,1)S(1)} %copy-done.5), custom_call_target="tpu_custom_call" | custom-call | flops 671088640 | bytes 5242880 | tf_op jit(solution)/shard_map/pack/pallas_call | solution.py:39
  5.3 2.7 %collective-permute-start.3 = (bf16[2,64,1280]{2,1,0:T(8,128)(2,1)}, bf16[2,64,1280]{2,1,0:T(8,128)(2,1)}, u32[]{:S(2)}, u32[]{:S(2)}) collective-permute-start(bf16[2,64,1280]{2,1,0:T(8,128)(2,1)} %get-tuple-element.57), channel_id=1, source_target_pairs={{0,16},{1,17},{2,18},{3,19},{4,20},{5,21},{6,22},{7,23},{8,24},{9,... | collective-permute-start | bytes 983048 | tf_op jit(solution)/shard_map/ppermute | solution.py:156
  9.2 4.6 %collective-permute-start.2 = (bf16[2,128,1280]{2,1,0:T(8,128)(2,1)}, bf16[2,128,1280]{2,1,0:T(8,128)(2,1)S(1)}, u32[]{:S(2)}, u32[]{:S(2)}) collective-permute-start(bf16[2,128,1280]{2,1,0:T(8,128)(2,1)} %get-tuple-element.52), channel_id=1, source_target_pairs={{4,12},{5,13},{6,14},{7,15},{8,0},{9,1},{10,2},{11,3},{12,20},{13,... | collective-permute-start | bytes 1966088 | tf_op jit(solution)/shard_map/ppermute | solution.py:156
  15.5 6.4 %own.1 = (f32[10,8,512]{2,1,0:T(8,128)S(1)}, f32[10,128,512]{2,1,0:T(8,128)S(1)}) custom-call(bf16[512,1280]{1,0:T(8,128)(2,1)S(1)} %copy-done.2, bf16[512,1280]{1,0:T(8,128)(2,1)S(1)} %copy-done.4, bf16[512,1280]{1,0:T(8,128)(2,1)S(1)} %copy-done.6), custom_call_target="tpu_custom_call" | custom-call | tf_op jit(solution)/shard_map/own/pallas_call | solution.py:124
  21.9 1.5 %copy-done.7 = f32[10,128,512]{2,1,0:T(8,128)} copy-done((f32[10,128,512]{2,1,0:T(8,128)}, f32[10,128,512]{2,1,0:T(8,128)S(1)}, u32[]{:S(2)}) %copy-start.7) | copy-done | bytes 2621464
  25.3 3.5 %constant_dynamic-slice_fusion.3 = (bf16[1280,1280]{1,0:T(8,128)(2,1)S(1)}, bf16[1280,1280]{1,0:T(8,128)(2,1)S(1)}) fusion(bf16[1280,5120]{1,0:T(8,128)(2,1)} %param.17, s32[]{:T(128)S(6)} %select_n.118, s32[]{:T(128)S(6)} %select_n.117), kind=kLoop, calls=%fused_computation.51 | loop fusion | bytes 13107208 | tf_op jit(solution)/shard_map/dynamic_slice | solution.py:191
  29.0 3.8 %collective-permute-done.1.refs_1_ = bf16[2,128,1280]{2,1,0:T(8,128)(2,1)} collective-permute-done((bf16[2,128,1280]{2,1,0:T(8,128)(2,1)}, bf16[2,128,1280]{2,1,0:T(8,128)(2,1)}, u32[]{:S(2)}, u32[]{:S(2)}) %collective-permute-start.1) | collective-permute-done | bytes 655392 | tf_op jit(solution)/shard_map/ppermute | solution.py:156
  32.8 6.3 %collective-permute-start.10 = (bf16[2,128,1280]{2,1,0:T(8,128)(2,1)}, bf16[2,128,1280]{2,1,0:T(8,128)(2,1)S(1)}, u32[]{:S(2)}, u32[]{:S(2)}) collective-permute-start(bf16[2,128,1280]{2,1,0:T(8,128)(2,1)} %collective-permute-done.1.refs_1_), channel_id=1, source_target_pairs={{4,0},{5,1},{6,2},{7,3},{8,12},{9,13},{10,14},{11,15},{12,8},{13,9... | collective-permute-start | bytes 1966088 | tf_op jit(solution)/shard_map/ppermute | solution.py:156
  39.3 5.4 %early.1 = (f32[10,8,512]{2,1,0:T(8,128)S(1)}, f32[10,128,512]{2,1,0:T(8,128)S(1)}) custom-call(bf16[512,1280]{1,0:T(8,128)(2,1)S(1)} %copy-done.2, bf16[2,128,1280]{2,1,0:T(8,128)(2,1)} %collective-permute-done.1.refs_1_, bf16[2,128,1280]{2,1,0:T(8,128)(2,1)S(1)} %collective-permute-done.2.refs_2_, f32[256,128]{1,0:T(8,128)S(1)} %broadcast_in_dim.177.refs_3_, ...), custom_call_target="tpu_custom_call" | custom-call | flops 671088640 | bytes 5242880 | tf_op jit(solution)/shard_map/early/pallas_call | solution.py:124
  51.8 8.2 %collective-permute-start.11 = (bf16[2,128,1280]{2,1,0:T(8,128)(2,1)S(1)}, bf16[2,128,1280]{2,1,0:T(8,128)(2,1)S(1)}, u32[]{:S(2)}, u32[]{:S(2)}) collective-permute-start(bf16[2,128,1280]{2,1,0:T(8,128)(2,1)S(1)} %pad_maximum_fusion), channel_id=1, source_target_pairs={{0,4},{1,5},{2,6},{3,7},{4,0},{5,1},{6,2},{7,3},{8,12},{9,13},{10,... | collective-permute-start | bytes 1966088 | tf_op jit(solution)/shard_map/ppermute | solution.py:156
  60.1 6.4 %first.1 = (f32[10,8,512]{2,1,0:T(8,128)S(1)}, f32[10,128,512]{2,1,0:T(8,128)S(1)}) custom-call(bf16[512,1280]{1,0:T(8,128)(2,1)S(1)} %copy-done.2, bf16[2,256,1280]{2,1,0:T(8,128)(2,1)} %collective-permute-done.refs_1_, bf16[2,64,1280]{2,1,0:T(8,128)(2,1)} %collective-permute-done.3.refs_2_, f32[320,128]{1,0:T(8,128)S(1)} %broadcast_in_dim.182.refs_3_, ...), custom_call_target="tpu_custom_call" | custom-call | flops 838860800 | bytes 5242880 | tf_op jit(solution)/shard_map/first/pallas_call | solution.py:124
  67.2 1.9 %collective-permute-start.8 = (bf16[2,64,1280]{2,1,0:T(8,128)(2,1)S(1)}, bf16[2,64,1280]{2,1,0:T(8,128)(2,1)S(1)}, u32[]{:S(2)}, u32[]{:S(2)}) collective-permute-start(bf16[2,64,1280]{2,1,0:T(8,128)(2,1)S(1)} %collective-permute-done.7.refs_2_), channel_id=1, source_target_pairs={{0,4},{1,5},{2,6},{3,7},{4,0},{5,1},{6,2},{7,3},{24,28},{25,29},{2... | collective-permute-start | bytes 983048 | tf_op jit(solution)/shard_map/ppermute | solution.py:156
  69.1 1.5 %collective-permute-start.9 = (bf16[2,64,1280]{2,1,0:T(8,128)(2,1)S(1)}, bf16[2,64,1280]{2,1,0:T(8,128)(2,1)S(1)}, u32[]{:S(2)}, u32[]{:S(2)}) collective-permute-start(bf16[2,64,1280]{2,1,0:T(8,128)(2,1)S(1)} %collective-permute-done.6.refs_1_), channel_id=1, source_target_pairs={{0,8},{1,9},{2,10},{3,11},{8,16},{9,17},{10,18},{11,19},{12,4},{13... | collective-permute-start | bytes 983048 | tf_op jit(solution)/shard_map/ppermute | solution.py:156
  70.6 3.4 %constant_dynamic-slice_fusion = (bf16[1280,1280]{1,0:T(8,128)(2,1)S(1)}, bf16[1280,1280]{1,0:T(8,128)(2,1)S(1)}) fusion(bf16[1280,5120]{1,0:T(8,128)(2,1)} %collective-permute-done.4, s32[]{:T(128)S(6)} %select_n.118, s32[]{:T(128)S(6)} %select_n.117), kind=kLoop, calls=%fused_computation.48 | loop fusion | bytes 13107208 | tf_op jit(solution)/shard_map/dynamic_slice | solution.py:191
  73.9 1.7 %collective-permute-done.11.refs_4_ = bf16[2,128,1280]{2,1,0:T(8,128)(2,1)S(1)} collective-permute-done((bf16[2,128,1280]{2,1,0:T(8,128)(2,1)S(1)}, bf16[2,128,1280]{2,1,0:T(8,128)(2,1)S(1)}, u32[]{:S(2)}, u32[]{:S(2)}) %collective-permute-start.11) | collective-permute-done | bytes 655392 | tf_op jit(solution)/shard_map/ppermute | solution.py:156
  75.7 5.5 %middle.1 = (f32[10,8,512]{2,1,0:T(8,128)S(1)}, f32[10,128,512]{2,1,0:T(8,128)S(1)}) custom-call(bf16[512,1280]{1,0:T(8,128)(2,1)S(1)} %copy-done.2, bf16[2,64,1280]{2,1,0:T(8,128)(2,1)S(1)} %collective-permute-done.6.refs_1_, bf16[2,64,1280]{2,1,0:T(8,128)(2,1)S(1)} %collective-permute-done.7.refs_2_, ...), custom_call_target="tpu_custom_call" | custom-call | flops 1006632960 | bytes 5242880 | tf_op jit(solution)/shard_map/middle/pallas_call | solution.py:124
  81.3 4.9 %collective-permute-done.9.refs_3_ = bf16[2,64,1280]{2,1,0:T(8,128)(2,1)S(1)} collective-permute-done((bf16[2,64,1280]{2,1,0:T(8,128)(2,1)S(1)}, bf16[2,64,1280]{2,1,0:T(8,128)(2,1)S(1)}, u32[]{:S(2)}, u32[]{:S(2)}) %collective-permute-start.9) | collective-permute-done | bytes 327712 | tf_op jit(solution)/shard_map/ppermute | solution.py:156
  86.2 1.9 %last0.1 = bf16[512,512]{1,0:T(8,128)(2,1)S(1)} custom-call(bf16[512,1280]{1,0:T(8,128)(2,1)S(1)} %copy-done.2, bf16[2,128,1280]{2,1,0:T(8,128)(2,1)S(1)} %collective-permute-done.5.refs_1_, bf16[2,64,1280]{2,1,0:T(8,128)(2,1)S(1)} %collective-permute-done.8.refs_2_, bf16[2,64,1280]{2,1,0:T(8,128)(2,1)S(1)} %collective-permute-done.9.refs_3_, ...), custom_call_target="tpu_custom_call" | custom-call | flops 268435456 | bytes 2097152 | tf_op jit(solution)/shard_map/last0/pallas_call | solution.py:124
  88.2 2.8 %last4.1 = bf16[512,768]{1,0:T(8,128)(2,1)S(1)} custom-call(bf16[512,1280]{1,0:T(8,128)(2,1)S(1)} %copy-done.2, bf16[2,128,1280]{2,1,0:T(8,128)(2,1)S(1)} %collective-permute-done.5.refs_1_, bf16[2,64,1280]{2,1,0:T(8,128)(2,1)S(1)} %collective-permute-done.8.refs_2_, bf16[2,64,1280]{2,1,0:T(8,128)(2,1)S(1)} %collective-permute-done.9.refs_3_, ...), custom_call_target="tpu_custom_call" | custom-call | flops 402653184 | bytes 3145728 | tf_op jit(solution)/shard_map/last4/pallas_call | solution.py:124
  94.8 1.6 %collective-permute-start.14 = (bf16[512,640]{1,0:T(8,128)(2,1)S(1)}, bf16[512,640]{1,0:T(8,128)(2,1)S(1)}, u32[]{:S(2)}, u32[]{:S(2)}) collective-permute-start(bf16[512,640]{1,0:T(8,128)(2,1)S(1)} %fusion.10), channel_id=1, source_target_pairs={{0,2},{1,3},{2,0},{3,1},{4,6},{5,7},{6,4},{7,5},{8,10},{9,11},{10,... | collective-permute-start | bytes 1966088 | tf_op jit(solution)/shard_map/ppermute | solution.py:156
  103.9 8.5 %collective-permute-done.14 = bf16[512,640]{1,0:T(8,128)(2,1)S(1)} collective-permute-done((bf16[512,640]{1,0:T(8,128)(2,1)S(1)}, bf16[512,640]{1,0:T(8,128)(2,1)S(1)}, u32[]{:S(2)}, u32[]{:S(2)}) %collective-permute-start.14) | collective-permute-done | bytes 655392 | tf_op jit(solution)/shard_map/ppermute | solution.py:156
  112.4 13.5 %collective-permute-done.15 = bf16[512,640]{1,0:T(8,128)(2,1)S(1)} collective-permute-done((bf16[512,640]{1,0:T(8,128)(2,1)S(1)}, bf16[512,640]{1,0:T(8,128)(2,1)S(1)}, u32[]{:S(2)}, u32[]{:S(2)}) %collective-permute-start.15) | collective-permute-done | bytes 655392 | tf_op jit(solution)/shard_map/ppermute | solution.py:156
  125.9 1.3 %add_convert_fusion = bf16[512,1280]{1,0:T(8,128)(2,1)} fusion(f32[512,1280]{1,0:T(8,128)S(1)} %fusion.1, bf16[512,640]{1,0:T(8,128)(2,1)S(1)} %collective-permute-done.15, bf16[512,640]{1,0:T(8,128)(2,1)S(1)} %collective-permute-done.14), kind=kLoop, calls=%fused_computation.3 | loop fusion | flops 3932160 | bytes 5242880 | tf_op jit(solution)/shard_map/convert_element_type | solution.py:306
  (95 shorter events, 25.8 us)
Async XLA Ops:
  0.0 23.5 %copy-start = (s32[8,8]{1,0:T(8,128)S(1)}, s32[8,8]{1,0:T(8,128)}, u32[]{:S(2)}) copy-start(s32[8,8]{1,0:T(8,128)} %param.16) | copy-start | bytes 772
  0.0 14.2 %copy-start.2 = (bf16[512,1280]{1,0:T(8,128)(2,1)S(1)}, bf16[512,1280]{1,0:T(8,128)(2,1)}, u32[]{:S(2)}) copy-start(bf16[512,1280]{1,0:T(8,128)(2,1)} %refs_0_.13) | copy-start | bytes 3932164
  0.0 44.7 %collective-permute-start.4 = (bf16[1280,5120]{1,0:T(8,128)(2,1)}, bf16[1280,5120]{1,0:T(8,128)(2,1)}, u32[]{:S(2)}, u32[]{:S(2)}) collective-permute-start(bf16[1280,5120]{1,0:T(8,128)(2,1)} %param.17), channel_id=1, source_target_pairs={{0,1},{1,0},{2,3},{3,2},{4,5},{5,4},{6,7},{7,6},{8,9},{9,8},{10,11... | collective-permute-start | bytes 39321608 | tf_op jit(solution)/shard_map/ppermute | solution.py:156
  5.3 19.5 %copy-start.16 = (pred[3,256]{1,0:T(4,128)(4,1)S(1)}, pred[3,256]{1,0:T(4,128)(4,1)}, u32[]{:S(2)}) copy-start(pred[3,256]{1,0:T(4,128)(4,1)} %constant.87.clone) | copy-start | bytes 2308
  5.3 19.8 %copy-start.15 = (pred[2,256]{1,0:T(4,128)(4,1)S(1)}, pred[2,256]{1,0:T(4,128)(4,1)}, u32[]{:S(2)}) copy-start(pred[2,256]{1,0:T(4,128)(4,1)} %constant.81.clone) | copy-start | bytes 1540
  5.3 19.9 %copy-start.14 = (s32[256]{0:T(256)S(1)}, s32[256]{0:T(256)}, u32[]{:S(2)}) copy-start(s32[256]{0:T(256)} %constant.88.clone) | copy-start | bytes 3076
  5.3 19.9 %copy-start.13 = (s32[256]{0:T(256)S(1)}, s32[256]{0:T(256)}, u32[]{:S(2)}) copy-start(s32[256]{0:T(256)} %constant.82.clone) | copy-start | bytes 3076
  5.3 39.3 %collective-permute-start.3 = (bf16[2,64,1280]{2,1,0:T(8,128)(2,1)}, bf16[2,64,1280]{2,1,0:T(8,128)(2,1)}, u32[]{:S(2)}, u32[]{:S(2)}) collective-permute-start(bf16[2,64,1280]{2,1,0:T(8,128)(2,1)} %get-tuple-element.57), channel_id=1, source_target_pairs={{0,16},{1,17},{2,18},{3,19},{4,20},{5,21},{6,22},{7,23},{8,24},{9,... | collective-permute-start | bytes 983048 | tf_op jit(solution)/shard_map/ppermute | solution.py:156
  7.9 24.9 %collective-permute-start.1 = (bf16[2,128,1280]{2,1,0:T(8,128)(2,1)}, bf16[2,128,1280]{2,1,0:T(8,128)(2,1)}, u32[]{:S(2)}, u32[]{:S(2)}) collective-permute-start(bf16[2,128,1280]{2,1,0:T(8,128)(2,1)} %get-tuple-element.51), channel_id=1, source_target_pairs={{0,8},{1,9},{2,10},{3,11},{8,16},{9,17},{10,18},{11,19},{12,4},{13... | collective-permute-start | bytes 1966088 | tf_op jit(solution)/shard_map/ppermute | solution.py:156
  9.2 23.6 %collective-permute-start.2 = (bf16[2,128,1280]{2,1,0:T(8,128)(2,1)}, bf16[2,128,1280]{2,1,0:T(8,128)(2,1)S(1)}, u32[]{:S(2)}, u32[]{:S(2)}) collective-permute-start(bf16[2,128,1280]{2,1,0:T(8,128)(2,1)} %get-tuple-element.52), channel_id=1, source_target_pairs={{4,12},{5,13},{6,14},{7,15},{8,0},{9,1},{10,2},{11,3},{12,20},{13,... | collective-permute-start | bytes 1966088 | tf_op jit(solution)/shard_map/ppermute | solution.py:156
  13.8 30.8 %collective-permute-start = (bf16[2,256,1280]{2,1,0:T(8,128)(2,1)}, bf16[2,256,1280]{2,1,0:T(8,128)(2,1)}, u32[]{:S(2)}, u32[]{:S(2)}) collective-permute-start(bf16[2,256,1280]{2,1,0:T(8,128)(2,1)} %get-tuple-element.50), channel_id=1, source_target_pairs={{0,4},{1,5},{2,6},{3,7},{4,0},{5,1},{6,2},{7,3},{8,12},{9,13},{10,... | collective-permute-start | bytes 3932168 | tf_op jit(solution)/shard_map/ppermute | solution.py:156
  25.3 14.0 %copy-start.8 = (f32[10,128,512]{2,1,0:T(8,128)S(1)}, f32[10,128,512]{2,1,0:T(8,128)}, u32[]{:S(2)}) copy-start(f32[10,128,512]{2,1,0:T(8,128)} %copy-done.7) | copy-start | bytes 7864324
  32.8 41.1 %collective-permute-start.10 = (bf16[2,128,1280]{2,1,0:T(8,128)(2,1)}, bf16[2,128,1280]{2,1,0:T(8,128)(2,1)S(1)}, u32[]{:S(2)}, u32[]{:S(2)}) collective-permute-start(bf16[2,128,1280]{2,1,0:T(8,128)(2,1)} %collective-permute-done.1.refs_1_), channel_id=1, source_target_pairs={{4,0},{5,1},{6,2},{7,3},{8,12},{9,13},{10,14},{11,15},{12,8},{13,9... | collective-permute-start | bytes 1966088 | tf_op jit(solution)/shard_map/ppermute | solution.py:156
  46.8 19.7 %collective-permute-start.6 = (bf16[2,64,1280]{2,1,0:T(8,128)(2,1)S(1)}, bf16[2,64,1280]{2,1,0:T(8,128)(2,1)S(1)}, u32[]{:S(2)}, u32[]{:S(2)}) collective-permute-start(bf16[2,64,1280]{2,1,0:T(8,128)(2,1)S(1)} %slice.46), channel_id=1, source_target_pairs={{0,8},{1,9},{2,10},{3,11},{8,16},{9,17},{10,18},{11,19},{12,4},{13... | collective-permute-start | bytes 983048 | tf_op jit(solution)/shard_map/ppermute | solution.py:156
  48.1 19.0 %collective-permute-start.7 = (bf16[2,64,1280]{2,1,0:T(8,128)(2,1)}, bf16[2,64,1280]{2,1,0:T(8,128)(2,1)S(1)}, u32[]{:S(2)}, u32[]{:S(2)}) collective-permute-start(bf16[2,64,1280]{2,1,0:T(8,128)(2,1)} %collective-permute-done.3.refs_2_), channel_id=1, source_target_pairs={{8,0},{9,1},{10,2},{11,3},{12,4},{13,5},{14,6},{15,7},{16,24},{17,... | collective-permute-start | bytes 983048 | tf_op jit(solution)/shard_map/ppermute | solution.py:156
  49.4 36.7 %collective-permute-start.5 = (bf16[2,128,1280]{2,1,0:T(8,128)(2,1)S(1)}, bf16[2,128,1280]{2,1,0:T(8,128)(2,1)S(1)}, u32[]{:S(2)}, u32[]{:S(2)}) collective-permute-start(bf16[2,128,1280]{2,1,0:T(8,128)(2,1)S(1)} %slice.45), channel_id=1, source_target_pairs={{0,8},{1,9},{2,10},{3,11},{8,16},{9,17},{10,18},{11,19},{12,4},{13... | collective-permute-start | bytes 1966088 | tf_op jit(solution)/shard_map/ppermute | solution.py:156
  51.8 23.9 %collective-permute-start.11 = (bf16[2,128,1280]{2,1,0:T(8,128)(2,1)S(1)}, bf16[2,128,1280]{2,1,0:T(8,128)(2,1)S(1)}, u32[]{:S(2)}, u32[]{:S(2)}) collective-permute-start(bf16[2,128,1280]{2,1,0:T(8,128)(2,1)S(1)} %pad_maximum_fusion), channel_id=1, source_target_pairs={{0,4},{1,5},{2,6},{3,7},{4,0},{5,1},{6,2},{7,3},{8,12},{9,13},{10,... | collective-permute-start | bytes 1966088 | tf_op jit(solution)/shard_map/ppermute | solution.py:156
  67.2 14.1 %collective-permute-start.8 = (bf16[2,64,1280]{2,1,0:T(8,128)(2,1)S(1)}, bf16[2,64,1280]{2,1,0:T(8,128)(2,1)S(1)}, u32[]{:S(2)}, u32[]{:S(2)}) collective-permute-start(bf16[2,64,1280]{2,1,0:T(8,128)(2,1)S(1)} %collective-permute-done.7.refs_2_), channel_id=1, source_target_pairs={{0,4},{1,5},{2,6},{3,7},{4,0},{5,1},{6,2},{7,3},{24,28},{25,29},{2... | collective-permute-start | bytes 983048 | tf_op jit(solution)/shard_map/ppermute | solution.py:156
  69.1 17.0 %collective-permute-start.9 = (bf16[2,64,1280]{2,1,0:T(8,128)(2,1)S(1)}, bf16[2,64,1280]{2,1,0:T(8,128)(2,1)S(1)}, u32[]{:S(2)}, u32[]{:S(2)}) collective-permute-start(bf16[2,64,1280]{2,1,0:T(8,128)(2,1)S(1)} %collective-permute-done.6.refs_1_), channel_id=1, source_target_pairs={{0,8},{1,9},{2,10},{3,11},{8,16},{9,17},{10,18},{11,19},{12,4},{13... | collective-permute-start | bytes 983048 | tf_op jit(solution)/shard_map/ppermute | solution.py:156
  88.1 4.2 %collective-permute-start.12 = (bf16[512,512]{1,0:T(8,128)(2,1)S(1)}, bf16[512,512]{1,0:T(8,128)(2,1)S(1)}, u32[]{:S(2)}, u32[]{:S(2)}) collective-permute-start(bf16[512,512]{1,0:T(8,128)(2,1)S(1)} %last0.1), channel_id=1, source_target_pairs={{0,1},{1,0},{2,3},{3,2},{4,5},{5,4},{6,7},{7,6},{8,9},{9,8},{10,11... | collective-permute-start | bytes 1572872 | tf_op jit(solution)/shard_map/ppermute | solution.py:156
  91.0 2.5 %collective-permute-start.13 = (bf16[512,768]{1,0:T(8,128)(2,1)S(1)}, bf16[512,768]{1,0:T(8,128)(2,1)S(1)}, u32[]{:S(2)}, u32[]{:S(2)}) collective-permute-start(bf16[512,768]{1,0:T(8,128)(2,1)S(1)} %last4.1), channel_id=1, source_target_pairs={{0,1},{1,0},{2,3},{3,2},{4,5},{5,4},{6,7},{7,6},{8,9},{9,8},{10,11... | collective-permute-start | bytes 2359304 | tf_op jit(solution)/shard_map/ppermute | solution.py:156
  94.8 17.6 %collective-permute-start.14 = (bf16[512,640]{1,0:T(8,128)(2,1)S(1)}, bf16[512,640]{1,0:T(8,128)(2,1)S(1)}, u32[]{:S(2)}, u32[]{:S(2)}) collective-permute-start(bf16[512,640]{1,0:T(8,128)(2,1)S(1)} %fusion.10), channel_id=1, source_target_pairs={{0,2},{1,3},{2,0},{3,1},{4,6},{5,7},{6,4},{7,5},{8,10},{9,11},{10,... | collective-permute-start | bytes 1966088 | tf_op jit(solution)/shard_map/ppermute | solution.py:156
  99.2 26.8 %collective-permute-start.15 = (bf16[512,640]{1,0:T(8,128)(2,1)S(1)}, bf16[512,640]{1,0:T(8,128)(2,1)S(1)}, u32[]{:S(2)}, u32[]{:S(2)}) collective-permute-start(bf16[512,640]{1,0:T(8,128)(2,1)S(1)} %fusion.11), channel_id=1, source_target_pairs={{0,2},{1,3},{2,0},{3,1},{4,6},{5,7},{6,4},{7,5},{8,10},{9,11},{10,... | collective-permute-start | bytes 1966088 | tf_op jit(solution)/shard_map/ppermute | solution.py:156
  102.9 24.3 %copy-start.1 = (s32[8,8]{1,0:T(8,128)S(1)}, s32[8,8]{1,0:T(8,128)}, u32[]{:S(2)}) copy-start(s32[8,8]{1,0:T(8,128)} %param.16) | copy-start | bytes 772
  (9 other events, 31.6 us)

commit v12 on v11

--- a/solution.py
+++ b/solution.py
@@ -243,7 +243,7 @@
         weights = weights + blocks_of(moved)
         chain_b = move(near_b, near_of)
         cross_three = move(z_three, lambda t: t ^ 1 if t in ends else None)
-        state, weights = lax.optimization_barrier((state, weights))
+        cross_two, state, weights = lax.optimization_barrier((cross_two, state, weights))
         carry = further(
             [near_b, z_three, cross_far, cross_two],
             [

time: 129 us -> 131 us (1.016)
  the two profiles are of different devices: /device:TPU:2 before, /device:TPU:0 now
where the time goes in v12:
time: 131 us
  waiting for transfers between devices  35.6 us (27%)
  starting transfers between devices  34.7 us (26%)
  Pallas kernels  30.8 us (24%)
  local copies, waits for them, and re-layouts  15 us (11%)
  matrix products  9.77 us (7%)
  other arithmetic  4.21 us (3%)
    ppermute x16, waiting for transfers between devices, move(): return lax.ppermute(array, AXES, route)  35.6 us
    ppermute x16, starting transfers between devices, move(): return lax.ppermute(array, AXES, route)  34.7 us
    pallas_call x6, Pallas kernels, attend(): pl.pallas_call(lambda *refs: attend_kernel(*refs, buffers=len(buffers), o...  28.3 us
    dynamic_slice x2, local copies, waits for them, and re-layouts, blocks_of(): lax.dynamic_slice_in_dim(source, number * out_width, out_width, 1)  6.87 us
    unnamed x34, local copies, waits for them, and re-layouts  5.48 us
    dot_general x6, matrix products, project(): jnp.dot(part, weights[index][low:high, first:last], preferred_element_typ...  5.02 us
    dot_general x6, matrix products, project(): jnp.dot(other, weights[index + 2][low:high, first:last], preferred_elemen...  4.74 us
  transfers between devices with their start and end apart: 16, of which 6 were waited for; matrix products, arithmetic and copies ran while one was open for 16% of the time, Pallas kernels for 22%

profile of v12, /device:TPU:0, one launch (start us, length us, event | category | flops | bytes accessed | tf_op | source)
XLA Modules:
  0.0 130.5 jit_solution(5599822428897077741)
XLA Ops:
  3.1 2.5 %pack.1 = (bf16[2,256,1280]{2,1,0:T(8,128)(2,1)}, bf16[2,128,1280]{2,1,0:T(8,128)(2,1)}, bf16[2,128,1280]{2,1,0:T(8,128)(2,1)}, bf16[2,64,1280]{2,1,0:T(8,128)(2,1)}) custom-call(bf16[512,1280]{1,0:T(8,128)(2,1)S(1)} %copy-done.3, bf16[512,1280]{1,0:T(8,128)(2,1)S(1)} %copy-done.5), custom_call_target="tpu_custom_call" | custom-call | flops 671088640 | bytes 5242880 | tf_op jit(solution)/shard_map/pack/pallas_call | solution.py:39
  5.6 2.7 %collective-permute-start = (bf16[2,256,1280]{2,1,0:T(8,128)(2,1)}, bf16[2,256,1280]{2,1,0:T(8,128)(2,1)}, u32[]{:S(2)}, u32[]{:S(2)}) collective-permute-start(bf16[2,256,1280]{2,1,0:T(8,128)(2,1)} %get-tuple-element.51), channel_id=1, source_target_pairs={{0,4},{1,5},{2,6},{3,7},{4,0},{5,1},{6,2},{7,3},{8,12},{9,13},{10,... | collective-permute-start | bytes 3932168 | tf_op jit(solution)/shard_map/ppermute | solution.py:156
  8.3 4.3 %collective-permute-start.1 = (bf16[2,128,1280]{2,1,0:T(8,128)(2,1)}, bf16[2,128,1280]{2,1,0:T(8,128)(2,1)}, u32[]{:S(2)}, u32[]{:S(2)}) collective-permute-start(bf16[2,128,1280]{2,1,0:T(8,128)(2,1)} %get-tuple-element.52), channel_id=1, source_target_pairs={{0,8},{1,9},{2,10},{3,11},{8,16},{9,17},{10,18},{11,19},{12,4},{13... | collective-permute-start | bytes 1966088 | tf_op jit(solution)/shard_map/ppermute | solution.py:156
  14.0 2.8 %collective-permute-start.3 = (bf16[2,64,1280]{2,1,0:T(8,128)(2,1)}, bf16[2,64,1280]{2,1,0:T(8,128)(2,1)}, u32[]{:S(2)}, u32[]{:S(2)}) collective-permute-start(bf16[2,64,1280]{2,1,0:T(8,128)(2,1)} %get-tuple-element.58), channel_id=1, source_target_pairs={{0,16},{1,17},{2,18},{3,19},{4,20},{5,21},{6,22},{7,23},{8,24},{9,... | collective-permute-start | bytes 983048 | tf_op jit(solution)/shard_map/ppermute | solution.py:156
  16.8 1.3 %copy-done.6 = bf16[512,1280]{1,0:T(8,128)(2,1)S(1)} copy-done((bf16[512,1280]{1,0:T(8,128)(2,1)S(1)}, bf16[512,1280]{1,0:T(8,128)(2,1)}, u32[]{:S(2)}) %copy-start.6) | copy-done | bytes 1310744
  18.1 6.4 %own.1 = (f32[10,8,512]{2,1,0:T(8,128)S(1)}, f32[10,128,512]{2,1,0:T(8,128)S(1)}) custom-call(bf16[512,1280]{1,0:T(8,128)(2,1)S(1)} %copy-done.2, bf16[512,1280]{1,0:T(8,128)(2,1)S(1)} %copy-done.4, bf16[512,1280]{1,0:T(8,128)(2,1)S(1)} %copy-done.6), custom_call_target="tpu_custom_call" | custom-call | tf_op jit(solution)/shard_map/own/pallas_call | solution.py:124
  24.5 1.5 %copy-done.7 = f32[10,128,512]{2,1,0:T(8,128)} copy-done((f32[10,128,512]{2,1,0:T(8,128)}, f32[10,128,512]{2,1,0:T(8,128)S(1)}, u32[]{:S(2)}) %copy-start.7) | copy-done | bytes 2621464
  27.9 3.5 %constant_dynamic-slice_fusion.3 = (bf16[1280,1280]{1,0:T(8,128)(2,1)S(1)}, bf16[1280,1280]{1,0:T(8,128)(2,1)S(1)}) fusion(bf16[1280,5120]{1,0:T(8,128)(2,1)} %param.17, s32[]{:T(128)S(6)} %select_n.118, s32[]{:T(128)S(6)} %select_n.117), kind=kLoop, calls=%fused_computation.51 | loop fusion | bytes 13107208 | tf_op jit(solution)/shard_map/dynamic_slice | solution.py:191
  33.2 5.4 %early.1 = (f32[10,8,512]{2,1,0:T(8,128)S(1)}, f32[10,128,512]{2,1,0:T(8,128)S(1)}) custom-call(bf16[512,1280]{1,0:T(8,128)(2,1)S(1)} %copy-done.2, bf16[2,128,1280]{2,1,0:T(8,128)(2,1)} %collective-permute-done.1.refs_1_, bf16[2,128,1280]{2,1,0:T(8,128)(2,1)S(1)} %collective-permute-done.2.refs_2_, f32[256,128]{1,0:T(8,128)S(1)} %broadcast_in_dim.177.refs_3_, ...), custom_call_target="tpu_custom_call" | custom-call | flops 671088640 | bytes 5242880 | tf_op jit(solution)/shard_map/early/pallas_call | solution.py:124
  38.6 6.9 %collective-permute-done.3.refs_2_ = bf16[2,64,1280]{2,1,0:T(8,128)(2,1)} collective-permute-done((bf16[2,64,1280]{2,1,0:T(8,128)(2,1)}, bf16[2,64,1280]{2,1,0:T(8,128)(2,1)}, u32[]{:S(2)}, u32[]{:S(2)}) %collective-permute-start.3) | collective-permute-done | bytes 327712 | tf_op jit(solution)/shard_map/ppermute | solution.py:156
  47.7 2.5 %collective-permute-start.5 = (bf16[2,128,1280]{2,1,0:T(8,128)(2,1)S(1)}, bf16[2,128,1280]{2,1,0:T(8,128)(2,1)S(1)}, u32[]{:S(2)}, u32[]{:S(2)}) collective-permute-start(bf16[2,128,1280]{2,1,0:T(8,128)(2,1)S(1)} %slice.45), channel_id=1, source_target_pairs={{0,8},{1,9},{2,10},{3,11},{8,16},{9,17},{10,18},{11,19},{12,4},{13... | collective-permute-start | bytes 1966088 | tf_op jit(solution)/shard_map/ppermute | solution.py:156
  50.2 4.3 %collective-permute-start.6 = (bf16[2,64,1280]{2,1,0:T(8,128)(2,1)S(1)}, bf16[2,64,1280]{2,1,0:T(8,128)(2,1)S(1)}, u32[]{:S(2)}, u32[]{:S(2)}) collective-permute-start(bf16[2,64,1280]{2,1,0:T(8,128)(2,1)S(1)} %slice.46), channel_id=1, source_target_pairs={{0,8},{1,9},{2,10},{3,11},{8,16},{9,17},{10,18},{11,19},{12,4},{13... | collective-permute-start | bytes 983048 | tf_op jit(solution)/shard_map/ppermute | solution.py:156
  57.0 6.4 %first.1 = (f32[10,8,512]{2,1,0:T(8,128)S(1)}, f32[10,128,512]{2,1,0:T(8,128)S(1)}) custom-call(bf16[512,1280]{1,0:T(8,128)(2,1)S(1)} %copy-done.2, bf16[2,256,1280]{2,1,0:T(8,128)(2,1)} %collective-permute-done.refs_1_, bf16[2,64,1280]{2,1,0:T(8,128)(2,1)} %collective-permute-done.3.refs_2_, f32[320,128]{1,0:T(8,128)S(1)} %broadcast_in_dim.182.refs_3_, ...), custom_call_target="tpu_custom_call" | custom-call | flops 838860800 | bytes 5242880 | tf_op jit(solution)/shard_map/first/pallas_call | solution.py:124
  63.5 6.0 %collective-permute-done.6.refs_1_ = bf16[2,64,1280]{2,1,0:T(8,128)(2,1)S(1)} collective-permute-done((bf16[2,64,1280]{2,1,0:T(8,128)(2,1)S(1)}, bf16[2,64,1280]{2,1,0:T(8,128)(2,1)S(1)}, u32[]{:S(2)}, u32[]{:S(2)}) %collective-permute-start.6) | collective-permute-done | bytes 327712 | tf_op jit(solution)/shard_map/ppermute | solution.py:156
  69.4 9.4 %collective-permute-start.8 = (bf16[2,64,1280]{2,1,0:T(8,128)(2,1)S(1)}, bf16[2,64,1280]{2,1,0:T(8,128)(2,1)S(1)}, u32[]{:S(2)}, u32[]{:S(2)}) collective-permute-start(bf16[2,64,1280]{2,1,0:T(8,128)(2,1)S(1)} %collective-permute-done.7.refs_2_), channel_id=1, source_target_pairs={{0,4},{1,5},{2,6},{3,7},{4,0},{5,1},{6,2},{7,3},{24,28},{25,29},{2... | collective-permute-start | bytes 983048 | tf_op jit(solution)/shard_map/ppermute | solution.py:156
  78.8 1.5 %collective-permute-start.9 = (bf16[2,64,1280]{2,1,0:T(8,128)(2,1)S(1)}, bf16[2,64,1280]{2,1,0:T(8,128)(2,1)S(1)}, u32[]{:S(2)}, u32[]{:S(2)}) collective-permute-start(bf16[2,64,1280]{2,1,0:T(8,128)(2,1)S(1)} %collective-permute-done.6.refs_1_), channel_id=1, source_target_pairs={{0,8},{1,9},{2,10},{3,11},{8,16},{9,17},{10,18},{11,19},{12,4},{13... | collective-permute-start | bytes 983048 | tf_op jit(solution)/shard_map/ppermute | solution.py:156
  80.3 3.4 %constant_dynamic-slice_fusion = (bf16[1280,1280]{1,0:T(8,128)(2,1)S(1)}, bf16[1280,1280]{1,0:T(8,128)(2,1)S(1)}) fusion(bf16[1280,5120]{1,0:T(8,128)(2,1)} %collective-permute-done.4, s32[]{:T(128)S(6)} %select_n.118, s32[]{:T(128)S(6)} %select_n.117), kind=kLoop, calls=%fused_computation.48 | loop fusion | bytes 13107208 | tf_op jit(solution)/shard_map/dynamic_slice | solution.py:191
  83.8 5.5 %middle.1 = (f32[10,8,512]{2,1,0:T(8,128)S(1)}, f32[10,128,512]{2,1,0:T(8,128)S(1)}) custom-call(bf16[512,1280]{1,0:T(8,128)(2,1)S(1)} %copy-done.2, bf16[2,64,1280]{2,1,0:T(8,128)(2,1)S(1)} %collective-permute-done.6.refs_1_, bf16[2,64,1280]{2,1,0:T(8,128)(2,1)S(1)} %collective-permute-done.7.refs_2_, ...), custom_call_target="tpu_custom_call" | custom-call | flops 1006632960 | bytes 5242880 | tf_op jit(solution)/shard_map/middle/pallas_call | solution.py:124
  89.4 1.9 %last0.1 = bf16[512,512]{1,0:T(8,128)(2,1)S(1)} custom-call(bf16[512,1280]{1,0:T(8,128)(2,1)S(1)} %copy-done.2, bf16[2,128,1280]{2,1,0:T(8,128)(2,1)S(1)} %collective-permute-done.5.refs_1_, bf16[2,64,1280]{2,1,0:T(8,128)(2,1)S(1)} %collective-permute-done.8.refs_2_, bf16[2,64,1280]{2,1,0:T(8,128)(2,1)S(1)} %collective-permute-done.9.refs_3_, ...), custom_call_target="tpu_custom_call" | custom-call | flops 268435456 | bytes 2097152 | tf_op jit(solution)/shard_map/last0/pallas_call | solution.py:124
  91.4 2.8 %last4.1 = bf16[512,768]{1,0:T(8,128)(2,1)S(1)} custom-call(bf16[512,1280]{1,0:T(8,128)(2,1)S(1)} %copy-done.2, bf16[2,128,1280]{2,1,0:T(8,128)(2,1)S(1)} %collective-permute-done.5.refs_1_, bf16[2,64,1280]{2,1,0:T(8,128)(2,1)S(1)} %collective-permute-done.8.refs_2_, bf16[2,64,1280]{2,1,0:T(8,128)(2,1)S(1)} %collective-permute-done.9.refs_3_, ...), custom_call_target="tpu_custom_call" | custom-call | flops 402653184 | bytes 3145728 | tf_op jit(solution)/shard_map/last4/pallas_call | solution.py:124
  98.1 1.6 %collective-permute-start.14 = (bf16[512,640]{1,0:T(8,128)(2,1)S(1)}, bf16[512,640]{1,0:T(8,128)(2,1)S(1)}, u32[]{:S(2)}, u32[]{:S(2)}) collective-permute-start(bf16[512,640]{1,0:T(8,128)(2,1)S(1)} %fusion.10), channel_id=1, source_target_pairs={{0,2},{1,3},{2,0},{3,1},{4,6},{5,7},{6,4},{7,5},{8,10},{9,11},{10,... | collective-permute-start | bytes 1966088 | tf_op jit(solution)/shard_map/ppermute | solution.py:156
  107.3 8.4 %collective-permute-done.14 = bf16[512,640]{1,0:T(8,128)(2,1)S(1)} collective-permute-done((bf16[512,640]{1,0:T(8,128)(2,1)S(1)}, bf16[512,640]{1,0:T(8,128)(2,1)S(1)}, u32[]{:S(2)}, u32[]{:S(2)}) %collective-permute-start.14) | collective-permute-done | bytes 655392 | tf_op jit(solution)/shard_map/ppermute | solution.py:156
  115.7 13.5 %collective-permute-done.15 = bf16[512,640]{1,0:T(8,128)(2,1)S(1)} collective-permute-done((bf16[512,640]{1,0:T(8,128)(2,1)S(1)}, bf16[512,640]{1,0:T(8,128)(2,1)S(1)}, u32[]{:S(2)}, u32[]{:S(2)}) %collective-permute-start.15) | collective-permute-done | bytes 655392 | tf_op jit(solution)/shard_map/ppermute | solution.py:156
  129.2 1.3 %add_convert_fusion = bf16[512,1280]{1,0:T(8,128)(2,1)} fusion(f32[512,1280]{1,0:T(8,128)S(1)} %fusion.1, bf16[512,640]{1,0:T(8,128)(2,1)S(1)} %collective-permute-done.15, bf16[512,640]{1,0:T(8,128)(2,1)S(1)} %collective-permute-done.14), kind=kLoop, calls=%fused_computation.3 | loop fusion | flops 3932160 | bytes 5242880 | tf_op jit(solution)/shard_map/convert_element_type | solution.py:306
  (95 shorter events, 24.4 us)
Async XLA Ops:
  0.0 26.0 %copy-start = (s32[8,8]{1,0:T(8,128)S(1)}, s32[8,8]{1,0:T(8,128)}, u32[]{:S(2)}) copy-start(s32[8,8]{1,0:T(8,128)} %param.16) | copy-start | bytes 772
  0.0 16.8 %copy-start.2 = (bf16[512,1280]{1,0:T(8,128)(2,1)S(1)}, bf16[512,1280]{1,0:T(8,128)(2,1)}, u32[]{:S(2)}) copy-start(bf16[512,1280]{1,0:T(8,128)(2,1)} %refs_0_.13) | copy-start | bytes 3932164
  0.0 45.6 %collective-permute-start.4 = (bf16[1280,5120]{1,0:T(8,128)(2,1)}, bf16[1280,5120]{1,0:T(8,128)(2,1)}, u32[]{:S(2)}, u32[]{:S(2)}) collective-permute-start(bf16[1280,5120]{1,0:T(8,128)(2,1)} %param.17), channel_id=1, source_target_pairs={{0,1},{1,0},{2,3},{3,2},{4,5},{5,4},{6,7},{7,6},{8,9},{9,8},{10,11... | collective-permute-start | bytes 39321608 | tf_op jit(solution)/shard_map/ppermute | solution.py:156
  3.1 13.7 %copy-start.4 = (bf16[512,1280]{1,0:T(8,128)(2,1)S(1)}, bf16[512,1280]{1,0:T(8,128)(2,1)}, u32[]{:S(2)}) copy-start(bf16[512,1280]{1,0:T(8,128)(2,1)} %refs_1_.3) | copy-start | bytes 3932164
  5.6 22.0 %copy-start.16 = (pred[2,256]{1,0:T(4,128)(4,1)S(1)}, pred[2,256]{1,0:T(4,128)(4,1)}, u32[]{:S(2)}) copy-start(pred[2,256]{1,0:T(4,128)(4,1)} %constant.81.clone) | copy-start | bytes 1540
  5.6 22.1 %copy-start.15 = (pred[3,256]{1,0:T(4,128)(4,1)S(1)}, pred[3,256]{1,0:T(4,128)(4,1)}, u32[]{:S(2)}) copy-start(pred[3,256]{1,0:T(4,128)(4,1)} %constant.87.clone) | copy-start | bytes 2308
  5.6 22.1 %copy-start.14 = (s32[256]{0:T(256)S(1)}, s32[256]{0:T(256)}, u32[]{:S(2)}) copy-start(s32[256]{0:T(256)} %constant.82.clone) | copy-start | bytes 3076
  5.6 22.2 %copy-start.13 = (s32[256]{0:T(256)S(1)}, s32[256]{0:T(256)}, u32[]{:S(2)}) copy-start(s32[256]{0:T(256)} %constant.88.clone) | copy-start | bytes 3076
  5.6 39.9 %collective-permute-start = (bf16[2,256,1280]{2,1,0:T(8,128)(2,1)}, bf16[2,256,1280]{2,1,0:T(8,128)(2,1)}, u32[]{:S(2)}, u32[]{:S(2)}) collective-permute-start(bf16[2,256,1280]{2,1,0:T(8,128)(2,1)} %get-tuple-element.51), channel_id=1, source_target_pairs={{0,4},{1,5},{2,6},{3,7},{4,0},{5,1},{6,2},{7,3},{8,12},{9,13},{10,... | collective-permute-start | bytes 3932168 | tf_op jit(solution)/shard_map/ppermute | solution.py:156
  8.3 23.3 %collective-permute-start.1 = (bf16[2,128,1280]{2,1,0:T(8,128)(2,1)}, bf16[2,128,1280]{2,1,0:T(8,128)(2,1)}, u32[]{:S(2)}, u32[]{:S(2)}) collective-permute-start(bf16[2,128,1280]{2,1,0:T(8,128)(2,1)} %get-tuple-element.52), channel_id=1, source_target_pairs={{0,8},{1,9},{2,10},{3,11},{8,16},{9,17},{10,18},{11,19},{12,4},{13... | collective-permute-start | bytes 1966088 | tf_op jit(solution)/shard_map/ppermute | solution.py:156
  12.7 19.2 %collective-permute-start.2 = (bf16[2,128,1280]{2,1,0:T(8,128)(2,1)}, bf16[2,128,1280]{2,1,0:T(8,128)(2,1)S(1)}, u32[]{:S(2)}, u32[]{:S(2)}) collective-permute-start(bf16[2,128,1280]{2,1,0:T(8,128)(2,1)} %get-tuple-element.53), channel_id=1, source_target_pairs={{4,12},{5,13},{6,14},{7,15},{8,0},{9,1},{10,2},{11,3},{12,20},{13,... | collective-permute-start | bytes 1966088 | tf_op jit(solution)/shard_map/ppermute | solution.py:156
  14.0 31.6 %collective-permute-start.3 = (bf16[2,64,1280]{2,1,0:T(8,128)(2,1)}, bf16[2,64,1280]{2,1,0:T(8,128)(2,1)}, u32[]{:S(2)}, u32[]{:S(2)}) collective-permute-start(bf16[2,64,1280]{2,1,0:T(8,128)(2,1)} %get-tuple-element.58), channel_id=1, source_target_pairs={{0,16},{1,17},{2,18},{3,19},{4,20},{5,21},{6,22},{7,23},{8,24},{9,... | collective-permute-start | bytes 983048 | tf_op jit(solution)/shard_map/ppermute | solution.py:156
  31.8 51.9 %collective-permute-start.10 = (bf16[2,128,1280]{2,1,0:T(8,128)(2,1)}, bf16[2,128,1280]{2,1,0:T(8,128)(2,1)S(1)}, u32[]{:S(2)}, u32[]{:S(2)}) collective-permute-start(bf16[2,128,1280]{2,1,0:T(8,128)(2,1)} %collective-permute-done.1.refs_1_), channel_id=1, source_target_pairs={{4,0},{5,1},{6,2},{7,3},{8,12},{9,13},{10,14},{11,15},{12,8},{13,9... | collective-permute-start | bytes 1966088 | tf_op jit(solution)/shard_map/ppermute | solution.py:156
  47.7 41.6 %collective-permute-start.5 = (bf16[2,128,1280]{2,1,0:T(8,128)(2,1)S(1)}, bf16[2,128,1280]{2,1,0:T(8,128)(2,1)S(1)}, u32[]{:S(2)}, u32[]{:S(2)}) collective-permute-start(bf16[2,128,1280]{2,1,0:T(8,128)(2,1)S(1)} %slice.45), channel_id=1, source_target_pairs={{0,8},{1,9},{2,10},{3,11},{8,16},{9,17},{10,18},{11,19},{12,4},{13... | collective-permute-start | bytes 1966088 | tf_op jit(solution)/shard_map/ppermute | solution.py:156
  50.2 19.2 %collective-permute-start.6 = (bf16[2,64,1280]{2,1,0:T(8,128)(2,1)S(1)}, bf16[2,64,1280]{2,1,0:T(8,128)(2,1)S(1)}, u32[]{:S(2)}, u32[]{:S(2)}) collective-permute-start(bf16[2,64,1280]{2,1,0:T(8,128)(2,1)S(1)} %slice.46), channel_id=1, source_target_pairs={{0,8},{1,9},{2,10},{3,11},{8,16},{9,17},{10,18},{11,19},{12,4},{13... | collective-permute-start | bytes 983048 | tf_op jit(solution)/shard_map/ppermute | solution.py:156
  54.5 15.0 %collective-permute-start.7 = (bf16[2,64,1280]{2,1,0:T(8,128)(2,1)}, bf16[2,64,1280]{2,1,0:T(8,128)(2,1)S(1)}, u32[]{:S(2)}, u32[]{:S(2)}) collective-permute-start(bf16[2,64,1280]{2,1,0:T(8,128)(2,1)} %collective-permute-done.3.refs_2_), channel_id=1, source_target_pairs={{8,0},{9,1},{10,2},{11,3},{12,4},{13,5},{14,6},{15,7},{16,24},{17,... | collective-permute-start | bytes 983048 | tf_op jit(solution)/shard_map/ppermute | solution.py:156
  56.8 26.8 %collective-permute-start.11 = (bf16[2,128,1280]{2,1,0:T(8,128)(2,1)S(1)}, bf16[2,128,1280]{2,1,0:T(8,128)(2,1)S(1)}, u32[]{:S(2)}, u32[]{:S(2)}) collective-permute-start(bf16[2,128,1280]{2,1,0:T(8,128)(2,1)S(1)} %pad_maximum_fusion), channel_id=1, source_target_pairs={{0,4},{1,5},{2,6},{3,7},{4,0},{5,1},{6,2},{7,3},{8,12},{9,13},{10,... | collective-permute-start | bytes 1966088 | tf_op jit(solution)/shard_map/ppermute | solution.py:156
  69.4 19.9 %collective-permute-start.8 = (bf16[2,64,1280]{2,1,0:T(8,128)(2,1)S(1)}, bf16[2,64,1280]{2,1,0:T(8,128)(2,1)S(1)}, u32[]{:S(2)}, u32[]{:S(2)}) collective-permute-start(bf16[2,64,1280]{2,1,0:T(8,128)(2,1)S(1)} %collective-permute-done.7.refs_2_), channel_id=1, source_target_pairs={{0,4},{1,5},{2,6},{3,7},{4,0},{5,1},{6,2},{7,3},{24,28},{25,29},{2... | collective-permute-start | bytes 983048 | tf_op jit(solution)/shard_map/ppermute | solution.py:156
  78.8 10.5 %collective-permute-start.9 = (bf16[2,64,1280]{2,1,0:T(8,128)(2,1)S(1)}, bf16[2,64,1280]{2,1,0:T(8,128)(2,1)S(1)}, u32[]{:S(2)}, u32[]{:S(2)}) collective-permute-start(bf16[2,64,1280]{2,1,0:T(8,128)(2,1)S(1)} %collective-permute-done.6.refs_1_), channel_id=1, source_target_pairs={{0,8},{1,9},{2,10},{3,11},{8,16},{9,17},{10,18},{11,19},{12,4},{13... | collective-permute-start | bytes 983048 | tf_op jit(solution)/shard_map/ppermute | solution.py:156
  91.3 4.2 %collective-permute-start.12 = (bf16[512,512]{1,0:T(8,128)(2,1)S(1)}, bf16[512,512]{1,0:T(8,128)(2,1)S(1)}, u32[]{:S(2)}, u32[]{:S(2)}) collective-permute-start(bf16[512,512]{1,0:T(8,128)(2,1)S(1)} %last0.1), channel_id=1, source_target_pairs={{0,1},{1,0},{2,3},{3,2},{4,5},{5,4},{6,7},{7,6},{8,9},{9,8},{10,11... | collective-permute-start | bytes 1572872 | tf_op jit(solution)/shard_map/ppermute | solution.py:156
  94.2 2.5 %collective-permute-start.13 = (bf16[512,768]{1,0:T(8,128)(2,1)S(1)}, bf16[512,768]{1,0:T(8,128)(2,1)S(1)}, u32[]{:S(2)}, u32[]{:S(2)}) collective-permute-start(bf16[512,768]{1,0:T(8,128)(2,1)S(1)} %last4.1), channel_id=1, source_target_pairs={{0,1},{1,0},{2,3},{3,2},{4,5},{5,4},{6,7},{7,6},{8,9},{9,8},{10,11... | collective-permute-start | bytes 2359304 | tf_op jit(solution)/shard_map/ppermute | solution.py:156
  98.1 17.6 %collective-permute-start.14 = (bf16[512,640]{1,0:T(8,128)(2,1)S(1)}, bf16[512,640]{1,0:T(8,128)(2,1)S(1)}, u32[]{:S(2)}, u32[]{:S(2)}) collective-permute-start(bf16[512,640]{1,0:T(8,128)(2,1)S(1)} %fusion.10), channel_id=1, source_target_pairs={{0,2},{1,3},{2,0},{3,1},{4,6},{5,7},{6,4},{7,5},{8,10},{9,11},{10,... | collective-permute-start | bytes 1966088 | tf_op jit(solution)/shard_map/ppermute | solution.py:156
  102.4 26.7 %collective-permute-start.15 = (bf16[512,640]{1,0:T(8,128)(2,1)S(1)}, bf16[512,640]{1,0:T(8,128)(2,1)S(1)}, u32[]{:S(2)}, u32[]{:S(2)}) collective-permute-start(bf16[512,640]{1,0:T(8,128)(2,1)S(1)} %fusion.11), channel_id=1, source_target_pairs={{0,2},{1,3},{2,0},{3,1},{4,6},{5,7},{6,4},{7,5},{8,10},{9,11},{10,... | collective-permute-start | bytes 1966088 | tf_op jit(solution)/shard_map/ppermute | solution.py:156
  106.3 24.3 %copy-start.1 = (s32[8,8]{1,0:T(8,128)S(1)}, s32[8,8]{1,0:T(8,128)}, u32[]{:S(2)}) copy-start(s32[8,8]{1,0:T(8,128)} %param.16) | copy-start | bytes 772
  (9 other events, 25.4 us)

commit v13 on v10

--- a/solution.py
+++ b/solution.py
@@ -186,12 +186,8 @@
             query_vectors, None, buffers, bias_of(pieces), carry, False, 0, head_count, name
         )
 
-    def blocks_of(*sources):
-        return [
-            lax.dynamic_slice_in_dim(source, number * out_width, out_width, 1)
-            for source in sources
-            for number in (away, home)
-        ]
+    def block_of(source, number):
+        return lax.dynamic_slice_in_dim(source, number * out_width, out_width, 1)
 
     if block_count == 8:
         a, ab = (row_count // 8, row_count // 4)
@@ -215,7 +211,7 @@
         z_two = move(sent_a, lambda t: t ^ 4)
         carry = attend(query_vectors, own_pair, [], None, None, False, 0, head_count, "own")
         state, out_weight = lax.optimization_barrier((carry[0], out_weight))
-        weights = blocks_of(out_weight)
+        weights = [block_of(out_weight, away), block_of(out_weight, home)]
         z_far, z_near, state, weights = lax.optimization_barrier((z_far, z_near, state, weights))
         carry = further(
             [z_far, z_near],
@@ -223,8 +219,8 @@
             (state, carry[1]),
             "early",
         )
-        x_rows, z_near, z_two, state, weights, moved = lax.optimization_barrier(
-            (x_rows, z_near, z_two, carry[0], weights, moved)
+        x_rows, z_near, z_two, state, moved = lax.optimization_barrier(
+            (x_rows, z_near, z_two, carry[0], moved)
         )
         near_b = move(x_rows[:, a:ab], near_of)
         near_c = move(x_rows[:, ab:], near_of)
@@ -240,7 +236,7 @@
         near_b, z_three, state, moved = lax.optimization_barrier(
             (near_b, z_three, carry[0], moved)
         )
-        weights = weights + blocks_of(moved)
+        weights = [weights[0], block_of(moved, away), weights[1]]
         chain_b = move(near_b, near_of)
         cross_three = move(z_three, lambda t: t ^ 1 if t in ends else None)
         near_c, state, weights = lax.optimization_barrier((near_c, state, weights))
@@ -273,7 +269,9 @@
         carry = attend(query_vectors, own_pair, [], None, None, False, 0, head_count, "own")
         carry = further([jnp.concatenate(received[:2], axis=1)], pieces[:2], carry, "first")
         buffers, pieces = ([jnp.concatenate(received[2:], axis=1)], pieces[2:])
-        weights = lax.optimization_barrier(blocks_of(out_weight, moved))
+        weights = lax.optimization_barrier(
+            [block_of(out_weight, away), block_of(moved, away), block_of(out_weight, home)]
+        )
 
     bias = bias_of(pieces)
     cut = 2 * (head_count // 4)
@@ -284,25 +282,28 @@
         )
         parts.append((part, move(part, same, core), low * HEAD_DIM, high * HEAD_DIM))
 
-    def project(index, first, last):
+    def project(first, last):
         total = 0.0
         for part, other, low, high in parts:
             total = total + jnp.dot(
-                part, weights[index][low:high, first:last], preferred_element_type=F32
+                part, weights[0][low:high, first:last], preferred_element_type=F32
             )
             total = total + jnp.dot(
-                other, weights[index + 2][low:high, first:last], preferred_element_type=F32
+                other, weights[1][low:high, first:last], preferred_element_type=F32
             )
         return total
 
     half = out_width // 2
     sent = []
     for first in (0, half):
-        sent.append(project(0, first, first + half).astype(BF16))
-        _, held = lax.optimization_barrier((sent[-1], [part[:2] for part in parts]))
+        sent.append(project(first, first + half).astype(BF16))
+        _, held, moved = lax.optimization_barrier(
+            (sent[-1], [part[:2] for part in parts], moved)
+        )
         parts = [kept + part[2:] for kept, part in zip(held, parts)]
     arrived = [move(block, same, lambda h: h ^ 2) for block in sent]
-    kept, arrived[0] = lax.optimization_barrier((project(1, 0, out_width), arrived[0]))
+    weights = [weights[2], block_of(moved, home)]
+    kept, arrived[0] = lax.optimization_barrier((project(0, out_width), arrived[0]))
     return (kept + jnp.concatenate(arrived, axis=1).astype(F32)).astype(BF16)
 
 

time: 125 us -> 129 us (1.032)
  waiting for transfers between devices: 35 us -> 23.7 us
  matrix products: 9.67 us -> 19 us
  local copies, waits for them, and re-layouts: 15 us -> 19 us
  starting transfers between devices: 29.1 us -> 31.5 us
    ppermute x16, waiting for transfers between devices: 35 us -> 23.7 us  [move(): return lax.ppermute(array, AXES, route)]
    dot_general x12, matrix products: 9.67 us -> 19 us  [the longest x6 12.7 us: project(): jnp.dot(other, weights[1][low:high, first:last], preferred_element_type=F32)]
    dynamic_slice x2, local copies, waits for them, and re-layouts: 6.87 us -> 10.1 us  [block_of(): return lax.dynamic_slice_in_dim(source, number * out_width, out_width, 1)]
    ppermute x16, starting transfers between devices: 29.1 us -> 31.5 us  [move(): return lax.ppermute(array, AXES, route)]
    unnamed x34 -> x40, local copies, waits for them, and re-layouts: 5.57 us -> 6.39 us
  transfers between devices with their start and end apart: 16 -> 16, of which waited for: 6 -> 5; matrix products, arithmetic and copies ran while one was open for 16% -> 25% of each run, Pallas kernels for 23% -> 23%
where the time goes in v13:
time: 129 us
  starting transfers between devices  31.5 us (24%)
  Pallas kernels  30.8 us (24%)
  waiting for transfers between devices  23.7 us (18%)
  local copies, waits for them, and re-layouts  19 us (15%)
  matrix products  19 us (15%)
  other arithmetic  4.09 us (3%)
    ppermute x16, starting transfers between devices, move(): return lax.ppermute(array, AXES, route)  31.5 us
    pallas_call x6, Pallas kernels, attend(): pl.pallas_call(lambda *refs: attend_kernel(*refs, buffers=len(buffers), o...  28.3 us
    ppermute x16, waiting for transfers between devices, move(): return lax.ppermute(array, AXES, route)  23.7 us
    dot_general x6, matrix products, project(): jnp.dot(other, weights[1][low:high, first:last], preferred_element_type=F32)  12.7 us
    dynamic_slice x2, local copies, waits for them, and re-layouts, block_of(): return lax.dynamic_slice_in_dim(source, number * out_width, out_width, 1)  10.1 us
    unnamed x40, local copies, waits for them, and re-layouts  6.39 us
    dot_general x6, matrix products, project(): jnp.dot(part, weights[0][low:high, first:last], preferred_element_type=F32)  6.3 us
  transfers between devices with their start and end apart: 16, of which 5 were waited for; matrix products, arithmetic and copies ran while one was open for 25% of the time, Pallas kernels for 23%

profile of v13, /device:TPU:2, one launch (start us, length us, event | category | flops | bytes accessed | tf_op | source)
XLA Modules:
  0.0 128.6 jit_solution(6651740816491761514)
XLA Ops:
  2.8 2.5 %pack.1 = (bf16[2,256,1280]{2,1,0:T(8,128)(2,1)}, bf16[2,128,1280]{2,1,0:T(8,128)(2,1)}, bf16[2,128,1280]{2,1,0:T(8,128)(2,1)}, bf16[2,64,1280]{2,1,0:T(8,128)(2,1)}) custom-call(bf16[512,1280]{1,0:T(8,128)(2,1)S(1)} %copy-done.3, bf16[512,1280]{1,0:T(8,128)(2,1)S(1)} %copy-done.5), custom_call_target="tpu_custom_call" | custom-call | flops 671088640 | bytes 5242880 | tf_op jit(solution)/shard_map/pack/pallas_call | solution.py:39
  6.7 4.6 %collective-permute-start.2 = (bf16[2,128,1280]{2,1,0:T(8,128)(2,1)}, bf16[2,128,1280]{2,1,0:T(8,128)(2,1)S(1)}, u32[]{:S(2)}, u32[]{:S(2)}) collective-permute-start(bf16[2,128,1280]{2,1,0:T(8,128)(2,1)} %get-tuple-element.52), channel_id=1, source_target_pairs={{4,12},{5,13},{6,14},{7,15},{8,0},{9,1},{10,2},{11,3},{12,20},{13,... | collective-permute-start | bytes 1966088 | tf_op jit(solution)/shard_map/ppermute | solution.py:156
  11.6 3.2 %collective-permute-start.3 = (bf16[2,64,1280]{2,1,0:T(8,128)(2,1)}, bf16[2,64,1280]{2,1,0:T(8,128)(2,1)}, u32[]{:S(2)}, u32[]{:S(2)}) collective-permute-start(bf16[2,64,1280]{2,1,0:T(8,128)(2,1)} %get-tuple-element.57), channel_id=1, source_target_pairs={{0,16},{1,17},{2,18},{3,19},{4,20},{5,21},{6,22},{7,23},{8,24},{9,... | collective-permute-start | bytes 983048 | tf_op jit(solution)/shard_map/ppermute | solution.py:156
  16.2 6.4 %own.1 = (f32[10,8,512]{2,1,0:T(8,128)S(1)}, f32[10,128,512]{2,1,0:T(8,128)S(1)}) custom-call(bf16[512,1280]{1,0:T(8,128)(2,1)S(1)} %copy-done.2, bf16[512,1280]{1,0:T(8,128)(2,1)S(1)} %copy-done.4, bf16[512,1280]{1,0:T(8,128)(2,1)S(1)} %copy-done.6), custom_call_target="tpu_custom_call" | custom-call | tf_op jit(solution)/shard_map/own/pallas_call | solution.py:124
  25.7 6.2 %constant_dynamic-slice_fusion.2 = (bf16[1280,1280]{1,0:T(8,128)(2,1)}, bf16[1280,1280]{1,0:T(8,128)(2,1)}) fusion(bf16[1280,5120]{1,0:T(8,128)(2,1)} %param.17, s32[]{:T(128)S(6)} %select_n.116, s32[]{:T(128)S(6)} %select_n.115), kind=kLoop, calls=%fused_computation.51 | loop fusion | bytes 13107208 | tf_op jit(solution)/shard_map/dynamic_slice | solution.py:190
  32.2 3.9 %collective-permute-start.11 = (bf16[2,128,1280]{2,1,0:T(8,128)(2,1)}, bf16[2,128,1280]{2,1,0:T(8,128)(2,1)S(1)}, u32[]{:S(2)}, u32[]{:S(2)}) collective-permute-start(bf16[2,128,1280]{2,1,0:T(8,128)(2,1)} %collective-permute-done.1.refs_1_), channel_id=1, source_target_pairs={{4,0},{5,1},{6,2},{7,3},{8,12},{9,13},{10,14},{11,15},{12,8},{13,9... | collective-permute-start | bytes 1966088 | tf_op jit(solution)/shard_map/ppermute | solution.py:156
  36.2 5.4 %early.1 = (f32[10,8,512]{2,1,0:T(8,128)S(1)}, f32[10,128,512]{2,1,0:T(8,128)S(1)}) custom-call(bf16[512,1280]{1,0:T(8,128)(2,1)S(1)} %copy-done.2, bf16[2,128,1280]{2,1,0:T(8,128)(2,1)} %collective-permute-done.1.refs_1_, bf16[2,128,1280]{2,1,0:T(8,128)(2,1)S(1)} %collective-permute-done.2.refs_2_, f32[256,128]{1,0:T(8,128)S(1)} %broadcast_in_dim.166.refs_3_, ...), custom_call_target="tpu_custom_call" | custom-call | flops 671088640 | bytes 5242880 | tf_op jit(solution)/shard_map/early/pallas_call | solution.py:124
  49.3 8.0 %collective-permute-start.5 = (bf16[2,128,1280]{2,1,0:T(8,128)(2,1)S(1)}, bf16[2,128,1280]{2,1,0:T(8,128)(2,1)S(1)}, u32[]{:S(2)}, u32[]{:S(2)}) collective-permute-start(bf16[2,128,1280]{2,1,0:T(8,128)(2,1)S(1)} %pad_maximum_fusion), channel_id=1, source_target_pairs={{0,4},{1,5},{2,6},{3,7},{4,0},{5,1},{6,2},{7,3},{8,12},{9,13},{10,... | collective-permute-start | bytes 1966088 | tf_op jit(solution)/shard_map/ppermute | solution.py:156
  57.4 6.4 %first.1 = (f32[10,8,512]{2,1,0:T(8,128)S(1)}, f32[10,128,512]{2,1,0:T(8,128)S(1)}) custom-call(bf16[512,1280]{1,0:T(8,128)(2,1)S(1)} %copy-done.2, bf16[2,256,1280]{2,1,0:T(8,128)(2,1)} %collective-permute-done.refs_1_, bf16[2,64,1280]{2,1,0:T(8,128)(2,1)} %collective-permute-done.3.refs_2_, f32[320,128]{1,0:T(8,128)S(1)} %broadcast_in_dim.171.refs_3_, ...), custom_call_target="tpu_custom_call" | custom-call | flops 838860800 | bytes 5242880 | tf_op jit(solution)/shard_map/first/pallas_call | solution.py:124
  64.6 1.9 %collective-permute-start.8 = (bf16[2,64,1280]{2,1,0:T(8,128)(2,1)S(1)}, bf16[2,64,1280]{2,1,0:T(8,128)(2,1)S(1)}, u32[]{:S(2)}, u32[]{:S(2)}) collective-permute-start(bf16[2,64,1280]{2,1,0:T(8,128)(2,1)S(1)} %collective-permute-done.7.refs_3_), channel_id=1, source_target_pairs={{0,4},{1,5},{2,6},{3,7},{4,0},{5,1},{6,2},{7,3},{24,28},{25,29},{2... | collective-permute-start | bytes 983048 | tf_op jit(solution)/shard_map/ppermute | solution.py:156
  68.0 3.9 %constant_dynamic-slice_fusion = bf16[1280,1280]{1,0:T(8,128)(2,1)} fusion(bf16[1280,5120]{1,0:T(8,128)(2,1)} %collective-permute-done.4, s32[]{:T(128)S(6)} %select_n.115), kind=kLoop, calls=%fused_computation.49 | loop fusion | bytes 6553604 | tf_op jit(solution)/shard_map/dynamic_slice | solution.py:190
  71.9 6.8 %collective-permute-done.10.refs_2_ = bf16[2,128,1280]{2,1,0:T(8,128)(2,1)S(1)} collective-permute-done((bf16[2,128,1280]{2,1,0:T(8,128)(2,1)S(1)}, bf16[2,128,1280]{2,1,0:T(8,128)(2,1)S(1)}, u32[]{:S(2)}, u32[]{:S(2)}) %collective-permute-start.10) | collective-permute-done | bytes 655392 | tf_op jit(solution)/shard_map/ppermute | solution.py:156
  78.8 5.5 %middle.1 = (f32[10,8,512]{2,1,0:T(8,128)S(1)}, f32[10,128,512]{2,1,0:T(8,128)S(1)}) custom-call(bf16[512,1280]{1,0:T(8,128)(2,1)S(1)} %copy-done.2, bf16[2,64,1280]{2,1,0:T(8,128)(2,1)S(1)} %collective-permute-done.6.refs_1_, bf16[2,128,1280]{2,1,0:T(8,128)(2,1)S(1)} %collective-permute-done.10.refs_2_, ...), custom_call_target="tpu_custom_call" | custom-call | flops 1006632960 | bytes 5242880 | tf_op jit(solution)/shard_map/middle/pallas_call | solution.py:124
  84.4 1.9 %last0.1 = bf16[512,512]{1,0:T(8,128)(2,1)S(1)} custom-call(bf16[512,1280]{1,0:T(8,128)(2,1)S(1)} %copy-done.2, bf16[2,128,1280]{2,1,0:T(8,128)(2,1)S(1)} %collective-permute-done.5.refs_1_, bf16[2,64,1280]{2,1,0:T(8,128)(2,1)S(1)} %collective-permute-done.8.refs_2_, bf16[2,64,1280]{2,1,0:T(8,128)(2,1)S(1)} %collective-permute-done.9.refs_3_, ...), custom_call_target="tpu_custom_call" | custom-call | flops 268435456 | bytes 2097152 | tf_op jit(solution)/shard_map/last0/pallas_call | solution.py:124
  86.4 2.8 %last4.1 = bf16[512,768]{1,0:T(8,128)(2,1)S(1)} custom-call(bf16[512,1280]{1,0:T(8,128)(2,1)S(1)} %copy-done.2, bf16[2,128,1280]{2,1,0:T(8,128)(2,1)S(1)} %collective-permute-done.5.refs_1_, bf16[2,64,1280]{2,1,0:T(8,128)(2,1)S(1)} %collective-permute-done.8.refs_2_, bf16[2,64,1280]{2,1,0:T(8,128)(2,1)S(1)} %collective-permute-done.9.refs_3_, ...), custom_call_target="tpu_custom_call" | custom-call | flops 402653184 | bytes 3145728 | tf_op jit(solution)/shard_map/last4/pallas_call | solution.py:124
  89.7 2.1 %fusion.21 = f32[512,640]{1,0:T(8,128)S(1)} fusion(bf16[512,768]{1,0:T(8,128)(2,1)S(1)} %last4.1, bf16[1280,1280]{1,0:T(8,128)(2,1)} %get-tuple-element.80), kind=kOutput, calls=%fused_computation.25 | convolution fusion | flops 503316480 | bytes 3080192 | tf_op jit(solution)/shard_map/dot_general | solution.py:288
  91.9 2.0 %fusion.26 = f32[512,640]{1,0:T(8,128)S(1)} fusion(bf16[512,512]{1,0:T(8,128)(2,1)} %collective-permute-done.12, bf16[1280,1280]{1,0:T(8,128)(2,1)} %constant_dynamic-slice_fusion), kind=kOutput, calls=%fused_computation.31 | convolution fusion | flops 335544320 | bytes 2490368 | tf_op jit(solution)/shard_map/dot_general | solution.py:291
  93.9 1.9 %fusion.19 = f32[512,640]{1,0:T(8,128)S(1)} fusion(bf16[512,768]{1,0:T(8,128)(2,1)} %collective-permute-done.13, bf16[1280,1280]{1,0:T(8,128)(2,1)S(1)} %copy-done.10), kind=kOutput, calls=%fused_computation.23 | convolution fusion | flops 503316480 | bytes 3080192 | tf_op jit(solution)/shard_map/dot_general | solution.py:291
  98.0 1.6 %fusion.23 = f32[512,640]{1,0:T(8,128)S(1)} fusion(bf16[512,512]{1,0:T(8,128)(2,1)} %collective-permute-done.12, bf16[1280,1280]{1,0:T(8,128)(2,1)S(1)} %copy-done.10), kind=kOutput, calls=%fused_computation.28 | convolution fusion | flops 335544320 | bytes 2490368 | tf_op jit(solution)/shard_map/dot_general | solution.py:291
  100.4 1.9 %fusion.15 = f32[512,640]{1,0:T(8,128)S(1)} fusion(bf16[512,768]{1,0:T(8,128)(2,1)} %collective-permute-done.13, bf16[1280,1280]{1,0:T(8,128)(2,1)S(1)} %copy-done.10), kind=kOutput, calls=%fused_computation.19 | convolution fusion | flops 503316480 | bytes 3080192 | tf_op jit(solution)/shard_map/dot_general | solution.py:291
  105.4 3.0 %fusion.2 = f32[512,1280]{1,0:T(8,128)S(1)} fusion(bf16[512,768]{1,0:T(8,128)(2,1)} %collective-permute-done.13, bf16[1280,5120]{1,0:T(8,128)(2,1)} %collective-permute-done.4, s32[]{:T(128)S(6)} %add.89, s32[]{:T(128)S(6)} %select_n.116), kind=kOutput, calls=%fused_computation.4 | convolution fusion | flops 1006632960 | bytes 5373960 | tf_op jit(solution)/shard_map/dot_general | solution.py:291
  108.4 2.3 %fusion.12 = f32[512,1280]{1,0:T(8,128)S(1)} fusion(bf16[512,512]{1,0:T(8,128)(2,1)} %collective-permute-done.12, bf16[1280,5120]{1,0:T(8,128)(2,1)} %collective-permute-done.4, s32[]{:T(128)S(6)} %select_n.116), kind=kOutput, calls=%fused_computation.16 | convolution fusion | flops 671088640 | bytes 4456452 | tf_op jit(solution)/shard_map/dot_general | solution.py:291
  111.7 2.4 %collective-permute-done.14 = bf16[512,640]{1,0:T(8,128)(2,1)S(1)} collective-permute-done((bf16[512,640]{1,0:T(8,128)(2,1)S(1)}, bf16[512,640]{1,0:T(8,128)(2,1)S(1)}, u32[]{:S(2)}, u32[]{:S(2)}) %collective-permute-start.14) | collective-permute-done | bytes 655392 | tf_op jit(solution)/shard_map/ppermute | solution.py:156
  114.1 13.1 %collective-permute-done.15 = bf16[512,640]{1,0:T(8,128)(2,1)S(1)} collective-permute-done((bf16[512,640]{1,0:T(8,128)(2,1)S(1)}, bf16[512,640]{1,0:T(8,128)(2,1)S(1)}, u32[]{:S(2)}, u32[]{:S(2)}) %collective-permute-start.15) | collective-permute-done | bytes 655392 | tf_op jit(solution)/shard_map/ppermute | solution.py:156
  (99 shorter events, 28.4 us)
Async XLA Ops:
  0.0 24.1 %copy-start = (s32[8,8]{1,0:T(8,128)S(1)}, s32[8,8]{1,0:T(8,128)}, u32[]{:S(2)}) copy-start(s32[8,8]{1,0:T(8,128)} %param.16) | copy-start | bytes 772
  0.0 14.8 %copy-start.2 = (bf16[512,1280]{1,0:T(8,128)(2,1)S(1)}, bf16[512,1280]{1,0:T(8,128)(2,1)}, u32[]{:S(2)}) copy-start(bf16[512,1280]{1,0:T(8,128)(2,1)} %refs_0_.13) | copy-start | bytes 3932164
  0.0 42.2 %collective-permute-start.4 = (bf16[1280,5120]{1,0:T(8,128)(2,1)}, bf16[1280,5120]{1,0:T(8,128)(2,1)}, u32[]{:S(2)}, u32[]{:S(2)}) collective-permute-start(bf16[1280,5120]{1,0:T(8,128)(2,1)} %param.17), channel_id=1, source_target_pairs={{0,1},{1,0},{2,3},{3,2},{4,5},{5,4},{6,7},{7,6},{8,9},{9,8},{10,11... | collective-permute-start | bytes 39321608 | tf_op jit(solution)/shard_map/ppermute | solution.py:156
  2.8 12.1 %copy-start.4 = (bf16[512,1280]{1,0:T(8,128)(2,1)S(1)}, bf16[512,1280]{1,0:T(8,128)(2,1)}, u32[]{:S(2)}) copy-start(bf16[512,1280]{1,0:T(8,128)(2,1)} %refs_1_.3) | copy-start | bytes 3932164
  5.3 20.0 %copy-start.19 = (pred[2,256]{1,0:T(4,128)(4,1)S(1)}, pred[2,256]{1,0:T(4,128)(4,1)}, u32[]{:S(2)}) copy-start(pred[2,256]{1,0:T(4,128)(4,1)} %constant.80.clone) | copy-start | bytes 1540
  5.3 20.3 %copy-start.18 = (pred[4,256]{1,0:T(4,128)(4,1)S(1)}, pred[4,256]{1,0:T(4,128)(4,1)}, u32[]{:S(2)}) copy-start(pred[4,256]{1,0:T(4,128)(4,1)} %constant.86.clone) | copy-start | bytes 3076
  5.3 20.4 %copy-start.17 = (s32[256]{0:T(256)S(1)}, s32[256]{0:T(256)}, u32[]{:S(2)}) copy-start(s32[256]{0:T(256)} %constant.81.clone) | copy-start | bytes 3076
  5.3 20.4 %copy-start.16 = (s32[256]{0:T(256)S(1)}, s32[256]{0:T(256)}, u32[]{:S(2)}) copy-start(s32[256]{0:T(256)} %constant.87.clone) | copy-start | bytes 3076
  5.3 26.9 %collective-permute-start.1 = (bf16[2,128,1280]{2,1,0:T(8,128)(2,1)}, bf16[2,128,1280]{2,1,0:T(8,128)(2,1)}, u32[]{:S(2)}, u32[]{:S(2)}) collective-permute-start(bf16[2,128,1280]{2,1,0:T(8,128)(2,1)} %get-tuple-element.51), channel_id=1, source_target_pairs={{0,8},{1,9},{2,10},{3,11},{8,16},{9,17},{10,18},{11,19},{12,4},{13... | collective-permute-start | bytes 1966088 | tf_op jit(solution)/shard_map/ppermute | solution.py:156
  6.7 25.4 %collective-permute-start.2 = (bf16[2,128,1280]{2,1,0:T(8,128)(2,1)}, bf16[2,128,1280]{2,1,0:T(8,128)(2,1)S(1)}, u32[]{:S(2)}, u32[]{:S(2)}) collective-permute-start(bf16[2,128,1280]{2,1,0:T(8,128)(2,1)} %get-tuple-element.52), channel_id=1, source_target_pairs={{4,12},{5,13},{6,14},{7,15},{8,0},{9,1},{10,2},{11,3},{12,20},{13,... | collective-permute-start | bytes 1966088 | tf_op jit(solution)/shard_map/ppermute | solution.py:156
  11.3 30.9 %collective-permute-start = (bf16[2,256,1280]{2,1,0:T(8,128)(2,1)}, bf16[2,256,1280]{2,1,0:T(8,128)(2,1)}, u32[]{:S(2)}, u32[]{:S(2)}) collective-permute-start(bf16[2,256,1280]{2,1,0:T(8,128)(2,1)} %get-tuple-element.50), channel_id=1, source_target_pairs={{0,4},{1,5},{2,6},{3,7},{4,0},{5,1},{6,2},{7,3},{8,12},{9,13},{10,... | collective-permute-start | bytes 3932168 | tf_op jit(solution)/shard_map/ppermute | solution.py:156
  11.6 29.9 %collective-permute-start.3 = (bf16[2,64,1280]{2,1,0:T(8,128)(2,1)}, bf16[2,64,1280]{2,1,0:T(8,128)(2,1)}, u32[]{:S(2)}, u32[]{:S(2)}) collective-permute-start(bf16[2,64,1280]{2,1,0:T(8,128)(2,1)} %get-tuple-element.57), channel_id=1, source_target_pairs={{0,16},{1,17},{2,18},{3,19},{4,20},{5,21},{6,22},{7,23},{8,24},{9,... | collective-permute-start | bytes 983048 | tf_op jit(solution)/shard_map/ppermute | solution.py:156
  32.2 46.5 %collective-permute-start.11 = (bf16[2,128,1280]{2,1,0:T(8,128)(2,1)}, bf16[2,128,1280]{2,1,0:T(8,128)(2,1)S(1)}, u32[]{:S(2)}, u32[]{:S(2)}) collective-permute-start(bf16[2,128,1280]{2,1,0:T(8,128)(2,1)} %collective-permute-done.1.refs_1_), channel_id=1, source_target_pairs={{4,0},{5,1},{6,2},{7,3},{8,12},{9,13},{10,14},{11,15},{12,8},{13,9... | collective-permute-start | bytes 1966088 | tf_op jit(solution)/shard_map/ppermute | solution.py:156
  44.4 19.5 %collective-permute-start.6 = (bf16[2,64,1280]{2,1,0:T(8,128)(2,1)S(1)}, bf16[2,64,1280]{2,1,0:T(8,128)(2,1)S(1)}, u32[]{:S(2)}, u32[]{:S(2)}) collective-permute-start(bf16[2,64,1280]{2,1,0:T(8,128)(2,1)S(1)} %slice.46), channel_id=1, source_target_pairs={{0,8},{1,9},{2,10},{3,11},{8,16},{9,17},{10,18},{11,19},{12,4},{13... | collective-permute-start | bytes 983048 | tf_op jit(solution)/shard_map/ppermute | solution.py:156
  45.7 19.0 %collective-permute-start.7 = (bf16[2,64,1280]{2,1,0:T(8,128)(2,1)}, bf16[2,64,1280]{2,1,0:T(8,128)(2,1)S(1)}, u32[]{:S(2)}, u32[]{:S(2)}) collective-permute-start(bf16[2,64,1280]{2,1,0:T(8,128)(2,1)} %collective-permute-done.3.refs_2_), channel_id=1, source_target_pairs={{8,0},{9,1},{10,2},{11,3},{12,4},{13,5},{14,6},{15,7},{16,24},{17,... | collective-permute-start | bytes 983048 | tf_op jit(solution)/shard_map/ppermute | solution.py:156
  47.0 31.7 %collective-permute-start.10 = (bf16[2,128,1280]{2,1,0:T(8,128)(2,1)S(1)}, bf16[2,128,1280]{2,1,0:T(8,128)(2,1)S(1)}, u32[]{:S(2)}, u32[]{:S(2)}) collective-permute-start(bf16[2,128,1280]{2,1,0:T(8,128)(2,1)S(1)} %slice.47), channel_id=1, source_target_pairs={{0,8},{1,9},{2,10},{3,11},{8,16},{9,17},{10,18},{11,19},{12,4},{13... | collective-permute-start | bytes 1966088 | tf_op jit(solution)/shard_map/ppermute | solution.py:156
  49.3 35.0 %collective-permute-start.5 = (bf16[2,128,1280]{2,1,0:T(8,128)(2,1)S(1)}, bf16[2,128,1280]{2,1,0:T(8,128)(2,1)S(1)}, u32[]{:S(2)}, u32[]{:S(2)}) collective-permute-start(bf16[2,128,1280]{2,1,0:T(8,128)(2,1)S(1)} %pad_maximum_fusion), channel_id=1, source_target_pairs={{0,4},{1,5},{2,6},{3,7},{4,0},{5,1},{6,2},{7,3},{8,12},{9,13},{10,... | collective-permute-start | bytes 1966088 | tf_op jit(solution)/shard_map/ppermute | solution.py:156
  64.6 19.7 %collective-permute-start.8 = (bf16[2,64,1280]{2,1,0:T(8,128)(2,1)S(1)}, bf16[2,64,1280]{2,1,0:T(8,128)(2,1)S(1)}, u32[]{:S(2)}, u32[]{:S(2)}) collective-permute-start(bf16[2,64,1280]{2,1,0:T(8,128)(2,1)S(1)} %collective-permute-done.7.refs_3_), channel_id=1, source_target_pairs={{0,4},{1,5},{2,6},{3,7},{4,0},{5,1},{6,2},{7,3},{24,28},{25,29},{2... | collective-permute-start | bytes 983048 | tf_op jit(solution)/shard_map/ppermute | solution.py:156
  66.5 17.8 %collective-permute-start.9 = (bf16[2,64,1280]{2,1,0:T(8,128)(2,1)S(1)}, bf16[2,64,1280]{2,1,0:T(8,128)(2,1)S(1)}, u32[]{:S(2)}, u32[]{:S(2)}) collective-permute-start(bf16[2,64,1280]{2,1,0:T(8,128)(2,1)S(1)} %collective-permute-done.6.refs_1_), channel_id=1, source_target_pairs={{0,8},{1,9},{2,10},{3,11},{8,16},{9,17},{10,18},{11,19},{12,4},{13... | collective-permute-start | bytes 983048 | tf_op jit(solution)/shard_map/ppermute | solution.py:156
  86.3 5.6 %collective-permute-start.12 = (bf16[512,512]{1,0:T(8,128)(2,1)S(1)}, bf16[512,512]{1,0:T(8,128)(2,1)}, u32[]{:S(2)}, u32[]{:S(2)}) collective-permute-start(bf16[512,512]{1,0:T(8,128)(2,1)S(1)} %last0.1), channel_id=1, source_target_pairs={{0,1},{1,0},{2,3},{3,2},{4,5},{5,4},{6,7},{7,6},{8,9},{9,8},{10,11... | collective-permute-start | bytes 1572872 | tf_op jit(solution)/shard_map/ppermute | solution.py:156
  89.2 4.7 %collective-permute-start.13 = (bf16[512,768]{1,0:T(8,128)(2,1)S(1)}, bf16[512,768]{1,0:T(8,128)(2,1)}, u32[]{:S(2)}, u32[]{:S(2)}) collective-permute-start(bf16[512,768]{1,0:T(8,128)(2,1)S(1)} %last4.1), channel_id=1, source_target_pairs={{0,1},{1,0},{2,3},{3,2},{4,5},{5,4},{6,7},{7,6},{8,9},{9,8},{10,11... | collective-permute-start | bytes 2359304 | tf_op jit(solution)/shard_map/ppermute | solution.py:156
  96.4 17.7 %collective-permute-start.14 = (bf16[512,640]{1,0:T(8,128)(2,1)S(1)}, bf16[512,640]{1,0:T(8,128)(2,1)S(1)}, u32[]{:S(2)}, u32[]{:S(2)}) collective-permute-start(bf16[512,640]{1,0:T(8,128)(2,1)S(1)} %fusion.10), channel_id=1, source_target_pairs={{0,2},{1,3},{2,0},{3,1},{4,6},{5,7},{6,4},{7,5},{8,10},{9,11},{10,... | collective-permute-start | bytes 1966088 | tf_op jit(solution)/shard_map/ppermute | solution.py:156
  102.9 24.2 %collective-permute-start.15 = (bf16[512,640]{1,0:T(8,128)(2,1)S(1)}, bf16[512,640]{1,0:T(8,128)(2,1)S(1)}, u32[]{:S(2)}, u32[]{:S(2)}) collective-permute-start(bf16[512,640]{1,0:T(8,128)(2,1)S(1)} %fusion.11), channel_id=1, source_target_pairs={{0,2},{1,3},{2,0},{3,1},{4,6},{5,7},{6,4},{7,5},{8,10},{9,11},{10,... | collective-permute-start | bytes 1966088 | tf_op jit(solution)/shard_map/ppermute | solution.py:156
  110.8 17.8 %copy-start.1 = (s32[8,8]{1,0:T(8,128)S(1)}, s32[8,8]{1,0:T(8,128)}, u32[]{:S(2)}) copy-start(s32[8,8]{1,0:T(8,128)} %param.16) | copy-start | bytes 772
  (12 other events, 51.3 us)
